TPU v7x, 32 devices: a whole 2x2x4 slice. The times are simulated.
32 devices in a mesh: shard: 4 (over y, core), ctx: 4 (over z), tp: 2 (over x).
Axes of the slice: x: 2, y: 2, z: 4, core: 2. Of those that a mesh axis runs over, the one named last changes fastest.
Arguments:
- tokens: bfloat16 [8, 1024, 768], P('shard', 'ctx'), may hold values from -4 to 4
- lengths: int32 [8], P('shard'), may hold values from 256 to 1024, as said below
- w_qkv: float32 [768, 3, 768], P(('shard', 'ctx'), None, 'tp'), may hold values from -0.21875 to 0.21875
- b_qv: float32 [2, 768], P(None, 'tp'), may hold values from -3 to 3
- w_out: float32 [768, 768], P('tp', ('shard', 'ctx')), may hold values from -0.625 to 0.625
- w_gu: float32 [768, 2, 3072], P(('shard', 'ctx'), None, 'tp'), may hold values from -0.21875 to 0.21875
- w_down: float32 [3072, 768], P('tp', ('shard', 'ctx')), may hold values from -0.109375 to 0.109375
- vectors: float32 [6, 768], replicated, may hold values from 0.25 to 1.75
- cotangent: bfloat16 [8, 1024, 768], P('shard', 'ctx'), may hold values from -6 to 6
Outputs:
- output: bfloat16 [8, 1024, 768], P('shard', 'ctx')
- input_grad: float32 [8, 1024, 768], P('shard', 'ctx')
- grad_qkv: float32 [768, 3, 768], P(('shard', 'ctx'), None, 'tp')
- grad_bqv: float32 [2, 768], P(None, 'tp')
- grad_out: float32 [768, 768], P('tp', ('shard', 'ctx'))
- grad_gu: float32 [768, 2, 3072], P(('shard', 'ctx'), None, 'tp')
- grad_down: float32 [3072, 768], P('tp', ('shard', 'ctx'))
- grad_vectors: float32 [6, 768], replicated
Inputs may be any that keep to these rules, and one draw needn't show every extreme that they name: `lengths`: sequence 0 has all 1024 slots valid and sequence 1 has 256.
All inputs are finite; a program needn't handle non-finite values.
Results may differ from a plain program's by a relative error of at most 0.018.
Values may be sent and summed in bfloat16 or wider, within the bound.
No kernel may reach another device: no remote copies, remote signals or barrier semaphores. Data moves between devices by JAX's collectives and lax.ppermute only.
A program may use at most 128 MiB of HBM per device.

v0:
```python
import math

import jax
import jax.numpy as jnp
from jax import lax
from jax.sharding import PartitionSpec as P

H = 12
HD = 64


epsilon = 1e-12


def alibi_slopes(first_head, head_count):
    power = 2 ** (H.bit_length() - 1)
    heads_index = first_head + jnp.arange(head_count, dtype=jnp.int32)
    early = -8.0 * (heads_index + 1).astype(jnp.float32) / power
    later = -4.0 * (2 * (heads_index - power) + 1).astype(jnp.float32) / power
    return jnp.exp2(jnp.where(heads_index < power, early, later))


def layer_norm(values, gain, shift):
    centred = values - jnp.mean(values, axis=-1, keepdims=True)
    spread = jnp.mean(centred * centred, axis=-1, keepdims=True)
    return centred * lax.rsqrt(spread + epsilon) * gain + shift


def gated_unit(gate_input, upper):
    return jax.nn.gelu(gate_input, approximate=False) * upper


def score_block(query_heads, key_heads, query_place, key_place, slopes, lengths):
    scores = (
        jnp.einsum("sqhe,skhe->shqk", query_heads, key_heads, preferred_element_type=jnp.float32)
        * 0.125
    )
    distance = jnp.abs(query_place[:, None] - key_place[None, :]).astype(jnp.float32)
    scores = scores - slopes[None, :, None, None] * distance[None, None]
    usable = key_place[None, :] < lengths[:, None]
    return jnp.where(usable[:, None, None, :], jnp.exp(scores), 0.0)


def backward_scores(
    query_heads,
    numer_heads,
    correction,
    key_heads,
    value_heads,
    query_place,
    key_place,
    slopes,
    lengths,
):
    weights = score_block(query_heads, key_heads, query_place, key_place, slopes, lengths)
    value_dots = jnp.einsum(
        "sqhe,skhe->shqk", numer_heads, value_heads, preferred_element_type=jnp.float32
    )
    grad_scores = (weights * (value_dots - correction[..., None])).astype(jnp.bfloat16)
    return (weights.astype(jnp.bfloat16), grad_scores)


def split_blocks(shard_piece, slot_count, ctx_count):
    piece_rows = shard_piece.shape[1]
    block_rows = math.gcd(piece_rows, 128)
    block_count = piece_rows // block_rows
    shaped = shard_piece.reshape(
        (shard_piece.shape[0], block_count, block_rows) + shard_piece.shape[2:]
    )
    blocks = jnp.moveaxis(shaped, 1, 0)
    row_ids = jnp.arange(piece_rows, dtype=jnp.int32)
    places = (row_ids % slot_count * ctx_count + row_ids // slot_count).reshape(
        block_count, block_rows
    )
    offsets = block_rows * jnp.arange(block_count, dtype=jnp.int32)
    return (blocks, places, offsets)


def on_device(tokens, lengths, w_qkv, b_qv, w_out, w_gu, w_down, vectors, cotangent):
    ctx_count = lax.axis_size("ctx")
    ctx_rank = lax.axis_index("ctx")
    seq_count, slot_count, model_width = tokens.shape
    local_width = b_qv.shape[1]
    head_count = local_width // HD
    slopes = alibi_slopes(lax.axis_index("tp") * head_count, head_count)
    slot_ids = jnp.arange(slot_count, dtype=jnp.int32)
    query_place = slot_ids * ctx_count + ctx_rank
    query_live = (query_place[None, :] < lengths[:, None]).astype(jnp.float32)
    live_rows = query_live[:, :, None]
    head_shape = (seq_count, slot_count, head_count, HD)
    whole_qkv, whole_out, whole_gu, whole_down = (
        lax.all_gather(w_qkv.astype(jnp.bfloat16), ("shard", "ctx"), axis=0, tiled=True),
        lax.all_gather(w_out.astype(jnp.bfloat16), ("shard", "ctx"), axis=1, tiled=True),
        lax.all_gather(w_gu.astype(jnp.bfloat16), ("shard", "ctx"), axis=0, tiled=True),
        lax.all_gather(w_down.astype(jnp.bfloat16), ("shard", "ctx"), axis=1, tiled=True),
    )
    inputs = tokens.astype(jnp.float32)
    projected = jnp.einsum("std,dcm->stcm", tokens, whole_qkv, preferred_element_type=jnp.float32)
    query_rows = (projected[:, :, 0] + b_qv[0]).astype(jnp.bfloat16)
    key_rows = projected[:, :, 1].astype(jnp.bfloat16)
    value_rows = (projected[:, :, 2] + b_qv[1]).astype(jnp.bfloat16)
    query_heads = query_rows.reshape(head_shape)
    pairs = jnp.stack([key_rows, value_rows], axis=2)
    start_numer = jnp.zeros((seq_count, head_count, slot_count, HD), jnp.float32)
    start_denom = jnp.zeros((seq_count, head_count, slot_count), jnp.float32)
    blocks, places, offsets = split_blocks(
        lax.all_gather(pairs, "ctx", axis=1, tiled=True), slot_count, ctx_count
    )

    def forward_advance(inner_state, block_item):
        key_block, key_place, row_offset = block_item
        numerator, denominator = inner_state
        key_heads = key_block[:, :, 0].reshape(seq_count, -1, head_count, HD)
        value_heads = key_block[:, :, 1].reshape(seq_count, -1, head_count, HD)
        weights = score_block(query_heads, key_heads, query_place, key_place, slopes, lengths)
        numerator = numerator + jnp.einsum(
            "shqk,skhe->shqe",
            weights.astype(jnp.bfloat16),
            value_heads,
            preferred_element_type=jnp.float32,
        )
        return ((numerator, denominator + jnp.sum(weights, axis=-1)), None)

    result_state, unused = lax.scan(
        forward_advance, (start_numer, start_denom), (blocks, places, offsets)
    )
    numerator, denominator = result_state
    denominator = denominator + (1.0 - query_live)[:, None, :]
    attention_q = jnp.transpose(numerator / denominator[..., None], (0, 2, 1, 3))
    denom_q = jnp.transpose(denominator, (0, 2, 1))
    mixed = attention_q.reshape(seq_count, slot_count, local_width).astype(jnp.bfloat16)
    attn_part = jnp.einsum("stm,mn->stn", mixed, whole_out, preferred_element_type=jnp.float32)
    attn_branch = lax.psum(attn_part, "tp") + vectors[4]
    hidden, first_pull = jax.vjp(layer_norm, inputs + attn_branch, vectors[0], vectors[1])
    hidden_low = hidden.astype(jnp.bfloat16)
    gated = jnp.einsum("std,dcf->stcf", hidden_low, whole_gu, preferred_element_type=jnp.float32)
    activated, unit_pull = jax.vjp(gated_unit, gated[:, :, 0], gated[:, :, 1])
    act_low = activated.astype(jnp.bfloat16)
    ffn_part = jnp.einsum("stf,fn->stn", act_low, whole_down, preferred_element_type=jnp.float32)
    ffn_branch = lax.psum(ffn_part, "tp") + vectors[5]
    normed, second_pull = jax.vjp(layer_norm, hidden + ffn_branch, vectors[2], vectors[3])
    output = (normed * live_rows).astype(jnp.bfloat16)
    upstream = cotangent.astype(jnp.float32) * live_rows
    grad_second, grad_gain_two, grad_shift_two = second_pull(upstream)
    grad_ffn = grad_second.astype(jnp.bfloat16)
    grad_down = jnp.einsum("stf,stn->fn", act_low, grad_ffn, preferred_element_type=jnp.float32)
    grad_ffn_bias = jnp.sum(grad_ffn.astype(jnp.float32), axis=(0, 1))
    grad_act = jnp.einsum("stn,fn->stf", grad_ffn, whole_down, preferred_element_type=jnp.float32)
    grad_gate, grad_upper = unit_pull(grad_act)
    grad_gated = jnp.stack([grad_gate, grad_upper], axis=2).astype(jnp.bfloat16)
    grad_gu = jnp.einsum(
        "std,stcf->dcf", hidden_low, grad_gated, preferred_element_type=jnp.float32
    )
    hidden_part = jnp.einsum(
        "stcf,dcf->std", grad_gated, whole_gu, preferred_element_type=jnp.float32
    )
    grad_hidden = grad_second + lax.psum(hidden_part, "tp")
    grad_first, grad_gain_one, grad_shift_one = first_pull(grad_hidden)
    grad_attn = grad_first.astype(jnp.bfloat16)
    grad_out = jnp.einsum("stm,stn->mn", mixed, grad_attn, preferred_element_type=jnp.float32)
    grad_out_bias = jnp.sum(grad_attn.astype(jnp.float32), axis=(0, 1))
    grad_mixed = jnp.einsum(
        "stn,mn->stm", grad_attn, whole_out, preferred_element_type=jnp.float32
    ).astype(jnp.bfloat16)
    grad_mixed_heads = grad_mixed.reshape(head_shape).astype(jnp.float32)
    correction = jnp.transpose(
        jnp.sum(grad_mixed_heads * attention_q, axis=-1) / denom_q, (0, 2, 1)
    )
    numer_heads = (grad_mixed_heads / denom_q[..., None]).astype(jnp.bfloat16)
    start_query = jnp.zeros(head_shape, jnp.float32)
    start_state = (
        start_query,
        jnp.zeros((seq_count, slot_count * ctx_count, 2, local_width), jnp.float32),
    )
    blocks, places, offsets = split_blocks(
        lax.all_gather(pairs, "ctx", axis=1, tiled=True), slot_count, ctx_count
    )

    def backward_advance(current_state, block_item):
        key_block, key_place, row_offset = block_item
        key_heads = key_block[:, :, 0].reshape(seq_count, -1, head_count, HD)
        value_heads = key_block[:, :, 1].reshape(seq_count, -1, head_count, HD)
        weights_low, grad_scores = backward_scores(
            query_heads,
            numer_heads,
            correction,
            key_heads,
            value_heads,
            query_place,
            key_place,
            slopes,
            lengths,
        )
        grad_query = current_state[0] + jnp.einsum(
            "shqk,skhe->sqhe", grad_scores, key_heads, preferred_element_type=jnp.float32
        )
        grad_key = (
            jnp.einsum(
                "shqk,sqhe->skhe", grad_scores, query_heads, preferred_element_type=jnp.float32
            )
            * 0.125
        )
        grad_value = jnp.einsum(
            "shqk,sqhe->skhe", weights_low, numer_heads, preferred_element_type=jnp.float32
        )
        stacked = jnp.stack(
            [
                grad_key.reshape(seq_count, -1, local_width),
                grad_value.reshape(seq_count, -1, local_width),
            ],
            axis=2,
        )
        buffer = lax.dynamic_update_slice_in_dim(current_state[1], stacked, row_offset, axis=1)
        return ((grad_query, buffer), None)

    result_state, unused = lax.scan(backward_advance, start_state, (blocks, places, offsets))
    grad_pairs = lax.psum_scatter(
        result_state[1].astype(jnp.bfloat16), "ctx", scatter_dimension=1, tiled=True
    )
    grad_query_low = (
        (result_state[0] * 0.125).astype(jnp.bfloat16).reshape(seq_count, slot_count, local_width)
    )
    grad_proj = jnp.concatenate([grad_query_low[:, :, None], grad_pairs], axis=2)
    grad_qkv = jnp.einsum("std,stcm->dcm", tokens, grad_proj, preferred_element_type=jnp.float32)
    bias_terms = jnp.stack(
        [
            jnp.sum(grad_query_low.astype(jnp.float32), axis=(0, 1)),
            jnp.sum(grad_pairs[:, :, 1].astype(jnp.float32), axis=(0, 1)),
        ]
    )
    input_part = jnp.einsum(
        "stcm,dcm->std", grad_proj, whole_qkv, preferred_element_type=jnp.float32
    )
    input_grad = grad_first + lax.psum(input_part.astype(jnp.bfloat16), "tp").astype(jnp.float32)
    grad_weights = (
        lax.psum_scatter(grad_qkv, ("shard", "ctx"), scatter_dimension=0, tiled=True),
        lax.psum_scatter(grad_out, ("shard", "ctx"), scatter_dimension=1, tiled=True),
        lax.psum_scatter(grad_gu, ("shard", "ctx"), scatter_dimension=0, tiled=True),
        lax.psum_scatter(grad_down, ("shard", "ctx"), scatter_dimension=1, tiled=True),
    )
    vector_terms = jnp.stack(
        [grad_gain_one, grad_shift_one, grad_gain_two, grad_shift_two, grad_out_bias, grad_ffn_bias]
    )
    grad_bqv, grad_vectors = lax.psum((bias_terms, vector_terms), ("shard", "ctx"))
    return (
        output,
        input_grad,
        grad_weights[0],
        grad_bqv,
        grad_weights[1],
        grad_weights[2],
        grad_weights[3],
        grad_vectors,
    )


def solution(mesh):
    placed = (
        P("shard", "ctx", None),
        P("shard"),
        P(("shard", "ctx"), None, "tp"),
        P(None, "tp"),
        P("tp", ("shard", "ctx")),
        P(("shard", "ctx"), None, "tp"),
        P("tp", ("shard", "ctx")),
        P(),
        P("shard", "ctx", None),
    )
    return jax.shard_map(
        on_device,
        mesh=mesh,
        in_specs=placed,
        out_specs=(
            P("shard", "ctx", None),
            P("shard", "ctx", None),
            P(("shard", "ctx"), None, "tp"),
            P(None, "tp"),
            P("tp", ("shard", "ctx")),
            P(("shard", "ctx"), None, "tp"),
            P("tp", ("shard", "ctx")),
            P(),
        ),
        check_vma=False,
    )
```

profile of v0, /device:TPU:0, one launch (start us, length us, event | category | flops | bytes accessed | tf_op | source)
XLA Modules:
  0.0 1021.4 jit_solution(10620313028883199364)
XLA Ops:
  9.7 44.3 %all-gather.5.cloned.1.call-done = bf16[768,3,384]{2,0,1:T(8,128)(2,1)} async-done(((bf16[48,3,384]{2,0,1:T(8,128)(2,1)}), bf16[768,3,384]{2,0,1:T(8,128)(2,1)}) %all-gather.5.cloned.1.call-update) | async-done | bytes 1769488 | tf_op jit(solution)/shard_map/all_gather | solution.py:92
  60.1 47.1 %all_gather.18 = bf16[384,768]{0,1:T(8,128)(2,1)S(1)} all-gather(bf16[384,48]{0,1:T(8,128)(2,1)S(1)} %convert_element_type.137), channel_id=1, replica_groups=mesh['shard'=4,'ctx'=4,'tp'=2] {'shard','ctx'}, dimensions={1}, use_global_device_ids=true | all-gather | bytes 626688 | tf_op jit(solution)/shard_map/all_gather | solution.py:93
  107.6 22.3 %all-gather.7.cloned.1.call-done = bf16[2,1024,2,384]{3,1,2,0:T(8,128)(2,1)} async-done(((bf16[2,256,2,384]{3,1,2,0:T(8,128)(2,1)}), bf16[2,1024,2,384]{3,1,2,0:T(8,128)(2,1)}) %all-gather.7.cloned.1.call-update) | async-done | bytes 3145744 | tf_op jit(solution)/shard_map/all_gather | solution.py:107
  129.9 4.7 copy.62
  134.6 29.5 %while.26 = (s32[]{:T(128)}, f32[2,6,256,64]{2,3,1,0:T(8,128)S(1)}, f32[2,6,256]{2,1,0:T(8,128)S(1)}, s32[8,128]{1,0:T(8,128)}, s32[2]{0:T(128)}, /*index=5*/bf1...) while((s32[]{:T(128)}, f32[2,6,256,64]{2,3,1,0:T(8,128)S(1)}, ...), condition=%wide.region_2.3_spmd.clone, body=%wide.region_0.2_spmd.clone.sunk | while | flops 103321416 | bytes 7393984 | solution.py:124
  168.9 48.1 %all-reduce.8.cloned.1.call-done = f32[2,256,768]{2,1,0:T(8,128)} async-done(((f32[2,256,768]{2,1,0:T(8,128)}), f32[2,256,768]{2,1,0:T(8,128)}) %all-reduce.8.cloned.1.call-update) | async-done | bytes 1572880 | tf_op jit(solution)/shard_map/psum | solution.py:133
  219.0 53.9 %all-gather.9.cloned.1.call-done = bf16[768,2,1536]{2,0,1:T(8,128)(2,1)} async-done(((bf16[48,2,1536]{2,0,1:T(8,128)(2,1)}), bf16[768,2,1536]{2,0,1:T(8,128)(2,1)}) %all-gather.9.cloned.1.call-update) | async-done | bytes 4718608 | tf_op jit(solution)/shard_map/all_gather | solution.py:94
  273.0 4.7 fusion.23
  280.3 7.7 multiply_convert_fusion.1
  288.0 28.5 %all-gather.11.cloned.1.call-done = bf16[1536,768]{0,1:T(8,128)(2,1)} async-done(((bf16[1536,48]{0,1:T(8,128)(2,1)}), bf16[1536,768]{0,1:T(8,128)(2,1)}) %all-gather.11.cloned.1.call-update) | async-done | bytes 2359312 | tf_op jit(solution)/shard_map/all_gather | solution.py:95
  316.6 4.2 fusion.48
  322.8 48.5 %all-reduce.10.cloned.1.call-done = f32[2,256,768]{2,1,0:T(8,128)} async-done(((f32[2,256,768]{2,1,0:T(8,128)}), f32[2,256,768]{2,1,0:T(8,128)}) %all-reduce.10.cloned.1.call-update) | async-done | bytes 1572880 | tf_op jit(solution)/shard_map/psum | solution.py:140
  383.5 3.8 fusion.60
  389.2 49.7 %all-reduce.12.cloned.1.call-done = f32[2,256,768]{2,1,0:T(8,128)} async-done(((f32[2,256,768]{2,1,0:T(8,128)}), f32[2,256,768]{2,1,0:T(8,128)}) %all-reduce.12.cloned.1.call-update) | async-done | bytes 1572880 | tf_op jit(solution)/shard_map/psum | solution.py:157
  439.0 4.4 multiply_reduce_fusion.1
  449.4 88.8 %while.27 = (s32[]{:T(128)}, f32[2,256,6,64]{1,3,2,0:T(8,128)S(1)}, bf16[2,1024,2,384]{3,1,2,0:T(8,128)(2,1)}, bf16[8,2,128,2,384]{2,4,1,3,0:T(8,128)(2,1)}, s32...) while((s32[]{:T(128)}, f32[2,256,6,64]{1,3,2,0:T(8,128)S(1)}, ...), condition=%wide.region_16.17_spmd.clone, body=%wide.region_15.16_spmd.clone.sunk | while | flops 255492928 | bytes 16990992 | solution.py:216
  467.8 3.6 dynamic_update_slice.5
  479.0 3.6 dynamic_update_slice.5
  490.2 3.6 dynamic_update_slice.5
  501.3 3.6 dynamic_update_slice.5
  512.5 3.6 dynamic_update_slice.5
  523.7 3.6 dynamic_update_slice.5
  538.8 59.9 %reduce-scatter.5.cloned.1.call-done = bf16[2,256,2,384]{3,1,2,0:T(8,128)(2,1)} async-done(((bf16[2,1024,2,384]{3,1,2,0:T(8,128)(2,1)}), bf16[2,256,2,384]{3,1,2,0:T(8,128)(2,1)}) %reduce-scatter.5.cloned.1.call-update) | async-done | bytes 786448 | tf_op jit(solution)/shard_map/reduce_scatter | solution.py:217
  598.7 3.9 bitcast_convert_fusion
  605.6 6.3 copy.71
  613.8 7.9 convolution_bitcast_fusion.1
  624.7 3.6 convolution_bitcast_fusion.2
  630.6 62.4 %all-reduce.1 = (f32[2,384]{1,0:T(2,128)}, f32[6,768]{1,0:T(8,128)}) all-reduce(f32[2,384]{1,0:T(2,128)S(1)} %pad_maximum_fusion.10, f32[6,768]{1,0:T(8,128)S(1)} %stack.63), channel_id=1, replica_groups=mesh['shard'=4,'ctx'=4,'tp'=2] {'shard','ctx'}, use_global_device_ids=true, to_apply=%region_22.23 | all-reduce | flops 5376 | bytes 43008 | tf_op jit(solution)/shard_map/psum | solution.py:244
  695.6 63.3 %all-reduce.16.cloned.1.call-done = f32[768,3,384]{2,1,0:T(4,128)} async-done(((f32[768,3,384]{2,1,0:T(4,128)}), f32[768,3,384]{2,1,0:T(4,128)}) %all-reduce.16.cloned.1.call-update) | async-done | bytes 3538960
  760.6 113.3 %reduce-scatter.9.cloned.1.call-done = f32[48,2,1536]{2,0,1:T(8,128)} async-done(((f32[768,2,1536]{2,0,1:T(8,128)}), f32[48,2,1536]{2,0,1:T(8,128)}) %reduce-scatter.9.cloned.1.call-update) | async-done | bytes 589840 | tf_op jit(solution)/shard_map/reduce_scatter | solution.py:238
  876.3 59.6 %reduce-scatter.7.cloned.1.call-done = f32[384,48]{0,1:T(8,128)} async-done(((f32[384,768]{0,1:T(8,128)}), f32[384,48]{0,1:T(8,128)}) %reduce-scatter.7.cloned.1.call-update) | async-done | bytes 73744 | tf_op jit(solution)/shard_map/reduce_scatter | solution.py:237
  935.8 79.1 %reduce-scatter.11.cloned.1.call-done = f32[1536,48]{0,1:T(8,128)} async-done(((f32[1536,768]{0,1:T(8,128)}), f32[1536,48]{0,1:T(8,128)}) %reduce-scatter.11.cloned.1.call-update) | async-done | bytes 294928 | tf_op jit(solution)/shard_map/reduce_scatter | solution.py:239
  (457 shorter events, 136.4 us)
Async XLA Ops:
  7.2 46.8 %all-gather.5.cloned.1.call-start = ((), (), s32[]{:S(2)}) async-start(), calls=%async_computation.4 | async-start | bytes 1880064 | tf_op jit(solution)/shard_map/all_gather | solution.py:92
  8.8 121.1 %all-gather.7.cloned.1.call-start = ((), (), s32[]{:S(2)}) async-start(), calls=%async_computation.5 | async-start | bytes 3932160 | tf_op jit(solution)/shard_map/all_gather | solution.py:107
  58.1 158.9 %all-reduce.8.cloned.1.call-start = ((), (), s32[]{:S(2)}) async-start(), calls=%async_computation.6 | async-start | bytes 3145728 | tf_op jit(solution)/shard_map/psum | solution.py:133
  58.2 49.3 %copy-start.60 = (s32[256]{0:T(256)}, s32[256]{0:T(256)S(1)}, u32[]{:S(2)}) copy-start(s32[256]{0:T(256)S(1)} %multiply_add_fusion.6) | copy-start | bytes 3076
  107.2 56.9 %copy-start.11 = (bf16[384,768]{0,1:T(8,128)(2,1)}, bf16[384,768]{0,1:T(8,128)(2,1)S(1)}, u32[]{:S(2)}) copy-start(bf16[384,768]{0,1:T(8,128)(2,1)S(1)} %all_gather.18) | copy-start | bytes 1769476
  134.6 29.5 %copy-start.42 = (f32[2,256]{1,0:T(2,128)S(1)}, f32[2,256]{1,0:T(2,128)}, u32[]{:S(2)}) copy-start(f32[2,256]{1,0:T(2,128)} %broadcast_subtract_fusion) | copy-start | bytes 6148
  166.5 50.5 %copy-start.18 = (bf16[2,256,768]{2,1,0:T(8,128)(2,1)S(1)}, bf16[2,256,768]{2,1,0:T(8,128)(2,1)}, u32[]{:S(2)}) copy-start(bf16[2,256,768]{2,1,0:T(8,128)(2,1)} %param.13) | copy-start | bytes 2359300
  166.6 106.4 %all-gather.9.cloned.1.call-start = ((), (), s32[]{:S(2)}) async-start(), calls=%async_computation.7 | async-start | bytes 5013504 | tf_op jit(solution)/shard_map/all_gather | solution.py:94
  167.5 149.1 %all-gather.11.cloned.1.call-start = ((), (), s32[]{:S(2)}) async-start(), calls=%async_computation.8 | async-start | bytes 2506752 | tf_op jit(solution)/shard_map/all_gather | solution.py:95
  168.2 203.0 %all-reduce.10.cloned.1.call-start = ((), (), s32[]{:S(2)}) async-start(), calls=%async_computation.9 | async-start | bytes 3145728 | tf_op jit(solution)/shard_map/psum | solution.py:140
  168.9 104.0 %copy-start.30 = (f32[768]{0:T(1024)}, f32[768]{0:T(1024)S(1)}, u32[]{:S(2)}) copy-start(f32[768]{0:T(1024)S(1)} %get-tuple-element.239) | copy-start | bytes 9220
  168.9 104.0 %copy-start.57 = (f32[768]{0:T(1024)}, f32[768]{0:T(1024)S(1)}, u32[]{:S(2)}) copy-start(f32[768]{0:T(1024)S(1)} %get-tuple-element.238) | copy-start | bytes 9220
  218.7 224.7 %copy-start = (f32[2,256,768]{2,1,0:T(8,128)}, f32[2,256,768]{2,1,0:T(8,128)S(1)}, u32[]{:S(2)}) copy-start(f32[2,256,768]{2,1,0:T(8,128)S(1)} %get-tuple-element.302) | copy-start | bytes 4718596
  218.7 54.3 %copy-start.34 = (f32[2,256]{1,0:T(2,128)}, f32[2,256]{1,0:T(2,128)S(1)}, u32[]{:S(2)}) copy-start(f32[2,256]{1,0:T(2,128)S(1)} %broadcast_multiply_fusion.3) | copy-start | bytes 6148
  219.0 53.9 %copy-start.48 = (f32[2,256]{1,0:T(2,128)}, f32[2,256]{1,0:T(2,128)S(1)}, u32[]{:S(2)}) copy-start(f32[2,256]{1,0:T(2,128)S(1)} %multiply_reduce_fusion.5) | copy-start | bytes 6148
  219.0 53.9 %copy-start.39 = (f32[2,256]{1,0:T(2,128)}, f32[2,256]{1,0:T(2,128)S(1)}, u32[]{:S(2)}) copy-start(f32[2,256]{1,0:T(2,128)S(1)} %fusion.83) | copy-start | bytes 6148
  288.0 32.8 %copy-start.16 = (bf16[2,256,1536]{2,1,0:T(8,128)(2,1)}, bf16[2,256,1536]{2,1,0:T(8,128)(2,1)S(1)}, u32[]{:S(2)}) copy-start(bf16[2,256,1536]{2,1,0:T(8,128)(2,1)S(1)} %get-tuple-element.299) | copy-start | bytes 4718596
  320.8 118.2 %all-reduce.12.cloned.1.call-start = ((), (), s32[]{:S(2)}) async-start(), calls=%async_computation.10 | async-start | bytes 3145728 | tf_op jit(solution)/shard_map/psum | solution.py:157
  371.2 7.0 slice-start
  373.4 4.9 slice-start.1
  377.0 6.5 slice-start.2
  379.0 4.5 slice-start.3
  387.3 211.4 %reduce-scatter.5.cloned.1.call-start = ((), (), s32[]{:S(2)}) async-start(), calls=%async_computation.11 | async-start | bytes 3932160 | tf_op jit(solution)/shard_map/reduce_scatter | solution.py:217
  439.0 4.4 copy-start.40
  538.2 154.9 %all-reduce.14.cloned.1.call-start = ((), (), s32[]{:S(2)}) async-start(), calls=%async_computation.12 | async-start | bytes 1572864 | tf_op jit(solution)/shard_map/psum | solution.py:234
  538.8 63.9 %copy-start.19 = (bf16[2,256,768]{2,1,0:T(8,128)(2,1)S(1)}, bf16[2,256,768]{2,1,0:T(8,128)(2,1)}, u32[]{:S(2)}) copy-start(bf16[2,256,768]{2,1,0:T(8,128)(2,1)} %param.13) | copy-start | bytes 2359300
  602.7 156.2 %all-reduce.16.cloned.1.call-start = ((), (), s32[]{:S(2)}) async-start(), calls=%async_computation.16 | async-start | bytes 9437184
  612.0 261.9 %reduce-scatter.9.cloned.1.call-start = ((), (), s32[]{:S(2)}) async-start(), calls=%async_computation.14 | async-start | bytes 10027008 | tf_op jit(solution)/shard_map/reduce_scatter | solution.py:238
  621.8 314.0 %reduce-scatter.7.cloned.1.call-start = ((), (), s32[]{:S(2)}) async-start(), calls=%async_computation.13 | async-start | bytes 1253376 | tf_op jit(solution)/shard_map/reduce_scatter | solution.py:237
  624.7 390.2 %reduce-scatter.11.cloned.1.call-start = ((), (), s32[]{:S(2)}) async-start(), calls=%async_computation.15 | async-start | bytes 5013504 | tf_op jit(solution)/shard_map/reduce_scatter | solution.py:239
  628.4 64.6 %copy-start.6 = (f32[2,256,768]{2,1,0:T(8,128)S(1)}, f32[2,256,768]{2,1,0:T(8,128)}, u32[]{:S(2)}) copy-start(f32[2,256,768]{2,1,0:T(8,128)} %copy-done.5) | copy-start | bytes 4718596
  628.4 64.6 %copy-start.47 = (f32[2,256]{1,0:T(2,128)S(1)}, f32[2,256]{1,0:T(2,128)}, u32[]{:S(2)}) copy-start(f32[2,256]{1,0:T(2,128)} %copy-done.46) | copy-start | bytes 6148
  (53 other events, 104.5 us)
Sparse Core Ops, SparseCore 0:
  10.8 43.1 all-gather.4
  58.2 71.6 all-gather.6
  166.7 50.2 all-reduce.7
  219.8 53.1 all-gather.8
  275.7 40.8 all-gather.10
  321.0 50.2 all-reduce.9
  387.4 51.5 all-reduce.11
  538.3 60.3 reduce-scatter.4
  602.8 34.2 all-reduce.13
  640.6 118.2 all-reduce.15
  763.0 110.8 reduce-scatter.8
  878.0 57.8 reduce-scatter.6
  940.2 74.5 reduce-scatter.10
where the time goes:
time: 1020 us
  waiting for transfers between devices  671 us (66%)
  blocking collectives  109 us (11%)
  local copies, waits for them, and re-layouts  94.3 us (9%)
  matrix products  63.8 us (6%)
  other arithmetic  49.9 us (5%)
  loops' own time  16.9 us (2%)
  between operations  15.4 us (2%)
    reduce_scatter x1, waiting for transfers between devices, on_device(): lax.psum_scatter(grad_gu, ('shard', 'ctx'), scatter_dimension=0, tiled=True)  113 us
    reduce_scatter x1, waiting for transfers between devices, on_device(): lax.psum_scatter(grad_down, ('shard', 'ctx'), scatter_dimension=1, tiled=...  79.1 us
    unnamed x14, waiting for transfers between devices  63.5 us
    psum x1, blocking collectives, on_device(): lax.psum((bias_terms, vector_terms), ('shard', 'ctx'))  62.4 us
    reduce_scatter x1, waiting for transfers between devices, on_device(): lax.psum_scatter(result_state[1].astype(jnp.bfloat16), 'ctx', scatter_dim...  59.9 us
    reduce_scatter x1, waiting for transfers between devices, on_device(): lax.psum_scatter(grad_out, ('shard', 'ctx'), scatter_dimension=1, tiled=T...  59.6 us
    all_gather x1, waiting for transfers between devices, on_device(): lax.all_gather(w_gu.astype(jnp.bfloat16), ('shard', 'ctx'), axis=0, tiled...  53.9 us
    psum x1, waiting for transfers between devices, on_device(): grad_hidden = grad_second + lax.psum(hidden_part, 'tp')  49.7 us
  transfers between devices with their start and end apart: 13, of which 12 were waited for; matrix products, arithmetic and copies ran while one was open for 5% of the time, Pallas kernels for 0%

commit v1 on v0

--- a/solution.py
+++ b/solution.py
@@ -1,15 +1,751 @@
+import functools
 import math
 
 import jax
 import jax.numpy as jnp
+import numpy as np
 from jax import lax
+from jax.experimental import pallas as pl
+from jax.experimental.pallas import tpu as pltpu
 from jax.sharding import PartitionSpec as P
 
 H = 12
 HD = 64
-
+LOG2E = math.log2(math.e)
+FAR = 1e30
+TILE = 64
+BLOCK = 384
 
 epsilon = 1e-12
+f32 = jnp.float32
+bf16 = jnp.bfloat16
+VMEM = pl.BlockSpec(memory_space=pltpu.VMEM)
+SMEM = pl.BlockSpec(memory_space=pltpu.SMEM)
+
+
+def slope_table():
+    power = 2 ** (H.bit_length() - 1)
+    heads = np.arange(H)
+    early = -8.0 * (heads + 1) / power
+    later = -4.0 * (2 * (heads - power) + 1) / power
+    return np.exp2(np.where(heads < power, early, later)).astype(np.float32)
+
+
+def dot_nn(a, b):
+    return jnp.dot(a, b, preferred_element_type=f32)
+
+
+def dot_nt(a, b):
+    return lax.dot_general(a, b, (((1,), (1,)), ((), ())), preferred_element_type=f32)
+
+
+def params(*semantics):
+    return pltpu.CompilerParams(
+        dimension_semantics=semantics or None, vmem_limit_bytes=56 * 1024 * 1024
+    )
+
+
+def cost(flops, nbytes, exps=0):
+    return pl.CostEstimate(flops=int(flops), bytes_accessed=int(nbytes), transcendentals=int(exps))
+
+
+def shape(dims, dtype):
+    return jax.ShapeDtypeStruct(dims, dtype)
+
+
+def xor_pairs(axis, distance):
+    return [(i, i ^ distance) for i in range(lax.axis_size(axis))]
+
+
+def swap(value, axis, distance):
+    return lax.ppermute(value, axis, xor_pairs(axis, distance))
+
+
+def live_mask(lens, rank, n_ctx, seqs, slots):
+    slot = lax.broadcasted_iota(jnp.int32, (slots, 1), 0)
+    place = slot * n_ctx + rank
+    return jnp.concatenate(
+        [jnp.where(place < lens[s], 1.0, 0.0).astype(f32) for s in range(seqs)], axis=0
+    )
+
+
+def normalise(z):
+    centred = z - jnp.mean(z, axis=-1, keepdims=True)
+    spread = jnp.mean(centred * centred, axis=-1, keepdims=True)
+    scale = lax.rsqrt(spread + epsilon)
+    return centred * scale, scale
+
+
+def normalise_back(grad_hat, hat, scale):
+    inner = jnp.mean(grad_hat * hat, axis=-1, keepdims=True)
+    return scale * (grad_hat - jnp.mean(grad_hat, axis=-1, keepdims=True) - hat * inner)
+
+
+def project_kernel(n, seqs, heads, ids, tok, bias, *refs):
+    pieces = refs[: 4 * n]
+    sends = refs[4 * n : 5 * n]
+    whole = refs[5 * n]
+    stage = refs[5 * n + 1]
+    y, c, z = ids[0], ids[1], ids[2]
+    rows = pieces[0].shape[0]
+    for k in range(4 * n):
+        ky, kc, kz = k // (2 * n), k // n % 2, k % n
+        index = ((y ^ ky) * 2 + (c ^ kc)) * n + (z ^ kz)
+        whole[pl.ds(pl.multiple_of(index * rows, rows), rows), :] = pieces[k][...]
+    slots = sends[0].shape[1]
+    width = heads * HD
+    per = seqs * heads // n
+    for s in range(seqs):
+        acc = dot_nn(tok[s * slots : (s + 1) * slots, :], whole[...]) + bias[...]
+        turned = acc.astype(bf16).T
+        for h in range(heads):
+            i = s * heads + h
+            at = ((i % n) * per + i // n) * 3
+            for part in range(3):
+                first = part * width + h * HD
+                stage[(at + part) * HD : (at + part + 1) * HD, :] = turned[first : first + HD, :]
+    size = per * 3 * HD
+    for d in range(n):
+        sends[d][...] = stage[pl.ds(pl.multiple_of((z ^ d) * size, size), size), :]
+
+
+def project(ids, tok, bias, pieces, n, seqs, heads):
+    slots = tok.shape[0] // seqs
+    size = seqs * heads // n * 3 * HD
+    model, wide = tok.shape[1], bias.shape[1]
+    return pl.pallas_call(
+        functools.partial(project_kernel, n, seqs, heads),
+        out_shape=[shape((size, slots), bf16)] * n + [shape((model, wide), bf16)],
+        in_specs=[SMEM] + [VMEM] * (2 + len(pieces)),
+        out_specs=[VMEM] * (n + 1),
+        scratch_shapes=[pltpu.VMEM((size * n, slots), bf16)],
+        compiler_params=params(),
+        cost_estimate=cost(2 * tok.shape[0] * model * wide, 6e6),
+        name="project",
+    )(ids, tok, bias, *pieces)
+
+
+def pair_scalars(n, heads, ids, lens, slopes):
+    j = pl.program_id(0)
+    z, t = ids[2], ids[3]
+    i = z + n * j
+    s = i // heads
+    h = i - s * heads
+    return z, lens[s], slopes[t * heads + h] * LOG2E
+
+
+def query_place(n, slots, z, d):
+    lane = lax.broadcasted_iota(jnp.int32, (1, slots), 1)
+    return lane * n + (z ^ d)
+
+
+def key_place(n, z, tile, length, slope):
+    row = lax.broadcasted_iota(jnp.int32, (TILE, 1), 0)
+    places = []
+    for d in range(n):
+        place = (tile * TILE + row) * n + (z ^ d)
+        places.append(jnp.where(place < length, place.astype(f32) * slope, FAR))
+    return jnp.concatenate(places, axis=0)
+
+
+def gather_rows(ref, tile, n):
+    rows = pl.ds(pl.multiple_of(tile * TILE, TILE), TILE)
+    return jnp.concatenate([ref[d, rows, :] for d in range(n)], axis=0)
+
+
+def attend_kernel(n, heads, ids, lens, slopes, *refs):
+    inputs = refs[:n]
+    outs = refs[n : 2 * n]
+    att_ref, den_ref = refs[2 * n], refs[2 * n + 1]
+    k_s, v_s, acc, den = refs[2 * n + 2 :]
+    slots = inputs[0].shape[1]
+    z, length, slope = pair_scalars(n, heads, ids, lens, slopes)
+    for d in range(n):
+        k_s[d] = inputs[d][HD : 2 * HD, :].T
+        v_s[d] = inputs[d][2 * HD : 3 * HD, :].T
+    acc[...] = jnp.zeros_like(acc)
+    den[...] = jnp.zeros_like(den)
+
+    def tile_step(tile, unused):
+        keys = gather_rows(k_s, tile, n)
+        values = gather_rows(v_s, tile, n).T
+        places = key_place(n, z, tile, length, slope)
+        for d in range(n):
+            cols = slice(d * slots, (d + 1) * slots)
+            there = query_place(n, slots, z, d).astype(f32) * slope
+            scores = dot_nn(keys, inputs[d][0:HD, :]) * (0.125 * LOG2E)
+            e = jnp.exp2(scores - jnp.abs(there - places))
+            den[:, cols] += jnp.sum(e, axis=0, keepdims=True)
+            acc[:, cols] += dot_nn(values, e.astype(bf16))
+        return unused
+
+    step = TILE * n
+    lax.fori_loop(0, (length + step - 1) // step, tile_step, 0)
+    for d in range(n):
+        cols = slice(d * slots, (d + 1) * slots)
+        padded = jnp.where(query_place(n, slots, z, d) < length, 0.0, 1.0)
+        total = den[:, cols] + padded
+        att = acc[:, cols] / total
+        att_ref[:, cols] = att
+        den_ref[0, :, cols] = total
+        outs[d][...] = att.astype(bf16)
+
+
+def attend(ids, lens, slopes, blocks, n, heads, per):
+    slots = blocks[0].shape[1]
+    every = n * slots
+    return pl.pallas_call(
+        functools.partial(attend_kernel, n, heads),
+        grid=(per,),
+        out_shape=[shape((per * HD, slots), bf16)] * n
+        + [shape((per * HD, every), f32), shape((per, 1, every), f32)],
+        in_specs=[SMEM] * 3 + [pl.BlockSpec((3 * HD, slots), lambda j: (j, 0))] * n,
+        out_specs=[pl.BlockSpec((HD, slots), lambda j: (j, 0))] * n
+        + [
+            pl.BlockSpec((HD, every), lambda j: (j, 0)),
+            pl.BlockSpec((1, 1, every), lambda j: (j, 0, 0)),
+        ],
+        scratch_shapes=[
+            pltpu.VMEM((n, slots, HD), bf16),
+            pltpu.VMEM((n, slots, HD), bf16),
+            pltpu.VMEM((HD, every), f32),
+            pltpu.VMEM((1, every), f32),
+        ],
+        compiler_params=params("arbitrary"),
+        cost_estimate=cost(per * every * every * HD * 8, 3e6, per * every * every),
+        name="attend",
+    )(ids, lens, slopes, *blocks)
+
+
+def attend_back_kernel(n, heads, ids, lens, slopes, *refs):
+    inputs = refs[:n]
+    grads = refs[n : 2 * n]
+    att_ref, den_ref = refs[2 * n], refs[2 * n + 1]
+    outs = refs[2 * n + 2 : 3 * n + 2]
+    k_s, v_s, q_s, g_s, dn, cor, dq, dk, dv = refs[3 * n + 2 :]
+    slots = inputs[0].shape[1]
+    z, length, slope = pair_scalars(n, heads, ids, lens, slopes)
+    for d in range(n):
+        cols = slice(d * slots, (d + 1) * slots)
+        k_s[d] = inputs[d][HD : 2 * HD, :].T
+        v_s[d] = inputs[d][2 * HD : 3 * HD, :].T
+        q_s[d] = inputs[d][0:HD, :].T
+        inverse = 1.0 / den_ref[0, :, cols]
+        mixed = grads[d][...].astype(f32)
+        numer = (mixed * inverse).astype(bf16)
+        dn[:, cols] = numer
+        g_s[d] = numer.T
+        cor[:, cols] = jnp.sum(mixed * att_ref[:, cols], axis=0, keepdims=True) * inverse
+    dq[...] = jnp.zeros_like(dq)
+    dk[...] = jnp.zeros_like(dk)
+    dv[...] = jnp.zeros_like(dv)
+
+    def tile_step(tile, unused):
+        keys = gather_rows(k_s, tile, n)
+        values = gather_rows(v_s, tile, n)
+        keys_t = keys.T
+        places = key_place(n, z, tile, length, slope)
+        grad_k = jnp.zeros((n * TILE, HD), f32)
+        grad_v = jnp.zeros((n * TILE, HD), f32)
+        for d in range(n):
+            cols = slice(d * slots, (d + 1) * slots)
+            there = query_place(n, slots, z, d).astype(f32) * slope
+            scores = dot_nn(keys, inputs[d][0:HD, :]) * (0.125 * LOG2E)
+            e = jnp.exp2(scores - jnp.abs(there - places))
+            inner = dot_nn(values, dn[:, cols])
+            ds = (e * (inner - cor[:, cols])).astype(bf16)
+            dq[:, cols] += dot_nn(keys_t, ds)
+            grad_k += dot_nn(ds, q_s[d])
+            grad_v += dot_nn(e.astype(bf16), g_s[d])
+        rows = pl.ds(pl.multiple_of(tile * TILE, TILE), TILE)
+        for d in range(n):
+            dk[d, rows, :] = grad_k[d * TILE : (d + 1) * TILE, :]
+            dv[d, rows, :] = grad_v[d * TILE : (d + 1) * TILE, :]
+        return unused
+
+    step = TILE * n
+    lax.fori_loop(0, (length + step - 1) // step, tile_step, 0)
+    for d in range(n):
+        cols = slice(d * slots, (d + 1) * slots)
+        outs[d][0:HD, :] = (dq[:, cols] * 0.125).astype(bf16)
+        outs[d][HD : 2 * HD, :] = (dk[d] * 0.125).astype(bf16).T
+        outs[d][2 * HD : 3 * HD, :] = dv[d].astype(bf16).T
+
+
+def attend_back(ids, lens, slopes, blocks, grads, att, den, n, heads, per):
+    slots = blocks[0].shape[1]
+    every = n * slots
+    rows = [pltpu.VMEM((n, slots, HD), bf16)] * 4
+    return pl.pallas_call(
+        functools.partial(attend_back_kernel, n, heads),
+        grid=(per,),
+        out_shape=[shape((per * 3 * HD, slots), bf16)] * n,
+        in_specs=[SMEM] * 3
+        + [pl.BlockSpec((3 * HD, slots), lambda j: (j, 0))] * n
+        + [pl.BlockSpec((HD, slots), lambda j: (j, 0))] * n
+        + [
+            pl.BlockSpec((HD, every), lambda j: (j, 0)),
+            pl.BlockSpec((1, 1, every), lambda j: (j, 0, 0)),
+        ],
+        out_specs=[pl.BlockSpec((3 * HD, slots), lambda j: (j, 0))] * n,
+        scratch_shapes=rows
+        + [
+            pltpu.VMEM((HD, every), bf16),
+            pltpu.VMEM((1, every), f32),
+            pltpu.VMEM((HD, every), f32),
+            pltpu.VMEM((n, slots, HD), f32),
+            pltpu.VMEM((n, slots, HD), f32),
+        ],
+        compiler_params=params("arbitrary"),
+        cost_estimate=cost(per * every * every * HD * 20, 5e6, per * every * every),
+        name="attend_back",
+    )(ids, lens, slopes, *blocks, *grads, att, den)
+
+
+def mix_kernel(n, seqs, heads, ids, wo, *refs):
+    inputs = refs[:n]
+    part, mixed, stage = refs[n], refs[n + 1], refs[n + 2]
+    z = ids[2]
+    slots = inputs[0].shape[1]
+    per = seqs * heads // n
+    size = per * HD
+    for d in range(n):
+        stage[pl.ds(pl.multiple_of((z ^ d) * size, size), size), :] = inputs[d][...]
+    for s in range(seqs):
+        columns = []
+        for h in range(heads):
+            i = s * heads + h
+            at = (i % n) * per + i // n
+            columns.append(stage[at * HD : (at + 1) * HD, :])
+        rows = slice(s * slots, (s + 1) * slots)
+        ours = jnp.concatenate(columns, axis=0).T
+        mixed[rows, :] = ours
+        part[rows, :] = dot_nt(ours, wo[...]).astype(bf16)
+
+
+def mix(ids, packed, blocks, n, seqs, heads):
+    slots = blocks[0].shape[1]
+    model = packed.shape[0]
+    width = heads * HD
+    tokens = seqs * slots
+    return pl.pallas_call(
+        functools.partial(mix_kernel, n, seqs, heads),
+        grid=(1,),
+        out_shape=[shape((tokens, model), bf16), shape((tokens, width), bf16)],
+        in_specs=[SMEM, pl.BlockSpec((model, width), lambda i: (0, 0))] + [VMEM] * n,
+        out_specs=[VMEM] * 2,
+        scratch_shapes=[pltpu.VMEM((seqs * heads * HD, slots), bf16)],
+        compiler_params=params("arbitrary"),
+        cost_estimate=cost(2 * tokens * model * width, 3e6),
+        name="mix",
+    )(ids, packed, *blocks)
+
+
+def unit_kernel(tok, own, other, vec, wg, wu, wd, hidden, low, act, gel, slope, part, acc):
+    j = pl.program_id(0)
+
+    @pl.when(j == 0)
+    def _():
+        branch = own[...].astype(f32) + other[...].astype(f32) + vec[4:5, :]
+        hat, _ = normalise(tok[...].astype(f32) + branch)
+        h = hat * vec[0:1, :] + vec[1:2, :]
+        hidden[...] = h
+        low[...] = h.astype(bf16)
+        acc[...] = jnp.zeros_like(acc)
+
+    gate = dot_nn(low[...], wg[...])
+    upper = dot_nn(low[...], wu[...])
+    phi = 0.5 * (1.0 + lax.erf(gate * math.sqrt(0.5)))
+    density = jnp.exp(gate * gate * -0.5) * (1.0 / math.sqrt(2.0 * math.pi))
+    unit = gate * phi
+    acted = (unit * upper).astype(bf16)
+    act[...] = acted
+    gel[...] = unit.astype(bf16)
+    slope[...] = (upper * (phi + gate * density)).astype(bf16)
+    acc[...] += dot_nt(acted, wd[...])
+
+    @pl.when(j == pl.num_programs(0) - 1)
+    def _():
+        part[...] = acc[...].astype(bf16)
+
+
+def unit(tok, own, other, vec, packed, width, hidden_units):
+    tokens, model = tok.shape
+    steps = hidden_units // BLOCK
+    first = width // BLOCK
+    fixed = lambda j: (0, 0)
+    moving = lambda j: (0, j)
+    whole = pl.BlockSpec((tokens, model), fixed)
+    weight = lambda start: pl.BlockSpec((model, BLOCK), lambda j: (0, start + j))
+    inner = pl.BlockSpec((tokens, BLOCK), moving)
+    return pl.pallas_call(
+        unit_kernel,
+        grid=(steps,),
+        out_shape=[shape((tokens, model), f32), shape((tokens, model), bf16)]
+        + [shape((tokens, hidden_units), bf16)] * 3
+        + [shape((tokens, model), bf16)],
+        in_specs=[
+            whole,
+            whole,
+            whole,
+            pl.BlockSpec(vec.shape, fixed),
+            weight(first),
+            weight(first + steps),
+            weight(first + 2 * steps),
+        ],
+        out_specs=[whole, whole, inner, inner, inner, whole],
+        scratch_shapes=[pltpu.VMEM((tokens, model), f32)],
+        compiler_params=params("arbitrary"),
+        cost_estimate=cost(6 * tokens * model * hidden_units, 20e6, 2 * tokens * hidden_units),
+        name="unit",
+    )(tok, own, other, vec, packed, packed, packed)
+
+
+def unit_back_kernel(
+    n, seqs, ids, lens, hidden, own, other, cot, vec, wg, wu, wd, gel, slope,
+    output, dz2, dffn, dgate, dup, part, sums, acc,
+):
+    j = pl.program_id(0)
+
+    @pl.when(j == 0)
+    def _():
+        live = live_mask(lens, ids[2], n, seqs, hidden.shape[0] // seqs)
+        branch = own[...].astype(f32) + other[...].astype(f32) + vec[5:6, :]
+        hat, scale = normalise(hidden[...] + branch)
+        output[...] = (live * (hat * vec[2:3, :] + vec[3:4, :])).astype(bf16)
+        gy = cot[...].astype(f32) * live
+        grad = normalise_back(gy * vec[2:3, :], hat, scale)
+        dz2[...] = grad
+        low = grad.astype(bf16)
+        dffn[...] = low
+        sums[0:1, :] = jnp.sum(gy * hat, axis=0, keepdims=True)
+        sums[1:2, :] = jnp.sum(gy, axis=0, keepdims=True)
+        sums[2:3, :] = jnp.sum(low.astype(f32), axis=0, keepdims=True)
+        sums[3:8, :] = jnp.zeros_like(sums[3:8, :])
+        acc[...] = jnp.zeros_like(acc)
+
+    dact = dot_nn(dffn[...], wd[...])
+    upper = (dact * gel[...].astype(f32)).astype(bf16)
+    gate = (dact * slope[...].astype(f32)).astype(bf16)
+    dgate[...] = gate
+    dup[...] = upper
+    acc[...] += dot_nt(gate, wg[...]) + dot_nt(upper, wu[...])
+
+    @pl.when(j == pl.num_programs(0) - 1)
+    def _():
+        part[...] = acc[...].astype(bf16)
+
+
+def unit_back(ids, lens, hidden, own, other, cot, vec, packed, gel, slope, n, seqs, width):
+    tokens, model = hidden.shape
+    hidden_units = gel.shape[1]
+    steps = hidden_units // BLOCK
+    first = width // BLOCK
+    fixed = lambda j: (0, 0)
+    whole = pl.BlockSpec((tokens, model), fixed)
+    weight = lambda start: pl.BlockSpec((model, BLOCK), lambda j: (0, start + j))
+    inner = pl.BlockSpec((tokens, BLOCK), lambda j: (0, j))
+    return pl.pallas_call(
+        functools.partial(unit_back_kernel, n, seqs),
+        grid=(steps,),
+        out_shape=[
+            shape((tokens, model), bf16),
+            shape((tokens, model), f32),
+            shape((tokens, model), bf16),
+            shape((tokens, hidden_units), bf16),
+            shape((tokens, hidden_units), bf16),
+            shape((tokens, model), bf16),
+            shape((8, model), f32),
+        ],
+        in_specs=[SMEM, SMEM, whole, whole, whole, whole, pl.BlockSpec(vec.shape, fixed)]
+        + [weight(first), weight(first + steps), weight(first + 2 * steps), inner, inner],
+        out_specs=[whole, whole, whole, inner, inner, whole, pl.BlockSpec((8, model), fixed)],
+        scratch_shapes=[pltpu.VMEM((tokens, model), f32)],
+        compiler_params=params("arbitrary"),
+        cost_estimate=cost(6 * tokens * model * hidden_units, 22e6),
+        name="unit_back",
+    )(ids, lens, hidden, own, other, cot, vec, packed, packed, packed, gel, slope)
+
+
+def row_starts(ids, quarter):
+    y, c = ids[0], ids[1]
+    keep = [(y * 2 + c) * quarter, ((1 - y) * 2 + c) * quarter]
+    send = [(y * 2 + 1 - c) * quarter, ((1 - y) * 2 + 1 - c) * quarter]
+    return send, keep
+
+
+def write_rows(ids, turned, right, send, keep):
+    quarter = turned.shape[0] // 4
+    for ref, starts in zip((send, keep), row_starts(ids, quarter)):
+        for k in range(2):
+            left = turned[pl.ds(pl.multiple_of(starts[k], quarter), quarter), :]
+            ref[k * quarter : (k + 1) * quarter, :] = dot_nn(left, right).astype(bf16)
+
+
+def weight_kernel(steps, ids, low, dffn, dgate, dup, act, send, keep, left):
+    j = pl.program_id(0)
+
+    @pl.when(j == 0)
+    def _():
+        left[0] = low[...].T
+        left[1] = dffn[...].T
+
+    @pl.when(j < steps)
+    def _():
+        write_rows(ids, left.at[0], dgate[...], send, keep)
+
+    @pl.when((j >= steps) & (j < 2 * steps))
+    def _():
+        write_rows(ids, left.at[0], dup[...], send, keep)
+
+    @pl.when(j >= 2 * steps)
+    def _():
+        write_rows(ids, left.at[1], act[...], send, keep)
+
+
+def weight_grads(ids, low, dffn, dgate, dup, act):
+    tokens, model = low.shape
+    hidden_units = act.shape[1]
+    steps = hidden_units // BLOCK
+    fixed = lambda j: (0, 0)
+    whole = pl.BlockSpec((tokens, model), fixed)
+    column = lambda start: pl.BlockSpec(
+        (tokens, BLOCK), lambda j: (0, jnp.clip(j - start, 0, steps - 1))
+    )
+    out = pl.BlockSpec((model // 2, BLOCK), lambda j: (0, j))
+    return pl.pallas_call(
+        functools.partial(weight_kernel, steps),
+        grid=(3 * steps,),
+        out_shape=[shape((model // 2, 3 * hidden_units), bf16)] * 2,
+        in_specs=[SMEM, whole, whole, column(0), column(steps), column(2 * steps)],
+        out_specs=[out, out],
+        scratch_shapes=[pltpu.VMEM((2, model, tokens), bf16)],
+        compiler_params=params("arbitrary"),
+        cost_estimate=cost(6 * tokens * model * hidden_units, 14e6),
+        name="weight_grads",
+    )(ids, low, dffn, dgate, dup, act)
+
+
+def mix_back_kernel(
+    n, seqs, heads, ids, tok, own, other, dz2, hown, hother, vec, wo, mixed, *refs
+):
+    sends = refs[:n]
+    dz1, send, keep, sums = refs[n : n + 4]
+    stage, left = refs[n + 4 :]
+    z = ids[2]
+    slots = sends[0].shape[1]
+    per = seqs * heads // n
+    branch = own[...].astype(f32) + other[...].astype(f32) + vec[4:5, :]
+    hat, scale = normalise(tok[...].astype(f32) + branch)
+    gh = dz2[...] + (hown[...].astype(f32) + hother[...].astype(f32))
+    grad = normalise_back(gh * vec[0:1, :], hat, scale)
+    dz1[...] = grad
+    low = grad.astype(bf16)
+    sums[0:1, :] = jnp.sum(gh * hat, axis=0, keepdims=True)
+    sums[1:2, :] = jnp.sum(gh, axis=0, keepdims=True)
+    sums[2:3, :] = jnp.sum(low.astype(f32), axis=0, keepdims=True)
+    sums[3:8, :] = jnp.zeros_like(sums[3:8, :])
+    for s in range(seqs):
+        turned = dot_nn(low[s * slots : (s + 1) * slots, :], wo[...]).astype(bf16).T
+        for h in range(heads):
+            i = s * heads + h
+            at = (i % n) * per + i // n
+            stage[at * HD : (at + 1) * HD, :] = turned[h * HD : (h + 1) * HD, :]
+    size = per * HD
+    for d in range(n):
+        sends[d][...] = stage[pl.ds(pl.multiple_of((z ^ d) * size, size), size), :]
+    left[...] = low.T
+    write_rows(ids, left, mixed[...], send, keep)
+
+
+def mix_back(ids, tok, own, other, dz2, hown, hother, vec, packed, mixed, n, seqs, heads):
+    tokens, model = tok.shape
+    slots = tokens // seqs
+    width = heads * HD
+    size = seqs * heads // n * HD
+    return pl.pallas_call(
+        functools.partial(mix_back_kernel, n, seqs, heads),
+        grid=(1,),
+        out_shape=[shape((size, slots), bf16)] * n
+        + [shape((tokens, model), f32)]
+        + [shape((model // 2, width), bf16)] * 2
+        + [shape((8, model), f32)],
+        in_specs=[SMEM]
+        + [VMEM] * 7
+        + [pl.BlockSpec((model, width), lambda i: (0, 0)), VMEM],
+        out_specs=[VMEM] * (n + 4),
+        scratch_shapes=[
+            pltpu.VMEM((size * n, slots), bf16),
+            pltpu.VMEM((model, tokens), bf16),
+        ],
+        compiler_params=params("arbitrary"),
+        cost_estimate=cost(4 * tokens * model * width, 10e6),
+        name="mix_back",
+    )(ids, tok, own, other, dz2, hown, hother, vec, packed, mixed)
+
+
+def project_back_kernel(n, seqs, heads, ids, tok, whole, *refs):
+    inputs = refs[:n]
+    part, send, keep, sums = refs[n : n + 4]
+    stage, right, left = refs[n + 4 :]
+    z = ids[2]
+    slots = inputs[0].shape[1]
+    per = seqs * heads // n
+    width = heads * HD
+    size = per * 3 * HD
+    for d in range(n):
+        stage[pl.ds(pl.multiple_of((z ^ d) * size, size), size), :] = inputs[d][...]
+    for s in range(seqs):
+        for c in range(3):
+            columns = []
+            for h in range(heads):
+                i = s * heads + h
+                at = ((i % n) * per + i // n) * 3 + c
+                columns.append(stage[at * HD : (at + 1) * HD, :])
+            ours = jnp.concatenate(columns, axis=0).T
+            right[s * slots : (s + 1) * slots, c * width : (c + 1) * width] = ours
+    part[...] = dot_nt(right[...], whole[...]).astype(bf16)
+    left[...] = tok[...].T
+    for c in range(3):
+        cols = slice(c * width, (c + 1) * width)
+        write_rows(ids, left, right[:, cols], send.at[:, cols], keep.at[:, cols])
+    ones = jnp.ones((8, right.shape[0]), bf16)
+    sums[...] = dot_nn(ones, right[...])
+
+
+def project_back(ids, tok, whole, blocks, n, seqs, heads):
+    tokens, model = tok.shape
+    slots = tokens // seqs
+    wide = whole.shape[1]
+    return pl.pallas_call(
+        functools.partial(project_back_kernel, n, seqs, heads),
+        out_shape=[
+            shape((tokens, model), bf16),
+            shape((model // 2, wide), bf16),
+            shape((model // 2, wide), bf16),
+            shape((8, wide), f32),
+        ],
+        in_specs=[SMEM] + [VMEM] * (2 + n),
+        out_specs=[VMEM] * 4,
+        scratch_shapes=[
+            pltpu.VMEM((seqs * heads * 3 * HD, slots), bf16),
+            pltpu.VMEM((tokens, wide), bf16),
+            pltpu.VMEM((model, tokens), bf16),
+        ],
+        compiler_params=params(),
+        cost_estimate=cost(4 * tokens * model * wide, 8e6),
+        name="project_back",
+    )(ids, tok, whole, *blocks)
+
+
+def own_rows(send, keep, n):
+    half = keep.shape[0] // 2
+    pair = keep.astype(f32) + swap(send, "shard", 1).astype(f32)
+    mine = pair[:half] + swap(pair[half:].astype(bf16), "shard", 2).astype(f32)
+    blocks = mine.reshape(n, half // n, mine.shape[1])
+    rank = lax.axis_index("ctx")
+    total = lax.dynamic_index_in_dim(blocks, rank, 0, keepdims=False)
+    for d in range(1, n):
+        block = lax.dynamic_index_in_dim(blocks, rank ^ d, 0, keepdims=False)
+        total = total + swap(block.astype(bf16), "ctx", d).astype(f32)
+    return total
+
+
+def everywhere_sum(value, n):
+    distance = 1
+    while distance < n:
+        value = value + swap(value, "ctx", distance)
+        distance *= 2
+    value = value + swap(value, "shard", 2)
+    return value + swap(value, "shard", 1)
+
+
+def fits(tokens, b_qv, w_qkv, w_gu):
+    n = lax.axis_size("ctx")
+    heads = b_qv.shape[1] // HD
+    return (
+        n == 4
+        and lax.axis_size("shard") == 4
+        and lax.axis_size("tp") == 2
+        and (tokens.shape[0] * heads) % n == 0
+        and w_qkv.shape[0] % 16 == 0
+        and tokens.shape[1] % 256 == 0
+        and b_qv.shape[1] == BLOCK
+        and w_gu.shape[2] % BLOCK == 0
+    )
+
+
+def on_device(tokens, lengths, w_qkv, b_qv, w_out, w_gu, w_down, vectors, cotangent):
+    if not fits(tokens, b_qv, w_qkv, w_gu):
+        return by_gather(tokens, lengths, w_qkv, b_qv, w_out, w_gu, w_down, vectors, cotangent)
+    n = lax.axis_size("ctx")
+    seqs, slots, model = tokens.shape
+    width = b_qv.shape[1]
+    heads = width // HD
+    per = seqs * heads // n
+    units = w_gu.shape[2]
+    rows = w_qkv.shape[0]
+    count = seqs * slots
+    shard = lax.axis_index("shard")
+    ids = jnp.stack(
+        [shard // 2, shard % 2, lax.axis_index("ctx"), lax.axis_index("tp")]
+    ).astype(jnp.int32)
+    slopes = jnp.asarray(slope_table())
+    tok = tokens.reshape(count, model)
+    cot = cotangent.reshape(count, model)
+
+    first = [w_qkv.astype(bf16).reshape(rows, 3 * width)]
+    first += [swap(first[0], "ctx", d) for d in range(1, n)]
+    first += [swap(piece, "shard", 2) for piece in first]
+    by_core = [swap(piece, "shard", 1) for piece in first]
+    pieces = first[:n] + by_core[:n] + first[n:] + by_core[n:]
+    packed = jnp.concatenate(
+        [w_out.T, w_gu.reshape(rows, 2 * units), w_down.T], axis=1
+    ).astype(bf16)
+    packed, pieces[0] = lax.optimization_barrier((packed, pieces[0]))
+    packed = lax.all_gather(packed, ("shard", "ctx"), axis=0, tiled=True)
+
+    bias = jnp.concatenate([b_qv[0], jnp.zeros_like(b_qv[0]), b_qv[1]])[None, :]
+    *sends, whole = project(ids, tok, bias, pieces, n, seqs, heads)
+    blocks = [sends[0]] + [swap(sends[d], "ctx", d) for d in range(1, n)]
+    *outs, att, den = attend(ids, lengths, slopes, blocks, n, heads, per)
+    outs = [outs[0]] + [swap(outs[d], "ctx", d) for d in range(1, n)]
+    part, mixed = mix(ids, packed, outs, n, seqs, heads)
+    part_other = swap(part, "tp", 1)
+    hidden, low, act, gel, slope, ffn = unit(tok, part, part_other, vectors, packed, width, units)
+    ffn_other = swap(ffn, "tp", 1)
+    output, dz2, dffn, dgate, dup, back, sums_two = unit_back(
+        ids, lengths, hidden, ffn, ffn_other, cot, vectors, packed, gel, slope, n, seqs, width
+    )
+    back_other = swap(back, "tp", 1)
+    unit_send, unit_keep = weight_grads(ids, low, dffn, dgate, dup, act)
+    *sends, dz1, out_send, out_keep, sums_one = mix_back(
+        ids, tok, part, part_other, dz2, back, back_other, vectors, packed, mixed, n, seqs, heads
+    )
+    grads = [sends[0]] + [swap(sends[d], "ctx", d) for d in range(1, n)]
+    outs = attend_back(ids, lengths, slopes, blocks, grads, att, den, n, heads, per)
+    outs = [outs[0]] + [swap(outs[d], "ctx", d) for d in range(1, n)]
+    dx, qkv_send, qkv_keep, sums_bias = project_back(ids, tok, whole, outs, n, seqs, heads)
+    input_grad = dz1 + (dx.astype(f32) + swap(dx, "tp", 1).astype(f32))
+
+    grad_unit = own_rows(unit_send, unit_keep, n)
+    grad_out = own_rows(out_send, out_keep, n)
+    grad_qkv = own_rows(qkv_send, qkv_keep, n)
+    bias_row = jnp.concatenate([sums_bias[0:1, :width], sums_bias[0:1, 2 * width :]], axis=1)
+    small = jnp.concatenate(
+        [sums_one[0:2], sums_two[0:2], sums_one[2:3], sums_two[2:3], bias_row, jnp.zeros_like(bias_row)]
+    )
+    small = everywhere_sum(small, n)
+    return (
+        output.reshape(tokens.shape),
+        input_grad.reshape(tokens.shape),
+        grad_qkv.reshape(w_qkv.shape),
+        small[6].reshape(2, width),
+        grad_out.T,
+        grad_unit[:, : 2 * units].reshape(w_gu.shape),
+        grad_unit[:, 2 * units :].T,
+        small[:6],
+    )
 
 
 def alibi_slopes(first_head, head_count):
@@ -76,7 +812,7 @@
     return (blocks, places, offsets)
 
 
-def on_device(tokens, lengths, w_qkv, b_qv, w_out, w_gu, w_down, vectors, cotangent):
+def by_gather(tokens, lengths, w_qkv, b_qv, w_out, w_gu, w_down, vectors, cotangent):
     ctx_count = lax.axis_size("ctx")
     ctx_rank = lax.axis_index("ctx")
     seq_count, slot_count, model_width = tokens.shape

time: 1020 us -> 450 us (0.44)
  waiting for transfers between devices: 671 us -> 209 us
  blocking collectives: 109 us -> 0 us
  starting transfers between devices: 0.94 us -> 98.2 us
  Pallas kernels: 0 us -> 86.8 us
  local copies, waits for them, and re-layouts: 94.3 us -> 23 us
  matrix products: 63.8 us -> 0 us
  other arithmetic: 49.9 us -> 18.8 us
  loops' own time: 16.9 us -> 0 us
    reduce_scatter x4 -> x0, waiting for transfers between devices: 312 us -> none  [the longest x1 113 us: on_device(): lax.psum_scatter(grad_gu, ('shard', 'ctx'), scatter_dimension=0, tiled=True)]
    ppermute x0 -> x50, waiting for transfers between devices: none -> 209 us  [swap(): return lax.ppermute(value, axis, xor_pairs(axis, distance))]
    all_gather x4 -> x1, waiting for transfers between devices: 149 us -> 0.02 us  [on_device(): packed = lax.all_gather(packed, ('shard', 'ctx'), axis=0, tiled=True)]
    psum x4 -> x0, waiting for transfers between devices: 146 us -> none  [the longest x1 49.7 us: on_device(): grad_hidden = grad_second + lax.psum(hidden_part, 'tp')]
    ppermute x0 -> x50, starting transfers between devices: none -> 98.1 us  [swap(): return lax.ppermute(value, axis, xor_pairs(axis, distance))]
    pallas_call x0 -> x9, Pallas kernels: none -> 86.8 us  [the longest x1 15.1 us: attend_back(): pl.pallas_call(functools.partial(attend_back_kernel, n, heads), grid=(per...]
    dot_general x68 -> x0, matrix products: 63.8 us -> none  [the longest x16 8.92 us: score_block(): jnp.einsum('sqhe,skhe->shqk', query_heads, key_heads, preferred_element_t...]
    unnamed x14 -> x1, waiting for transfers between devices: 63.5 us -> 0.02 us
  transfers between devices with their start and end apart: 13 -> 51, of which waited for: 12 -> 22; matrix products, arithmetic and copies ran while one was open for 5% -> 6% of each run, Pallas kernels for 0% -> 10%
where the time goes in v1:
time: 450 us; the launch traced here: 451 us
  waiting for transfers between devices  209 us (46%)
  starting transfers between devices  98.2 us (22%)
  Pallas kernels  86.8 us (19%)
  local copies, waits for them, and re-layouts  23 us (5%)
  other arithmetic  18.8 us (4%)
  between operations  14.6 us (3%)
    ppermute x50, waiting for transfers between devices, swap(): return lax.ppermute(value, axis, xor_pairs(axis, distance))  209 us
    ppermute x50, starting transfers between devices, swap(): return lax.ppermute(value, axis, xor_pairs(axis, distance))  98.1 us
    pallas_call x1, Pallas kernels, attend_back(): pl.pallas_call(functools.partial(attend_back_kernel, n, heads), grid=(per...  15.1 us
    pallas_call x1, Pallas kernels, unit_back(): pl.pallas_call(functools.partial(unit_back_kernel, n, seqs), grid=(steps,...  14.8 us
    pallas_call x1, Pallas kernels, weight_grads(): pl.pallas_call(functools.partial(weight_kernel, steps), grid=(3 * steps,)...  13.5 us
    pallas_call x1, Pallas kernels, unit(): pl.pallas_call(unit_kernel, grid=(steps,), out_shape=[shape((tokens, mode...  12 us
    pallas_call x1, Pallas kernels, attend(): pl.pallas_call(functools.partial(attend_kernel, n, heads), grid=(per,), o...  11.4 us
    unnamed x87, local copies, waits for them, and re-layouts  9.66 us
  transfers between devices with their start and end apart: 51, of which 22 were waited for; matrix products, arithmetic and copies ran while one was open for 6% of the time, Pallas kernels for 10%

profile of v1, /device:TPU:0, one launch (start us, length us, event | category | flops | bytes accessed | tf_op | source)
XLA Modules:
  0.0 450.7 jit_solution(8481688206253695329)
XLA Ops:
  10.5 3.1 collective-permute-start
  18.3 6.7 %collective-permute-done.1.refs_2_ = bf16[48,1152]{1,0:T(8,128)(2,1)S(1)} collective-permute-done((bf16[48,1152]{1,0:T(8,128)(2,1)S(1)}, bf16[48,1152]{1,0:T(8,128)(2,1)S(1)}, u32[]{:S(2)}, u32[]{:S(2)}) %collective-permute-start.1) | collective-permute-done | bytes 110624 | tf_op jit(solution)/shard_map/ppermute | solution.py:61
  37.3 4.8 %project.1 = (bf16[576,256]{1,0:T(8,128)(2,1)}, bf16[576,256]{1,0:T(8,128)(2,1)}, bf16[576,256]{1,0:T(8,128)(2,1)}, bf16[576,256]{1,0:T(8,128)(2,1)}, bf16[768,1152]{1,0:T(8,128)(2,1)}) custom-call(s32[4]{0:T(128)} %pad_add_fusion.ids, bf16[512,768]{1,0:T(8,128)(2,1)} %bitcast.69, f32[1,1152]{1,0:T(1,128)} %broadcast_in_dim.10.bias, ...), custom_call_target="tpu_custom_call" | custom-call | flops 905969664 | bytes 6000000 | tf_op jit(solution)/shard_map/project/pallas_call | solution.py:116
  42.0 5.5 %collective-permute-start.15 = (bf16[576,256]{1,0:T(8,128)(2,1)}, bf16[576,256]{1,0:T(8,128)(2,1)S(1)}, u32[]{:S(2)}, u32[]{:S(2)}) collective-permute-start(bf16[576,256]{1,0:T(8,128)(2,1)} %get-tuple-element.57), channel_id=1, source_target_pairs={{0,2},{2,0},{4,6},{6,4},{1,3},{3,1},{5,7},{7,5},{8,10},{10,8},{12,... | collective-permute-start | bytes 884744 | tf_op jit(solution)/shard_map/ppermute | solution.py:61
  47.5 2.9 collective-permute-start.16
  51.8 22.2 %collective-permute-done.15.refs_1_ = bf16[576,256]{1,0:T(8,128)(2,1)S(1)} collective-permute-done((bf16[576,256]{1,0:T(8,128)(2,1)}, bf16[576,256]{1,0:T(8,128)(2,1)S(1)}, u32[]{:S(2)}, u32[]{:S(2)}) %collective-permute-start.15) | collective-permute-done | bytes 294944 | tf_op jit(solution)/shard_map/ppermute | solution.py:61
  75.7 15.5 %collective-permute-done.17.refs_3_ = bf16[576,256]{1,0:T(8,128)(2,1)S(1)} collective-permute-done((bf16[576,256]{1,0:T(8,128)(2,1)}, bf16[576,256]{1,0:T(8,128)(2,1)S(1)}, u32[]{:S(2)}, u32[]{:S(2)}) %collective-permute-start.17) | collective-permute-done | bytes 294944 | tf_op jit(solution)/shard_map/ppermute | solution.py:61
  91.9 11.4 %attend.1 = (bf16[192,256]{1,0:T(8,128)(2,1)}, bf16[192,256]{1,0:T(8,128)(2,1)}, bf16[192,256]{1,0:T(8,128)(2,1)}, bf16[192,256]{1,0:T(8,128)(2,1)}, f32[192,1024]{1,0:T(8,128)}, /*index=5*/f32[3,1,1024]{2,1,0:T(1,128)}) custom-call(s32[4]{0:T(128)} %pad_add_fusion.ids, s32[2]{0:T(128)} %lens.5, f32[12]{0:T(128)} %constant.74.clone.slopes, ...), custom_call_target="tpu_custom_call" | custom-call | flops 1610612736 | bytes 3000000 | tf_op jit(solution)/shard_map/attend/pallas_call | solution.py:197
  103.3 14.1 %collective-permute-start.18 = (bf16[192,256]{1,0:T(8,128)(2,1)}, bf16[192,256]{1,0:T(8,128)(2,1)S(1)}, u32[]{:S(2)}, u32[]{:S(2)}) collective-permute-start(bf16[192,256]{1,0:T(8,128)(2,1)} %get-tuple-element.61), channel_id=1, source_target_pairs={{0,2},{2,0},{4,6},{6,4},{1,3},{3,1},{5,7},{7,5},{8,10},{10,8},{12,... | collective-permute-start | bytes 294920 | tf_op jit(solution)/shard_map/ppermute | solution.py:61
  121.2 6.5 %collective-permute-done.19.refs_2_ = bf16[192,256]{1,0:T(8,128)(2,1)S(1)} collective-permute-done((bf16[192,256]{1,0:T(8,128)(2,1)}, bf16[192,256]{1,0:T(8,128)(2,1)S(1)}, u32[]{:S(2)}, u32[]{:S(2)}) %collective-permute-start.19) | collective-permute-done | bytes 98336 | tf_op jit(solution)/shard_map/ppermute | solution.py:61
  132.5 16.4 %collective-permute-done.21.other = bf16[512,768]{1,0:T(8,128)(2,1)S(1)} collective-permute-done((bf16[512,768]{1,0:T(8,128)(2,1)}, bf16[512,768]{1,0:T(8,128)(2,1)S(1)}, u32[]{:S(2)}, u32[]{:S(2)}) %collective-permute-start.21) | collective-permute-done | bytes 786464 | tf_op jit(solution)/shard_map/ppermute | solution.py:61
  149.8 12.0 %unit.1 = (f32[512,768]{1,0:T(8,128)}, bf16[512,768]{1,0:T(8,128)(2,1)}, bf16[512,1536]{1,0:T(8,128)(2,1)}, bf16[512,1536]{1,0:T(8,128)(2,1)}, bf16[512,1536]{1,0:T(8,128)(2,1)}, /*index=5*/bf16[512,768]{1,0:T(8,128)(2,1)}) custom-call(bf16[512,768]{1,0:T(8,128)(2,1)} %bitcast.70, bf16[512,768]{1,0:T(8,128)(2,1)} %get-tuple-element.64.own, ...), custom_call_target="tpu_custom_call" | custom-call | flops 3623878656 | bytes 20000000 | tf_op jit(solution)/shard_map/unit/pallas_call | solution.py:381
  163.6 15.5 %collective-permute-done.22.other = bf16[512,768]{1,0:T(8,128)(2,1)S(1)} collective-permute-done((bf16[512,768]{1,0:T(8,128)(2,1)}, bf16[512,768]{1,0:T(8,128)(2,1)S(1)}, u32[]{:S(2)}, u32[]{:S(2)}) %collective-permute-start.22) | collective-permute-done | bytes 786464 | tf_op jit(solution)/shard_map/ppermute | solution.py:61
  180.0 14.8 %unit_back.1 = (bf16[512,768]{1,0:T(8,128)(2,1)}, f32[512,768]{1,0:T(8,128)}, bf16[512,768]{1,0:T(8,128)(2,1)}, bf16[512,1536]{1,0:T(8,128)(2,1)}, bf16[512,1536...) custom-call(s32[4]{0:T(128)} %pad_add_fusion.ids, s32[2]{0:T(128)} %lens.5, ...), custom_call_target="tpu_custom_call" | custom-call | flops 3623878656 | bytes 22000000 | tf_op jit(solution)/shard_map/unit_back/pallas_call | solution.py:448
  194.8 13.5 %weight_grads.1 = (bf16[384,4608]{1,0:T(8,128)(2,1)}, bf16[384,4608]{1,0:T(8,128)(2,1)}) custom-call(s32[4]{0:T(128)} %pad_add_fusion.ids, bf16[512,768]{1,0:T(8,128)(2,1)} %get-tuple-element.93.low, bf16[512,768]{1,0:T(8,128)(2,1)} %get-tuple-element.94.dffn, bf16[512,1536]{1,0:T(8,128)(2,1)} %get-tuple-element.95.dgate, ...), custom_call_target="tpu_custom_call" | custom-call | flops 3623878656 | bytes 14000000 | tf_op jit(solution)/shard_map/weight_grads/pallas_call | solution.py:516
  210.2 18.1 %collective-permute-done.23.hother = bf16[512,768]{1,0:T(8,128)(2,1)S(1)} collective-permute-done((bf16[512,768]{1,0:T(8,128)(2,1)S(1)}, bf16[512,768]{1,0:T(8,128)(2,1)S(1)}, u32[]{:S(2)}, u32[]{:S(2)}) %collective-permute-start.23) | collective-permute-done | bytes 786464 | tf_op jit(solution)/shard_map/ppermute | solution.py:61
  229.2 6.7 %mix_back.1 = (bf16[192,256]{1,0:T(8,128)(2,1)}, bf16[192,256]{1,0:T(8,128)(2,1)}, bf16[192,256]{1,0:T(8,128)(2,1)}, bf16[192,256]{1,0:T(8,128)(2,1)}, f32[512,7...) custom-call(s32[4]{0:T(128)} %pad_add_fusion.ids, ...), custom_call_target="tpu_custom_call" | custom-call | flops 603979776 | bytes 10000000 | tf_op jit(solution)/shard_map/mix_back/pallas_call | solution.py:566
  238.6 3.0 collective-permute-start.25
  244.9 4.8 %collective-permute-done.26.refs_7_ = bf16[192,256]{1,0:T(8,128)(2,1)S(1)} collective-permute-done((bf16[192,256]{1,0:T(8,128)(2,1)}, bf16[192,256]{1,0:T(8,128)(2,1)S(1)}, u32[]{:S(2)}, u32[]{:S(2)}) %collective-permute-start.26) | collective-permute-done | bytes 98336 | tf_op jit(solution)/shard_map/ppermute | solution.py:61
  250.3 15.1 %attend_back.1 = (bf16[576,256]{1,0:T(8,128)(2,1)}, bf16[576,256]{1,0:T(8,128)(2,1)}, bf16[576,256]{1,0:T(8,128)(2,1)}, bf16[576,256]{1,0:T(8,128)(2,1)}) custom-call(s32[4]{0:T(128)} %pad_add_fusion.ids, s32[2]{0:T(128)} %lens.5, f32[12]{0:T(128)} %constant.74.clone.slopes, bf16[576,256]{1,0:T(8,128)(2,1)} %get-tuple-element.56.refs_0_, ...), custom_call_target="tpu_custom_call" | custom-call | flops 4026531840 | bytes 5000000 | tf_op jit(solution)/shard_map/attend_back/pallas_call | solution.py:279
  274.8 8.7 %collective-permute-start.41 = (bf16[192,384]{1,0:T(8,128)(2,1)}, bf16[192,384]{1,0:T(8,128)(2,1)}, u32[]{:S(2)}, u32[]{:S(2)}) collective-permute-start(bf16[192,384]{1,0:T(8,128)(2,1)} %slice.97), channel_id=1, source_target_pairs={{0,16},{8,24},{16,0},{24,8},{1,17},{9,25},{17,1},{25,9},{2,18},{10... | collective-permute-start | bytes 442376 | tf_op jit(solution)/shard_map/ppermute | solution.py:61
  283.5 7.5 %collective-permute-done.28.refs_2_ = bf16[576,256]{1,0:T(8,128)(2,1)S(1)} collective-permute-done((bf16[576,256]{1,0:T(8,128)(2,1)}, bf16[576,256]{1,0:T(8,128)(2,1)S(1)}, u32[]{:S(2)}, u32[]{:S(2)}) %collective-permute-start.28) | collective-permute-done | bytes 294944 | tf_op jit(solution)/shard_map/ppermute | solution.py:61
  291.7 5.8 %project_back.1 = (bf16[512,768]{1,0:T(8,128)(2,1)}, bf16[384,1152]{1,0:T(8,128)(2,1)}, bf16[384,1152]{1,0:T(8,128)(2,1)}, f32[8,1152]{1,0:T(8,128)}) custom-call(s32[4]{0:T(128)} %pad_add_fusion.ids, bf16[512,768]{1,0:T(8,128)(2,1)} %bitcast.72, bf16[768,1152]{1,0:T(8,128)(2,1)} %get-tuple-element.74.whole, bf16[576,256]{1,0:T(8,128)(2,1)} %get-tuple-element.81.refs_0_, ...), custom_call_target="tpu_custom_call" | custom-call | flops 1811939328 | bytes 8000000 | tf_op jit(solution)/shard_map/project_back/pallas_call | solution.py:620
  300.7 3.9 collective-permute-start.36
  317.1 10.2 %collective-permute-start.38 = (f32[8,768]{1,0:T(8,128)}, f32[8,768]{1,0:T(8,128)}, u32[]{:S(2)}, u32[]{:S(2)}) collective-permute-start(f32[8,768]{1,0:T(8,128)} %add.104), channel_id=1, source_target_pairs={{0,16},{8,24},{16,0},{24,8},{1,17},{9,25},{17,1},{25,9},{2,18},{10... | collective-permute-start | bytes 73736 | tf_op jit(solution)/shard_map/ppermute | solution.py:61
  334.5 3.0 convert_add_fusion
  345.2 3.3 add_add_fusion
  348.5 42.6 %collective-permute-done.32 = bf16[192,1152]{1,0:T(8,128)(2,1)} collective-permute-done((bf16[192,1152]{1,0:T(8,128)(2,1)}, bf16[192,1152]{1,0:T(8,128)(2,1)}, u32[]{:S(2)}, u32[]{:S(2)}) %collective-permute-start.32) | collective-permute-done | bytes 442400 | tf_op jit(solution)/shard_map/ppermute | solution.py:61
  393.8 2.9 collective-permute-start.33
  400.3 2.9 collective-permute-start.47
  403.2 19.8 %collective-permute-done.34 = bf16[48,1152]{1,0:T(8,128)(2,1)S(1)} collective-permute-done((bf16[48,1152]{1,0:T(8,128)(2,1)S(1)}, bf16[48,1152]{1,0:T(8,128)(2,1)S(1)}, u32[]{:S(2)}, u32[]{:S(2)}) %collective-permute-start.34) | collective-permute-done | bytes 110624 | tf_op jit(solution)/shard_map/ppermute | solution.py:61
  423.7 17.9 %collective-permute-done.48 = bf16[48,4608]{1,0:T(8,128)(2,1)S(1)} collective-permute-done((bf16[48,4608]{1,0:T(8,128)(2,1)S(1)}, bf16[48,4608]{1,0:T(8,128)(2,1)S(1)}, u32[]{:S(2)}, u32[]{:S(2)}) %collective-permute-start.48) | collective-permute-done | bytes 442400 | tf_op jit(solution)/shard_map/ppermute | solution.py:61
  (212 shorter events, 95.1 us)
Async XLA Ops:
  7.2 120.6 %all-gather.2.cloned.1.call-start = ((), (), s32[]{:S(2)}) async-start(), calls=%async_computation | async-start | bytes 8146944 | tf_op jit(solution)/shard_map/all_gather | solution.py:706
  13.7 11.3 %collective-permute-start.1 = (bf16[48,1152]{1,0:T(8,128)(2,1)S(1)}, bf16[48,1152]{1,0:T(8,128)(2,1)S(1)}, u32[]{:S(2)}, u32[]{:S(2)}) collective-permute-start(bf16[48,1152]{1,0:T(8,128)(2,1)S(1)} %bitcast.84), channel_id=1, source_target_pairs={{0,4},{2,6},{4,0},{6,2},{1,5},{3,7},{5,1},{7,3},{8,12},{10,14},{12... | collective-permute-start | bytes 331784 | tf_op jit(solution)/shard_map/ppermute | solution.py:61
  16.3 10.3 %collective-permute-start.2 = (bf16[48,1152]{1,0:T(8,128)(2,1)S(1)}, bf16[48,1152]{1,0:T(8,128)(2,1)S(1)}, u32[]{:S(2)}, u32[]{:S(2)}) collective-permute-start(bf16[48,1152]{1,0:T(8,128)(2,1)S(1)} %bitcast.85), channel_id=1, source_target_pairs={{0,6},{2,4},{4,2},{6,0},{1,7},{3,5},{5,3},{7,1},{8,14},{10,12},{12... | collective-permute-start | bytes 331784 | tf_op jit(solution)/shard_map/ppermute | solution.py:61
  16.3 10.3 %collective-permute-start.3 = (bf16[48,1152]{1,0:T(8,128)(2,1)S(1)}, bf16[48,1152]{1,0:T(8,128)(2,1)S(1)}, u32[]{:S(2)}, u32[]{:S(2)}) collective-permute-start(bf16[48,1152]{1,0:T(8,128)(2,1)S(1)} %bitcast.86), channel_id=1, source_target_pairs={{0,8},{8,0},{16,24},{24,16},{1,9},{9,1},{17,25},{25,17},{2,10},{10... | collective-permute-start | bytes 331784 | tf_op jit(solution)/shard_map/ppermute | solution.py:61
  16.3 10.9 %collective-permute-start.7 = (bf16[48,1152]{1,0:T(8,128)(2,1)S(1)}, bf16[48,1152]{1,0:T(8,128)(2,1)S(1)}, u32[]{:S(2)}, u32[]{:S(2)}) collective-permute-start(bf16[48,1152]{1,0:T(8,128)(2,1)S(1)} %bitcast.87), channel_id=1, source_target_pairs={{0,16},{8,24},{16,0},{24,8},{1,17},{9,25},{17,1},{25,9},{2,18},{10... | collective-permute-start | bytes 331784 | tf_op jit(solution)/shard_map/ppermute | solution.py:61
  18.0 11.3 %collective-permute-start.4 = (bf16[48,1152]{1,0:T(8,128)(2,1)S(1)}, bf16[48,1152]{1,0:T(8,128)(2,1)S(1)}, u32[]{:S(2)}, u32[]{:S(2)}) collective-permute-start(bf16[48,1152]{1,0:T(8,128)(2,1)S(1)} %collective-permute-done.refs_1_), channel_id=1, source_target_pairs={{0,8},{8,0},{16,24},{24,16},{1,9},{9,1},{17,25},{25,17},{2,10},{10... | collective-permute-start | bytes 331784 | tf_op jit(solution)/shard_map/ppermute | solution.py:61
  42.0 31.9 %collective-permute-start.15 = (bf16[576,256]{1,0:T(8,128)(2,1)}, bf16[576,256]{1,0:T(8,128)(2,1)S(1)}, u32[]{:S(2)}, u32[]{:S(2)}) collective-permute-start(bf16[576,256]{1,0:T(8,128)(2,1)} %get-tuple-element.57), channel_id=1, source_target_pairs={{0,2},{2,0},{4,6},{6,4},{1,3},{3,1},{5,7},{7,5},{8,10},{10,8},{12,... | collective-permute-start | bytes 884744 | tf_op jit(solution)/shard_map/ppermute | solution.py:61
  47.5 28.2 %collective-permute-start.16 = (bf16[576,256]{1,0:T(8,128)(2,1)}, bf16[576,256]{1,0:T(8,128)(2,1)S(1)}, u32[]{:S(2)}, u32[]{:S(2)}) collective-permute-start(bf16[576,256]{1,0:T(8,128)(2,1)} %get-tuple-element.58), channel_id=1, source_target_pairs={{0,4},{2,6},{4,0},{6,2},{1,5},{3,7},{5,1},{7,3},{8,12},{10,14},{12... | collective-permute-start | bytes 884744 | tf_op jit(solution)/shard_map/ppermute | solution.py:61
  50.4 40.8 %collective-permute-start.17 = (bf16[576,256]{1,0:T(8,128)(2,1)}, bf16[576,256]{1,0:T(8,128)(2,1)S(1)}, u32[]{:S(2)}, u32[]{:S(2)}) collective-permute-start(bf16[576,256]{1,0:T(8,128)(2,1)} %get-tuple-element.59), channel_id=1, source_target_pairs={{0,6},{2,4},{4,2},{6,0},{1,7},{3,5},{5,3},{7,1},{8,14},{10,12},{12... | collective-permute-start | bytes 884744 | tf_op jit(solution)/shard_map/ppermute | solution.py:61
  103.3 17.9 %collective-permute-start.18 = (bf16[192,256]{1,0:T(8,128)(2,1)}, bf16[192,256]{1,0:T(8,128)(2,1)S(1)}, u32[]{:S(2)}, u32[]{:S(2)}) collective-permute-start(bf16[192,256]{1,0:T(8,128)(2,1)} %get-tuple-element.61), channel_id=1, source_target_pairs={{0,2},{2,0},{4,6},{6,4},{1,3},{3,1},{5,7},{7,5},{8,10},{10,8},{12,... | collective-permute-start | bytes 294920 | tf_op jit(solution)/shard_map/ppermute | solution.py:61
  131.2 17.6 %collective-permute-start.21 = (bf16[512,768]{1,0:T(8,128)(2,1)}, bf16[512,768]{1,0:T(8,128)(2,1)S(1)}, u32[]{:S(2)}, u32[]{:S(2)}) collective-permute-start(bf16[512,768]{1,0:T(8,128)(2,1)} %get-tuple-element.64.own), channel_id=1, source_target_pairs={{0,1},{1,0},{2,3},{3,2},{4,5},{5,4},{6,7},{7,6},{8,9},{9,8},{10,11... | collective-permute-start | bytes 2359304 | tf_op jit(solution)/shard_map/ppermute | solution.py:61
  161.8 17.3 %collective-permute-start.22 = (bf16[512,768]{1,0:T(8,128)(2,1)}, bf16[512,768]{1,0:T(8,128)(2,1)S(1)}, u32[]{:S(2)}, u32[]{:S(2)}) collective-permute-start(bf16[512,768]{1,0:T(8,128)(2,1)} %get-tuple-element.66.own), channel_id=1, source_target_pairs={{0,1},{1,0},{2,3},{3,2},{4,5},{5,4},{6,7},{7,6},{8,9},{9,8},{10,11... | collective-permute-start | bytes 2359304 | tf_op jit(solution)/shard_map/ppermute | solution.py:61
  208.3 126.1 %collective-permute-start.45 = (bf16[384,4608]{1,0:T(8,128)(2,1)}, bf16[384,4608]{1,0:T(8,128)(2,1)}, u32[]{:S(2)}, u32[]{:S(2)}) collective-permute-start(bf16[384,4608]{1,0:T(8,128)(2,1)} %get-tuple-element.99), channel_id=1, source_target_pairs={{0,8},{8,0},{16,24},{24,16},{1,9},{9,1},{17,25},{25,17},{2,10},{10... | collective-permute-start | bytes 10616840 | tf_op jit(solution)/shard_map/ppermute | solution.py:61
  208.4 19.9 %collective-permute-start.23 = (bf16[512,768]{1,0:T(8,128)(2,1)S(1)}, bf16[512,768]{1,0:T(8,128)(2,1)S(1)}, u32[]{:S(2)}, u32[]{:S(2)}) collective-permute-start(bf16[512,768]{1,0:T(8,128)(2,1)S(1)} %copy-done.6), channel_id=1, source_target_pairs={{0,1},{1,0},{2,3},{3,2},{4,5},{5,4},{6,7},{7,6},{8,9},{9,8},{10,11... | collective-permute-start | bytes 2359304 | tf_op jit(solution)/shard_map/ppermute | solution.py:61
  243.0 31.0 %collective-permute-start.40 = (bf16[384,384]{1,0:T(8,128)(2,1)}, bf16[384,384]{1,0:T(8,128)(2,1)S(1)}, u32[]{:S(2)}, u32[]{:S(2)}) collective-permute-start(bf16[384,384]{1,0:T(8,128)(2,1)} %get-tuple-element.92), channel_id=1, source_target_pairs={{0,8},{8,0},{16,24},{24,16},{1,9},{9,1},{17,25},{25,17},{2,10},{10... | collective-permute-start | bytes 884744 | tf_op jit(solution)/shard_map/ppermute | solution.py:61
  265.4 18.0 %collective-permute-start.27 = (bf16[576,256]{1,0:T(8,128)(2,1)}, bf16[576,256]{1,0:T(8,128)(2,1)S(1)}, u32[]{:S(2)}, u32[]{:S(2)}) collective-permute-start(bf16[576,256]{1,0:T(8,128)(2,1)} %get-tuple-element.82), channel_id=1, source_target_pairs={{0,2},{2,0},{4,6},{6,4},{1,3},{3,1},{5,7},{7,5},{8,10},{10,8},{12,... | collective-permute-start | bytes 884744 | tf_op jit(solution)/shard_map/ppermute | solution.py:61
  267.3 23.6 %collective-permute-start.28 = (bf16[576,256]{1,0:T(8,128)(2,1)}, bf16[576,256]{1,0:T(8,128)(2,1)S(1)}, u32[]{:S(2)}, u32[]{:S(2)}) collective-permute-start(bf16[576,256]{1,0:T(8,128)(2,1)} %get-tuple-element.83), channel_id=1, source_target_pairs={{0,4},{2,6},{4,0},{6,2},{1,5},{3,7},{5,1},{7,3},{8,12},{10,14},{12... | collective-permute-start | bytes 884744 | tf_op jit(solution)/shard_map/ppermute | solution.py:61
  267.3 23.6 %collective-permute-start.29 = (bf16[576,256]{1,0:T(8,128)(2,1)}, bf16[576,256]{1,0:T(8,128)(2,1)S(1)}, u32[]{:S(2)}, u32[]{:S(2)}) collective-permute-start(bf16[576,256]{1,0:T(8,128)(2,1)} %get-tuple-element.84), channel_id=1, source_target_pairs={{0,6},{2,4},{4,2},{6,0},{1,7},{3,5},{5,3},{7,1},{8,14},{10,12},{12... | collective-permute-start | bytes 884744 | tf_op jit(solution)/shard_map/ppermute | solution.py:61
  274.8 34.9 %collective-permute-start.41 = (bf16[192,384]{1,0:T(8,128)(2,1)}, bf16[192,384]{1,0:T(8,128)(2,1)}, u32[]{:S(2)}, u32[]{:S(2)}) collective-permute-start(bf16[192,384]{1,0:T(8,128)(2,1)} %slice.97), channel_id=1, source_target_pairs={{0,16},{8,24},{16,0},{24,8},{1,17},{9,25},{17,1},{25,9},{2,18},{10... | collective-permute-start | bytes 442376 | tf_op jit(solution)/shard_map/ppermute | solution.py:61
  312.1 19.6 %collective-permute-start.44 = (bf16[48,384]{1,0:T(8,128)(2,1)}, bf16[48,384]{1,0:T(8,128)(2,1)}, u32[]{:S(2)}, u32[]{:S(2)}) collective-permute-start(bf16[48,384]{1,0:T(8,128)(2,1)} %get-tuple-element.117), channel_id=1, source_target_pairs={{0,6},{2,4},{4,2},{6,0},{1,7},{3,5},{5,3},{7,1},{8,14},{10,12},{12... | collective-permute-start | bytes 110600 | tf_op jit(solution)/shard_map/ppermute | solution.py:61
  314.3 17.5 %collective-permute-start.43 = (bf16[48,384]{1,0:T(8,128)(2,1)}, bf16[48,384]{1,0:T(8,128)(2,1)}, u32[]{:S(2)}, u32[]{:S(2)}) collective-permute-start(bf16[48,384]{1,0:T(8,128)(2,1)} %get-tuple-element.118), channel_id=1, source_target_pairs={{0,4},{2,6},{4,0},{6,2},{1,5},{3,7},{5,1},{7,3},{8,12},{10,14},{12... | collective-permute-start | bytes 110600 | tf_op jit(solution)/shard_map/ppermute | solution.py:61
  314.3 18.0 %collective-permute-start.42 = (bf16[48,384]{1,0:T(8,128)(2,1)}, bf16[48,384]{1,0:T(8,128)(2,1)}, u32[]{:S(2)}, u32[]{:S(2)}) collective-permute-start(bf16[48,384]{1,0:T(8,128)(2,1)} %get-tuple-element.116), channel_id=1, source_target_pairs={{0,2},{2,0},{4,6},{6,4},{1,3},{3,1},{5,7},{7,5},{8,10},{10,8},{12,... | collective-permute-start | bytes 110600 | tf_op jit(solution)/shard_map/ppermute | solution.py:61
  317.1 12.3 %collective-permute-start.38 = (f32[8,768]{1,0:T(8,128)}, f32[8,768]{1,0:T(8,128)}, u32[]{:S(2)}, u32[]{:S(2)}) collective-permute-start(f32[8,768]{1,0:T(8,128)} %add.104), channel_id=1, source_target_pairs={{0,16},{8,24},{16,0},{24,8},{1,17},{9,25},{17,1},{25,9},{2,18},{10... | collective-permute-start | bytes 73736 | tf_op jit(solution)/shard_map/ppermute | solution.py:61
  329.4 15.7 %collective-permute-start.30 = (bf16[512,768]{1,0:T(8,128)(2,1)}, bf16[512,768]{1,0:T(8,128)(2,1)}, u32[]{:S(2)}, u32[]{:S(2)}) collective-permute-start(bf16[512,768]{1,0:T(8,128)(2,1)} %get-tuple-element.85), channel_id=1, source_target_pairs={{0,1},{1,0},{2,3},{3,2},{4,5},{5,4},{6,7},{7,6},{8,9},{9,8},{10,11... | collective-permute-start | bytes 2359304 | tf_op jit(solution)/shard_map/ppermute | solution.py:61
  331.7 10.9 %collective-permute-start.31 = (bf16[384,1152]{1,0:T(8,128)(2,1)}, bf16[384,1152]{1,0:T(8,128)(2,1)S(1)}, u32[]{:S(2)}, u32[]{:S(2)}) collective-permute-start(bf16[384,1152]{1,0:T(8,128)(2,1)} %get-tuple-element.87), channel_id=1, source_target_pairs={{0,8},{8,0},{16,24},{24,16},{1,9},{9,1},{17,25},{25,17},{2,10},{10... | collective-permute-start | bytes 2654216 | tf_op jit(solution)/shard_map/ppermute | solution.py:61
  340.5 56.2 %collective-permute-start.46 = (bf16[192,4608]{1,0:T(8,128)(2,1)S(1)}, bf16[192,4608]{1,0:T(8,128)(2,1)}, u32[]{:S(2)}, u32[]{:S(2)}) collective-permute-start(bf16[192,4608]{1,0:T(8,128)(2,1)S(1)} %slice.95), channel_id=1, source_target_pairs={{0,16},{8,24},{16,0},{24,8},{1,17},{9,25},{17,1},{25,9},{2,18},{10... | collective-permute-start | bytes 5308424 | tf_op jit(solution)/shard_map/ppermute | solution.py:61
  343.6 47.5 %collective-permute-start.32 = (bf16[192,1152]{1,0:T(8,128)(2,1)}, bf16[192,1152]{1,0:T(8,128)(2,1)}, u32[]{:S(2)}, u32[]{:S(2)}) collective-permute-start(bf16[192,1152]{1,0:T(8,128)(2,1)} %slice.96), channel_id=1, source_target_pairs={{0,16},{8,24},{16,0},{24,8},{1,17},{9,25},{17,1},{25,9},{2,18},{10... | collective-permute-start | bytes 1327112 | tf_op jit(solution)/shard_map/ppermute | solution.py:61
  393.0 29.9 %collective-permute-start.34 = (bf16[48,1152]{1,0:T(8,128)(2,1)S(1)}, bf16[48,1152]{1,0:T(8,128)(2,1)S(1)}, u32[]{:S(2)}, u32[]{:S(2)}) collective-permute-start(bf16[48,1152]{1,0:T(8,128)(2,1)S(1)} %get-tuple-element.115), channel_id=1, source_target_pairs={{0,4},{2,6},{4,0},{6,2},{1,5},{3,7},{5,1},{7,3},{8,12},{10,14},{12... | collective-permute-start | bytes 331784 | tf_op jit(solution)/shard_map/ppermute | solution.py:61
  393.8 29.1 %collective-permute-start.33 = (bf16[48,1152]{1,0:T(8,128)(2,1)S(1)}, bf16[48,1152]{1,0:T(8,128)(2,1)S(1)}, u32[]{:S(2)}, u32[]{:S(2)}) collective-permute-start(bf16[48,1152]{1,0:T(8,128)(2,1)S(1)} %get-tuple-element.113), channel_id=1, source_target_pairs={{0,2},{2,0},{4,6},{6,4},{1,3},{3,1},{5,7},{7,5},{8,10},{10,8},{12,... | collective-permute-start | bytes 331784 | tf_op jit(solution)/shard_map/ppermute | solution.py:61
  398.7 25.0 %collective-permute-start.49 = (bf16[48,4608]{1,0:T(8,128)(2,1)S(1)}, bf16[48,4608]{1,0:T(8,128)(2,1)S(1)}, u32[]{:S(2)}, u32[]{:S(2)}) collective-permute-start(bf16[48,4608]{1,0:T(8,128)(2,1)S(1)} %get-tuple-element.111), channel_id=1, source_target_pairs={{0,6},{2,4},{4,2},{6,0},{1,7},{3,5},{5,3},{7,1},{8,14},{10,12},{12... | collective-permute-start | bytes 1327112 | tf_op jit(solution)/shard_map/ppermute | solution.py:61
  399.4 42.1 %collective-permute-start.48 = (bf16[48,4608]{1,0:T(8,128)(2,1)S(1)}, bf16[48,4608]{1,0:T(8,128)(2,1)S(1)}, u32[]{:S(2)}, u32[]{:S(2)}) collective-permute-start(bf16[48,4608]{1,0:T(8,128)(2,1)S(1)} %get-tuple-element.112), channel_id=1, source_target_pairs={{0,4},{2,6},{4,0},{6,2},{1,5},{3,7},{5,1},{7,3},{8,12},{10,14},{12... | collective-permute-start | bytes 1327112 | tf_op jit(solution)/shard_map/ppermute | solution.py:61
  400.3 41.3 %collective-permute-start.47 = (bf16[48,4608]{1,0:T(8,128)(2,1)S(1)}, bf16[48,4608]{1,0:T(8,128)(2,1)S(1)}, u32[]{:S(2)}, u32[]{:S(2)}) collective-permute-start(bf16[48,4608]{1,0:T(8,128)(2,1)S(1)} %get-tuple-element.110), channel_id=1, source_target_pairs={{0,2},{2,0},{4,6},{6,4},{1,3},{3,1},{5,7},{7,5},{8,10},{10,8},{12,... | collective-permute-start | bytes 1327112 | tf_op jit(solution)/shard_map/ppermute | solution.py:61
  (62 other events, 480.2 us)
Sparse Core Ops, SparseCore 0:
  10.8 97.6 all-gather.1

commit v2 on v1

--- a/solution.py
+++ b/solution.py
@@ -15,6 +15,7 @@
 FAR = 1e30
 TILE = 64
 BLOCK = 384
+EXTRA = 16
 
 epsilon = 1e-12
 f32 = jnp.float32
@@ -516,7 +517,7 @@
     return pl.pallas_call(
         functools.partial(weight_kernel, steps),
         grid=(3 * steps,),
-        out_shape=[shape((model // 2, 3 * hidden_units), bf16)] * 2,
+        out_shape=[shape((model // 2, 3 * hidden_units + BLOCK), bf16)] * 2,
         in_specs=[SMEM, whole, whole, column(0), column(steps), column(2 * steps)],
         out_specs=[out, out],
         scratch_shapes=[pltpu.VMEM((2, model, tokens), bf16)],
@@ -527,7 +528,7 @@
 
 
 def mix_back_kernel(
-    n, seqs, heads, ids, tok, own, other, dz2, hown, hother, vec, wo, mixed, *refs
+    n, seqs, heads, ids, tok, own, other, dz2, hown, hother, vec, wo, mixed, far, near, *refs
 ):
     sends = refs[:n]
     dz1, send, keep, sums = refs[n : n + 4]
@@ -558,22 +559,25 @@
     write_rows(ids, left, mixed[...], send, keep)
 
 
-def mix_back(ids, tok, own, other, dz2, hown, hother, vec, packed, mixed, n, seqs, heads):
+def mix_back(ids, tok, own, other, dz2, hown, hother, vec, packed, mixed, grads, n, seqs, heads):
     tokens, model = tok.shape
     slots = tokens // seqs
     width = heads * HD
     size = seqs * heads // n * HD
+    last = pl.BlockSpec((model // 2, width), lambda i: (0, grads[0].shape[1] // width - 1))
     return pl.pallas_call(
         functools.partial(mix_back_kernel, n, seqs, heads),
         grid=(1,),
         out_shape=[shape((size, slots), bf16)] * n
         + [shape((tokens, model), f32)]
-        + [shape((model // 2, width), bf16)] * 2
+        + [shape(grads[0].shape, bf16)] * 2
         + [shape((8, model), f32)],
         in_specs=[SMEM]
         + [VMEM] * 7
-        + [pl.BlockSpec((model, width), lambda i: (0, 0)), VMEM],
-        out_specs=[VMEM] * (n + 4),
+        + [pl.BlockSpec((model, width), lambda i: (0, 0)), VMEM]
+        + [pl.BlockSpec(memory_space=pl.ANY)] * 2,
+        out_specs=[VMEM] * (n + 1) + [last, last, VMEM],
+        input_output_aliases={10: n + 1, 11: n + 2},
         scratch_shapes=[
             pltpu.VMEM((size * n, slots), bf16),
             pltpu.VMEM((model, tokens), bf16),
@@ -581,13 +585,13 @@
         compiler_params=params("arbitrary"),
         cost_estimate=cost(4 * tokens * model * width, 10e6),
         name="mix_back",
-    )(ids, tok, own, other, dz2, hown, hother, vec, packed, mixed)
-
-
-def project_back_kernel(n, seqs, heads, ids, tok, whole, *refs):
+    )(ids, tok, own, other, dz2, hown, hother, vec, packed, mixed, *grads)
+
+
+def project_back_kernel(n, seqs, heads, ids, tok, whole, small, *refs):
     inputs = refs[:n]
-    part, send, keep, sums = refs[n : n + 4]
-    stage, right, left = refs[n + 4 :]
+    part, send, keep = refs[n : n + 3]
+    stage, right, left = refs[n + 3 :]
     z = ids[2]
     slots = inputs[0].shape[1]
     per = seqs * heads // n
@@ -610,10 +614,17 @@
         cols = slice(c * width, (c + 1) * width)
         write_rows(ids, left, right[:, cols], send.at[:, cols], keep.at[:, cols])
     ones = jnp.ones((8, right.shape[0]), bf16)
-    sums[...] = dot_nn(ones, right[...])
-
-
-def project_back(ids, tok, whole, blocks, n, seqs, heads):
+    sums = dot_nn(ones, right[...])
+    line = jnp.concatenate([sums[:, :width], sums[:, 2 * width :]], axis=1)
+    row = lax.broadcasted_iota(jnp.int32, (8, 1), 0)
+    rows = jnp.where(row == 6, line, small[...])
+    rows = jnp.concatenate([rows, jnp.zeros_like(rows)], axis=0).astype(bf16)
+    for ref in (send, keep):
+        ref[ref.shape[0] - EXTRA :, :] = jnp.zeros((EXTRA, ref.shape[1]), bf16)
+        ref[ref.shape[0] - EXTRA :, : 2 * width] = rows
+
+
+def project_back(ids, tok, whole, small, blocks, n, seqs, heads):
     tokens, model = tok.shape
     slots = tokens // seqs
     wide = whole.shape[1]
@@ -621,12 +632,11 @@
         functools.partial(project_back_kernel, n, seqs, heads),
         out_shape=[
             shape((tokens, model), bf16),
-            shape((model // 2, wide), bf16),
-            shape((model // 2, wide), bf16),
-            shape((8, wide), f32),
+            shape((model // 2 + EXTRA, wide), bf16),
+            shape((model // 2 + EXTRA, wide), bf16),
         ],
-        in_specs=[SMEM] + [VMEM] * (2 + n),
-        out_specs=[VMEM] * 4,
+        in_specs=[SMEM] + [VMEM] * (3 + n),
+        out_specs=[VMEM] * 3,
         scratch_shapes=[
             pltpu.VMEM((seqs * heads * 3 * HD, slots), bf16),
             pltpu.VMEM((tokens, wide), bf16),
@@ -635,29 +645,73 @@
         compiler_params=params(),
         cost_estimate=cost(4 * tokens * model * wide, 8e6),
         name="project_back",
-    )(ids, tok, whole, *blocks)
-
-
-def own_rows(send, keep, n):
-    half = keep.shape[0] // 2
-    pair = keep.astype(f32) + swap(send, "shard", 1).astype(f32)
-    mine = pair[:half] + swap(pair[half:].astype(bf16), "shard", 2).astype(f32)
-    blocks = mine.reshape(n, half // n, mine.shape[1])
-    rank = lax.axis_index("ctx")
-    total = lax.dynamic_index_in_dim(blocks, rank, 0, keepdims=False)
-    for d in range(1, n):
-        block = lax.dynamic_index_in_dim(blocks, rank ^ d, 0, keepdims=False)
-        total = total + swap(block.astype(bf16), "ctx", d).astype(f32)
-    return total
-
-
-def everywhere_sum(value, n):
-    distance = 1
-    while distance < n:
-        value = value + swap(value, "ctx", distance)
-        distance *= 2
-    value = value + swap(value, "shard", 2)
-    return value + swap(value, "shard", 1)
+    )(ids, tok, whole, small, *blocks)
+
+
+def fold_core_kernel(extra, keep, recv, mine, send):
+    half = (keep.shape[0] - extra) // 2
+    mine[0:half, :] = keep[0:half, :].astype(f32) + recv[0:half, :].astype(f32)
+    rest = (keep[half:, :].astype(f32) + recv[half:, :].astype(f32)).astype(bf16)
+    send[...] = rest
+    if extra:
+        mine[half:, :] = rest[half:, :].astype(f32)
+
+
+def fold_core(keep, recv, extra):
+    rows, wide = keep.shape
+    out = (rows - extra) // 2 + extra
+    steps = 1 if extra else 3
+    column = lambda size: pl.BlockSpec((size, wide // steps), lambda j: (0, j))
+    return pl.pallas_call(
+        functools.partial(fold_core_kernel, extra),
+        grid=(steps,),
+        out_shape=[shape((out, wide), f32), shape((out, wide), bf16)],
+        in_specs=[column(rows)] * 2,
+        out_specs=[column(out)] * 2,
+        compiler_params=params("arbitrary"),
+        cost_estimate=cost(rows * wide, 7 * rows * wide),
+        name="fold_core",
+    )(keep, recv)
+
+
+def fold_y_kernel(n, extra, ids, mine, recv, own, *refs):
+    sends, stage = refs[:-1], refs[-1]
+    z = ids[2]
+    rows = mine.shape[0] - extra
+    size = rows // n
+    stage[...] = mine[...] + recv[...].astype(f32)
+    for d in range(n):
+        block = stage[pl.ds(pl.multiple_of((z ^ d) * size, size), size), :]
+        if d:
+            sends[d - 1][0:size, :] = block.astype(bf16)
+            if extra:
+                sends[d - 1][size:, :] = stage[rows:, :].astype(bf16)
+        else:
+            own[0:size, :] = block
+            if extra:
+                own[size:, :] = stage[rows:, :].astype(bf16).astype(f32)
+
+
+def fold_y(ids, mine, recv, n, extra):
+    rows, wide = mine.shape
+    out = (rows - extra) // n + extra
+    steps = 1 if extra else 3
+    column = lambda size: pl.BlockSpec((size, wide // steps), lambda j: (0, j))
+    return pl.pallas_call(
+        functools.partial(fold_y_kernel, n, extra),
+        grid=(steps,),
+        out_shape=[shape((out, wide), f32)] + [shape((out, wide), bf16)] * (n - 1),
+        in_specs=[SMEM] + [column(rows)] * 2,
+        out_specs=[column(out)] * n,
+        scratch_shapes=[pltpu.VMEM((rows, wide // steps), f32)],
+        compiler_params=params("arbitrary"),
+        cost_estimate=cost(rows * wide, 9 * rows * wide),
+        name="fold_y",
+    )(ids, mine, recv)
+
+
+def fold_z(own, got):
+    return (own + got[0].astype(f32)) + (got[1].astype(f32) + got[2].astype(f32))
 
 
 def fits(tokens, b_qv, w_qkv, w_gu):
@@ -718,32 +772,46 @@
         ids, lengths, hidden, ffn, ffn_other, cot, vectors, packed, gel, slope, n, seqs, width
     )
     back_other = swap(back, "tp", 1)
-    unit_send, unit_keep = weight_grads(ids, low, dffn, dgate, dup, act)
-    *sends, dz1, out_send, out_keep, sums_one = mix_back(
-        ids, tok, part, part_other, dz2, back, back_other, vectors, packed, mixed, n, seqs, heads
+    unit_grads = weight_grads(ids, low, dffn, dgate, dup, act)
+    back_other, *unit_grads = lax.optimization_barrier((back_other, *unit_grads))
+    *sends, dz1, far, near, sums_one = mix_back(
+        ids, tok, part, part_other, dz2, back, back_other, vectors, packed, mixed, unit_grads,
+        n, seqs, heads,
     )
     grads = [sends[0]] + [swap(sends[d], "ctx", d) for d in range(1, n)]
+    got = swap(far, "shard", 1)
+    mine, far = fold_core(near, got, 0)
+    *grads, far = lax.optimization_barrier((*grads, far))
+    got = swap(far, "shard", 2)
     outs = attend_back(ids, lengths, slopes, blocks, grads, att, den, n, heads, per)
     outs = [outs[0]] + [swap(outs[d], "ctx", d) for d in range(1, n)]
-    dx, qkv_send, qkv_keep, sums_bias = project_back(ids, tok, whole, outs, n, seqs, heads)
-    input_grad = dz1 + (dx.astype(f32) + swap(dx, "tp", 1).astype(f32))
-
-    grad_unit = own_rows(unit_send, unit_keep, n)
-    grad_out = own_rows(out_send, out_keep, n)
-    grad_qkv = own_rows(qkv_send, qkv_keep, n)
-    bias_row = jnp.concatenate([sums_bias[0:1, :width], sums_bias[0:1, 2 * width :]], axis=1)
+    *outs, got = lax.optimization_barrier((*outs, got))
+    rest_own, *rest_sends = fold_y(ids, mine, got, n, 0)
+    *outs, rest_own = lax.optimization_barrier((*outs, rest_own))
     small = jnp.concatenate(
-        [sums_one[0:2], sums_two[0:2], sums_one[2:3], sums_two[2:3], bias_row, jnp.zeros_like(bias_row)]
-    )
-    small = everywhere_sum(small, n)
+        [sums_one[0:2], sums_two[0:2], sums_one[2:3], sums_two[2:3], jnp.zeros_like(sums_one[:2])]
+    )
+    dx, far, near = project_back(ids, tok, whole, small, outs, n, seqs, heads)
+    got = swap(far, "shard", 1)
+    dx_other = swap(dx, "tp", 1)
+    mine, far = fold_core(near, got, EXTRA)
+    got = swap(far, "shard", 2)
+    own, *sends = fold_y(ids, mine, got, n, EXTRA)
+    rest_got = [swap(block, "ctx", d + 1) for d, block in enumerate(rest_sends)]
+    got = [swap(block, "ctx", d + 1) for d, block in enumerate(sends)]
+    *rest_got, got[0] = lax.optimization_barrier((*rest_got, got[0]))
+    rest = fold_z(rest_own, rest_got)
+    last = fold_z(own, got)
+    input_grad = dz1 + (dx.astype(f32) + dx_other.astype(f32))
+    small = last[rows : rows + 8, : 2 * width]
     return (
         output.reshape(tokens.shape),
         input_grad.reshape(tokens.shape),
-        grad_qkv.reshape(w_qkv.shape),
+        last[:rows].reshape(w_qkv.shape),
         small[6].reshape(2, width),
-        grad_out.T,
-        grad_unit[:, : 2 * units].reshape(w_gu.shape),
-        grad_unit[:, 2 * units :].T,
+        rest[:, 3 * units :].T,
+        rest[:, : 2 * units].reshape(w_gu.shape),
+        rest[:, 2 * units : 3 * units].T,
         small[:6],
     )
 

time: 450 us -> 377 us (0.84)
  waiting for transfers between devices: 209 us -> 152 us
  starting transfers between devices: 98.2 us -> 77.1 us
  Pallas kernels: 86.8 us -> 104 us
  other arithmetic: 18.8 us -> 7.33 us
    ppermute x50 -> x41, waiting for transfers between devices: 209 us -> 152 us  [swap(): return lax.ppermute(value, axis, xor_pairs(axis, distance))]
    ppermute x50 -> x41, starting transfers between devices: 98.1 us -> 77.1 us  [swap(): return lax.ppermute(value, axis, xor_pairs(axis, distance))]
    pallas_call x0 -> x4, Pallas kernels: none -> 16.6 us  [the longest x2 9.37 us: fold_core(): pl.pallas_call(functools.partial(fold_core_kernel, extra), grid=(steps,),...]
    add x13 -> x3, other arithmetic: 12.9 us -> 1.71 us  [the longest x1 1.41 us: on_device(): input_grad = dz1 + (dx.astype(f32) + dx_other.astype(f32))]
    unnamed x87 -> x89, local copies, waits for them, and re-layouts: 9.66 us -> 10.2 us
  transfers between devices with their start and end apart: 51 -> 42, of which waited for: 22 -> 21; matrix products, arithmetic and copies ran while one was open for 6% -> 2% of each run, Pallas kernels for 10% -> 15%
where the time goes in v2:
time: 377 us; the launch traced here: 373 us
  waiting for transfers between devices  152 us (40%)
  Pallas kernels  104 us (28%)
  starting transfers between devices  77.1 us (20%)
  local copies, waits for them, and re-layouts  19.2 us (5%)
  between operations  14.5 us (4%)
  other arithmetic  7.33 us (2%)
    ppermute x41, waiting for transfers between devices, swap(): return lax.ppermute(value, axis, xor_pairs(axis, distance))  152 us
    ppermute x41, starting transfers between devices, swap(): return lax.ppermute(value, axis, xor_pairs(axis, distance))  77.1 us
    pallas_call x1, Pallas kernels, attend_back(): pl.pallas_call(functools.partial(attend_back_kernel, n, heads), grid=(per...  15 us
    pallas_call x1, Pallas kernels, unit_back(): pl.pallas_call(functools.partial(unit_back_kernel, n, seqs), grid=(steps,...  14.8 us
    pallas_call x1, Pallas kernels, weight_grads(): pl.pallas_call(functools.partial(weight_kernel, steps), grid=(3 * steps,)...  13.5 us
    pallas_call x1, Pallas kernels, unit(): pl.pallas_call(unit_kernel, grid=(steps,), out_shape=[shape((tokens, mode...  12 us
    pallas_call x1, Pallas kernels, attend(): pl.pallas_call(functools.partial(attend_kernel, n, heads), grid=(per,), o...  11.4 us
    unnamed x89, local copies, waits for them, and re-layouts  10.2 us
  transfers between devices with their start and end apart: 42, of which 21 were waited for; matrix products, arithmetic and copies ran while one was open for 2% of the time, Pallas kernels for 15%

profile of v2, /device:TPU:0, one launch (start us, length us, event | category | flops | bytes accessed | tf_op | source)
XLA Modules:
  0.0 373.3 jit_solution(11346548492605345005)
XLA Ops:
  15.3 3.6 collective-permute-start.2
  19.8 3.4 collective-permute-done.2.refs_3_
  24.0 10.3 %collective-permute-done.1.refs_2_ = bf16[48,1152]{1,0:T(8,128)(2,1)S(1)} collective-permute-done((bf16[48,1152]{1,0:T(8,128)(2,1)S(1)}, bf16[48,1152]{1,0:T(8,128)(2,1)S(1)}, u32[]{:S(2)}, u32[]{:S(2)}) %collective-permute-start.1) | collective-permute-done | bytes 110624 | tf_op jit(solution)/shard_map/ppermute | solution.py:62
  42.2 4.8 %project.1 = (bf16[576,256]{1,0:T(8,128)(2,1)}, bf16[576,256]{1,0:T(8,128)(2,1)}, bf16[576,256]{1,0:T(8,128)(2,1)}, bf16[576,256]{1,0:T(8,128)(2,1)}, bf16[768,1152]{1,0:T(8,128)(2,1)}) custom-call(s32[4]{0:T(128)} %pad_add_fusion.ids, bf16[512,768]{1,0:T(8,128)(2,1)} %bitcast.25, f32[1,1152]{1,0:T(1,128)} %broadcast_in_dim.10.bias, ...), custom_call_target="tpu_custom_call" | custom-call | flops 905969664 | bytes 6000000 | tf_op jit(solution)/shard_map/project/pallas_call | solution.py:117
  47.3 4.4 %collective-permute-start.16 = (bf16[576,256]{1,0:T(8,128)(2,1)}, bf16[576,256]{1,0:T(8,128)(2,1)S(1)}, u32[]{:S(2)}, u32[]{:S(2)}) collective-permute-start(bf16[576,256]{1,0:T(8,128)(2,1)} %get-tuple-element.91), channel_id=1, source_target_pairs={{0,4},{2,6},{4,0},{6,2},{1,5},{3,7},{5,1},{7,3},{8,12},{10,14},{12... | collective-permute-start | bytes 884744 | tf_op jit(solution)/shard_map/ppermute | solution.py:62
  51.8 21.9 %collective-permute-done.15.refs_1_ = bf16[576,256]{1,0:T(8,128)(2,1)S(1)} collective-permute-done((bf16[576,256]{1,0:T(8,128)(2,1)}, bf16[576,256]{1,0:T(8,128)(2,1)S(1)}, u32[]{:S(2)}, u32[]{:S(2)}) %collective-permute-start.15) | collective-permute-done | bytes 294944 | tf_op jit(solution)/shard_map/ppermute | solution.py:62
  73.7 9.4 %collective-permute-done.16.refs_2_ = bf16[576,256]{1,0:T(8,128)(2,1)S(1)} collective-permute-done((bf16[576,256]{1,0:T(8,128)(2,1)}, bf16[576,256]{1,0:T(8,128)(2,1)S(1)}, u32[]{:S(2)}, u32[]{:S(2)}) %collective-permute-start.16) | collective-permute-done | bytes 294944 | tf_op jit(solution)/shard_map/ppermute | solution.py:62
  83.1 7.1 %collective-permute-done.17.refs_3_ = bf16[576,256]{1,0:T(8,128)(2,1)S(1)} collective-permute-done((bf16[576,256]{1,0:T(8,128)(2,1)}, bf16[576,256]{1,0:T(8,128)(2,1)S(1)}, u32[]{:S(2)}, u32[]{:S(2)}) %collective-permute-start.17) | collective-permute-done | bytes 294944 | tf_op jit(solution)/shard_map/ppermute | solution.py:62
  90.9 11.4 %attend.1 = (bf16[192,256]{1,0:T(8,128)(2,1)}, bf16[192,256]{1,0:T(8,128)(2,1)}, bf16[192,256]{1,0:T(8,128)(2,1)}, bf16[192,256]{1,0:T(8,128)(2,1)}, f32[192,1024]{1,0:T(8,128)}, /*index=5*/f32[3,1,1024]{2,1,0:T(1,128)}) custom-call(s32[4]{0:T(128)} %pad_add_fusion.ids, s32[2]{0:T(128)} %lens.5, f32[12]{0:T(128)} %constant.40.clone.slopes, ...), custom_call_target="tpu_custom_call" | custom-call | flops 1610612736 | bytes 3000000 | tf_op jit(solution)/shard_map/attend/pallas_call | solution.py:198
  102.3 16.9 %collective-permute-start.18 = (bf16[192,256]{1,0:T(8,128)(2,1)}, bf16[192,256]{1,0:T(8,128)(2,1)S(1)}, u32[]{:S(2)}, u32[]{:S(2)}) collective-permute-start(bf16[192,256]{1,0:T(8,128)(2,1)} %get-tuple-element.94), channel_id=1, source_target_pairs={{0,2},{2,0},{4,6},{6,4},{1,3},{3,1},{5,7},{7,5},{8,10},{10,8},{12,... | collective-permute-start | bytes 294920 | tf_op jit(solution)/shard_map/ppermute | solution.py:62
  122.1 5.8 %collective-permute-done.19.refs_2_ = bf16[192,256]{1,0:T(8,128)(2,1)S(1)} collective-permute-done((bf16[192,256]{1,0:T(8,128)(2,1)}, bf16[192,256]{1,0:T(8,128)(2,1)S(1)}, u32[]{:S(2)}, u32[]{:S(2)}) %collective-permute-start.19) | collective-permute-done | bytes 98336 | tf_op jit(solution)/shard_map/ppermute | solution.py:62
  133.0 14.2 %collective-permute-done.21.other = bf16[512,768]{1,0:T(8,128)(2,1)S(1)} collective-permute-done((bf16[512,768]{1,0:T(8,128)(2,1)}, bf16[512,768]{1,0:T(8,128)(2,1)S(1)}, u32[]{:S(2)}, u32[]{:S(2)}) %collective-permute-start.21) | collective-permute-done | bytes 786464 | tf_op jit(solution)/shard_map/ppermute | solution.py:62
  148.0 12.0 %unit.1 = (f32[512,768]{1,0:T(8,128)}, bf16[512,768]{1,0:T(8,128)(2,1)}, bf16[512,1536]{1,0:T(8,128)(2,1)}, bf16[512,1536]{1,0:T(8,128)(2,1)}, bf16[512,1536]{1,0:T(8,128)(2,1)}, /*index=5*/bf16[512,768]{1,0:T(8,128)(2,1)}) custom-call(bf16[512,768]{1,0:T(8,128)(2,1)} %bitcast.26, bf16[512,768]{1,0:T(8,128)(2,1)} %get-tuple-element.97.own, ...), custom_call_target="tpu_custom_call" | custom-call | flops 3623878656 | bytes 20000000 | tf_op jit(solution)/shard_map/unit/pallas_call | solution.py:382
  161.9 13.3 %collective-permute-done.22.other = bf16[512,768]{1,0:T(8,128)(2,1)S(1)} collective-permute-done((bf16[512,768]{1,0:T(8,128)(2,1)}, bf16[512,768]{1,0:T(8,128)(2,1)S(1)}, u32[]{:S(2)}, u32[]{:S(2)}) %collective-permute-start.22) | collective-permute-done | bytes 786464 | tf_op jit(solution)/shard_map/ppermute | solution.py:62
  176.1 14.8 %unit_back.1 = (bf16[512,768]{1,0:T(8,128)(2,1)}, f32[512,768]{1,0:T(8,128)}, bf16[512,768]{1,0:T(8,128)(2,1)}, bf16[512,1536]{1,0:T(8,128)(2,1)}, bf16[512,1536...) custom-call(s32[4]{0:T(128)} %pad_add_fusion.ids, s32[2]{0:T(128)} %lens.5, ...), custom_call_target="tpu_custom_call" | custom-call | flops 3623878656 | bytes 22000000 | tf_op jit(solution)/shard_map/unit_back/pallas_call | solution.py:449
  192.7 13.5 %weight_grads.1 = (bf16[384,4992]{1,0:T(8,128)(2,1)}, bf16[384,4992]{1,0:T(8,128)(2,1)}) custom-call(s32[4]{0:T(128)} %pad_add_fusion.ids, bf16[512,768]{1,0:T(8,128)(2,1)} %get-tuple-element.105.low, bf16[512,768]{1,0:T(8,128)(2,1)} %get-tuple-element.106.dffn, bf16[512,1536]{1,0:T(8,128)(2,1)} %get-tuple-element.107.dgate, ...), custom_call_target="tpu_custom_call" | custom-call | flops 3623878656 | bytes 14000000 | tf_op jit(solution)/shard_map/weight_grads/pallas_call | solution.py:517
  207.1 6.8 %mix_back.1 = (bf16[192,256]{1,0:T(8,128)(2,1)}, bf16[192,256]{1,0:T(8,128)(2,1)}, bf16[192,256]{1,0:T(8,128)(2,1)}, bf16[192,256]{1,0:T(8,128)(2,1)}, f32[512,7...) custom-call(s32[4]{0:T(128)} %pad_add_fusion.ids, ...), custom_call_target="tpu_custom_call", output_to_operand_aliasing={{5}: (10, {}), {6}: (11, {})} | custom-call | flops 603979776 | bytes 10000000 | tf_op jit(solution)/shard_map/mix_back/pallas_call | solution.py:568
  213.9 8.5 %collective-permute-start.24 = (bf16[192,256]{1,0:T(8,128)(2,1)}, bf16[192,256]{1,0:T(8,128)(2,1)S(1)}, u32[]{:S(2)}, u32[]{:S(2)}) collective-permute-start(bf16[192,256]{1,0:T(8,128)(2,1)} %get-tuple-element.121), channel_id=1, source_target_pairs={{0,2},{2,0},{4,6},{6,4},{1,3},{3,1},{5,7},{7,5},{8,10},{10,8},{12,... | collective-permute-start | bytes 294920 | tf_op jit(solution)/shard_map/ppermute | solution.py:62
  222.4 4.3 %collective-permute-start.25 = (bf16[192,256]{1,0:T(8,128)(2,1)}, bf16[192,256]{1,0:T(8,128)(2,1)S(1)}, u32[]{:S(2)}, u32[]{:S(2)}) collective-permute-start(bf16[192,256]{1,0:T(8,128)(2,1)} %get-tuple-element.122), channel_id=1, source_target_pairs={{0,4},{2,6},{4,0},{6,2},{1,5},{3,7},{5,1},{7,3},{8,12},{10,14},{12... | collective-permute-start | bytes 294920 | tf_op jit(solution)/shard_map/ppermute | solution.py:62
  230.1 6.5 %fold_core.2 = (f32[192,4992]{1,0:T(8,128)}, bf16[192,4992]{1,0:T(8,128)(2,1)}) custom-call(bf16[384,4992]{1,0:T(8,128)(2,1)} %get-tuple-element.124.keep, bf16[384,4992]{1,0:T(8,128)(2,1)} %copy-done), custom_call_target="tpu_custom_call" | custom-call | flops 1916928 | bytes 13418496 | tf_op jit(solution)/shard_map/fold_core/pallas_call | solution.py:665
  237.3 15.0 %attend_back.1 = (bf16[576,256]{1,0:T(8,128)(2,1)}, bf16[576,256]{1,0:T(8,128)(2,1)}, bf16[576,256]{1,0:T(8,128)(2,1)}, bf16[576,256]{1,0:T(8,128)(2,1)}) custom-call(s32[4]{0:T(128)} %pad_add_fusion.ids, s32[2]{0:T(128)} %lens.5, f32[12]{0:T(128)} %constant.40.clone.slopes, bf16[576,256]{1,0:T(8,128)(2,1)} %get-tuple-element.89.refs_0_, ...), custom_call_target="tpu_custom_call" | custom-call | flops 4026531840 | bytes 5000000 | tf_op jit(solution)/shard_map/attend_back/pallas_call | solution.py:280
  260.3 4.6 %collective-permute-done.28.refs_1_ = bf16[576,256]{1,0:T(8,128)(2,1)S(1)} collective-permute-done((bf16[576,256]{1,0:T(8,128)(2,1)}, bf16[576,256]{1,0:T(8,128)(2,1)S(1)}, u32[]{:S(2)}, u32[]{:S(2)}) %collective-permute-start.28) | collective-permute-done | bytes 294944 | tf_op jit(solution)/shard_map/ppermute | solution.py:62
  264.9 12.2 %collective-permute-done.29.refs_2_ = bf16[576,256]{1,0:T(8,128)(2,1)S(1)} collective-permute-done((bf16[576,256]{1,0:T(8,128)(2,1)}, bf16[576,256]{1,0:T(8,128)(2,1)S(1)}, u32[]{:S(2)}, u32[]{:S(2)}) %collective-permute-start.29) | collective-permute-done | bytes 294944 | tf_op jit(solution)/shard_map/ppermute | solution.py:62
  277.1 3.3 collective-permute-done.31.recv
  281.7 4.9 %fold_y.2 = (f32[48,4992]{1,0:T(8,128)}, bf16[48,4992]{1,0:T(8,128)(2,1)}, bf16[48,4992]{1,0:T(8,128)(2,1)}, bf16[48,4992]{1,0:T(8,128)(2,1)}) custom-call(s32[4]{0:T(128)} %pad_add_fusion.ids, f32[192,4992]{1,0:T(8,128)} %get-tuple-element.142.mine, bf16[192,4992]{1,0:T(8,128)(2,1)} %copy-done.2), custom_call_target="tpu_custom_call" | custom-call | flops 958464 | bytes 8626176 | tf_op jit(solution)/shard_map/fold_y/pallas_call | solution.py:700
  286.7 6.0 %project_back.1 = (bf16[512,768]{1,0:T(8,128)(2,1)}, bf16[400,1152]{1,0:T(8,128)(2,1)}, bf16[400,1152]{1,0:T(8,128)(2,1)}) custom-call(s32[4]{0:T(128)} %pad_add_fusion.ids, bf16[512,768]{1,0:T(8,128)(2,1)} %bitcast.28, bf16[768,1152]{1,0:T(8,128)(2,1)} %get-tuple-element.117.whole, f32[8,768]{1,0:T(8,128)} %concatenate.12.small, ...), custom_call_target="tpu_custom_call" | custom-call | flops 1811939328 | bytes 8000000 | tf_op jit(solution)/shard_map/project_back/pallas_call | solution.py:631
  302.3 4.0 %collective-permute-start.35 = (bf16[48,4992]{1,0:T(8,128)(2,1)S(1)}, bf16[48,4992]{1,0:T(8,128)(2,1)S(1)}, u32[]{:S(2)}, u32[]{:S(2)}) collective-permute-start(bf16[48,4992]{1,0:T(8,128)(2,1)S(1)} %copy-done.19), channel_id=1, source_target_pairs={{0,2},{2,0},{4,6},{6,4},{1,3},{3,1},{5,7},{7,5},{8,10},{10,8},{12,... | collective-permute-start | bytes 1437704 | tf_op jit(solution)/shard_map/ppermute | solution.py:62
  309.7 4.1 %collective-permute-done.34.recv = bf16[208,1152]{1,0:T(8,128)(2,1)S(1)} collective-permute-done((bf16[208,1152]{1,0:T(8,128)(2,1)}, bf16[208,1152]{1,0:T(8,128)(2,1)S(1)}, u32[]{:S(2)}, u32[]{:S(2)}) %collective-permute-start.34) | collective-permute-done | bytes 479264 | tf_op jit(solution)/shard_map/ppermute | solution.py:62
  316.8 4.0 %collective-permute-start.38 = (bf16[64,1152]{1,0:T(8,128)(2,1)}, bf16[64,1152]{1,0:T(8,128)(2,1)S(1)}, u32[]{:S(2)}, u32[]{:S(2)}) collective-permute-start(bf16[64,1152]{1,0:T(8,128)(2,1)} %get-tuple-element.158), channel_id=1, source_target_pairs={{0,2},{2,0},{4,6},{6,4},{1,3},{3,1},{5,7},{7,5},{8,10},{10,8},{12,... | collective-permute-start | bytes 442376 | tf_op jit(solution)/shard_map/ppermute | solution.py:62
  320.9 7.2 %collective-permute-done.35 = bf16[48,4992]{1,0:T(8,128)(2,1)S(1)} collective-permute-done((bf16[48,4992]{1,0:T(8,128)(2,1)S(1)}, bf16[48,4992]{1,0:T(8,128)(2,1)S(1)}, u32[]{:S(2)}, u32[]{:S(2)}) %collective-permute-start.35) | collective-permute-done | bytes 479264 | tf_op jit(solution)/shard_map/ppermute | solution.py:62
  331.4 9.8 %collective-permute-done.36 = bf16[48,4992]{1,0:T(8,128)(2,1)S(1)} collective-permute-done((bf16[48,4992]{1,0:T(8,128)(2,1)S(1)}, bf16[48,4992]{1,0:T(8,128)(2,1)S(1)}, u32[]{:S(2)}, u32[]{:S(2)}) %collective-permute-start.36) | collective-permute-done | bytes 479264 | tf_op jit(solution)/shard_map/ppermute | solution.py:62
  342.0 19.4 %collective-permute-done.39 = bf16[64,1152]{1,0:T(8,128)(2,1)S(1)} collective-permute-done((bf16[64,1152]{1,0:T(8,128)(2,1)}, bf16[64,1152]{1,0:T(8,128)(2,1)S(1)}, u32[]{:S(2)}, u32[]{:S(2)}) %collective-permute-start.39) | collective-permute-done | bytes 147488 | tf_op jit(solution)/shard_map/ppermute | solution.py:62
  (185 shorter events, 71.4 us)
Async XLA Ops:
  7.2 120.8 %all-gather.2.cloned.1.call-start = ((), (), s32[]{:S(2)}) async-start(), calls=%async_computation | async-start | bytes 8146944 | tf_op jit(solution)/shard_map/all_gather | solution.py:760
  12.3 11.2 %collective-permute-start.7 = (bf16[48,1152]{1,0:T(8,128)(2,1)S(1)}, bf16[48,1152]{1,0:T(8,128)(2,1)S(1)}, u32[]{:S(2)}, u32[]{:S(2)}) collective-permute-start(bf16[48,1152]{1,0:T(8,128)(2,1)S(1)} %bitcast.35), channel_id=1, source_target_pairs={{0,16},{8,24},{16,0},{24,8},{1,17},{9,25},{17,1},{25,9},{2,18},{10... | collective-permute-start | bytes 331784 | tf_op jit(solution)/shard_map/ppermute | solution.py:62
  18.9 15.4 %collective-permute-start.1 = (bf16[48,1152]{1,0:T(8,128)(2,1)S(1)}, bf16[48,1152]{1,0:T(8,128)(2,1)S(1)}, u32[]{:S(2)}, u32[]{:S(2)}) collective-permute-start(bf16[48,1152]{1,0:T(8,128)(2,1)S(1)} %bitcast.38), channel_id=1, source_target_pairs={{0,4},{2,6},{4,0},{6,2},{1,5},{3,7},{5,1},{7,3},{8,12},{10,14},{12... | collective-permute-start | bytes 331784 | tf_op jit(solution)/shard_map/ppermute | solution.py:62
  19.0 15.4 %collective-permute-start = (bf16[48,1152]{1,0:T(8,128)(2,1)S(1)}, bf16[48,1152]{1,0:T(8,128)(2,1)S(1)}, u32[]{:S(2)}, u32[]{:S(2)}) collective-permute-start(bf16[48,1152]{1,0:T(8,128)(2,1)S(1)} %bitcast.39), channel_id=1, source_target_pairs={{0,2},{2,0},{4,6},{6,4},{1,3},{3,1},{5,7},{7,5},{8,10},{10,8},{12,... | collective-permute-start | bytes 331784 | tf_op jit(solution)/shard_map/ppermute | solution.py:62
  23.2 13.8 %collective-permute-start.10 = (bf16[48,1152]{1,0:T(8,128)(2,1)S(1)}, bf16[48,1152]{1,0:T(8,128)(2,1)S(1)}, u32[]{:S(2)}, u32[]{:S(2)}) collective-permute-start(bf16[48,1152]{1,0:T(8,128)(2,1)S(1)} %collective-permute-done.2.refs_3_), channel_id=1, source_target_pairs={{0,16},{8,24},{16,0},{24,8},{1,17},{9,25},{17,1},{25,9},{2,18},{10... | collective-permute-start | bytes 331784 | tf_op jit(solution)/shard_map/ppermute | solution.py:62
  23.5 14.0 %collective-permute-start.6 = (bf16[48,1152]{1,0:T(8,128)(2,1)S(1)}, bf16[48,1152]{1,0:T(8,128)(2,1)S(1)}, u32[]{:S(2)}, u32[]{:S(2)}) collective-permute-start(bf16[48,1152]{1,0:T(8,128)(2,1)S(1)} %collective-permute-done.2.refs_3_), channel_id=1, source_target_pairs={{0,8},{8,0},{16,24},{24,16},{1,9},{9,1},{17,25},{25,17},{2,10},{10... | collective-permute-start | bytes 331784 | tf_op jit(solution)/shard_map/ppermute | solution.py:62
  23.5 13.5 %collective-permute-start.11 = (bf16[48,1152]{1,0:T(8,128)(2,1)S(1)}, bf16[48,1152]{1,0:T(8,128)(2,1)S(1)}, u32[]{:S(2)}, u32[]{:S(2)}) collective-permute-start(bf16[48,1152]{1,0:T(8,128)(2,1)S(1)} %collective-permute-done.7.refs_8_), channel_id=1, source_target_pairs={{0,8},{8,0},{16,24},{24,16},{1,9},{9,1},{17,25},{25,17},{2,10},{10... | collective-permute-start | bytes 331784 | tf_op jit(solution)/shard_map/ppermute | solution.py:62
  47.0 26.7 %collective-permute-start.15 = (bf16[576,256]{1,0:T(8,128)(2,1)}, bf16[576,256]{1,0:T(8,128)(2,1)S(1)}, u32[]{:S(2)}, u32[]{:S(2)}) collective-permute-start(bf16[576,256]{1,0:T(8,128)(2,1)} %get-tuple-element.90), channel_id=1, source_target_pairs={{0,2},{2,0},{4,6},{6,4},{1,3},{3,1},{5,7},{7,5},{8,10},{10,8},{12,... | collective-permute-start | bytes 884744 | tf_op jit(solution)/shard_map/ppermute | solution.py:62
  47.3 35.7 %collective-permute-start.16 = (bf16[576,256]{1,0:T(8,128)(2,1)}, bf16[576,256]{1,0:T(8,128)(2,1)S(1)}, u32[]{:S(2)}, u32[]{:S(2)}) collective-permute-start(bf16[576,256]{1,0:T(8,128)(2,1)} %get-tuple-element.91), channel_id=1, source_target_pairs={{0,4},{2,6},{4,0},{6,2},{1,5},{3,7},{5,1},{7,3},{8,12},{10,14},{12... | collective-permute-start | bytes 884744 | tf_op jit(solution)/shard_map/ppermute | solution.py:62
  51.8 38.4 %collective-permute-start.17 = (bf16[576,256]{1,0:T(8,128)(2,1)}, bf16[576,256]{1,0:T(8,128)(2,1)S(1)}, u32[]{:S(2)}, u32[]{:S(2)}) collective-permute-start(bf16[576,256]{1,0:T(8,128)(2,1)} %get-tuple-element.92), channel_id=1, source_target_pairs={{0,6},{2,4},{4,2},{6,0},{1,7},{3,5},{5,3},{7,1},{8,14},{10,12},{12... | collective-permute-start | bytes 884744 | tf_op jit(solution)/shard_map/ppermute | solution.py:62
  102.3 19.9 %collective-permute-start.18 = (bf16[192,256]{1,0:T(8,128)(2,1)}, bf16[192,256]{1,0:T(8,128)(2,1)S(1)}, u32[]{:S(2)}, u32[]{:S(2)}) collective-permute-start(bf16[192,256]{1,0:T(8,128)(2,1)} %get-tuple-element.94), channel_id=1, source_target_pairs={{0,2},{2,0},{4,6},{6,4},{1,3},{3,1},{5,7},{7,5},{8,10},{10,8},{12,... | collective-permute-start | bytes 294920 | tf_op jit(solution)/shard_map/ppermute | solution.py:62
  119.2 8.8 %collective-permute-start.19 = (bf16[192,256]{1,0:T(8,128)(2,1)}, bf16[192,256]{1,0:T(8,128)(2,1)S(1)}, u32[]{:S(2)}, u32[]{:S(2)}) collective-permute-start(bf16[192,256]{1,0:T(8,128)(2,1)} %get-tuple-element.95), channel_id=1, source_target_pairs={{0,4},{2,6},{4,0},{6,2},{1,5},{3,7},{5,1},{7,3},{8,12},{10,14},{12... | collective-permute-start | bytes 294920 | tf_op jit(solution)/shard_map/ppermute | solution.py:62
  119.2 8.8 %collective-permute-start.20 = (bf16[192,256]{1,0:T(8,128)(2,1)}, bf16[192,256]{1,0:T(8,128)(2,1)S(1)}, u32[]{:S(2)}, u32[]{:S(2)}) collective-permute-start(bf16[192,256]{1,0:T(8,128)(2,1)} %get-tuple-element.96), channel_id=1, source_target_pairs={{0,6},{2,4},{4,2},{6,0},{1,7},{3,5},{5,3},{7,1},{8,14},{10,12},{12... | collective-permute-start | bytes 294920 | tf_op jit(solution)/shard_map/ppermute | solution.py:62
  131.4 15.7 %collective-permute-start.21 = (bf16[512,768]{1,0:T(8,128)(2,1)}, bf16[512,768]{1,0:T(8,128)(2,1)S(1)}, u32[]{:S(2)}, u32[]{:S(2)}) collective-permute-start(bf16[512,768]{1,0:T(8,128)(2,1)} %get-tuple-element.97.own), channel_id=1, source_target_pairs={{0,1},{1,0},{2,3},{3,2},{4,5},{5,4},{6,7},{7,6},{8,9},{9,8},{10,11... | collective-permute-start | bytes 2359304 | tf_op jit(solution)/shard_map/ppermute | solution.py:62
  160.1 15.1 %collective-permute-start.22 = (bf16[512,768]{1,0:T(8,128)(2,1)}, bf16[512,768]{1,0:T(8,128)(2,1)S(1)}, u32[]{:S(2)}, u32[]{:S(2)}) collective-permute-start(bf16[512,768]{1,0:T(8,128)(2,1)} %get-tuple-element.99.own), channel_id=1, source_target_pairs={{0,1},{1,0},{2,3},{3,2},{4,5},{5,4},{6,7},{7,6},{8,9},{9,8},{10,11... | collective-permute-start | bytes 2359304 | tf_op jit(solution)/shard_map/ppermute | solution.py:62
  190.9 15.3 %collective-permute-start.23 = (bf16[512,768]{1,0:T(8,128)(2,1)}, bf16[512,768]{1,0:T(8,128)(2,1)S(1)}, u32[]{:S(2)}, u32[]{:S(2)}) collective-permute-start(bf16[512,768]{1,0:T(8,128)(2,1)} %get-tuple-element.104.hown), channel_id=1, source_target_pairs={{0,1},{1,0},{2,3},{3,2},{4,5},{5,4},{6,7},{7,6},{8,9},{9,8},{10,11... | collective-permute-start | bytes 2359304 | tf_op jit(solution)/shard_map/ppermute | solution.py:62
  213.9 14.3 %collective-permute-start.27 = (bf16[384,4992]{1,0:T(8,128)(2,1)}, bf16[384,4992]{1,0:T(8,128)(2,1)S(1)}, u32[]{:S(2)}, u32[]{:S(2)}) collective-permute-start(bf16[384,4992]{1,0:T(8,128)(2,1)} %get-tuple-element.125), channel_id=1, source_target_pairs={{0,8},{8,0},{16,24},{24,16},{1,9},{9,1},{17,25},{25,17},{2,10},{10... | collective-permute-start | bytes 11501576 | tf_op jit(solution)/shard_map/ppermute | solution.py:62
  213.9 22.7 %collective-permute-start.24 = (bf16[192,256]{1,0:T(8,128)(2,1)}, bf16[192,256]{1,0:T(8,128)(2,1)S(1)}, u32[]{:S(2)}, u32[]{:S(2)}) collective-permute-start(bf16[192,256]{1,0:T(8,128)(2,1)} %get-tuple-element.121), channel_id=1, source_target_pairs={{0,2},{2,0},{4,6},{6,4},{1,3},{3,1},{5,7},{7,5},{8,10},{10,8},{12,... | collective-permute-start | bytes 294920 | tf_op jit(solution)/shard_map/ppermute | solution.py:62
  222.4 14.1 %collective-permute-start.25 = (bf16[192,256]{1,0:T(8,128)(2,1)}, bf16[192,256]{1,0:T(8,128)(2,1)S(1)}, u32[]{:S(2)}, u32[]{:S(2)}) collective-permute-start(bf16[192,256]{1,0:T(8,128)(2,1)} %get-tuple-element.122), channel_id=1, source_target_pairs={{0,4},{2,6},{4,0},{6,2},{1,5},{3,7},{5,1},{7,3},{8,12},{10,14},{12... | collective-permute-start | bytes 294920 | tf_op jit(solution)/shard_map/ppermute | solution.py:62
  226.8 9.8 %collective-permute-start.26 = (bf16[192,256]{1,0:T(8,128)(2,1)}, bf16[192,256]{1,0:T(8,128)(2,1)S(1)}, u32[]{:S(2)}, u32[]{:S(2)}) collective-permute-start(bf16[192,256]{1,0:T(8,128)(2,1)} %get-tuple-element.123), channel_id=1, source_target_pairs={{0,6},{2,4},{4,2},{6,0},{1,7},{3,5},{5,3},{7,1},{8,14},{10,12},{12... | collective-permute-start | bytes 294920 | tf_op jit(solution)/shard_map/ppermute | solution.py:62
  236.6 43.8 %collective-permute-start.31 = (bf16[192,4992]{1,0:T(8,128)(2,1)}, bf16[192,4992]{1,0:T(8,128)(2,1)S(1)}, u32[]{:S(2)}, u32[]{:S(2)}) collective-permute-start(bf16[192,4992]{1,0:T(8,128)(2,1)} %get-tuple-element.137), channel_id=1, source_target_pairs={{0,16},{8,24},{16,0},{24,8},{1,17},{9,25},{17,1},{25,9},{2,18},{10... | collective-permute-start | bytes 5750792 | tf_op jit(solution)/shard_map/ppermute | solution.py:62
  252.3 12.6 %collective-permute-start.28 = (bf16[576,256]{1,0:T(8,128)(2,1)}, bf16[576,256]{1,0:T(8,128)(2,1)S(1)}, u32[]{:S(2)}, u32[]{:S(2)}) collective-permute-start(bf16[576,256]{1,0:T(8,128)(2,1)} %get-tuple-element.134), channel_id=1, source_target_pairs={{0,2},{2,0},{4,6},{6,4},{1,3},{3,1},{5,7},{7,5},{8,10},{10,8},{12,... | collective-permute-start | bytes 884744 | tf_op jit(solution)/shard_map/ppermute | solution.py:62
  253.4 23.7 %collective-permute-start.29 = (bf16[576,256]{1,0:T(8,128)(2,1)}, bf16[576,256]{1,0:T(8,128)(2,1)S(1)}, u32[]{:S(2)}, u32[]{:S(2)}) collective-permute-start(bf16[576,256]{1,0:T(8,128)(2,1)} %get-tuple-element.135), channel_id=1, source_target_pairs={{0,4},{2,6},{4,0},{6,2},{1,5},{3,7},{5,1},{7,3},{8,12},{10,14},{12... | collective-permute-start | bytes 884744 | tf_op jit(solution)/shard_map/ppermute | solution.py:62
  254.0 23.1 %collective-permute-start.30 = (bf16[576,256]{1,0:T(8,128)(2,1)}, bf16[576,256]{1,0:T(8,128)(2,1)S(1)}, u32[]{:S(2)}, u32[]{:S(2)}) collective-permute-start(bf16[576,256]{1,0:T(8,128)(2,1)} %get-tuple-element.136), channel_id=1, source_target_pairs={{0,6},{2,4},{4,2},{6,0},{1,7},{3,5},{5,3},{7,1},{8,14},{10,12},{12... | collective-permute-start | bytes 884744 | tf_op jit(solution)/shard_map/ppermute | solution.py:62
  292.6 35.4 %collective-permute-start.32 = (bf16[512,768]{1,0:T(8,128)(2,1)}, bf16[512,768]{1,0:T(8,128)(2,1)S(1)}, u32[]{:S(2)}, u32[]{:S(2)}) collective-permute-start(bf16[512,768]{1,0:T(8,128)(2,1)} %get-tuple-element.149), channel_id=1, source_target_pairs={{0,1},{1,0},{2,3},{3,2},{4,5},{5,4},{6,7},{7,6},{8,9},{9,8},{10,11... | collective-permute-start | bytes 2359304 | tf_op jit(solution)/shard_map/ppermute | solution.py:62
  299.2 14.6 %collective-permute-start.34 = (bf16[208,1152]{1,0:T(8,128)(2,1)}, bf16[208,1152]{1,0:T(8,128)(2,1)S(1)}, u32[]{:S(2)}, u32[]{:S(2)}) collective-permute-start(bf16[208,1152]{1,0:T(8,128)(2,1)} %get-tuple-element.153), channel_id=1, source_target_pairs={{0,16},{8,24},{16,0},{24,8},{1,17},{9,25},{17,1},{25,9},{2,18},{10... | collective-permute-start | bytes 1437704 | tf_op jit(solution)/shard_map/ppermute | solution.py:62
  302.3 25.8 %collective-permute-start.35 = (bf16[48,4992]{1,0:T(8,128)(2,1)S(1)}, bf16[48,4992]{1,0:T(8,128)(2,1)S(1)}, u32[]{:S(2)}, u32[]{:S(2)}) collective-permute-start(bf16[48,4992]{1,0:T(8,128)(2,1)S(1)} %copy-done.19), channel_id=1, source_target_pairs={{0,2},{2,0},{4,6},{6,4},{1,3},{3,1},{5,7},{7,5},{8,10},{10,8},{12,... | collective-permute-start | bytes 1437704 | tf_op jit(solution)/shard_map/ppermute | solution.py:62
  306.3 34.9 %collective-permute-start.36 = (bf16[48,4992]{1,0:T(8,128)(2,1)S(1)}, bf16[48,4992]{1,0:T(8,128)(2,1)S(1)}, u32[]{:S(2)}, u32[]{:S(2)}) collective-permute-start(bf16[48,4992]{1,0:T(8,128)(2,1)S(1)} %copy-done.18), channel_id=1, source_target_pairs={{0,4},{2,6},{4,0},{6,2},{1,5},{3,7},{5,1},{7,3},{8,12},{10,14},{12... | collective-permute-start | bytes 1437704 | tf_op jit(solution)/shard_map/ppermute | solution.py:62
  308.2 33.8 %collective-permute-start.37 = (bf16[48,4992]{1,0:T(8,128)(2,1)S(1)}, bf16[48,4992]{1,0:T(8,128)(2,1)S(1)}, u32[]{:S(2)}, u32[]{:S(2)}) collective-permute-start(bf16[48,4992]{1,0:T(8,128)(2,1)S(1)} %copy-done.17), channel_id=1, source_target_pairs={{0,6},{2,4},{4,2},{6,0},{1,7},{3,5},{5,3},{7,1},{8,14},{10,12},{12... | collective-permute-start | bytes 1437704 | tf_op jit(solution)/shard_map/ppermute | solution.py:62
  316.8 25.2 %collective-permute-start.38 = (bf16[64,1152]{1,0:T(8,128)(2,1)}, bf16[64,1152]{1,0:T(8,128)(2,1)S(1)}, u32[]{:S(2)}, u32[]{:S(2)}) collective-permute-start(bf16[64,1152]{1,0:T(8,128)(2,1)} %get-tuple-element.158), channel_id=1, source_target_pairs={{0,2},{2,0},{4,6},{6,4},{1,3},{3,1},{5,7},{7,5},{8,10},{10,8},{12,... | collective-permute-start | bytes 442376 | tf_op jit(solution)/shard_map/ppermute | solution.py:62
  328.1 33.3 %collective-permute-start.39 = (bf16[64,1152]{1,0:T(8,128)(2,1)}, bf16[64,1152]{1,0:T(8,128)(2,1)S(1)}, u32[]{:S(2)}, u32[]{:S(2)}) collective-permute-start(bf16[64,1152]{1,0:T(8,128)(2,1)} %get-tuple-element.160), channel_id=1, source_target_pairs={{0,4},{2,6},{4,0},{6,2},{1,5},{3,7},{5,1},{7,3},{8,12},{10,14},{12... | collective-permute-start | bytes 442376 | tf_op jit(solution)/shard_map/ppermute | solution.py:62
  328.1 33.3 %collective-permute-start.40 = (bf16[64,1152]{1,0:T(8,128)(2,1)}, bf16[64,1152]{1,0:T(8,128)(2,1)S(1)}, u32[]{:S(2)}, u32[]{:S(2)}) collective-permute-start(bf16[64,1152]{1,0:T(8,128)(2,1)} %get-tuple-element.161), channel_id=1, source_target_pairs={{0,6},{2,4},{4,2},{6,0},{1,7},{3,5},{5,3},{7,1},{8,14},{10,12},{12... | collective-permute-start | bytes 442376 | tf_op jit(solution)/shard_map/ppermute | solution.py:62
  (55 other events, 418.1 us)
Sparse Core Ops, SparseCore 0:
  12.4 97.7 all-gather.1

commit v3 on v2

--- a/solution.py
+++ b/solution.py
@@ -14,7 +14,8 @@
 LOG2E = math.log2(math.e)
 FAR = 1e30
 TILE = 64
-BLOCK = 384
+BLOCK = 512
+WIDTH = 384
 EXTRA = 16
 
 epsilon = 1e-12
@@ -62,12 +63,9 @@
     return lax.ppermute(value, axis, xor_pairs(axis, distance))
 
 
-def live_mask(lens, rank, n_ctx, seqs, slots):
+def live_mask(length, rank, n_ctx, slots):
     slot = lax.broadcasted_iota(jnp.int32, (slots, 1), 0)
-    place = slot * n_ctx + rank
-    return jnp.concatenate(
-        [jnp.where(place < lens[s], 1.0, 0.0).astype(f32) for s in range(seqs)], axis=0
-    )
+    return jnp.where(slot * n_ctx + rank < length, 1.0, 0.0).astype(f32)
 
 
 def normalise(z):
@@ -305,7 +303,8 @@
 
 def mix_kernel(n, seqs, heads, ids, wo, *refs):
     inputs = refs[:n]
-    part, mixed, stage = refs[n], refs[n + 1], refs[n + 2]
+    parts = refs[n : n + seqs]
+    mixed, stage = refs[n + seqs :]
     z = ids[2]
     slots = inputs[0].shape[1]
     per = seqs * heads // n
@@ -321,7 +320,7 @@
         rows = slice(s * slots, (s + 1) * slots)
         ours = jnp.concatenate(columns, axis=0).T
         mixed[rows, :] = ours
-        part[rows, :] = dot_nt(ours, wo[...]).astype(bf16)
+        parts[s][...] = dot_nt(ours, wo[...]).astype(bf16)
 
 
 def mix(ids, packed, blocks, n, seqs, heads):
@@ -332,9 +331,10 @@
     return pl.pallas_call(
         functools.partial(mix_kernel, n, seqs, heads),
         grid=(1,),
-        out_shape=[shape((tokens, model), bf16), shape((tokens, width), bf16)],
-        in_specs=[SMEM, pl.BlockSpec((model, width), lambda i: (0, 0))] + [VMEM] * n,
-        out_specs=[VMEM] * 2,
+        out_shape=[shape((slots, model), bf16)] * seqs + [shape((tokens, width), bf16)],
+        in_specs=[SMEM, pl.BlockSpec((model, width), lambda i: (0, packed.shape[1] // width - 1))]
+        + [VMEM] * n,
+        out_specs=[VMEM] * (seqs + 1),
         scratch_shapes=[pltpu.VMEM((seqs * heads * HD, slots), bf16)],
         compiler_params=params("arbitrary"),
         cost_estimate=cost(2 * tokens * model * width, 3e6),
@@ -370,15 +370,14 @@
         part[...] = acc[...].astype(bf16)
 
 
-def unit(tok, own, other, vec, packed, width, hidden_units):
-    tokens, model = tok.shape
+def unit(s, tok, own, other, vec, front, back):
+    tokens, model = own.shape
+    hidden_units = back.shape[1] // 2
     steps = hidden_units // BLOCK
-    first = width // BLOCK
     fixed = lambda j: (0, 0)
-    moving = lambda j: (0, j)
     whole = pl.BlockSpec((tokens, model), fixed)
     weight = lambda start: pl.BlockSpec((model, BLOCK), lambda j: (0, start + j))
-    inner = pl.BlockSpec((tokens, BLOCK), moving)
+    inner = pl.BlockSpec((tokens, BLOCK), lambda j: (0, j))
     return pl.pallas_call(
         unit_kernel,
         grid=(steps,),
@@ -386,31 +385,31 @@
         + [shape((tokens, hidden_units), bf16)] * 3
         + [shape((tokens, model), bf16)],
         in_specs=[
-            whole,
+            pl.BlockSpec((tokens, model), lambda j: (s, 0)),
             whole,
             whole,
             pl.BlockSpec(vec.shape, fixed),
-            weight(first),
-            weight(first + steps),
-            weight(first + 2 * steps),
+            weight(0),
+            weight(0),
+            weight(steps),
         ],
         out_specs=[whole, whole, inner, inner, inner, whole],
         scratch_shapes=[pltpu.VMEM((tokens, model), f32)],
         compiler_params=params("arbitrary"),
-        cost_estimate=cost(6 * tokens * model * hidden_units, 20e6, 2 * tokens * hidden_units),
+        cost_estimate=cost(6 * tokens * model * hidden_units, 13e6, 2 * tokens * hidden_units),
         name="unit",
-    )(tok, own, other, vec, packed, packed, packed)
+    )(tok, own, other, vec, front, back, back)
 
 
 def unit_back_kernel(
-    n, seqs, ids, lens, hidden, own, other, cot, vec, wg, wu, wd, gel, slope,
+    n, s, ids, lens, hidden, own, other, cot, vec, wg, wu, wd, gel, slope,
     output, dz2, dffn, dgate, dup, part, sums, acc,
 ):
     j = pl.program_id(0)
 
     @pl.when(j == 0)
     def _():
-        live = live_mask(lens, ids[2], n, seqs, hidden.shape[0] // seqs)
+        live = live_mask(lens[s], ids[2], n, hidden.shape[0])
         branch = own[...].astype(f32) + other[...].astype(f32) + vec[5:6, :]
         hat, scale = normalise(hidden[...] + branch)
         output[...] = (live * (hat * vec[2:3, :] + vec[3:4, :])).astype(bf16)
@@ -437,17 +436,16 @@
         part[...] = acc[...].astype(bf16)
 
 
-def unit_back(ids, lens, hidden, own, other, cot, vec, packed, gel, slope, n, seqs, width):
+def unit_back(s, ids, lens, hidden, own, other, cot, vec, front, back, gel, slope, n):
     tokens, model = hidden.shape
     hidden_units = gel.shape[1]
     steps = hidden_units // BLOCK
-    first = width // BLOCK
     fixed = lambda j: (0, 0)
     whole = pl.BlockSpec((tokens, model), fixed)
     weight = lambda start: pl.BlockSpec((model, BLOCK), lambda j: (0, start + j))
     inner = pl.BlockSpec((tokens, BLOCK), lambda j: (0, j))
     return pl.pallas_call(
-        functools.partial(unit_back_kernel, n, seqs),
+        functools.partial(unit_back_kernel, n, s),
         grid=(steps,),
         out_shape=[
             shape((tokens, model), bf16),
@@ -458,14 +456,15 @@
             shape((tokens, model), bf16),
             shape((8, model), f32),
         ],
-        in_specs=[SMEM, SMEM, whole, whole, whole, whole, pl.BlockSpec(vec.shape, fixed)]
-        + [weight(first), weight(first + steps), weight(first + 2 * steps), inner, inner],
+        in_specs=[SMEM, SMEM, whole, whole, whole]
+        + [pl.BlockSpec((tokens, model), lambda j: (s, 0)), pl.BlockSpec(vec.shape, fixed)]
+        + [weight(0), weight(0), weight(steps), inner, inner],
         out_specs=[whole, whole, whole, inner, inner, whole, pl.BlockSpec((8, model), fixed)],
         scratch_shapes=[pltpu.VMEM((tokens, model), f32)],
         compiler_params=params("arbitrary"),
-        cost_estimate=cost(6 * tokens * model * hidden_units, 22e6),
+        cost_estimate=cost(6 * tokens * model * hidden_units, 14e6),
         name="unit_back",
-    )(ids, lens, hidden, own, other, cot, vec, packed, packed, packed, gel, slope)
+    )(ids, lens, hidden, own, other, cot, vec, front, back, back, gel, slope)
 
 
 def row_starts(ids, quarter):
@@ -475,79 +474,99 @@
     return send, keep
 
 
-def write_rows(ids, turned, right, send, keep):
+def arrange(ids, turned, left):
     quarter = turned.shape[0] // 4
-    for ref, starts in zip((send, keep), row_starts(ids, quarter)):
-        for k in range(2):
-            left = turned[pl.ds(pl.multiple_of(starts[k], quarter), quarter), :]
-            ref[k * quarter : (k + 1) * quarter, :] = dot_nn(left, right).astype(bf16)
-
-
-def weight_kernel(steps, ids, low, dffn, dgate, dup, act, send, keep, left):
+    send, keep = row_starts(ids, quarter)
+    for k, start in enumerate(send + keep):
+        rows = pl.ds(pl.multiple_of(start, quarter), quarter)
+        left[k * quarter : (k + 1) * quarter, :] = turned[rows, :]
+
+
+def write_rows(left, right, send, keep):
+    grad = dot_nn(left[...], right).astype(bf16)
+    half = grad.shape[0] // 2
+    send[0:half, :] = grad[:half]
+    keep[0:half, :] = grad[half:]
+
+
+def weight_kernel(steps, seqs, ids, *refs):
+    low, dffn, dgate, dup, act = (refs[i * seqs : (i + 1) * seqs] for i in range(5))
+    send, keep, left, turned = refs[5 * seqs :]
     j = pl.program_id(0)
+    joined = lambda group: jnp.concatenate([ref[...] for ref in group], axis=0)
 
     @pl.when(j == 0)
     def _():
-        left[0] = low[...].T
-        left[1] = dffn[...].T
+        for k, group in enumerate((low, dffn)):
+            turned[...] = joined(group).T
+            arrange(ids, turned, left.at[k])
 
     @pl.when(j < steps)
     def _():
-        write_rows(ids, left.at[0], dgate[...], send, keep)
+        write_rows(left.at[0], joined(dgate), send, keep)
 
     @pl.when((j >= steps) & (j < 2 * steps))
     def _():
-        write_rows(ids, left.at[0], dup[...], send, keep)
+        write_rows(left.at[0], joined(dup), send, keep)
 
     @pl.when(j >= 2 * steps)
     def _():
-        write_rows(ids, left.at[1], act[...], send, keep)
+        write_rows(left.at[1], joined(act), send, keep)
 
 
 def weight_grads(ids, low, dffn, dgate, dup, act):
-    tokens, model = low.shape
-    hidden_units = act.shape[1]
+    seqs = len(low)
+    tokens, model = low[0].shape
+    hidden_units = act[0].shape[1]
     steps = hidden_units // BLOCK
-    fixed = lambda j: (0, 0)
-    whole = pl.BlockSpec((tokens, model), fixed)
+    whole = pl.BlockSpec((tokens, model), lambda j: (0, 0))
     column = lambda start: pl.BlockSpec(
         (tokens, BLOCK), lambda j: (0, jnp.clip(j - start, 0, steps - 1))
     )
     out = pl.BlockSpec((model // 2, BLOCK), lambda j: (0, j))
     return pl.pallas_call(
-        functools.partial(weight_kernel, steps),
+        functools.partial(weight_kernel, steps, seqs),
         grid=(3 * steps,),
-        out_shape=[shape((model // 2, 3 * hidden_units + BLOCK), bf16)] * 2,
-        in_specs=[SMEM, whole, whole, column(0), column(steps), column(2 * steps)],
+        out_shape=[shape((model // 2, 3 * hidden_units + WIDTH), bf16)] * 2,
+        in_specs=[SMEM]
+        + [whole] * (2 * seqs)
+        + [column(0)] * seqs
+        + [column(steps)] * seqs
+        + [column(2 * steps)] * seqs,
         out_specs=[out, out],
-        scratch_shapes=[pltpu.VMEM((2, model, tokens), bf16)],
+        scratch_shapes=[
+            pltpu.VMEM((2, model, tokens * seqs), bf16),
+            pltpu.VMEM((model, tokens * seqs), bf16),
+        ],
         compiler_params=params("arbitrary"),
-        cost_estimate=cost(6 * tokens * model * hidden_units, 14e6),
+        cost_estimate=cost(6 * tokens * seqs * model * hidden_units, 14e6),
         name="weight_grads",
-    )(ids, low, dffn, dgate, dup, act)
-
-
-def mix_back_kernel(
-    n, seqs, heads, ids, tok, own, other, dz2, hown, hother, vec, wo, mixed, far, near, *refs
-):
+    )(ids, *low, *dffn, *dgate, *dup, *act)
+
+
+def mix_back_kernel(n, seqs, heads, ids, tok, vec, wo, mixed, far, near, *refs):
+    own, other, dz2, hown, hother = (refs[i * seqs : (i + 1) * seqs] for i in range(5))
+    refs = refs[5 * seqs :]
     sends = refs[:n]
     dz1, send, keep, sums = refs[n : n + 4]
-    stage, left = refs[n + 4 :]
+    stage, left, turned_low = refs[n + 4 :]
     z = ids[2]
     slots = sends[0].shape[1]
     per = seqs * heads // n
-    branch = own[...].astype(f32) + other[...].astype(f32) + vec[4:5, :]
-    hat, scale = normalise(tok[...].astype(f32) + branch)
-    gh = dz2[...] + (hown[...].astype(f32) + hother[...].astype(f32))
-    grad = normalise_back(gh * vec[0:1, :], hat, scale)
-    dz1[...] = grad
-    low = grad.astype(bf16)
-    sums[0:1, :] = jnp.sum(gh * hat, axis=0, keepdims=True)
-    sums[1:2, :] = jnp.sum(gh, axis=0, keepdims=True)
-    sums[2:3, :] = jnp.sum(low.astype(f32), axis=0, keepdims=True)
-    sums[3:8, :] = jnp.zeros_like(sums[3:8, :])
+    sums[...] = jnp.zeros_like(sums)
     for s in range(seqs):
-        turned = dot_nn(low[s * slots : (s + 1) * slots, :], wo[...]).astype(bf16).T
+        rows = slice(s * slots, (s + 1) * slots)
+        branch = own[s][...].astype(f32) + other[s][...].astype(f32) + vec[4:5, :]
+        hat, scale = normalise(tok[rows, :].astype(f32) + branch)
+        gh = dz2[s][...] + (hown[s][...].astype(f32) + hother[s][...].astype(f32))
+        grad = normalise_back(gh * vec[0:1, :], hat, scale)
+        dz1[rows, :] = grad
+        low = grad.astype(bf16)
+        sums[0:1, :] += jnp.sum(gh * hat, axis=0, keepdims=True)
+        sums[1:2, :] += jnp.sum(gh, axis=0, keepdims=True)
+        sums[2:3, :] += jnp.sum(low.astype(f32), axis=0, keepdims=True)
+        turned_low[:, rows] = low.T
+        turned = dot_nn(low, wo[...]).astype(bf16).T
         for h in range(heads):
             i = s * heads + h
             at = (i % n) * per + i // n
@@ -555,11 +574,12 @@
     size = per * HD
     for d in range(n):
         sends[d][...] = stage[pl.ds(pl.multiple_of((z ^ d) * size, size), size), :]
-    left[...] = low.T
-    write_rows(ids, left, mixed[...], send, keep)
-
-
-def mix_back(ids, tok, own, other, dz2, hown, hother, vec, packed, mixed, grads, n, seqs, heads):
+    arrange(ids, turned_low, left)
+    write_rows(left, mixed[...], send, keep)
+
+
+def mix_back(ids, tok, vec, front, mixed, grads, own, other, dz2, hown, hother, n, heads):
+    seqs = len(own)
     tokens, model = tok.shape
     slots = tokens // seqs
     width = heads * HD
@@ -572,26 +592,27 @@
         + [shape((tokens, model), f32)]
         + [shape(grads[0].shape, bf16)] * 2
         + [shape((8, model), f32)],
-        in_specs=[SMEM]
-        + [VMEM] * 7
-        + [pl.BlockSpec((model, width), lambda i: (0, 0)), VMEM]
-        + [pl.BlockSpec(memory_space=pl.ANY)] * 2,
+        in_specs=[SMEM, VMEM, VMEM]
+        + [pl.BlockSpec((model, width), lambda i: (0, front.shape[1] // width - 1)), VMEM]
+        + [pl.BlockSpec(memory_space=pl.ANY)] * 2
+        + [VMEM] * (5 * seqs),
         out_specs=[VMEM] * (n + 1) + [last, last, VMEM],
-        input_output_aliases={10: n + 1, 11: n + 2},
+        input_output_aliases={5: n + 1, 6: n + 2},
         scratch_shapes=[
             pltpu.VMEM((size * n, slots), bf16),
+            pltpu.VMEM((model, tokens), bf16),
             pltpu.VMEM((model, tokens), bf16),
         ],
         compiler_params=params("arbitrary"),
         cost_estimate=cost(4 * tokens * model * width, 10e6),
         name="mix_back",
-    )(ids, tok, own, other, dz2, hown, hother, vec, packed, mixed, *grads)
+    )(ids, tok, vec, front, mixed, *grads, *own, *other, *dz2, *hown, *hother)
 
 
 def project_back_kernel(n, seqs, heads, ids, tok, whole, small, *refs):
     inputs = refs[:n]
     part, send, keep = refs[n : n + 3]
-    stage, right, left = refs[n + 3 :]
+    stage, right, left, turned = refs[n + 3 :]
     z = ids[2]
     slots = inputs[0].shape[1]
     per = seqs * heads // n
@@ -609,10 +630,11 @@
             ours = jnp.concatenate(columns, axis=0).T
             right[s * slots : (s + 1) * slots, c * width : (c + 1) * width] = ours
     part[...] = dot_nt(right[...], whole[...]).astype(bf16)
-    left[...] = tok[...].T
+    turned[...] = tok[...].T
+    arrange(ids, turned, left)
     for c in range(3):
         cols = slice(c * width, (c + 1) * width)
-        write_rows(ids, left, right[:, cols], send.at[:, cols], keep.at[:, cols])
+        write_rows(left, right[:, cols], send.at[:, cols], keep.at[:, cols])
     ones = jnp.ones((8, right.shape[0]), bf16)
     sums = dot_nn(ones, right[...])
     line = jnp.concatenate([sums[:, :width], sums[:, 2 * width :]], axis=1)
@@ -641,6 +663,7 @@
             pltpu.VMEM((seqs * heads * 3 * HD, slots), bf16),
             pltpu.VMEM((tokens, wide), bf16),
             pltpu.VMEM((model, tokens), bf16),
+            pltpu.VMEM((model, tokens), bf16),
         ],
         compiler_params=params(),
         cost_estimate=cost(4 * tokens * model * wide, 8e6),
@@ -724,8 +747,9 @@
         and (tokens.shape[0] * heads) % n == 0
         and w_qkv.shape[0] % 16 == 0
         and tokens.shape[1] % 256 == 0
-        and b_qv.shape[1] == BLOCK
+        and b_qv.shape[1] == WIDTH
         and w_gu.shape[2] % BLOCK == 0
+        and w_gu.shape[2] % WIDTH == 0
     )
 
 
@@ -753,31 +777,44 @@
     first += [swap(piece, "shard", 2) for piece in first]
     by_core = [swap(piece, "shard", 1) for piece in first]
     pieces = first[:n] + by_core[:n] + first[n:] + by_core[n:]
-    packed = jnp.concatenate(
-        [w_out.T, w_gu.reshape(rows, 2 * units), w_down.T], axis=1
-    ).astype(bf16)
-    packed, pieces[0] = lax.optimization_barrier((packed, pieces[0]))
-    packed = lax.all_gather(packed, ("shard", "ctx"), axis=0, tiled=True)
+    front = jnp.concatenate([w_gu[:, 0], w_out.T], axis=1).astype(bf16)
+    back = jnp.concatenate([w_gu[:, 1], w_down.T], axis=1).astype(bf16)
+    front, pieces[0] = lax.optimization_barrier((front, pieces[0]))
+    front = lax.all_gather(front, ("shard", "ctx"), axis=0, tiled=True)
 
     bias = jnp.concatenate([b_qv[0], jnp.zeros_like(b_qv[0]), b_qv[1]])[None, :]
     *sends, whole = project(ids, tok, bias, pieces, n, seqs, heads)
     blocks = [sends[0]] + [swap(sends[d], "ctx", d) for d in range(1, n)]
+    *blocks, back = lax.optimization_barrier((*blocks, back))
+    back = lax.all_gather(back, ("shard", "ctx"), axis=0, tiled=True)
     *outs, att, den = attend(ids, lengths, slopes, blocks, n, heads, per)
     outs = [outs[0]] + [swap(outs[d], "ctx", d) for d in range(1, n)]
-    part, mixed = mix(ids, packed, outs, n, seqs, heads)
-    part_other = swap(part, "tp", 1)
-    hidden, low, act, gel, slope, ffn = unit(tok, part, part_other, vectors, packed, width, units)
-    ffn_other = swap(ffn, "tp", 1)
-    output, dz2, dffn, dgate, dup, back, sums_two = unit_back(
-        ids, lengths, hidden, ffn, ffn_other, cot, vectors, packed, gel, slope, n, seqs, width
-    )
-    back_other = swap(back, "tp", 1)
+    *part, mixed = mix(ids, front, outs, n, seqs, heads)
+    part_other = [swap(value, "tp", 1) for value in part]
+    hidden, low, act, gel, slope, ffn = zip(
+        *(
+            unit(s, tok, part[s], part_other[s], vectors, front, back)
+            for s in range(seqs)
+        )
+    )
+    ffn_other = [swap(value, "tp", 1) for value in ffn]
+    output, dz2, dffn, dgate, dup, dlow, sums_two = zip(
+        *(
+            unit_back(
+                s, ids, lengths, hidden[s], ffn[s], ffn_other[s], cot, vectors, front, back,
+                gel[s], slope[s], n,
+            )
+            for s in range(seqs)
+        )
+    )
+    dlow_other = [swap(value, "tp", 1) for value in dlow]
     unit_grads = weight_grads(ids, low, dffn, dgate, dup, act)
-    back_other, *unit_grads = lax.optimization_barrier((back_other, *unit_grads))
+    *dlow_other, far, near = lax.optimization_barrier((*dlow_other, *unit_grads))
     *sends, dz1, far, near, sums_one = mix_back(
-        ids, tok, part, part_other, dz2, back, back_other, vectors, packed, mixed, unit_grads,
-        n, seqs, heads,
-    )
+        ids, tok, vectors, front, mixed, (far, near), part, part_other, dz2, dlow, dlow_other,
+        n, heads,
+    )
+    sums_two = sum(sums_two)
     grads = [sends[0]] + [swap(sends[d], "ctx", d) for d in range(1, n)]
     got = swap(far, "shard", 1)
     mine, far = fold_core(near, got, 0)
@@ -805,7 +842,7 @@
     input_grad = dz1 + (dx.astype(f32) + dx_other.astype(f32))
     small = last[rows : rows + 8, : 2 * width]
     return (
-        output.reshape(tokens.shape),
+        jnp.stack(output),
         input_grad.reshape(tokens.shape),
         last[:rows].reshape(w_qkv.shape),
         small[6].reshape(2, width),

time: 377 us -> 348 us (0.923)
  starting transfers between devices: 77.1 us -> 53.8 us
  waiting for transfers between devices: 152 us -> 146 us
  Pallas kernels: 104 us -> 108 us
    ppermute x41 -> x44, starting transfers between devices: 77.1 us -> 53.7 us  [swap(): return lax.ppermute(value, axis, xor_pairs(axis, distance))]
    ppermute x41 -> x44, waiting for transfers between devices: 152 us -> 131 us  [swap(): return lax.ppermute(value, axis, xor_pairs(axis, distance))]
    all_gather x1 -> x2, waiting for transfers between devices: 0.02 us -> 14.9 us  [the longest x1 14.9 us: on_device(): back = lax.all_gather(back, ('shard', 'ctx'), axis=0, tiled=True)]
    pallas_call x1 -> x2, Pallas kernels: 12 us -> 15.5 us  [unit(): pl.pallas_call(unit_kernel, grid=(steps,), out_shape=[shape((tokens, mode...]
    pallas_call x2 -> x3, Pallas kernels: 28.3 us -> 29.5 us  [the longest x2 17.9 us: unit_back(): pl.pallas_call(functools.partial(unit_back_kernel, n, s), grid=(steps,),...]
    unnamed x89 -> x105, local copies, waits for them, and re-layouts: 10.2 us -> 11.2 us
  transfers between devices with their start and end apart: 42 -> 46, of which waited for: 21 -> 21; matrix products, arithmetic and copies ran while one was open for 2% -> 2% of each run, Pallas kernels for 15% -> 26%
where the time goes in v3:
time: 348 us; the launch traced here: 347 us
  waiting for transfers between devices  146 us (42%)
  Pallas kernels  108 us (31%)
  starting transfers between devices  53.8 us (15%)
  local copies, waits for them, and re-layouts  18.7 us (5%)
  between operations  14.6 us (4%)
  other arithmetic  6.5 us (2%)
    ppermute x44, waiting for transfers between devices, swap(): return lax.ppermute(value, axis, xor_pairs(axis, distance))  131 us
    ppermute x44, starting transfers between devices, swap(): return lax.ppermute(value, axis, xor_pairs(axis, distance))  53.7 us
    pallas_call x2, Pallas kernels, unit_back(): pl.pallas_call(functools.partial(unit_back_kernel, n, s), grid=(steps,),...  17.9 us
    pallas_call x2, Pallas kernels, unit(): pl.pallas_call(unit_kernel, grid=(steps,), out_shape=[shape((tokens, mode...  15.5 us
    pallas_call x1, Pallas kernels, attend_back(): pl.pallas_call(functools.partial(attend_back_kernel, n, heads), grid=(per...  15 us
    all_gather x1, waiting for transfers between devices, on_device(): back = lax.all_gather(back, ('shard', 'ctx'), axis=0, tiled=True)  14.9 us
    pallas_call x1, Pallas kernels, weight_grads(): pl.pallas_call(functools.partial(weight_kernel, steps, seqs), grid=(3 * s...  11.6 us
    pallas_call x1, Pallas kernels, attend(): pl.pallas_call(functools.partial(attend_kernel, n, heads), grid=(per,), o...  11.4 us
  transfers between devices with their start and end apart: 46, of which 21 were waited for; matrix products, arithmetic and copies ran while one was open for 2% of the time, Pallas kernels for 26%

profile of v3, /device:TPU:0, one launch (start us, length us, event | category | flops | bytes accessed | tf_op | source)
XLA Modules:
  0.0 347.3 jit_solution(13699793204320455343)
XLA Ops:
  11.1 3.1 collective-permute-start.7
  14.2 3.6 %collective-permute-start.2 = (bf16[48,1152]{1,0:T(8,128)(2,1)S(1)}, bf16[48,1152]{1,0:T(8,128)(2,1)S(1)}, u32[]{:S(2)}, u32[]{:S(2)}) collective-permute-start(bf16[48,1152]{1,0:T(8,128)(2,1)S(1)} %bitcast.42), channel_id=1, source_target_pairs={{0,6},{2,4},{4,2},{6,0},{1,7},{3,5},{5,3},{7,1},{8,14},{10,12},{12... | collective-permute-start | bytes 331784 | tf_op jit(solution)/shard_map/ppermute | solution.py:63
  18.6 3.4 collective-permute-done.2.refs_3_
  22.8 7.4 %collective-permute-done.1.refs_2_ = bf16[48,1152]{1,0:T(8,128)(2,1)S(1)} collective-permute-done((bf16[48,1152]{1,0:T(8,128)(2,1)S(1)}, bf16[48,1152]{1,0:T(8,128)(2,1)S(1)}, u32[]{:S(2)}, u32[]{:S(2)}) %collective-permute-start.1) | collective-permute-done | bytes 110624 | tf_op jit(solution)/shard_map/ppermute | solution.py:63
  38.8 4.8 %project.1 = (bf16[576,256]{1,0:T(8,128)(2,1)}, bf16[576,256]{1,0:T(8,128)(2,1)}, bf16[576,256]{1,0:T(8,128)(2,1)}, bf16[576,256]{1,0:T(8,128)(2,1)}, bf16[768,1152]{1,0:T(8,128)(2,1)}) custom-call(s32[4]{0:T(128)} %pad_add_fusion.ids, bf16[512,768]{1,0:T(8,128)(2,1)} %bitcast.28, f32[1,1152]{1,0:T(1,128)} %broadcast_in_dim.10.bias, ...), custom_call_target="tpu_custom_call" | custom-call | flops 905969664 | bytes 6000000 | tf_op jit(solution)/shard_map/project/pallas_call | solution.py:115
  44.1 4.5 %collective-permute-start.16 = (bf16[576,256]{1,0:T(8,128)(2,1)}, bf16[576,256]{1,0:T(8,128)(2,1)S(1)}, u32[]{:S(2)}, u32[]{:S(2)}) collective-permute-start(bf16[576,256]{1,0:T(8,128)(2,1)} %get-tuple-element.111), channel_id=1, source_target_pairs={{0,4},{2,6},{4,0},{6,2},{1,5},{3,7},{5,1},{7,3},{8,12},{10,14},{12... | collective-permute-start | bytes 884744 | tf_op jit(solution)/shard_map/ppermute | solution.py:63
  49.3 17.9 %collective-permute-done.15.refs_1_ = bf16[576,256]{1,0:T(8,128)(2,1)S(1)} collective-permute-done((bf16[576,256]{1,0:T(8,128)(2,1)}, bf16[576,256]{1,0:T(8,128)(2,1)S(1)}, u32[]{:S(2)}, u32[]{:S(2)}) %collective-permute-start.15) | collective-permute-done | bytes 294944 | tf_op jit(solution)/shard_map/ppermute | solution.py:63
  67.2 8.1 %collective-permute-done.17.refs_3_ = bf16[576,256]{1,0:T(8,128)(2,1)S(1)} collective-permute-done((bf16[576,256]{1,0:T(8,128)(2,1)}, bf16[576,256]{1,0:T(8,128)(2,1)S(1)}, u32[]{:S(2)}, u32[]{:S(2)}) %collective-permute-start.17) | collective-permute-done | bytes 294944 | tf_op jit(solution)/shard_map/ppermute | solution.py:63
  76.0 11.4 %attend.1 = (bf16[192,256]{1,0:T(8,128)(2,1)}, bf16[192,256]{1,0:T(8,128)(2,1)}, bf16[192,256]{1,0:T(8,128)(2,1)}, bf16[192,256]{1,0:T(8,128)(2,1)}, f32[192,1024]{1,0:T(8,128)}, /*index=5*/f32[3,1,1024]{2,1,0:T(1,128)}) custom-call(s32[4]{0:T(128)} %pad_add_fusion.ids, s32[2]{0:T(128)} %lens.7, f32[12]{0:T(128)} %constant.40.clone.slopes, ...), custom_call_target="tpu_custom_call" | custom-call | flops 1610612736 | bytes 3000000 | tf_op jit(solution)/shard_map/attend/pallas_call | solution.py:196
  87.4 6.5 %collective-permute-start.18 = (bf16[192,256]{1,0:T(8,128)(2,1)}, bf16[192,256]{1,0:T(8,128)(2,1)S(1)}, u32[]{:S(2)}, u32[]{:S(2)}) collective-permute-start(bf16[192,256]{1,0:T(8,128)(2,1)} %get-tuple-element.118), channel_id=1, source_target_pairs={{0,2},{2,0},{4,6},{6,4},{1,3},{3,1},{5,7},{7,5},{8,10},{10,8},{12,... | collective-permute-start | bytes 294920 | tf_op jit(solution)/shard_map/ppermute | solution.py:63
  96.3 7.0 %collective-permute-done.18.refs_1_ = bf16[192,256]{1,0:T(8,128)(2,1)S(1)} collective-permute-done((bf16[192,256]{1,0:T(8,128)(2,1)}, bf16[192,256]{1,0:T(8,128)(2,1)S(1)}, u32[]{:S(2)}, u32[]{:S(2)}) %collective-permute-start.18) | collective-permute-done | bytes 98336 | tf_op jit(solution)/shard_map/ppermute | solution.py:63
  103.2 4.9 %collective-permute-done.19.refs_2_ = bf16[192,256]{1,0:T(8,128)(2,1)S(1)} collective-permute-done((bf16[192,256]{1,0:T(8,128)(2,1)}, bf16[192,256]{1,0:T(8,128)(2,1)S(1)}, u32[]{:S(2)}, u32[]{:S(2)}) %collective-permute-start.19) | collective-permute-done | bytes 98336 | tf_op jit(solution)/shard_map/ppermute | solution.py:63
  113.6 10.2 %collective-permute-done.23.other.refs_3_ = bf16[256,768]{1,0:T(8,128)(2,1)S(1)} collective-permute-done((bf16[256,768]{1,0:T(8,128)(2,1)}, bf16[256,768]{1,0:T(8,128)(2,1)S(1)}, u32[]{:S(2)}, u32[]{:S(2)}) %collective-permute-start.23) | collective-permute-done | bytes 393248 | tf_op jit(solution)/shard_map/ppermute | solution.py:63
  123.7 14.9 %all-gather.5.cloned.1.call-done.wu.wd = bf16[768,3072]{1,0:T(8,128)(2,1)} async-done(((bf16[48,3072]{1,0:T(8,128)(2,1)}), bf16[768,3072]{1,0:T(8,128)(2,1)}) %all-gather.5.cloned.1.call-update) | async-done | bytes 4718608 | tf_op jit(solution)/shard_map/all_gather | solution.py:789
  138.6 7.7 %unit.3 = (f32[256,768]{1,0:T(8,128)}, bf16[256,768]{1,0:T(8,128)(2,1)}, bf16[256,1536]{1,0:T(8,128)(2,1)}, bf16[256,1536]{1,0:T(8,128)(2,1)}, bf16[256,1536]{1,0:T(8,128)(2,1)}, /*index=5*/bf16[256,768]{1,0:T(8,128)(2,1)}) custom-call(bf16[512,768]{1,0:T(8,128)(2,1)} %bitcast.29, bf16[256,768]{1,0:T(8,128)(2,1)} %get-tuple-element.128.own.refs_1_, ...), custom_call_target="tpu_custom_call" | custom-call | flops 1811939328 | bytes 13000000 | tf_op jit(solution)/shard_map/unit/pallas_call | solution.py:381
  148.6 7.9 %unit.2 = (f32[256,768]{1,0:T(8,128)}, bf16[256,768]{1,0:T(8,128)(2,1)}, bf16[256,1536]{1,0:T(8,128)(2,1)}, bf16[256,1536]{1,0:T(8,128)(2,1)}, bf16[256,1536]{1,0:T(8,128)(2,1)}, /*index=5*/bf16[256,768]{1,0:T(8,128)(2,1)}) custom-call(bf16[512,768]{1,0:T(8,128)(2,1)} %bitcast.30, bf16[256,768]{1,0:T(8,128)(2,1)} %get-tuple-element.121.own.refs_0_, ...), custom_call_target="tpu_custom_call" | custom-call | flops 1811939328 | bytes 13000000 | tf_op jit(solution)/shard_map/unit/pallas_call | solution.py:381
  158.6 9.0 %unit_back.3 = (bf16[256,768]{1,0:T(8,128)(2,1)}, f32[256,768]{1,0:T(8,128)}, bf16[256,768]{1,0:T(8,128)(2,1)}, bf16[256,1536]{1,0:T(8,128)(2,1)}, bf16[256,1536...) custom-call(s32[4]{0:T(128)} %pad_add_fusion.ids, s32[2]{0:T(128)} %lens.7, ...), custom_call_target="tpu_custom_call" | custom-call | flops 1811939328 | bytes 14000000 | tf_op jit(solution)/shard_map/unit_back/pallas_call | solution.py:447
  169.8 9.0 %unit_back.2 = (bf16[256,768]{1,0:T(8,128)(2,1)}, f32[256,768]{1,0:T(8,128)}, bf16[256,768]{1,0:T(8,128)(2,1)}, bf16[256,1536]{1,0:T(8,128)(2,1)}, bf16[256,1536...) custom-call(s32[4]{0:T(128)} %pad_add_fusion.ids, s32[2]{0:T(128)} %lens.7, ...), custom_call_target="tpu_custom_call" | custom-call | flops 1811939328 | bytes 14000000 | tf_op jit(solution)/shard_map/unit_back/pallas_call | solution.py:447
  179.4 11.6 %weight_grads.1 = (bf16[384,4992]{1,0:T(8,128)(2,1)}, bf16[384,4992]{1,0:T(8,128)(2,1)}) custom-call(s32[4]{0:T(128)} %pad_add_fusion.ids, bf16[256,768]{1,0:T(8,128)(2,1)} %get-tuple-element.137.refs_0_, bf16[256,768]{1,0:T(8,128)(2,1)} %get-tuple-element.138.refs_1_, bf16[256,768]{1,0:T(8,128)(2,1)} %get-tuple-element.139.refs_2_, ...), custom_call_target="tpu_custom_call" | custom-call | flops 3623878656 | bytes 14000000 | tf_op jit(solution)/shard_map/weight_grads/pallas_call | solution.py:527
  191.9 6.7 %mix_back.1 = (bf16[192,256]{1,0:T(8,128)(2,1)}, bf16[192,256]{1,0:T(8,128)(2,1)}, bf16[192,256]{1,0:T(8,128)(2,1)}, bf16[192,256]{1,0:T(8,128)(2,1)}, f32[512,7...) custom-call(s32[4]{0:T(128)} %pad_add_fusion.ids, ...), custom_call_target="tpu_custom_call", output_to_operand_aliasing={{5}: (5, {}), {6}: (6, {})} | custom-call | flops 603979776 | bytes 10000000 | tf_op jit(solution)/shard_map/mix_back/pallas_call | solution.py:588
  207.4 6.5 %fold_core.2 = (f32[192,4992]{1,0:T(8,128)}, bf16[192,4992]{1,0:T(8,128)(2,1)}) custom-call(bf16[384,4992]{1,0:T(8,128)(2,1)} %get-tuple-element.164.keep, bf16[384,4992]{1,0:T(8,128)(2,1)} %copy-done), custom_call_target="tpu_custom_call" | custom-call | flops 1916928 | bytes 13418496 | tf_op jit(solution)/shard_map/fold_core/pallas_call | solution.py:688
  214.6 15.0 %attend_back.1 = (bf16[576,256]{1,0:T(8,128)(2,1)}, bf16[576,256]{1,0:T(8,128)(2,1)}, bf16[576,256]{1,0:T(8,128)(2,1)}, bf16[576,256]{1,0:T(8,128)(2,1)}) custom-call(s32[4]{0:T(128)} %pad_add_fusion.ids, s32[2]{0:T(128)} %lens.7, f32[12]{0:T(128)} %constant.40.clone.slopes, bf16[576,256]{1,0:T(8,128)(2,1)} %get-tuple-element.113.refs_0_, ...), custom_call_target="tpu_custom_call" | custom-call | flops 4026531840 | bytes 5000000 | tf_op jit(solution)/shard_map/attend_back/pallas_call | solution.py:278
  237.0 17.4 %collective-permute-done.32.refs_2_ = bf16[576,256]{1,0:T(8,128)(2,1)S(1)} collective-permute-done((bf16[576,256]{1,0:T(8,128)(2,1)}, bf16[576,256]{1,0:T(8,128)(2,1)S(1)}, u32[]{:S(2)}, u32[]{:S(2)}) %collective-permute-start.32) | collective-permute-done | bytes 294944 | tf_op jit(solution)/shard_map/ppermute | solution.py:63
  254.4 3.6 %collective-permute-done.34.recv = bf16[192,4992]{1,0:T(8,128)(2,1)S(1)} collective-permute-done((bf16[192,4992]{1,0:T(8,128)(2,1)}, bf16[192,4992]{1,0:T(8,128)(2,1)S(1)}, u32[]{:S(2)}, u32[]{:S(2)}) %collective-permute-start.34) | collective-permute-done | bytes 1916960 | tf_op jit(solution)/shard_map/ppermute | solution.py:63
  259.3 4.8 %fold_y.2 = (f32[48,4992]{1,0:T(8,128)}, bf16[48,4992]{1,0:T(8,128)(2,1)}, bf16[48,4992]{1,0:T(8,128)(2,1)}, bf16[48,4992]{1,0:T(8,128)(2,1)}) custom-call(s32[4]{0:T(128)} %pad_add_fusion.ids, f32[192,4992]{1,0:T(8,128)} %get-tuple-element.182.mine, bf16[192,4992]{1,0:T(8,128)(2,1)} %copy-done.1), custom_call_target="tpu_custom_call" | custom-call | flops 958464 | bytes 8626176 | tf_op jit(solution)/shard_map/fold_y/pallas_call | solution.py:723
  264.2 6.0 %project_back.1 = (bf16[512,768]{1,0:T(8,128)(2,1)}, bf16[400,1152]{1,0:T(8,128)(2,1)}, bf16[400,1152]{1,0:T(8,128)(2,1)}) custom-call(s32[4]{0:T(128)} %pad_add_fusion.ids, bf16[512,768]{1,0:T(8,128)(2,1)} %bitcast.32, bf16[768,1152]{1,0:T(8,128)(2,1)} %get-tuple-element.156.whole, f32[8,768]{1,0:T(8,128)} %concatenate.17.small, ...), custom_call_target="tpu_custom_call" | custom-call | flops 1811939328 | bytes 8000000 | tf_op jit(solution)/shard_map/project_back/pallas_call | solution.py:653
  277.1 3.3 collective-permute-start.38
  283.8 6.0 %collective-permute-done.37.recv = bf16[208,1152]{1,0:T(8,128)(2,1)S(1)} collective-permute-done((bf16[208,1152]{1,0:T(8,128)(2,1)}, bf16[208,1152]{1,0:T(8,128)(2,1)S(1)}, u32[]{:S(2)}, u32[]{:S(2)}) %collective-permute-start.37) | collective-permute-done | bytes 479264 | tf_op jit(solution)/shard_map/ppermute | solution.py:63
  292.9 3.4 collective-permute-start.41
  296.3 5.1 %collective-permute-done.38 = bf16[48,4992]{1,0:T(8,128)(2,1)S(1)} collective-permute-done((bf16[48,4992]{1,0:T(8,128)(2,1)S(1)}, bf16[48,4992]{1,0:T(8,128)(2,1)S(1)}, u32[]{:S(2)}, u32[]{:S(2)}) %collective-permute-start.38) | collective-permute-done | bytes 479264 | tf_op jit(solution)/shard_map/ppermute | solution.py:63
  304.7 11.2 %collective-permute-done.39 = bf16[48,4992]{1,0:T(8,128)(2,1)S(1)} collective-permute-done((bf16[48,4992]{1,0:T(8,128)(2,1)S(1)}, bf16[48,4992]{1,0:T(8,128)(2,1)S(1)}, u32[]{:S(2)}, u32[]{:S(2)}) %collective-permute-start.39) | collective-permute-done | bytes 479264 | tf_op jit(solution)/shard_map/ppermute | solution.py:63
  315.9 19.6 %collective-permute-done.42 = bf16[64,1152]{1,0:T(8,128)(2,1)S(1)} collective-permute-done((bf16[64,1152]{1,0:T(8,128)(2,1)}, bf16[64,1152]{1,0:T(8,128)(2,1)S(1)}, u32[]{:S(2)}, u32[]{:S(2)}) %collective-permute-start.42) | collective-permute-done | bytes 147488 | tf_op jit(solution)/shard_map/ppermute | solution.py:63
  (215 shorter events, 71.7 us)
Async XLA Ops:
  7.2 101.0 %all-gather.3.cloned.1.call-start = ((), (), s32[]{:S(2)}) async-start(), calls=%async_computation | async-start | bytes 3133440 | tf_op jit(solution)/shard_map/all_gather | solution.py:783
  11.1 127.5 %all-gather.5.cloned.1.call-start = ((), (), s32[]{:S(2)}) async-start(), calls=%async_computation.1 | async-start | bytes 5013504 | tf_op jit(solution)/shard_map/all_gather | solution.py:789
  11.1 11.2 %collective-permute-start.7 = (bf16[48,1152]{1,0:T(8,128)(2,1)S(1)}, bf16[48,1152]{1,0:T(8,128)(2,1)S(1)}, u32[]{:S(2)}, u32[]{:S(2)}) collective-permute-start(bf16[48,1152]{1,0:T(8,128)(2,1)S(1)} %bitcast.40), channel_id=1, source_target_pairs={{0,16},{8,24},{16,0},{24,8},{1,17},{9,25},{17,1},{25,9},{2,18},{10... | collective-permute-start | bytes 331784 | tf_op jit(solution)/shard_map/ppermute | solution.py:63
  17.8 12.5 %collective-permute-start.1 = (bf16[48,1152]{1,0:T(8,128)(2,1)S(1)}, bf16[48,1152]{1,0:T(8,128)(2,1)S(1)}, u32[]{:S(2)}, u32[]{:S(2)}) collective-permute-start(bf16[48,1152]{1,0:T(8,128)(2,1)S(1)} %bitcast.43), channel_id=1, source_target_pairs={{0,4},{2,6},{4,0},{6,2},{1,5},{3,7},{5,1},{7,3},{8,12},{10,14},{12... | collective-permute-start | bytes 331784 | tf_op jit(solution)/shard_map/ppermute | solution.py:63
  17.8 12.7 %collective-permute-start = (bf16[48,1152]{1,0:T(8,128)(2,1)S(1)}, bf16[48,1152]{1,0:T(8,128)(2,1)S(1)}, u32[]{:S(2)}, u32[]{:S(2)}) collective-permute-start(bf16[48,1152]{1,0:T(8,128)(2,1)S(1)} %bitcast.44), channel_id=1, source_target_pairs={{0,2},{2,0},{4,6},{6,4},{1,3},{3,1},{5,7},{7,5},{8,10},{10,8},{12,... | collective-permute-start | bytes 331784 | tf_op jit(solution)/shard_map/ppermute | solution.py:63
  22.3 11.1 %collective-permute-start.6 = (bf16[48,1152]{1,0:T(8,128)(2,1)S(1)}, bf16[48,1152]{1,0:T(8,128)(2,1)S(1)}, u32[]{:S(2)}, u32[]{:S(2)}) collective-permute-start(bf16[48,1152]{1,0:T(8,128)(2,1)S(1)} %collective-permute-done.2.refs_3_), channel_id=1, source_target_pairs={{0,8},{8,0},{16,24},{24,16},{1,9},{9,1},{17,25},{25,17},{2,10},{10... | collective-permute-start | bytes 331784 | tf_op jit(solution)/shard_map/ppermute | solution.py:63
  43.6 23.6 %collective-permute-start.15 = (bf16[576,256]{1,0:T(8,128)(2,1)}, bf16[576,256]{1,0:T(8,128)(2,1)S(1)}, u32[]{:S(2)}, u32[]{:S(2)}) collective-permute-start(bf16[576,256]{1,0:T(8,128)(2,1)} %get-tuple-element.110), channel_id=1, source_target_pairs={{0,2},{2,0},{4,6},{6,4},{1,3},{3,1},{5,7},{7,5},{8,10},{10,8},{12,... | collective-permute-start | bytes 884744 | tf_op jit(solution)/shard_map/ppermute | solution.py:63
  44.1 23.1 %collective-permute-start.16 = (bf16[576,256]{1,0:T(8,128)(2,1)}, bf16[576,256]{1,0:T(8,128)(2,1)S(1)}, u32[]{:S(2)}, u32[]{:S(2)}) collective-permute-start(bf16[576,256]{1,0:T(8,128)(2,1)} %get-tuple-element.111), channel_id=1, source_target_pairs={{0,4},{2,6},{4,0},{6,2},{1,5},{3,7},{5,1},{7,3},{8,12},{10,14},{12... | collective-permute-start | bytes 884744 | tf_op jit(solution)/shard_map/ppermute | solution.py:63
  48.5 26.7 %collective-permute-start.17 = (bf16[576,256]{1,0:T(8,128)(2,1)}, bf16[576,256]{1,0:T(8,128)(2,1)S(1)}, u32[]{:S(2)}, u32[]{:S(2)}) collective-permute-start(bf16[576,256]{1,0:T(8,128)(2,1)} %get-tuple-element.112), channel_id=1, source_target_pairs={{0,6},{2,4},{4,2},{6,0},{1,7},{3,5},{5,3},{7,1},{8,14},{10,12},{12... | collective-permute-start | bytes 884744 | tf_op jit(solution)/shard_map/ppermute | solution.py:63
  87.4 15.9 %collective-permute-start.18 = (bf16[192,256]{1,0:T(8,128)(2,1)}, bf16[192,256]{1,0:T(8,128)(2,1)S(1)}, u32[]{:S(2)}, u32[]{:S(2)}) collective-permute-start(bf16[192,256]{1,0:T(8,128)(2,1)} %get-tuple-element.118), channel_id=1, source_target_pairs={{0,2},{2,0},{4,6},{6,4},{1,3},{3,1},{5,7},{7,5},{8,10},{10,8},{12,... | collective-permute-start | bytes 294920 | tf_op jit(solution)/shard_map/ppermute | solution.py:63
  93.8 14.3 %collective-permute-start.19 = (bf16[192,256]{1,0:T(8,128)(2,1)}, bf16[192,256]{1,0:T(8,128)(2,1)S(1)}, u32[]{:S(2)}, u32[]{:S(2)}) collective-permute-start(bf16[192,256]{1,0:T(8,128)(2,1)} %get-tuple-element.119), channel_id=1, source_target_pairs={{0,4},{2,6},{4,0},{6,2},{1,5},{3,7},{5,1},{7,3},{8,12},{10,14},{12... | collective-permute-start | bytes 294920 | tf_op jit(solution)/shard_map/ppermute | solution.py:63
  93.8 14.3 %collective-permute-start.20 = (bf16[192,256]{1,0:T(8,128)(2,1)}, bf16[192,256]{1,0:T(8,128)(2,1)S(1)}, u32[]{:S(2)}, u32[]{:S(2)}) collective-permute-start(bf16[192,256]{1,0:T(8,128)(2,1)} %get-tuple-element.120), channel_id=1, source_target_pairs={{0,6},{2,4},{4,2},{6,0},{1,7},{3,5},{5,3},{7,1},{8,14},{10,12},{12... | collective-permute-start | bytes 294920 | tf_op jit(solution)/shard_map/ppermute | solution.py:63
  111.5 12.2 %collective-permute-start.23 = (bf16[256,768]{1,0:T(8,128)(2,1)}, bf16[256,768]{1,0:T(8,128)(2,1)S(1)}, u32[]{:S(2)}, u32[]{:S(2)}) collective-permute-start(bf16[256,768]{1,0:T(8,128)(2,1)} %get-tuple-element.128.own.refs_1_), channel_id=1, source_target_pairs={{0,1},{1,0},{2,3},{3,2},{4,5},{5,4},{6,7},{7,6},{8,9},{9,8},{10,11... | collective-permute-start | bytes 1179656 | tf_op jit(solution)/shard_map/ppermute | solution.py:63
  113.1 34.7 %collective-permute-start.21 = (bf16[256,768]{1,0:T(8,128)(2,1)}, bf16[256,768]{1,0:T(8,128)(2,1)S(1)}, u32[]{:S(2)}, u32[]{:S(2)}) collective-permute-start(bf16[256,768]{1,0:T(8,128)(2,1)} %get-tuple-element.121.own.refs_0_), channel_id=1, source_target_pairs={{0,1},{1,0},{2,3},{3,2},{4,5},{5,4},{6,7},{7,6},{8,9},{9,8},{10,11... | collective-permute-start | bytes 1179656 | tf_op jit(solution)/shard_map/ppermute | solution.py:63
  146.3 11.5 %collective-permute-start.24 = (bf16[256,768]{1,0:T(8,128)(2,1)}, bf16[256,768]{1,0:T(8,128)(2,1)S(1)}, u32[]{:S(2)}, u32[]{:S(2)}) collective-permute-start(bf16[256,768]{1,0:T(8,128)(2,1)} %get-tuple-element.130.own), channel_id=1, source_target_pairs={{0,1},{1,0},{2,3},{3,2},{4,5},{5,4},{6,7},{7,6},{8,9},{9,8},{10,11... | collective-permute-start | bytes 1179656 | tf_op jit(solution)/shard_map/ppermute | solution.py:63
  156.5 12.6 %collective-permute-start.22 = (bf16[256,768]{1,0:T(8,128)(2,1)}, bf16[256,768]{1,0:T(8,128)(2,1)S(1)}, u32[]{:S(2)}, u32[]{:S(2)}) collective-permute-start(bf16[256,768]{1,0:T(8,128)(2,1)} %get-tuple-element.124.own), channel_id=1, source_target_pairs={{0,1},{1,0},{2,3},{3,2},{4,5},{5,4},{6,7},{7,6},{8,9},{9,8},{10,11... | collective-permute-start | bytes 1179656 | tf_op jit(solution)/shard_map/ppermute | solution.py:63
  167.6 23.4 %collective-permute-start.26 = (bf16[256,768]{1,0:T(8,128)(2,1)}, bf16[256,768]{1,0:T(8,128)(2,1)S(1)}, u32[]{:S(2)}, u32[]{:S(2)}) collective-permute-start(bf16[256,768]{1,0:T(8,128)(2,1)} %get-tuple-element.136.refs_7_), channel_id=1, source_target_pairs={{0,1},{1,0},{2,3},{3,2},{4,5},{5,4},{6,7},{7,6},{8,9},{9,8},{10,11... | collective-permute-start | bytes 1179656 | tf_op jit(solution)/shard_map/ppermute | solution.py:63
  178.8 12.2 %collective-permute-start.25 = (bf16[256,768]{1,0:T(8,128)(2,1)}, bf16[256,768]{1,0:T(8,128)(2,1)S(1)}, u32[]{:S(2)}, u32[]{:S(2)}) collective-permute-start(bf16[256,768]{1,0:T(8,128)(2,1)} %get-tuple-element.135.refs_6_), channel_id=1, source_target_pairs={{0,1},{1,0},{2,3},{3,2},{4,5},{5,4},{6,7},{7,6},{8,9},{9,8},{10,11... | collective-permute-start | bytes 1179656 | tf_op jit(solution)/shard_map/ppermute | solution.py:63
  198.7 15.2 %collective-permute-start.27 = (bf16[192,256]{1,0:T(8,128)(2,1)}, bf16[192,256]{1,0:T(8,128)(2,1)S(1)}, u32[]{:S(2)}, u32[]{:S(2)}) collective-permute-start(bf16[192,256]{1,0:T(8,128)(2,1)} %get-tuple-element.161), channel_id=1, source_target_pairs={{0,2},{2,0},{4,6},{6,4},{1,3},{3,1},{5,7},{7,5},{8,10},{10,8},{12,... | collective-permute-start | bytes 294920 | tf_op jit(solution)/shard_map/ppermute | solution.py:63
  200.2 13.7 %collective-permute-start.28 = (bf16[192,256]{1,0:T(8,128)(2,1)}, bf16[192,256]{1,0:T(8,128)(2,1)S(1)}, u32[]{:S(2)}, u32[]{:S(2)}) collective-permute-start(bf16[192,256]{1,0:T(8,128)(2,1)} %get-tuple-element.162), channel_id=1, source_target_pairs={{0,4},{2,6},{4,0},{6,2},{1,5},{3,7},{5,1},{7,3},{8,12},{10,14},{12... | collective-permute-start | bytes 294920 | tf_op jit(solution)/shard_map/ppermute | solution.py:63
  201.2 12.8 %collective-permute-start.29 = (bf16[192,256]{1,0:T(8,128)(2,1)}, bf16[192,256]{1,0:T(8,128)(2,1)S(1)}, u32[]{:S(2)}, u32[]{:S(2)}) collective-permute-start(bf16[192,256]{1,0:T(8,128)(2,1)} %get-tuple-element.163), channel_id=1, source_target_pairs={{0,6},{2,4},{4,2},{6,0},{1,7},{3,5},{5,3},{7,1},{8,14},{10,12},{12... | collective-permute-start | bytes 294920 | tf_op jit(solution)/shard_map/ppermute | solution.py:63
  214.0 44.1 %collective-permute-start.34 = (bf16[192,4992]{1,0:T(8,128)(2,1)}, bf16[192,4992]{1,0:T(8,128)(2,1)S(1)}, u32[]{:S(2)}, u32[]{:S(2)}) collective-permute-start(bf16[192,4992]{1,0:T(8,128)(2,1)} %get-tuple-element.177), channel_id=1, source_target_pairs={{0,16},{8,24},{16,0},{24,8},{1,17},{9,25},{17,1},{25,9},{2,18},{10... | collective-permute-start | bytes 5750792 | tf_op jit(solution)/shard_map/ppermute | solution.py:63
  231.2 23.2 %collective-permute-start.32 = (bf16[576,256]{1,0:T(8,128)(2,1)}, bf16[576,256]{1,0:T(8,128)(2,1)S(1)}, u32[]{:S(2)}, u32[]{:S(2)}) collective-permute-start(bf16[576,256]{1,0:T(8,128)(2,1)} %get-tuple-element.175), channel_id=1, source_target_pairs={{0,4},{2,6},{4,0},{6,2},{1,5},{3,7},{5,1},{7,3},{8,12},{10,14},{12... | collective-permute-start | bytes 884744 | tf_op jit(solution)/shard_map/ppermute | solution.py:63
  231.2 23.2 %collective-permute-start.33 = (bf16[576,256]{1,0:T(8,128)(2,1)}, bf16[576,256]{1,0:T(8,128)(2,1)S(1)}, u32[]{:S(2)}, u32[]{:S(2)}) collective-permute-start(bf16[576,256]{1,0:T(8,128)(2,1)} %get-tuple-element.176), channel_id=1, source_target_pairs={{0,6},{2,4},{4,2},{6,0},{1,7},{3,5},{5,3},{7,1},{8,14},{10,12},{12... | collective-permute-start | bytes 884744 | tf_op jit(solution)/shard_map/ppermute | solution.py:63
  270.2 31.2 %collective-permute-start.35 = (bf16[512,768]{1,0:T(8,128)(2,1)}, bf16[512,768]{1,0:T(8,128)(2,1)S(1)}, u32[]{:S(2)}, u32[]{:S(2)}) collective-permute-start(bf16[512,768]{1,0:T(8,128)(2,1)} %get-tuple-element.189), channel_id=1, source_target_pairs={{0,1},{1,0},{2,3},{3,2},{4,5},{5,4},{6,7},{7,6},{8,9},{9,8},{10,11... | collective-permute-start | bytes 2359304 | tf_op jit(solution)/shard_map/ppermute | solution.py:63
  276.6 13.2 %collective-permute-start.37 = (bf16[208,1152]{1,0:T(8,128)(2,1)}, bf16[208,1152]{1,0:T(8,128)(2,1)S(1)}, u32[]{:S(2)}, u32[]{:S(2)}) collective-permute-start(bf16[208,1152]{1,0:T(8,128)(2,1)} %get-tuple-element.193), channel_id=1, source_target_pairs={{0,16},{8,24},{16,0},{24,8},{1,17},{9,25},{17,1},{25,9},{2,18},{10... | collective-permute-start | bytes 1437704 | tf_op jit(solution)/shard_map/ppermute | solution.py:63
  277.1 24.3 %collective-permute-start.38 = (bf16[48,4992]{1,0:T(8,128)(2,1)S(1)}, bf16[48,4992]{1,0:T(8,128)(2,1)S(1)}, u32[]{:S(2)}, u32[]{:S(2)}) collective-permute-start(bf16[48,4992]{1,0:T(8,128)(2,1)S(1)} %copy-done.27), channel_id=1, source_target_pairs={{0,2},{2,0},{4,6},{6,4},{1,3},{3,1},{5,7},{7,5},{8,10},{10,8},{12,... | collective-permute-start | bytes 1437704 | tf_op jit(solution)/shard_map/ppermute | solution.py:63
  280.4 35.5 %collective-permute-start.39 = (bf16[48,4992]{1,0:T(8,128)(2,1)S(1)}, bf16[48,4992]{1,0:T(8,128)(2,1)S(1)}, u32[]{:S(2)}, u32[]{:S(2)}) collective-permute-start(bf16[48,4992]{1,0:T(8,128)(2,1)S(1)} %copy-done.26), channel_id=1, source_target_pairs={{0,4},{2,6},{4,0},{6,2},{1,5},{3,7},{5,1},{7,3},{8,12},{10,14},{12... | collective-permute-start | bytes 1437704 | tf_op jit(solution)/shard_map/ppermute | solution.py:63
  280.8 35.0 %collective-permute-start.40 = (bf16[48,4992]{1,0:T(8,128)(2,1)S(1)}, bf16[48,4992]{1,0:T(8,128)(2,1)S(1)}, u32[]{:S(2)}, u32[]{:S(2)}) collective-permute-start(bf16[48,4992]{1,0:T(8,128)(2,1)S(1)} %copy-done.25), channel_id=1, source_target_pairs={{0,6},{2,4},{4,2},{6,0},{1,7},{3,5},{5,3},{7,1},{8,14},{10,12},{12... | collective-permute-start | bytes 1437704 | tf_op jit(solution)/shard_map/ppermute | solution.py:63
  292.9 23.0 %collective-permute-start.41 = (bf16[64,1152]{1,0:T(8,128)(2,1)}, bf16[64,1152]{1,0:T(8,128)(2,1)S(1)}, u32[]{:S(2)}, u32[]{:S(2)}) collective-permute-start(bf16[64,1152]{1,0:T(8,128)(2,1)} %get-tuple-element.198), channel_id=1, source_target_pairs={{0,2},{2,0},{4,6},{6,4},{1,3},{3,1},{5,7},{7,5},{8,10},{10,8},{12,... | collective-permute-start | bytes 442376 | tf_op jit(solution)/shard_map/ppermute | solution.py:63
  301.4 34.1 %collective-permute-start.42 = (bf16[64,1152]{1,0:T(8,128)(2,1)}, bf16[64,1152]{1,0:T(8,128)(2,1)S(1)}, u32[]{:S(2)}, u32[]{:S(2)}) collective-permute-start(bf16[64,1152]{1,0:T(8,128)(2,1)} %get-tuple-element.200), channel_id=1, source_target_pairs={{0,4},{2,6},{4,0},{6,2},{1,5},{3,7},{5,1},{7,3},{8,12},{10,14},{12... | collective-permute-start | bytes 442376 | tf_op jit(solution)/shard_map/ppermute | solution.py:63
  301.4 34.1 %collective-permute-start.43 = (bf16[64,1152]{1,0:T(8,128)(2,1)}, bf16[64,1152]{1,0:T(8,128)(2,1)S(1)}, u32[]{:S(2)}, u32[]{:S(2)}) collective-permute-start(bf16[64,1152]{1,0:T(8,128)(2,1)} %get-tuple-element.201), channel_id=1, source_target_pairs={{0,6},{2,4},{4,2},{6,0},{1,7},{3,5},{5,3},{7,1},{8,14},{10,12},{12... | collective-permute-start | bytes 442376 | tf_op jit(solution)/shard_map/ppermute | solution.py:63
  (67 other events, 546.5 us)
Sparse Core Ops, SparseCore 0:
  11.2 55.5 all-gather.2
  75.4 63.1 all-gather.4

commit v4 on v3

--- a/solution.py
+++ b/solution.py
@@ -63,6 +63,10 @@
     return lax.ppermute(value, axis, xor_pairs(axis, distance))
 
 
+def after(values, *done):
+    return lax.optimization_barrier((*values, *done))[: len(values)]
+
+
 def live_mask(length, rank, n_ctx, slots):
     slot = lax.broadcasted_iota(jnp.int32, (slots, 1), 0)
     return jnp.where(slot * n_ctx + rank < length, 1.0, 0.0).astype(f32)
@@ -78,6 +82,32 @@
 def normalise_back(grad_hat, hat, scale):
     inner = jnp.mean(grad_hat * hat, axis=-1, keepdims=True)
     return scale * (grad_hat - jnp.mean(grad_hat, axis=-1, keepdims=True) - hat * inner)
+
+
+def assemble_kernel(n, ids, *refs):
+    pieces, whole = refs[:4], refs[4]
+    y, c, z = ids[0], ids[1], ids[2]
+    rows = pieces[0].shape[0] // n
+    for k in range(4):
+        for kz in range(n):
+            index = ((y ^ (k // 2)) * 2 + (c ^ (k % 2))) * n + (z ^ kz)
+            place = pl.ds(pl.multiple_of(index * rows, rows), rows)
+            whole[place, :] = pieces[k][kz * rows : (kz + 1) * rows, :]
+
+
+def assemble(ids, pieces, n):
+    rows, wide = pieces[0].shape
+    column = lambda size: pl.BlockSpec((size, wide // 3), lambda j: (0, j))
+    return pl.pallas_call(
+        functools.partial(assemble_kernel, n),
+        grid=(3,),
+        out_shape=shape((4 * rows, wide), bf16),
+        in_specs=[SMEM] + [column(rows)] * 4,
+        out_specs=column(4 * rows),
+        compiler_params=params("arbitrary"),
+        cost_estimate=cost(0, 16 * rows * wide),
+        name="assemble",
+    )(ids, *pieces)
 
 
 def project_kernel(n, seqs, heads, ids, tok, bias, *refs):
@@ -372,7 +402,7 @@
 
 def unit(s, tok, own, other, vec, front, back):
     tokens, model = own.shape
-    hidden_units = back.shape[1] // 2
+    hidden_units = back.shape[1]
     steps = hidden_units // BLOCK
     fixed = lambda j: (0, 0)
     whole = pl.BlockSpec((tokens, model), fixed)
@@ -390,15 +420,15 @@
             whole,
             pl.BlockSpec(vec.shape, fixed),
             weight(0),
+            weight(steps),
             weight(0),
-            weight(steps),
         ],
         out_specs=[whole, whole, inner, inner, inner, whole],
         scratch_shapes=[pltpu.VMEM((tokens, model), f32)],
         compiler_params=params("arbitrary"),
         cost_estimate=cost(6 * tokens * model * hidden_units, 13e6, 2 * tokens * hidden_units),
         name="unit",
-    )(tok, own, other, vec, front, back, back)
+    )(tok, own, other, vec, front, front, back)
 
 
 def unit_back_kernel(
@@ -458,13 +488,13 @@
         ],
         in_specs=[SMEM, SMEM, whole, whole, whole]
         + [pl.BlockSpec((tokens, model), lambda j: (s, 0)), pl.BlockSpec(vec.shape, fixed)]
-        + [weight(0), weight(0), weight(steps), inner, inner],
+        + [weight(0), weight(steps), weight(0), inner, inner],
         out_specs=[whole, whole, whole, inner, inner, whole, pl.BlockSpec((8, model), fixed)],
         scratch_shapes=[pltpu.VMEM((tokens, model), f32)],
         compiler_params=params("arbitrary"),
         cost_estimate=cost(6 * tokens * model * hidden_units, 14e6),
         name="unit_back",
-    )(ids, lens, hidden, own, other, cot, vec, front, back, back, gel, slope)
+    )(ids, lens, hidden, own, other, cot, vec, front, front, back, gel, slope)
 
 
 def row_starts(ids, quarter):
@@ -527,7 +557,7 @@
     return pl.pallas_call(
         functools.partial(weight_kernel, steps, seqs),
         grid=(3 * steps,),
-        out_shape=[shape((model // 2, 3 * hidden_units + WIDTH), bf16)] * 2,
+        out_shape=[shape((model // 2, 3 * hidden_units), bf16)] * 2,
         in_specs=[SMEM]
         + [whole] * (2 * seqs)
         + [column(0)] * seqs
@@ -544,7 +574,7 @@
     )(ids, *low, *dffn, *dgate, *dup, *act)
 
 
-def mix_back_kernel(n, seqs, heads, ids, tok, vec, wo, mixed, far, near, *refs):
+def mix_back_kernel(n, seqs, heads, ids, tok, vec, wo, mixed, *refs):
     own, other, dz2, hown, hother = (refs[i * seqs : (i + 1) * seqs] for i in range(5))
     refs = refs[5 * seqs :]
     sends = refs[:n]
@@ -576,28 +606,29 @@
         sends[d][...] = stage[pl.ds(pl.multiple_of((z ^ d) * size, size), size), :]
     arrange(ids, turned_low, left)
     write_rows(left, mixed[...], send, keep)
-
-
-def mix_back(ids, tok, vec, front, mixed, grads, own, other, dz2, hown, hother, n, heads):
+    for ref in (send, keep):
+        ref[ref.shape[0] - EXTRA :, :] = jnp.zeros((EXTRA, ref.shape[1]), bf16)
+
+
+def mix_back(ids, tok, vec, front, mixed, own, other, dz2, hown, hother, n, heads):
     seqs = len(own)
     tokens, model = tok.shape
     slots = tokens // seqs
     width = heads * HD
     size = seqs * heads // n * HD
-    last = pl.BlockSpec((model // 2, width), lambda i: (0, grads[0].shape[1] // width - 1))
+    rows = model // 2 + EXTRA
+    last = pl.BlockSpec((rows, width), lambda i: (0, 3))
     return pl.pallas_call(
         functools.partial(mix_back_kernel, n, seqs, heads),
         grid=(1,),
         out_shape=[shape((size, slots), bf16)] * n
         + [shape((tokens, model), f32)]
-        + [shape(grads[0].shape, bf16)] * 2
+        + [shape((rows, 4 * width), bf16)] * 2
         + [shape((8, model), f32)],
         in_specs=[SMEM, VMEM, VMEM]
         + [pl.BlockSpec((model, width), lambda i: (0, front.shape[1] // width - 1)), VMEM]
-        + [pl.BlockSpec(memory_space=pl.ANY)] * 2
         + [VMEM] * (5 * seqs),
         out_specs=[VMEM] * (n + 1) + [last, last, VMEM],
-        input_output_aliases={5: n + 1, 6: n + 2},
         scratch_shapes=[
             pltpu.VMEM((size * n, slots), bf16),
             pltpu.VMEM((model, tokens), bf16),
@@ -606,10 +637,10 @@
         compiler_params=params("arbitrary"),
         cost_estimate=cost(4 * tokens * model * width, 10e6),
         name="mix_back",
-    )(ids, tok, vec, front, mixed, *grads, *own, *other, *dz2, *hown, *hother)
-
-
-def project_back_kernel(n, seqs, heads, ids, tok, whole, small, *refs):
+    )(ids, tok, vec, front, mixed, *own, *other, *dz2, *hown, *hother)
+
+
+def project_back_kernel(n, seqs, heads, ids, tok, whole, small, far, near, *refs):
     inputs = refs[:n]
     part, send, keep = refs[n : n + 3]
     stage, right, left, turned = refs[n + 3 :]
@@ -646,29 +677,27 @@
         ref[ref.shape[0] - EXTRA :, : 2 * width] = rows
 
 
-def project_back(ids, tok, whole, small, blocks, n, seqs, heads):
+def project_back(ids, tok, whole, small, grads, blocks, n, seqs, heads):
     tokens, model = tok.shape
     slots = tokens // seqs
     wide = whole.shape[1]
     return pl.pallas_call(
         functools.partial(project_back_kernel, n, seqs, heads),
-        out_shape=[
-            shape((tokens, model), bf16),
-            shape((model // 2 + EXTRA, wide), bf16),
-            shape((model // 2 + EXTRA, wide), bf16),
-        ],
-        in_specs=[SMEM] + [VMEM] * (3 + n),
-        out_specs=[VMEM] * 3,
+        grid=(1,),
+        out_shape=[shape((tokens, model), bf16)] + [shape(grads[0].shape, bf16)] * 2,
+        in_specs=[SMEM] + [VMEM] * 3 + [pl.BlockSpec(memory_space=pl.ANY)] * 2 + [VMEM] * n,
+        out_specs=[VMEM] + [pl.BlockSpec((grads[0].shape[0], wide), lambda i: (0, 0))] * 2,
+        input_output_aliases={4: 1, 5: 2},
         scratch_shapes=[
             pltpu.VMEM((seqs * heads * 3 * HD, slots), bf16),
             pltpu.VMEM((tokens, wide), bf16),
             pltpu.VMEM((model, tokens), bf16),
             pltpu.VMEM((model, tokens), bf16),
         ],
-        compiler_params=params(),
+        compiler_params=params("arbitrary"),
         cost_estimate=cost(4 * tokens * model * wide, 8e6),
         name="project_back",
-    )(ids, tok, whole, small, *blocks)
+    )(ids, tok, whole, small, *grads, *blocks)
 
 
 def fold_core_kernel(extra, keep, recv, mine, send):
@@ -777,20 +806,30 @@
     first += [swap(piece, "shard", 2) for piece in first]
     by_core = [swap(piece, "shard", 1) for piece in first]
     pieces = first[:n] + by_core[:n] + first[n:] + by_core[n:]
-    front = jnp.concatenate([w_gu[:, 0], w_out.T], axis=1).astype(bf16)
-    back = jnp.concatenate([w_gu[:, 1], w_down.T], axis=1).astype(bf16)
-    front, pieces[0] = lax.optimization_barrier((front, pieces[0]))
-    front = lax.all_gather(front, ("shard", "ctx"), axis=0, tiled=True)
+    front = jnp.concatenate([w_gu.reshape(rows, 2 * units), w_out.T], axis=1).astype(bf16)
+    back = w_down.T.astype(bf16)
+    (front,) = after([front], *pieces[1:n])
+    front = [front] + [swap(front, "ctx", d) for d in range(1, n)]
 
     bias = jnp.concatenate([b_qv[0], jnp.zeros_like(b_qv[0]), b_qv[1]])[None, :]
     *sends, whole = project(ids, tok, bias, pieces, n, seqs, heads)
     blocks = [sends[0]] + [swap(sends[d], "ctx", d) for d in range(1, n)]
-    *blocks, back = lax.optimization_barrier((*blocks, back))
-    back = lax.all_gather(back, ("shard", "ctx"), axis=0, tiled=True)
+    front = jnp.concatenate(after(front, whole), axis=0)
+    front_y = swap(front, "shard", 2)
+    (back,) = after([back], *blocks)
+    back = [back] + [swap(back, "ctx", d) for d in range(1, n)]
     *outs, att, den = attend(ids, lengths, slopes, blocks, n, heads, per)
+    front, front_y = after([front, front_y], outs[0])
+    front = [front, swap(front, "shard", 1), front_y, swap(front_y, "shard", 1)]
+    back = jnp.concatenate(after(back, outs[0]), axis=0)
+    back_y = swap(back, "shard", 2)
     outs = [outs[0]] + [swap(outs[d], "ctx", d) for d in range(1, n)]
+    front = assemble(ids, front, n)
     *part, mixed = mix(ids, front, outs, n, seqs, heads)
     part_other = [swap(value, "tp", 1) for value in part]
+    back, back_y = after([back, back_y], part[0])
+    back = [back, swap(back, "shard", 1), back_y, swap(back_y, "shard", 1)]
+    back = assemble(ids, back, n)
     hidden, low, act, gel, slope, ffn = zip(
         *(
             unit(s, tok, part[s], part_other[s], vectors, front, back)
@@ -808,35 +847,36 @@
         )
     )
     dlow_other = [swap(value, "tp", 1) for value in dlow]
-    unit_grads = weight_grads(ids, low, dffn, dgate, dup, act)
-    *dlow_other, far, near = lax.optimization_barrier((*dlow_other, *unit_grads))
-    *sends, dz1, far, near, sums_one = mix_back(
-        ids, tok, vectors, front, mixed, (far, near), part, part_other, dz2, dlow, dlow_other,
-        n, heads,
+    far, near = weight_grads(ids, low, dffn, dgate, dup, act)
+    *dlow_other, far = lax.optimization_barrier((*dlow_other, far))
+    got = swap(far, "shard", 1)
+    *sends, dz1, last_far, last_near, sums_one = mix_back(
+        ids, tok, vectors, front, mixed, part, part_other, dz2, dlow, dlow_other, n, heads
     )
     sums_two = sum(sums_two)
     grads = [sends[0]] + [swap(sends[d], "ctx", d) for d in range(1, n)]
-    got = swap(far, "shard", 1)
+    got, sends[0] = lax.optimization_barrier((got, sends[0]))
     mine, far = fold_core(near, got, 0)
     *grads, far = lax.optimization_barrier((*grads, far))
     got = swap(far, "shard", 2)
     outs = attend_back(ids, lengths, slopes, blocks, grads, att, den, n, heads, per)
     outs = [outs[0]] + [swap(outs[d], "ctx", d) for d in range(1, n)]
-    *outs, got = lax.optimization_barrier((*outs, got))
     rest_own, *rest_sends = fold_y(ids, mine, got, n, 0)
     *outs, rest_own = lax.optimization_barrier((*outs, rest_own))
     small = jnp.concatenate(
         [sums_one[0:2], sums_two[0:2], sums_one[2:3], sums_two[2:3], jnp.zeros_like(sums_one[:2])]
     )
-    dx, far, near = project_back(ids, tok, whole, small, outs, n, seqs, heads)
+    dx, far, near = project_back(
+        ids, tok, whole, small, (last_far, last_near), outs, n, seqs, heads
+    )
     got = swap(far, "shard", 1)
     dx_other = swap(dx, "tp", 1)
     mine, far = fold_core(near, got, EXTRA)
     got = swap(far, "shard", 2)
+    rest_got = [swap(block, "ctx", d + 1) for d, block in enumerate(rest_sends)]
+    *rest_got, got = lax.optimization_barrier((*rest_got, got))
     own, *sends = fold_y(ids, mine, got, n, EXTRA)
-    rest_got = [swap(block, "ctx", d + 1) for d, block in enumerate(rest_sends)]
     got = [swap(block, "ctx", d + 1) for d, block in enumerate(sends)]
-    *rest_got, got[0] = lax.optimization_barrier((*rest_got, got[0]))
     rest = fold_z(rest_own, rest_got)
     last = fold_z(own, got)
     input_grad = dz1 + (dx.astype(f32) + dx_other.astype(f32))
@@ -844,11 +884,11 @@
     return (
         jnp.stack(output),
         input_grad.reshape(tokens.shape),
-        last[:rows].reshape(w_qkv.shape),
+        last[:rows, : 3 * width].reshape(w_qkv.shape),
         small[6].reshape(2, width),
-        rest[:, 3 * units :].T,
+        last[:rows, 3 * width :].T,
         rest[:, : 2 * units].reshape(w_gu.shape),
-        rest[:, 2 * units : 3 * units].T,
+        rest[:, 2 * units :].T,
         small[:6],
     )
 

time: 348 us -> 324 us (0.931)
  waiting for transfers between devices: 146 us -> 101 us
  starting transfers between devices: 53.8 us -> 75.4 us
  between operations: 14.6 us -> 1.35 us
  Pallas kernels: 108 us -> 118 us
    ppermute x44 -> x56, waiting for transfers between devices: 131 us -> 101 us  [swap(): return lax.ppermute(value, axis, xor_pairs(axis, distance))]
    ppermute x44 -> x56, starting transfers between devices: 53.7 us -> 75.4 us  [swap(): return lax.ppermute(value, axis, xor_pairs(axis, distance))]
    all_gather x2 -> x0, waiting for transfers between devices: 14.9 us -> none  [the longest x1 14.9 us: on_device(): back = lax.all_gather(back, ('shard', 'ctx'), axis=0, tiled=True)]
    pallas_call x1 -> x3, Pallas kernels: 6.01 us -> 15.8 us  [the longest x2 9.79 us: assemble(): pl.pallas_call(functools.partial(assemble_kernel, n), grid=(3,), out_shap...]
    unnamed x105 -> x131, local copies, waits for them, and re-layouts: 11.2 us -> 14.7 us
  transfers between devices with their start and end apart: 46 -> 56, of which waited for: 21 -> 18; matrix products, arithmetic and copies ran while one was open for 2% -> 3% of each run, Pallas kernels for 26% -> 34%
where the time goes in v4:
time: 324 us
  Pallas kernels  118 us (36%)
  waiting for transfers between devices  101 us (31%)
  starting transfers between devices  75.4 us (23%)
  local copies, waits for them, and re-layouts  22.1 us (7%)
  other arithmetic  6.44 us (2%)
    ppermute x56, waiting for transfers between devices, swap(): return lax.ppermute(value, axis, xor_pairs(axis, distance))  101 us
    ppermute x56, starting transfers between devices, swap(): return lax.ppermute(value, axis, xor_pairs(axis, distance))  75.4 us
    pallas_call x2, Pallas kernels, unit_back(): pl.pallas_call(functools.partial(unit_back_kernel, n, s), grid=(steps,),...  17.9 us
    pallas_call x2, Pallas kernels, unit(): pl.pallas_call(unit_kernel, grid=(steps,), out_shape=[shape((tokens, mode...  15.4 us
    pallas_call x1, Pallas kernels, attend_back(): pl.pallas_call(functools.partial(attend_back_kernel, n, heads), grid=(per...  15 us
    unnamed x131, local copies, waits for them, and re-layouts  14.7 us
    pallas_call x1, Pallas kernels, weight_grads(): pl.pallas_call(functools.partial(weight_kernel, steps, seqs), grid=(3 * s...  11.4 us
    pallas_call x1, Pallas kernels, attend(): pl.pallas_call(functools.partial(attend_kernel, n, heads), grid=(per,), o...  11.4 us
  transfers between devices with their start and end apart: 56, of which 18 were waited for; matrix products, arithmetic and copies ran while one was open for 3% of the time, Pallas kernels for 34%

profile of v4, /device:TPU:0, one launch (start us, length us, event | category | flops | bytes accessed | tf_op | source)
XLA Modules:
  0.0 324.1 jit_solution(502735750250775362)
XLA Ops:
  1.6 3.1 collective-permute-start
  11.7 4.4 %collective-permute-done.1.refs_2_ = bf16[48,1152]{1,0:T(8,128)(2,1)S(1)} collective-permute-done((bf16[48,1152]{1,0:T(8,128)(2,1)S(1)}, bf16[48,1152]{1,0:T(8,128)(2,1)S(1)}, u32[]{:S(2)}, u32[]{:S(2)}) %collective-permute-start.1) | collective-permute-done | bytes 110624 | tf_op jit(solution)/shard_map/ppermute | solution.py:63
  29.3 4.8 %project.1 = (bf16[576,256]{1,0:T(8,128)(2,1)}, bf16[576,256]{1,0:T(8,128)(2,1)}, bf16[576,256]{1,0:T(8,128)(2,1)}, bf16[576,256]{1,0:T(8,128)(2,1)}, bf16[768,1152]{1,0:T(8,128)(2,1)}) custom-call(s32[4]{0:T(128)} %pad_add_fusion.ids, bf16[512,768]{1,0:T(8,128)(2,1)} %bitcast.26, f32[1,1152]{1,0:T(1,128)} %broadcast_in_dim.10.bias, ...), custom_call_target="tpu_custom_call" | custom-call | flops 905969664 | bytes 6000000 | tf_op jit(solution)/shard_map/project/pallas_call | solution.py:145
  34.1 11.7 %collective-permute-done.4 = bf16[48,3456]{1,0:T(8,128)(2,1)S(1)} collective-permute-done((bf16[48,3456]{1,0:T(8,128)(2,1)S(1)}, bf16[48,3456]{1,0:T(8,128)(2,1)S(1)}, u32[]{:S(2)}, u32[]{:S(2)}) %collective-permute-start.4) | collective-permute-done | bytes 331808 | tf_op jit(solution)/shard_map/ppermute | solution.py:63
  47.6 5.0 %collective-permute-start.19 = (bf16[576,256]{1,0:T(8,128)(2,1)S(1)}, bf16[576,256]{1,0:T(8,128)(2,1)S(1)}, u32[]{:S(2)}, u32[]{:S(2)}) collective-permute-start(bf16[576,256]{1,0:T(8,128)(2,1)S(1)} %copy-done.40), channel_id=1, source_target_pairs={{0,2},{2,0},{4,6},{6,4},{1,3},{3,1},{5,7},{7,5},{8,10},{10,8},{12,... | collective-permute-start | bytes 884744 | tf_op jit(solution)/shard_map/ppermute | solution.py:63
  55.1 6.0 %collective-permute-done.19.refs_1_ = bf16[576,256]{1,0:T(8,128)(2,1)S(1)} collective-permute-done((bf16[576,256]{1,0:T(8,128)(2,1)S(1)}, bf16[576,256]{1,0:T(8,128)(2,1)S(1)}, u32[]{:S(2)}, u32[]{:S(2)}) %collective-permute-start.19) | collective-permute-done | bytes 294944 | tf_op jit(solution)/shard_map/ppermute | solution.py:63
  61.2 13.9 %collective-permute-done.20.refs_2_ = bf16[576,256]{1,0:T(8,128)(2,1)S(1)} collective-permute-done((bf16[576,256]{1,0:T(8,128)(2,1)S(1)}, bf16[576,256]{1,0:T(8,128)(2,1)S(1)}, u32[]{:S(2)}, u32[]{:S(2)}) %collective-permute-start.20) | collective-permute-done | bytes 294944 | tf_op jit(solution)/shard_map/ppermute | solution.py:63
  75.1 3.8 %collective-permute-start.28 = (bf16[48,1536]{1,0:T(8,128)(2,1)S(1)}, bf16[48,1536]{1,0:T(8,128)(2,1)S(1)}, u32[]{:S(2)}, u32[]{:S(2)}) collective-permute-start(bf16[48,1536]{1,0:T(8,128)(2,1)S(1)} %convert_bitcast_fusion), channel_id=1, source_target_pairs={{0,2},{2,0},{4,6},{6,4},{1,3},{3,1},{5,7},{7,5},{8,10},{10,8},{12,... | collective-permute-start | bytes 442376 | tf_op jit(solution)/shard_map/ppermute | solution.py:63
  81.3 11.4 %attend.1 = (bf16[192,256]{1,0:T(8,128)(2,1)}, bf16[192,256]{1,0:T(8,128)(2,1)}, bf16[192,256]{1,0:T(8,128)(2,1)}, bf16[192,256]{1,0:T(8,128)(2,1)}, f32[192,1024]{1,0:T(8,128)}, /*index=5*/f32[3,1,1024]{2,1,0:T(1,128)}) custom-call(s32[4]{0:T(128)} %pad_add_fusion.ids, s32[2]{0:T(128)} %lens.7, f32[12]{0:T(128)} %constant.40.clone.slopes, ...), custom_call_target="tpu_custom_call" | custom-call | flops 1610612736 | bytes 3000000 | tf_op jit(solution)/shard_map/attend/pallas_call | solution.py:226
  94.7 3.7 %collective-permute-start.25 = (bf16[192,256]{1,0:T(8,128)(2,1)}, bf16[192,256]{1,0:T(8,128)(2,1)S(1)}, u32[]{:S(2)}, u32[]{:S(2)}) collective-permute-start(bf16[192,256]{1,0:T(8,128)(2,1)} %get-tuple-element.123), channel_id=1, source_target_pairs={{0,4},{2,6},{4,0},{6,2},{1,5},{3,7},{5,1},{7,3},{8,12},{10,14},{12... | collective-permute-start | bytes 294920 | tf_op jit(solution)/shard_map/ppermute | solution.py:63
  100.6 5.8 %assemble.2.wo.wg.wu = bf16[768,3456]{1,0:T(8,128)(2,1)} custom-call(s32[4]{0:T(128)} %pad_add_fusion.ids, bf16[192,3456]{1,0:T(8,128)(2,1)} %copy-done.1, bf16[192,3456]{1,0:T(8,128)(2,1)} %copy-done.7, bf16[192,3456]{1,0:T(8,128)(2,1)} %copy-done.6, bf16[192,3456]{1,0:T(8,128)(2,1)} %copy-done.8), custom_call_target="tpu_custom_call" | custom-call | bytes 10616832 | tf_op jit(solution)/shard_map/assemble/pallas_call | solution.py:101
  107.7 2.7 mix.1
  114.7 4.0 %assemble.3.wd = bf16[768,1536]{1,0:T(8,128)(2,1)} custom-call(s32[4]{0:T(128)} %pad_add_fusion.ids, bf16[192,1536]{1,0:T(8,128)(2,1)} %copy-done.10, bf16[192,1536]{1,0:T(8,128)(2,1)} %copy-done.15, bf16[192,1536]{1,0:T(8,128)(2,1)} %copy-done.14, bf16[192,1536]{1,0:T(8,128)(2,1)} %copy-done.16), custom_call_target="tpu_custom_call" | custom-call | bytes 4718592 | tf_op jit(solution)/shard_map/assemble/pallas_call | solution.py:101
  118.7 4.5 %collective-permute-done.27.other.refs_2_ = bf16[256,768]{1,0:T(8,128)(2,1)S(1)} collective-permute-done((bf16[256,768]{1,0:T(8,128)(2,1)}, bf16[256,768]{1,0:T(8,128)(2,1)S(1)}, u32[]{:S(2)}, u32[]{:S(2)}) %collective-permute-start.27) | collective-permute-done | bytes 393248 | tf_op jit(solution)/shard_map/ppermute | solution.py:63
  124.0 7.7 %unit.2 = (f32[256,768]{1,0:T(8,128)}, bf16[256,768]{1,0:T(8,128)(2,1)}, bf16[256,1536]{1,0:T(8,128)(2,1)}, bf16[256,1536]{1,0:T(8,128)(2,1)}, bf16[256,1536]{1,0:T(8,128)(2,1)}, /*index=5*/bf16[256,768]{1,0:T(8,128)(2,1)}) custom-call(bf16[512,768]{1,0:T(8,128)(2,1)} %bitcast.27, bf16[256,768]{1,0:T(8,128)(2,1)} %get-tuple-element.125.own.refs_0_, ...), custom_call_target="tpu_custom_call" | custom-call | flops 1811939328 | bytes 13000000 | tf_op jit(solution)/shard_map/unit/pallas_call | solution.py:411
  134.0 7.7 %unit.3 = (f32[256,768]{1,0:T(8,128)}, bf16[256,768]{1,0:T(8,128)(2,1)}, bf16[256,1536]{1,0:T(8,128)(2,1)}, bf16[256,1536]{1,0:T(8,128)(2,1)}, bf16[256,1536]{1,0:T(8,128)(2,1)}, /*index=5*/bf16[256,768]{1,0:T(8,128)(2,1)}) custom-call(bf16[512,768]{1,0:T(8,128)(2,1)} %bitcast.28, bf16[256,768]{1,0:T(8,128)(2,1)} %get-tuple-element.138.own.refs_1_, ...), custom_call_target="tpu_custom_call" | custom-call | flops 1811939328 | bytes 13000000 | tf_op jit(solution)/shard_map/unit/pallas_call | solution.py:411
  143.0 8.9 %unit_back.2 = (bf16[256,768]{1,0:T(8,128)(2,1)}, f32[256,768]{1,0:T(8,128)}, bf16[256,768]{1,0:T(8,128)(2,1)}, bf16[256,1536]{1,0:T(8,128)(2,1)}, bf16[256,1536...) custom-call(s32[4]{0:T(128)} %pad_add_fusion.ids, s32[2]{0:T(128)} %lens.7, ...), custom_call_target="tpu_custom_call" | custom-call | flops 1811939328 | bytes 14000000 | tf_op jit(solution)/shard_map/unit_back/pallas_call | solution.py:477
  154.3 9.0 %unit_back.3 = (bf16[256,768]{1,0:T(8,128)(2,1)}, f32[256,768]{1,0:T(8,128)}, bf16[256,768]{1,0:T(8,128)(2,1)}, bf16[256,1536]{1,0:T(8,128)(2,1)}, bf16[256,1536...) custom-call(s32[4]{0:T(128)} %pad_add_fusion.ids, s32[2]{0:T(128)} %lens.7, ...), custom_call_target="tpu_custom_call" | custom-call | flops 1811939328 | bytes 14000000 | tf_op jit(solution)/shard_map/unit_back/pallas_call | solution.py:477
  163.9 11.4 %weight_grads.1 = (bf16[384,4608]{1,0:T(8,128)(2,1)}, bf16[384,4608]{1,0:T(8,128)(2,1)}) custom-call(s32[4]{0:T(128)} %pad_add_fusion.ids, bf16[256,768]{1,0:T(8,128)(2,1)} %get-tuple-element.149.refs_0_, bf16[256,768]{1,0:T(8,128)(2,1)} %get-tuple-element.150.refs_1_, bf16[256,768]{1,0:T(8,128)(2,1)} %get-tuple-element.151.refs_2_, ...), custom_call_target="tpu_custom_call" | custom-call | flops 3623878656 | bytes 14000000 | tf_op jit(solution)/shard_map/weight_grads/pallas_call | solution.py:557
  176.2 6.7 %mix_back.1 = (bf16[192,256]{1,0:T(8,128)(2,1)}, bf16[192,256]{1,0:T(8,128)(2,1)}, bf16[192,256]{1,0:T(8,128)(2,1)}, bf16[192,256]{1,0:T(8,128)(2,1)}, f32[512,7...) custom-call(s32[4]{0:T(128)} %pad_add_fusion.ids, ...), custom_call_target="tpu_custom_call" | custom-call | flops 603979776 | bytes 10000000 | tf_op jit(solution)/shard_map/mix_back/pallas_call | solution.py:621
  189.3 6.3 %fold_core.2 = (f32[192,4608]{1,0:T(8,128)}, bf16[192,4608]{1,0:T(8,128)(2,1)}) custom-call(bf16[384,4608]{1,0:T(8,128)(2,1)} %get-tuple-element.172.keep, bf16[384,4608]{1,0:T(8,128)(2,1)} %copy-done), custom_call_target="tpu_custom_call" | custom-call | flops 1769472 | bytes 12386304 | tf_op jit(solution)/shard_map/fold_core/pallas_call | solution.py:717
  196.8 15.0 %attend_back.1 = (bf16[576,256]{1,0:T(8,128)(2,1)}, bf16[576,256]{1,0:T(8,128)(2,1)}, bf16[576,256]{1,0:T(8,128)(2,1)}, bf16[576,256]{1,0:T(8,128)(2,1)}) custom-call(s32[4]{0:T(128)} %pad_add_fusion.ids, s32[2]{0:T(128)} %lens.7, f32[12]{0:T(128)} %constant.40.clone.slopes, bf16[576,256]{1,0:T(8,128)(2,1)} %get-tuple-element.115.refs_0_, ...), custom_call_target="tpu_custom_call" | custom-call | flops 4026531840 | bytes 5000000 | tf_op jit(solution)/shard_map/attend_back/pallas_call | solution.py:308
  212.4 3.9 %collective-permute-start.45 = (bf16[576,256]{1,0:T(8,128)(2,1)}, bf16[576,256]{1,0:T(8,128)(2,1)S(1)}, u32[]{:S(2)}, u32[]{:S(2)}) collective-permute-start(bf16[576,256]{1,0:T(8,128)(2,1)} %get-tuple-element.185), channel_id=1, source_target_pairs={{0,6},{2,4},{4,2},{6,0},{1,7},{3,5},{5,3},{7,1},{8,14},{10,12},{12... | collective-permute-start | bytes 884744 | tf_op jit(solution)/shard_map/ppermute | solution.py:63
  218.5 16.8 %collective-permute-done.46.recv = bf16[192,4608]{1,0:T(8,128)(2,1)S(1)} collective-permute-done((bf16[192,4608]{1,0:T(8,128)(2,1)}, bf16[192,4608]{1,0:T(8,128)(2,1)S(1)}, u32[]{:S(2)}, u32[]{:S(2)}) %collective-permute-start.46) | collective-permute-done | bytes 1769504 | tf_op jit(solution)/shard_map/ppermute | solution.py:63
  236.5 4.7 %fold_y.2 = (f32[48,4608]{1,0:T(8,128)}, bf16[48,4608]{1,0:T(8,128)(2,1)}, bf16[48,4608]{1,0:T(8,128)(2,1)}, bf16[48,4608]{1,0:T(8,128)(2,1)}) custom-call(s32[4]{0:T(128)} %pad_add_fusion.ids, f32[192,4608]{1,0:T(8,128)} %get-tuple-element.186.mine, bf16[192,4608]{1,0:T(8,128)(2,1)} %copy-done.2), custom_call_target="tpu_custom_call" | custom-call | flops 884736 | bytes 7962624 | tf_op jit(solution)/shard_map/fold_y/pallas_call | solution.py:752
  242.1 6.0 %project_back.1 = (bf16[512,768]{1,0:T(8,128)(2,1)}, bf16[400,1536]{1,0:T(8,128)(2,1)}, bf16[400,1536]{1,0:T(8,128)(2,1)}) custom-call(s32[4]{0:T(128)} %pad_add_fusion.ids, bf16[512,768]{1,0:T(8,128)(2,1)} %bitcast.30, bf16[768,1152]{1,0:T(8,128)(2,1)} %get-tuple-element.110.whole, ...), custom_call_target="tpu_custom_call", output_to_operand_aliasing={{1}: (4, {}), {2}: (5, {})} | custom-call | flops 1811939328 | bytes 8000000 | tf_op jit(solution)/shard_map/project_back/pallas_call | solution.py:684
  252.4 3.3 %fold_core.3 = (f32[208,1536]{1,0:T(8,128)}, bf16[208,1536]{1,0:T(8,128)(2,1)}) custom-call(bf16[400,1536]{1,0:T(8,128)(2,1)} %get-tuple-element.194.keep, bf16[400,1536]{1,0:T(8,128)(2,1)} %copy-done.9), custom_call_target="tpu_custom_call" | custom-call | flops 614400 | bytes 4300800 | tf_op jit(solution)/shard_map/fold_core/pallas_call | solution.py:717
  263.0 5.4 %collective-permute-done.47 = bf16[512,768]{1,0:T(8,128)(2,1)S(1)} collective-permute-done((bf16[512,768]{1,0:T(8,128)(2,1)}, bf16[512,768]{1,0:T(8,128)(2,1)S(1)}, u32[]{:S(2)}, u32[]{:S(2)}) %collective-permute-start.47) | collective-permute-done | bytes 786464 | tf_op jit(solution)/shard_map/ppermute | solution.py:63
  269.8 8.7 %collective-permute-done.49 = bf16[48,4608]{1,0:T(8,128)(2,1)S(1)} collective-permute-done((bf16[48,4608]{1,0:T(8,128)(2,1)S(1)}, bf16[48,4608]{1,0:T(8,128)(2,1)S(1)}, u32[]{:S(2)}, u32[]{:S(2)}) %collective-permute-start.49) | collective-permute-done | bytes 442400 | tf_op jit(solution)/shard_map/ppermute | solution.py:63
  278.5 13.4 %collective-permute-done.50 = bf16[48,4608]{1,0:T(8,128)(2,1)S(1)} collective-permute-done((bf16[48,4608]{1,0:T(8,128)(2,1)S(1)}, bf16[48,4608]{1,0:T(8,128)(2,1)S(1)}, u32[]{:S(2)}, u32[]{:S(2)}) %collective-permute-start.50) | collective-permute-done | bytes 442400 | tf_op jit(solution)/shard_map/ppermute | solution.py:63
  295.3 8.9 %collective-permute-start.53 = (bf16[64,1536]{1,0:T(8,128)(2,1)}, bf16[64,1536]{1,0:T(8,128)(2,1)S(1)}, u32[]{:S(2)}, u32[]{:S(2)}) collective-permute-start(bf16[64,1536]{1,0:T(8,128)(2,1)} %get-tuple-element.203), channel_id=1, source_target_pairs={{0,2},{2,0},{4,6},{6,4},{1,3},{3,1},{5,7},{7,5},{8,10},{10,8},{12,... | collective-permute-start | bytes 589832 | tf_op jit(solution)/shard_map/ppermute | solution.py:63
  311.2 10.2 %collective-permute-done.54 = bf16[64,1536]{1,0:T(8,128)(2,1)S(1)} collective-permute-done((bf16[64,1536]{1,0:T(8,128)(2,1)}, bf16[64,1536]{1,0:T(8,128)(2,1)S(1)}, u32[]{:S(2)}, u32[]{:S(2)}) %collective-permute-start.54) | collective-permute-done | bytes 196640 | tf_op jit(solution)/shard_map/ppermute | solution.py:63
  (261 shorter events, 83.8 us)
Async XLA Ops:
  18.3 15.8 %collective-permute-start.3 = (bf16[48,3456]{1,0:T(8,128)(2,1)S(1)}, bf16[48,3456]{1,0:T(8,128)(2,1)S(1)}, u32[]{:S(2)}, u32[]{:S(2)}) collective-permute-start(bf16[48,3456]{1,0:T(8,128)(2,1)S(1)} %pad_maximum_fusion.1), channel_id=1, source_target_pairs={{0,2},{2,0},{4,6},{6,4},{1,3},{3,1},{5,7},{7,5},{8,10},{10,8},{12,... | collective-permute-start | bytes 995336 | tf_op jit(solution)/shard_map/ppermute | solution.py:63
  20.0 25.8 %collective-permute-start.4 = (bf16[48,3456]{1,0:T(8,128)(2,1)S(1)}, bf16[48,3456]{1,0:T(8,128)(2,1)S(1)}, u32[]{:S(2)}, u32[]{:S(2)}) collective-permute-start(bf16[48,3456]{1,0:T(8,128)(2,1)S(1)} %pad_maximum_fusion.1), channel_id=1, source_target_pairs={{0,4},{2,6},{4,0},{6,2},{1,5},{3,7},{5,1},{7,3},{8,12},{10,14},{12... | collective-permute-start | bytes 995336 | tf_op jit(solution)/shard_map/ppermute | solution.py:63
  22.1 23.7 %collective-permute-start.5 = (bf16[48,3456]{1,0:T(8,128)(2,1)S(1)}, bf16[48,3456]{1,0:T(8,128)(2,1)S(1)}, u32[]{:S(2)}, u32[]{:S(2)}) collective-permute-start(bf16[48,3456]{1,0:T(8,128)(2,1)S(1)} %pad_maximum_fusion.1), channel_id=1, source_target_pairs={{0,6},{2,4},{4,2},{6,0},{1,7},{3,5},{5,3},{7,1},{8,14},{10,12},{12... | collective-permute-start | bytes 995336 | tf_op jit(solution)/shard_map/ppermute | solution.py:63
  46.0 46.8 %collective-permute-start.18 = (bf16[192,3456]{1,0:T(8,128)(2,1)S(1)}, bf16[192,3456]{1,0:T(8,128)(2,1)S(1)}, u32[]{:S(2)}, u32[]{:S(2)}) collective-permute-start(bf16[192,3456]{1,0:T(8,128)(2,1)S(1)} %constant_dynamic-update-slice_fusion.refs_0_), channel_id=1, source_target_pairs={{0,16},{8,24},{16,0},{24,8},{1,17},{9,25},{17,1},{25,9},{2,18},{10... | collective-permute-start | bytes 3981320 | tf_op jit(solution)/shard_map/ppermute | solution.py:63
  47.6 13.6 %collective-permute-start.19 = (bf16[576,256]{1,0:T(8,128)(2,1)S(1)}, bf16[576,256]{1,0:T(8,128)(2,1)S(1)}, u32[]{:S(2)}, u32[]{:S(2)}) collective-permute-start(bf16[576,256]{1,0:T(8,128)(2,1)S(1)} %copy-done.40), channel_id=1, source_target_pairs={{0,2},{2,0},{4,6},{6,4},{1,3},{3,1},{5,7},{7,5},{8,10},{10,8},{12,... | collective-permute-start | bytes 884744 | tf_op jit(solution)/shard_map/ppermute | solution.py:63
  52.6 22.5 %collective-permute-start.20 = (bf16[576,256]{1,0:T(8,128)(2,1)S(1)}, bf16[576,256]{1,0:T(8,128)(2,1)S(1)}, u32[]{:S(2)}, u32[]{:S(2)}) collective-permute-start(bf16[576,256]{1,0:T(8,128)(2,1)S(1)} %copy-done.39), channel_id=1, source_target_pairs={{0,4},{2,6},{4,0},{6,2},{1,5},{3,7},{5,1},{7,3},{8,12},{10,14},{12... | collective-permute-start | bytes 884744 | tf_op jit(solution)/shard_map/ppermute | solution.py:63
  53.7 21.5 %collective-permute-start.21 = (bf16[576,256]{1,0:T(8,128)(2,1)S(1)}, bf16[576,256]{1,0:T(8,128)(2,1)S(1)}, u32[]{:S(2)}, u32[]{:S(2)}) collective-permute-start(bf16[576,256]{1,0:T(8,128)(2,1)S(1)} %copy-done.38), channel_id=1, source_target_pairs={{0,6},{2,4},{4,2},{6,0},{1,7},{3,5},{5,3},{7,1},{8,14},{10,12},{12... | collective-permute-start | bytes 884744 | tf_op jit(solution)/shard_map/ppermute | solution.py:63
  75.1 17.6 %collective-permute-start.28 = (bf16[48,1536]{1,0:T(8,128)(2,1)S(1)}, bf16[48,1536]{1,0:T(8,128)(2,1)S(1)}, u32[]{:S(2)}, u32[]{:S(2)}) collective-permute-start(bf16[48,1536]{1,0:T(8,128)(2,1)S(1)} %convert_bitcast_fusion), channel_id=1, source_target_pairs={{0,2},{2,0},{4,6},{6,4},{1,3},{3,1},{5,7},{7,5},{8,10},{10,8},{12,... | collective-permute-start | bytes 442376 | tf_op jit(solution)/shard_map/ppermute | solution.py:63
  79.0 13.8 %collective-permute-start.29 = (bf16[48,1536]{1,0:T(8,128)(2,1)S(1)}, bf16[48,1536]{1,0:T(8,128)(2,1)S(1)}, u32[]{:S(2)}, u32[]{:S(2)}) collective-permute-start(bf16[48,1536]{1,0:T(8,128)(2,1)S(1)} %convert_bitcast_fusion), channel_id=1, source_target_pairs={{0,4},{2,6},{4,0},{6,2},{1,5},{3,7},{5,1},{7,3},{8,12},{10,14},{12... | collective-permute-start | bytes 442376 | tf_op jit(solution)/shard_map/ppermute | solution.py:63
  79.8 12.9 %collective-permute-start.30 = (bf16[48,1536]{1,0:T(8,128)(2,1)S(1)}, bf16[48,1536]{1,0:T(8,128)(2,1)S(1)}, u32[]{:S(2)}, u32[]{:S(2)}) collective-permute-start(bf16[48,1536]{1,0:T(8,128)(2,1)S(1)} %convert_bitcast_fusion), channel_id=1, source_target_pairs={{0,6},{2,4},{4,2},{6,0},{1,7},{3,5},{5,3},{7,1},{8,14},{10,12},{12... | collective-permute-start | bytes 442376 | tf_op jit(solution)/shard_map/ppermute | solution.py:63
  93.5 17.0 %collective-permute-start.31 = (bf16[192,1536]{1,0:T(8,128)(2,1)S(1)}, bf16[192,1536]{1,0:T(8,128)(2,1)S(1)}, u32[]{:S(2)}, u32[]{:S(2)}) collective-permute-start(bf16[192,1536]{1,0:T(8,128)(2,1)S(1)} %constant_dynamic-update-slice_fusion.4.refs_0_), channel_id=1, source_target_pairs={{0,16},{8,24},{16,0},{24,8},{1,17},{9,25},{17,1},{25,9},{2,18},{10... | collective-permute-start | bytes 1769480 | tf_op jit(solution)/shard_map/ppermute | solution.py:63
  93.8 12.6 %collective-permute-start.24 = (bf16[192,256]{1,0:T(8,128)(2,1)}, bf16[192,256]{1,0:T(8,128)(2,1)S(1)}, u32[]{:S(2)}, u32[]{:S(2)}) collective-permute-start(bf16[192,256]{1,0:T(8,128)(2,1)} %get-tuple-element.122), channel_id=1, source_target_pairs={{0,2},{2,0},{4,6},{6,4},{1,3},{3,1},{5,7},{7,5},{8,10},{10,8},{12,... | collective-permute-start | bytes 294920 | tf_op jit(solution)/shard_map/ppermute | solution.py:63
  94.7 11.7 %collective-permute-start.25 = (bf16[192,256]{1,0:T(8,128)(2,1)}, bf16[192,256]{1,0:T(8,128)(2,1)S(1)}, u32[]{:S(2)}, u32[]{:S(2)}) collective-permute-start(bf16[192,256]{1,0:T(8,128)(2,1)} %get-tuple-element.123), channel_id=1, source_target_pairs={{0,4},{2,6},{4,0},{6,2},{1,5},{3,7},{5,1},{7,3},{8,12},{10,14},{12... | collective-permute-start | bytes 294920 | tf_op jit(solution)/shard_map/ppermute | solution.py:63
  111.0 12.2 %collective-permute-start.27 = (bf16[256,768]{1,0:T(8,128)(2,1)}, bf16[256,768]{1,0:T(8,128)(2,1)S(1)}, u32[]{:S(2)}, u32[]{:S(2)}) collective-permute-start(bf16[256,768]{1,0:T(8,128)(2,1)} %get-tuple-element.125.own.refs_0_), channel_id=1, source_target_pairs={{0,1},{1,0},{2,3},{3,2},{4,5},{5,4},{6,7},{7,6},{8,9},{9,8},{10,11... | collective-permute-start | bytes 1179656 | tf_op jit(solution)/shard_map/ppermute | solution.py:63
  112.5 20.7 %collective-permute-start.35 = (bf16[256,768]{1,0:T(8,128)(2,1)}, bf16[256,768]{1,0:T(8,128)(2,1)S(1)}, u32[]{:S(2)}, u32[]{:S(2)}) collective-permute-start(bf16[256,768]{1,0:T(8,128)(2,1)} %get-tuple-element.138.own.refs_1_), channel_id=1, source_target_pairs={{0,1},{1,0},{2,3},{3,2},{4,5},{5,4},{6,7},{7,6},{8,9},{9,8},{10,11... | collective-permute-start | bytes 1179656 | tf_op jit(solution)/shard_map/ppermute | solution.py:63
  141.6 11.9 %collective-permute-start.36 = (bf16[256,768]{1,0:T(8,128)(2,1)}, bf16[256,768]{1,0:T(8,128)(2,1)S(1)}, u32[]{:S(2)}, u32[]{:S(2)}) collective-permute-start(bf16[256,768]{1,0:T(8,128)(2,1)} %get-tuple-element.140.own), channel_id=1, source_target_pairs={{0,1},{1,0},{2,3},{3,2},{4,5},{5,4},{6,7},{7,6},{8,9},{9,8},{10,11... | collective-permute-start | bytes 1179656 | tf_op jit(solution)/shard_map/ppermute | solution.py:63
  152.0 23.3 %collective-permute-start.37 = (bf16[256,768]{1,0:T(8,128)(2,1)}, bf16[256,768]{1,0:T(8,128)(2,1)S(1)}, u32[]{:S(2)}, u32[]{:S(2)}) collective-permute-start(bf16[256,768]{1,0:T(8,128)(2,1)} %get-tuple-element.147.refs_6_), channel_id=1, source_target_pairs={{0,1},{1,0},{2,3},{3,2},{4,5},{5,4},{6,7},{7,6},{8,9},{9,8},{10,11... | collective-permute-start | bytes 1179656 | tf_op jit(solution)/shard_map/ppermute | solution.py:63
  163.3 12.0 %collective-permute-start.38 = (bf16[256,768]{1,0:T(8,128)(2,1)}, bf16[256,768]{1,0:T(8,128)(2,1)S(1)}, u32[]{:S(2)}, u32[]{:S(2)}) collective-permute-start(bf16[256,768]{1,0:T(8,128)(2,1)} %get-tuple-element.148.refs_7_), channel_id=1, source_target_pairs={{0,1},{1,0},{2,3},{3,2},{4,5},{5,4},{6,7},{7,6},{8,9},{9,8},{10,11... | collective-permute-start | bytes 1179656 | tf_op jit(solution)/shard_map/ppermute | solution.py:63
  175.3 12.1 %collective-permute-start.42 = (bf16[384,4608]{1,0:T(8,128)(2,1)}, bf16[384,4608]{1,0:T(8,128)(2,1)S(1)}, u32[]{:S(2)}, u32[]{:S(2)}) collective-permute-start(bf16[384,4608]{1,0:T(8,128)(2,1)} %get-tuple-element.173), channel_id=1, source_target_pairs={{0,8},{8,0},{16,24},{24,16},{1,9},{9,1},{17,25},{25,17},{2,10},{10... | collective-permute-start | bytes 10616840 | tf_op jit(solution)/shard_map/ppermute | solution.py:63
  182.9 12.6 %collective-permute-start.39 = (bf16[192,256]{1,0:T(8,128)(2,1)}, bf16[192,256]{1,0:T(8,128)(2,1)S(1)}, u32[]{:S(2)}, u32[]{:S(2)}) collective-permute-start(bf16[192,256]{1,0:T(8,128)(2,1)} %get-tuple-element.169), channel_id=1, source_target_pairs={{0,2},{2,0},{4,6},{6,4},{1,3},{3,1},{5,7},{7,5},{8,10},{10,8},{12,... | collective-permute-start | bytes 294920 | tf_op jit(solution)/shard_map/ppermute | solution.py:63
  195.6 39.7 %collective-permute-start.46 = (bf16[192,4608]{1,0:T(8,128)(2,1)}, bf16[192,4608]{1,0:T(8,128)(2,1)S(1)}, u32[]{:S(2)}, u32[]{:S(2)}) collective-permute-start(bf16[192,4608]{1,0:T(8,128)(2,1)} %get-tuple-element.187), channel_id=1, source_target_pairs={{0,16},{8,24},{16,0},{24,8},{1,17},{9,25},{17,1},{25,9},{2,18},{10... | collective-permute-start | bytes 5308424 | tf_op jit(solution)/shard_map/ppermute | solution.py:63
  211.9 29.3 %collective-permute-start.43 = (bf16[576,256]{1,0:T(8,128)(2,1)}, bf16[576,256]{1,0:T(8,128)(2,1)S(1)}, u32[]{:S(2)}, u32[]{:S(2)}) collective-permute-start(bf16[576,256]{1,0:T(8,128)(2,1)} %get-tuple-element.183), channel_id=1, source_target_pairs={{0,2},{2,0},{4,6},{6,4},{1,3},{3,1},{5,7},{7,5},{8,10},{10,8},{12,... | collective-permute-start | bytes 884744 | tf_op jit(solution)/shard_map/ppermute | solution.py:63
  212.4 28.8 %collective-permute-start.44 = (bf16[576,256]{1,0:T(8,128)(2,1)}, bf16[576,256]{1,0:T(8,128)(2,1)S(1)}, u32[]{:S(2)}, u32[]{:S(2)}) collective-permute-start(bf16[576,256]{1,0:T(8,128)(2,1)} %get-tuple-element.184), channel_id=1, source_target_pairs={{0,4},{2,6},{4,0},{6,2},{1,5},{3,7},{5,1},{7,3},{8,12},{10,14},{12... | collective-permute-start | bytes 884744 | tf_op jit(solution)/shard_map/ppermute | solution.py:63
  212.4 28.8 %collective-permute-start.45 = (bf16[576,256]{1,0:T(8,128)(2,1)}, bf16[576,256]{1,0:T(8,128)(2,1)S(1)}, u32[]{:S(2)}, u32[]{:S(2)}) collective-permute-start(bf16[576,256]{1,0:T(8,128)(2,1)} %get-tuple-element.185), channel_id=1, source_target_pairs={{0,6},{2,4},{4,2},{6,0},{1,7},{3,5},{5,3},{7,1},{8,14},{10,12},{12... | collective-permute-start | bytes 884744 | tf_op jit(solution)/shard_map/ppermute | solution.py:63
  248.2 20.2 %collective-permute-start.47 = (bf16[512,768]{1,0:T(8,128)(2,1)}, bf16[512,768]{1,0:T(8,128)(2,1)S(1)}, u32[]{:S(2)}, u32[]{:S(2)}) collective-permute-start(bf16[512,768]{1,0:T(8,128)(2,1)} %get-tuple-element.193), channel_id=1, source_target_pairs={{0,1},{1,0},{2,3},{3,2},{4,5},{5,4},{6,7},{7,6},{8,9},{9,8},{10,11... | collective-permute-start | bytes 2359304 | tf_op jit(solution)/shard_map/ppermute | solution.py:63
  255.6 36.2 %collective-permute-start.52 = (bf16[208,1536]{1,0:T(8,128)(2,1)}, bf16[208,1536]{1,0:T(8,128)(2,1)S(1)}, u32[]{:S(2)}, u32[]{:S(2)}) collective-permute-start(bf16[208,1536]{1,0:T(8,128)(2,1)} %get-tuple-element.200), channel_id=1, source_target_pairs={{0,16},{8,24},{16,0},{24,8},{1,17},{9,25},{17,1},{25,9},{2,18},{10... | collective-permute-start | bytes 1916936 | tf_op jit(solution)/shard_map/ppermute | solution.py:63
  256.7 21.7 %collective-permute-start.49 = (bf16[48,4608]{1,0:T(8,128)(2,1)S(1)}, bf16[48,4608]{1,0:T(8,128)(2,1)S(1)}, u32[]{:S(2)}, u32[]{:S(2)}) collective-permute-start(bf16[48,4608]{1,0:T(8,128)(2,1)S(1)} %copy-done.34), channel_id=1, source_target_pairs={{0,2},{2,0},{4,6},{6,4},{1,3},{3,1},{5,7},{7,5},{8,10},{10,8},{12,... | collective-permute-start | bytes 1327112 | tf_op jit(solution)/shard_map/ppermute | solution.py:63
  258.9 32.9 %collective-permute-start.50 = (bf16[48,4608]{1,0:T(8,128)(2,1)S(1)}, bf16[48,4608]{1,0:T(8,128)(2,1)S(1)}, u32[]{:S(2)}, u32[]{:S(2)}) collective-permute-start(bf16[48,4608]{1,0:T(8,128)(2,1)S(1)} %copy-done.33), channel_id=1, source_target_pairs={{0,4},{2,6},{4,0},{6,2},{1,5},{3,7},{5,1},{7,3},{8,12},{10,14},{12... | collective-permute-start | bytes 1327112 | tf_op jit(solution)/shard_map/ppermute | solution.py:63
  260.6 31.3 %collective-permute-start.51 = (bf16[48,4608]{1,0:T(8,128)(2,1)S(1)}, bf16[48,4608]{1,0:T(8,128)(2,1)S(1)}, u32[]{:S(2)}, u32[]{:S(2)}) collective-permute-start(bf16[48,4608]{1,0:T(8,128)(2,1)S(1)} %copy-done.32), channel_id=1, source_target_pairs={{0,6},{2,4},{4,2},{6,0},{1,7},{3,5},{5,3},{7,1},{8,14},{10,12},{12... | collective-permute-start | bytes 1327112 | tf_op jit(solution)/shard_map/ppermute | solution.py:63
  295.3 16.0 %collective-permute-start.53 = (bf16[64,1536]{1,0:T(8,128)(2,1)}, bf16[64,1536]{1,0:T(8,128)(2,1)S(1)}, u32[]{:S(2)}, u32[]{:S(2)}) collective-permute-start(bf16[64,1536]{1,0:T(8,128)(2,1)} %get-tuple-element.203), channel_id=1, source_target_pairs={{0,2},{2,0},{4,6},{6,4},{1,3},{3,1},{5,7},{7,5},{8,10},{10,8},{12,... | collective-permute-start | bytes 589832 | tf_op jit(solution)/shard_map/ppermute | solution.py:63
  304.2 17.2 %collective-permute-start.54 = (bf16[64,1536]{1,0:T(8,128)(2,1)}, bf16[64,1536]{1,0:T(8,128)(2,1)S(1)}, u32[]{:S(2)}, u32[]{:S(2)}) collective-permute-start(bf16[64,1536]{1,0:T(8,128)(2,1)} %get-tuple-element.204), channel_id=1, source_target_pairs={{0,4},{2,6},{4,0},{6,2},{1,5},{3,7},{5,1},{7,3},{8,12},{10,14},{12... | collective-permute-start | bytes 589832 | tf_op jit(solution)/shard_map/ppermute | solution.py:63
  305.7 15.7 %collective-permute-start.55 = (bf16[64,1536]{1,0:T(8,128)(2,1)}, bf16[64,1536]{1,0:T(8,128)(2,1)S(1)}, u32[]{:S(2)}, u32[]{:S(2)}) collective-permute-start(bf16[64,1536]{1,0:T(8,128)(2,1)} %get-tuple-element.205), channel_id=1, source_target_pairs={{0,6},{2,4},{4,2},{6,0},{1,7},{3,5},{5,3},{7,1},{8,14},{10,12},{12... | collective-permute-start | bytes 589832 | tf_op jit(solution)/shard_map/ppermute | solution.py:63
  (86 other events, 633.5 us)

commit v5 on v4

--- a/solution.py
+++ b/solution.py
@@ -700,11 +700,13 @@
     )(ids, tok, whole, small, *grads, *blocks)
 
 
-def fold_core_kernel(extra, keep, recv, mine, send):
+def fold_core_kernel(extra, keep, recv, mine, *sends):
     half = (keep.shape[0] - extra) // 2
     mine[0:half, :] = keep[0:half, :].astype(f32) + recv[0:half, :].astype(f32)
     rest = (keep[half:, :].astype(f32) + recv[half:, :].astype(f32)).astype(bf16)
-    send[...] = rest
+    size = sends[0].shape[1]
+    for k, send in enumerate(sends):
+        send[...] = rest[:, k * size : (k + 1) * size]
     if extra:
         mine[half:, :] = rest[half:, :].astype(f32)
 
@@ -713,25 +715,28 @@
     rows, wide = keep.shape
     out = (rows - extra) // 2 + extra
     steps = 1 if extra else 3
+    parts = 2 if extra else 1
     column = lambda size: pl.BlockSpec((size, wide // steps), lambda j: (0, j))
     return pl.pallas_call(
         functools.partial(fold_core_kernel, extra),
         grid=(steps,),
-        out_shape=[shape((out, wide), f32), shape((out, wide), bf16)],
+        out_shape=[shape((out, wide), f32)] + [shape((out, wide // parts), bf16)] * parts,
         in_specs=[column(rows)] * 2,
-        out_specs=[column(out)] * 2,
+        out_specs=[column(out)]
+        + [pl.BlockSpec((out, wide // steps // parts), lambda j: (0, j))] * parts,
         compiler_params=params("arbitrary"),
         cost_estimate=cost(rows * wide, 7 * rows * wide),
         name="fold_core",
     )(keep, recv)
 
 
-def fold_y_kernel(n, extra, ids, mine, recv, own, *refs):
-    sends, stage = refs[:-1], refs[-1]
+def fold_y_kernel(n, extra, parts, ids, mine, *refs):
+    recvs, own, sends, stage = refs[:parts], refs[parts], refs[parts + 1 : -1], refs[-1]
     z = ids[2]
     rows = mine.shape[0] - extra
     size = rows // n
-    stage[...] = mine[...] + recv[...].astype(f32)
+    recv = jnp.concatenate([ref[...] for ref in recvs], axis=1)
+    stage[...] = mine[...] + recv.astype(f32)
     for d in range(n):
         block = stage[pl.ds(pl.multiple_of((z ^ d) * size, size), size), :]
         if d:
@@ -744,22 +749,24 @@
                 own[size:, :] = stage[rows:, :].astype(bf16).astype(f32)
 
 
-def fold_y(ids, mine, recv, n, extra):
+def fold_y(ids, mine, recvs, n, extra):
     rows, wide = mine.shape
     out = (rows - extra) // n + extra
     steps = 1 if extra else 3
+    parts = len(recvs)
     column = lambda size: pl.BlockSpec((size, wide // steps), lambda j: (0, j))
     return pl.pallas_call(
-        functools.partial(fold_y_kernel, n, extra),
+        functools.partial(fold_y_kernel, n, extra, parts),
         grid=(steps,),
         out_shape=[shape((out, wide), f32)] + [shape((out, wide), bf16)] * (n - 1),
-        in_specs=[SMEM] + [column(rows)] * 2,
+        in_specs=[SMEM, column(rows)]
+        + [pl.BlockSpec((rows, wide // steps // parts), lambda j: (0, j))] * parts,
         out_specs=[column(out)] * n,
         scratch_shapes=[pltpu.VMEM((rows, wide // steps), f32)],
         compiler_params=params("arbitrary"),
         cost_estimate=cost(rows * wide, 9 * rows * wide),
         name="fold_y",
-    )(ids, mine, recv)
+    )(ids, mine, *recvs)
 
 
 def fold_z(own, got):
@@ -861,7 +868,7 @@
     got = swap(far, "shard", 2)
     outs = attend_back(ids, lengths, slopes, blocks, grads, att, den, n, heads, per)
     outs = [outs[0]] + [swap(outs[d], "ctx", d) for d in range(1, n)]
-    rest_own, *rest_sends = fold_y(ids, mine, got, n, 0)
+    rest_own, *rest_sends = fold_y(ids, mine, [got], n, 0)
     *outs, rest_own = lax.optimization_barrier((*outs, rest_own))
     small = jnp.concatenate(
         [sums_one[0:2], sums_two[0:2], sums_one[2:3], sums_two[2:3], jnp.zeros_like(sums_one[:2])]
@@ -870,11 +877,11 @@
         ids, tok, whole, small, (last_far, last_near), outs, n, seqs, heads
     )
     got = swap(far, "shard", 1)
+    mine, *far = fold_core(near, got, EXTRA)
+    got = [swap(half, "shard", 2) for half in far]
     dx_other = swap(dx, "tp", 1)
-    mine, far = fold_core(near, got, EXTRA)
-    got = swap(far, "shard", 2)
     rest_got = [swap(block, "ctx", d + 1) for d, block in enumerate(rest_sends)]
-    *rest_got, got = lax.optimization_barrier((*rest_got, got))
+    rest_got[0], got[0] = lax.optimization_barrier((rest_got[0], got[0]))
     own, *sends = fold_y(ids, mine, got, n, EXTRA)
     got = [swap(block, "ctx", d + 1) for d, block in enumerate(sends)]
     rest = fold_z(rest_own, rest_got)

time: 324 us -> 311 us (0.960)
  starting transfers between devices: 75.4 us -> 67.1 us
  waiting for transfers between devices: 101 us -> 94.1 us
    ppermute x56 -> x57, starting transfers between devices: 75.4 us -> 67.1 us  [swap(): return lax.ppermute(value, axis, xor_pairs(axis, distance))]
    ppermute x56 -> x57, waiting for transfers between devices: 101 us -> 94.1 us  [swap(): return lax.ppermute(value, axis, xor_pairs(axis, distance))]
    unnamed x131 -> x133, local copies, waits for them, and re-layouts: 14.7 us -> 14.1 us
  transfers between devices with their start and end apart: 56 -> 57, of which waited for: 18 -> 16; matrix products, arithmetic and copies ran while one was open for 3% -> 3% of each run, Pallas kernels for 34% -> 36%
where the time goes in v5:
time: 311 us; the launch traced here: 309 us
  Pallas kernels  118 us (38%)
  waiting for transfers between devices  94.1 us (30%)
  starting transfers between devices  67.1 us (22%)
  local copies, waits for them, and re-layouts  21.6 us (7%)
  other arithmetic  6.38 us (2%)
    ppermute x57, waiting for transfers between devices, swap(): return lax.ppermute(value, axis, xor_pairs(axis, distance))  94.1 us
    ppermute x57, starting transfers between devices, swap(): return lax.ppermute(value, axis, xor_pairs(axis, distance))  67.1 us
    pallas_call x2, Pallas kernels, unit_back(): pl.pallas_call(functools.partial(unit_back_kernel, n, s), grid=(steps,),...  18 us
    pallas_call x2, Pallas kernels, unit(): pl.pallas_call(unit_kernel, grid=(steps,), out_shape=[shape((tokens, mode...  15.3 us
    pallas_call x1, Pallas kernels, attend_back(): pl.pallas_call(functools.partial(attend_back_kernel, n, heads), grid=(per...  15.1 us
    unnamed x133, local copies, waits for them, and re-layouts  14.1 us
    pallas_call x1, Pallas kernels, weight_grads(): pl.pallas_call(functools.partial(weight_kernel, steps, seqs), grid=(3 * s...  11.4 us
    pallas_call x1, Pallas kernels, attend(): pl.pallas_call(functools.partial(attend_kernel, n, heads), grid=(per,), o...  11.4 us
  transfers between devices with their start and end apart: 57, of which 16 were waited for; matrix products, arithmetic and copies ran while one was open for 3% of the time, Pallas kernels for 36%

profile of v5, /device:TPU:0, one launch (start us, length us, event | category | flops | bytes accessed | tf_op | source)
XLA Modules:
  0.0 308.5 jit_solution(3627802787563910959)
XLA Ops:
  1.6 3.1 %collective-permute-start = (bf16[48,1152]{1,0:T(8,128)(2,1)S(1)}, bf16[48,1152]{1,0:T(8,128)(2,1)S(1)}, u32[]{:S(2)}, u32[]{:S(2)}) collective-permute-start(bf16[48,1152]{1,0:T(8,128)(2,1)S(1)} %bitcast.40), channel_id=1, source_target_pairs={{0,2},{2,0},{4,6},{6,4},{1,3},{3,1},{5,7},{7,5},{8,10},{10,8},{12,... | collective-permute-start | bytes 331784 | tf_op jit(solution)/shard_map/ppermute | solution.py:63
  4.8 2.6 collective-permute-start.1
  11.7 4.4 %collective-permute-done.1.refs_2_ = bf16[48,1152]{1,0:T(8,128)(2,1)S(1)} collective-permute-done((bf16[48,1152]{1,0:T(8,128)(2,1)S(1)}, bf16[48,1152]{1,0:T(8,128)(2,1)S(1)}, u32[]{:S(2)}, u32[]{:S(2)}) %collective-permute-start.1) | collective-permute-done | bytes 110624 | tf_op jit(solution)/shard_map/ppermute | solution.py:63
  22.1 2.5 collective-permute-start.5
  29.3 4.8 %project.1 = (bf16[576,256]{1,0:T(8,128)(2,1)}, bf16[576,256]{1,0:T(8,128)(2,1)}, bf16[576,256]{1,0:T(8,128)(2,1)}, bf16[576,256]{1,0:T(8,128)(2,1)}, bf16[768,1152]{1,0:T(8,128)(2,1)}) custom-call(s32[4]{0:T(128)} %pad_add_fusion.ids, bf16[512,768]{1,0:T(8,128)(2,1)} %bitcast.26, f32[1,1152]{1,0:T(1,128)} %broadcast_in_dim.10.bias, ...), custom_call_target="tpu_custom_call" | custom-call | flops 905969664 | bytes 6000000 | tf_op jit(solution)/shard_map/project/pallas_call | solution.py:145
  34.1 11.7 %collective-permute-done.4 = bf16[48,3456]{1,0:T(8,128)(2,1)S(1)} collective-permute-done((bf16[48,3456]{1,0:T(8,128)(2,1)S(1)}, bf16[48,3456]{1,0:T(8,128)(2,1)S(1)}, u32[]{:S(2)}, u32[]{:S(2)}) %collective-permute-start.4) | collective-permute-done | bytes 331808 | tf_op jit(solution)/shard_map/ppermute | solution.py:63
  47.6 5.0 %collective-permute-start.19 = (bf16[576,256]{1,0:T(8,128)(2,1)S(1)}, bf16[576,256]{1,0:T(8,128)(2,1)S(1)}, u32[]{:S(2)}, u32[]{:S(2)}) collective-permute-start(bf16[576,256]{1,0:T(8,128)(2,1)S(1)} %copy-done.41), channel_id=1, source_target_pairs={{0,2},{2,0},{4,6},{6,4},{1,3},{3,1},{5,7},{7,5},{8,10},{10,8},{12,... | collective-permute-start | bytes 884744 | tf_op jit(solution)/shard_map/ppermute | solution.py:63
  55.1 6.0 %collective-permute-done.19.refs_1_ = bf16[576,256]{1,0:T(8,128)(2,1)S(1)} collective-permute-done((bf16[576,256]{1,0:T(8,128)(2,1)S(1)}, bf16[576,256]{1,0:T(8,128)(2,1)S(1)}, u32[]{:S(2)}, u32[]{:S(2)}) %collective-permute-start.19) | collective-permute-done | bytes 294944 | tf_op jit(solution)/shard_map/ppermute | solution.py:63
  61.2 13.9 %collective-permute-done.20.refs_2_ = bf16[576,256]{1,0:T(8,128)(2,1)S(1)} collective-permute-done((bf16[576,256]{1,0:T(8,128)(2,1)S(1)}, bf16[576,256]{1,0:T(8,128)(2,1)S(1)}, u32[]{:S(2)}, u32[]{:S(2)}) %collective-permute-start.20) | collective-permute-done | bytes 294944 | tf_op jit(solution)/shard_map/ppermute | solution.py:63
  75.1 3.8 %collective-permute-start.28 = (bf16[48,1536]{1,0:T(8,128)(2,1)S(1)}, bf16[48,1536]{1,0:T(8,128)(2,1)S(1)}, u32[]{:S(2)}, u32[]{:S(2)}) collective-permute-start(bf16[48,1536]{1,0:T(8,128)(2,1)S(1)} %convert_bitcast_fusion), channel_id=1, source_target_pairs={{0,2},{2,0},{4,6},{6,4},{1,3},{3,1},{5,7},{7,5},{8,10},{10,8},{12,... | collective-permute-start | bytes 442376 | tf_op jit(solution)/shard_map/ppermute | solution.py:63
  81.3 11.4 %attend.1 = (bf16[192,256]{1,0:T(8,128)(2,1)}, bf16[192,256]{1,0:T(8,128)(2,1)}, bf16[192,256]{1,0:T(8,128)(2,1)}, bf16[192,256]{1,0:T(8,128)(2,1)}, f32[192,1024]{1,0:T(8,128)}, /*index=5*/f32[3,1,1024]{2,1,0:T(1,128)}) custom-call(s32[4]{0:T(128)} %pad_add_fusion.ids, s32[2]{0:T(128)} %lens.7, f32[12]{0:T(128)} %constant.40.clone.slopes, ...), custom_call_target="tpu_custom_call" | custom-call | flops 1610612736 | bytes 3000000 | tf_op jit(solution)/shard_map/attend/pallas_call | solution.py:226
  100.0 5.8 %assemble.2.wo.wg.wu = bf16[768,3456]{1,0:T(8,128)(2,1)} custom-call(s32[4]{0:T(128)} %pad_add_fusion.ids, bf16[192,3456]{1,0:T(8,128)(2,1)} %copy-done.1, bf16[192,3456]{1,0:T(8,128)(2,1)} %copy-done.7, bf16[192,3456]{1,0:T(8,128)(2,1)} %copy-done.6, bf16[192,3456]{1,0:T(8,128)(2,1)} %copy-done.8), custom_call_target="tpu_custom_call" | custom-call | bytes 10616832 | tf_op jit(solution)/shard_map/assemble/pallas_call | solution.py:101
  107.5 2.7 mix.1
  114.5 4.1 %assemble.3.wd = bf16[768,1536]{1,0:T(8,128)(2,1)} custom-call(s32[4]{0:T(128)} %pad_add_fusion.ids, bf16[192,1536]{1,0:T(8,128)(2,1)} %copy-done.10, bf16[192,1536]{1,0:T(8,128)(2,1)} %copy-done.14, bf16[192,1536]{1,0:T(8,128)(2,1)} %copy-done.13, bf16[192,1536]{1,0:T(8,128)(2,1)} %copy-done.15), custom_call_target="tpu_custom_call" | custom-call | bytes 4718592 | tf_op jit(solution)/shard_map/assemble/pallas_call | solution.py:101
  118.6 4.4 %collective-permute-done.27.other.refs_2_ = bf16[256,768]{1,0:T(8,128)(2,1)S(1)} collective-permute-done((bf16[256,768]{1,0:T(8,128)(2,1)}, bf16[256,768]{1,0:T(8,128)(2,1)S(1)}, u32[]{:S(2)}, u32[]{:S(2)}) %collective-permute-start.27) | collective-permute-done | bytes 393248 | tf_op jit(solution)/shard_map/ppermute | solution.py:63
  123.8 7.7 %unit.2 = (f32[256,768]{1,0:T(8,128)}, bf16[256,768]{1,0:T(8,128)(2,1)}, bf16[256,1536]{1,0:T(8,128)(2,1)}, bf16[256,1536]{1,0:T(8,128)(2,1)}, bf16[256,1536]{1,0:T(8,128)(2,1)}, /*index=5*/bf16[256,768]{1,0:T(8,128)(2,1)}) custom-call(bf16[512,768]{1,0:T(8,128)(2,1)} %bitcast.27, bf16[256,768]{1,0:T(8,128)(2,1)} %get-tuple-element.124.own.refs_0_, ...), custom_call_target="tpu_custom_call" | custom-call | flops 1811939328 | bytes 13000000 | tf_op jit(solution)/shard_map/unit/pallas_call | solution.py:411
  133.8 7.7 %unit.3 = (f32[256,768]{1,0:T(8,128)}, bf16[256,768]{1,0:T(8,128)(2,1)}, bf16[256,1536]{1,0:T(8,128)(2,1)}, bf16[256,1536]{1,0:T(8,128)(2,1)}, bf16[256,1536]{1,0:T(8,128)(2,1)}, /*index=5*/bf16[256,768]{1,0:T(8,128)(2,1)}) custom-call(bf16[512,768]{1,0:T(8,128)(2,1)} %bitcast.28, bf16[256,768]{1,0:T(8,128)(2,1)} %get-tuple-element.137.own.refs_1_, ...), custom_call_target="tpu_custom_call" | custom-call | flops 1811939328 | bytes 13000000 | tf_op jit(solution)/shard_map/unit/pallas_call | solution.py:411
  142.8 9.0 %unit_back.2 = (bf16[256,768]{1,0:T(8,128)(2,1)}, f32[256,768]{1,0:T(8,128)}, bf16[256,768]{1,0:T(8,128)(2,1)}, bf16[256,1536]{1,0:T(8,128)(2,1)}, bf16[256,1536...) custom-call(s32[4]{0:T(128)} %pad_add_fusion.ids, s32[2]{0:T(128)} %lens.7, ...), custom_call_target="tpu_custom_call" | custom-call | flops 1811939328 | bytes 14000000 | tf_op jit(solution)/shard_map/unit_back/pallas_call | solution.py:477
  154.1 9.0 %unit_back.3 = (bf16[256,768]{1,0:T(8,128)(2,1)}, f32[256,768]{1,0:T(8,128)}, bf16[256,768]{1,0:T(8,128)(2,1)}, bf16[256,1536]{1,0:T(8,128)(2,1)}, bf16[256,1536...) custom-call(s32[4]{0:T(128)} %pad_add_fusion.ids, s32[2]{0:T(128)} %lens.7, ...), custom_call_target="tpu_custom_call" | custom-call | flops 1811939328 | bytes 14000000 | tf_op jit(solution)/shard_map/unit_back/pallas_call | solution.py:477
  163.7 11.4 %weight_grads.1 = (bf16[384,4608]{1,0:T(8,128)(2,1)}, bf16[384,4608]{1,0:T(8,128)(2,1)}) custom-call(s32[4]{0:T(128)} %pad_add_fusion.ids, bf16[256,768]{1,0:T(8,128)(2,1)} %get-tuple-element.148.refs_0_, bf16[256,768]{1,0:T(8,128)(2,1)} %get-tuple-element.149.refs_1_, bf16[256,768]{1,0:T(8,128)(2,1)} %get-tuple-element.150.refs_2_, ...), custom_call_target="tpu_custom_call" | custom-call | flops 3623878656 | bytes 14000000 | tf_op jit(solution)/shard_map/weight_grads/pallas_call | solution.py:557
  176.1 6.7 %mix_back.1 = (bf16[192,256]{1,0:T(8,128)(2,1)}, bf16[192,256]{1,0:T(8,128)(2,1)}, bf16[192,256]{1,0:T(8,128)(2,1)}, bf16[192,256]{1,0:T(8,128)(2,1)}, f32[512,7...) custom-call(s32[4]{0:T(128)} %pad_add_fusion.ids, ...), custom_call_target="tpu_custom_call" | custom-call | flops 603979776 | bytes 10000000 | tf_op jit(solution)/shard_map/mix_back/pallas_call | solution.py:621
  189.1 6.3 %fold_core.2 = (f32[192,4608]{1,0:T(8,128)}, bf16[192,4608]{1,0:T(8,128)(2,1)}) custom-call(bf16[384,4608]{1,0:T(8,128)(2,1)} %get-tuple-element.171.keep, bf16[384,4608]{1,0:T(8,128)(2,1)} %copy-done), custom_call_target="tpu_custom_call" | custom-call | flops 1769472 | bytes 12386304 | tf_op jit(solution)/shard_map/fold_core/pallas_call | solution.py:720
  196.4 15.1 %attend_back.1 = (bf16[576,256]{1,0:T(8,128)(2,1)}, bf16[576,256]{1,0:T(8,128)(2,1)}, bf16[576,256]{1,0:T(8,128)(2,1)}, bf16[576,256]{1,0:T(8,128)(2,1)}) custom-call(s32[4]{0:T(128)} %pad_add_fusion.ids, s32[2]{0:T(128)} %lens.7, f32[12]{0:T(128)} %constant.40.clone.slopes, bf16[576,256]{1,0:T(8,128)(2,1)} %get-tuple-element.114.refs_0_, ...), custom_call_target="tpu_custom_call" | custom-call | flops 4026531840 | bytes 5000000 | tf_op jit(solution)/shard_map/attend_back/pallas_call | solution.py:308
  212.2 3.8 %collective-permute-start.45 = (bf16[576,256]{1,0:T(8,128)(2,1)}, bf16[576,256]{1,0:T(8,128)(2,1)S(1)}, u32[]{:S(2)}, u32[]{:S(2)}) collective-permute-start(bf16[576,256]{1,0:T(8,128)(2,1)} %get-tuple-element.184), channel_id=1, source_target_pairs={{0,6},{2,4},{4,2},{6,0},{1,7},{3,5},{5,3},{7,1},{8,14},{10,12},{12... | collective-permute-start | bytes 884744 | tf_op jit(solution)/shard_map/ppermute | solution.py:63
  218.1 17.0 %collective-permute-done.46.refs_0_ = bf16[192,4608]{1,0:T(8,128)(2,1)S(1)} collective-permute-done((bf16[192,4608]{1,0:T(8,128)(2,1)}, bf16[192,4608]{1,0:T(8,128)(2,1)S(1)}, u32[]{:S(2)}, u32[]{:S(2)}) %collective-permute-start.46) | collective-permute-done | bytes 1769504 | tf_op jit(solution)/shard_map/ppermute | solution.py:63
  236.4 4.7 %fold_y.2 = (f32[48,4608]{1,0:T(8,128)}, bf16[48,4608]{1,0:T(8,128)(2,1)}, bf16[48,4608]{1,0:T(8,128)(2,1)}, bf16[48,4608]{1,0:T(8,128)(2,1)}) custom-call(s32[4]{0:T(128)} %pad_add_fusion.ids, f32[192,4608]{1,0:T(8,128)} %get-tuple-element.185.mine, bf16[192,4608]{1,0:T(8,128)(2,1)} %copy-done.2), custom_call_target="tpu_custom_call" | custom-call | flops 884736 | bytes 7962624 | tf_op jit(solution)/shard_map/fold_y/pallas_call | solution.py:758
  242.0 6.1 %project_back.1 = (bf16[512,768]{1,0:T(8,128)(2,1)}, bf16[400,1536]{1,0:T(8,128)(2,1)}, bf16[400,1536]{1,0:T(8,128)(2,1)}) custom-call(s32[4]{0:T(128)} %pad_add_fusion.ids, bf16[512,768]{1,0:T(8,128)(2,1)} %bitcast.30, bf16[768,1152]{1,0:T(8,128)(2,1)} %get-tuple-element.109.whole, ...), custom_call_target="tpu_custom_call", output_to_operand_aliasing={{1}: (4, {}), {2}: (5, {})} | custom-call | flops 1811939328 | bytes 8000000 | tf_op jit(solution)/shard_map/project_back/pallas_call | solution.py:684
  256.0 3.2 %fold_core.3 = (f32[208,1536]{1,0:T(8,128)}, bf16[208,768]{1,0:T(8,128)(2,1)}, bf16[208,768]{1,0:T(8,128)(2,1)}) custom-call(bf16[400,1536]{1,0:T(8,128)(2,1)} %get-tuple-element.193.keep, bf16[400,1536]{1,0:T(8,128)(2,1)} %copy-done.9), custom_call_target="tpu_custom_call" | custom-call | flops 614400 | bytes 4300800 | tf_op jit(solution)/shard_map/fold_core/pallas_call | solution.py:720
  260.0 8.2 %collective-permute-done.47 = bf16[512,768]{1,0:T(8,128)(2,1)S(1)} collective-permute-done((bf16[512,768]{1,0:T(8,128)(2,1)}, bf16[512,768]{1,0:T(8,128)(2,1)S(1)}, u32[]{:S(2)}, u32[]{:S(2)}) %collective-permute-start.47) | collective-permute-done | bytes 786464 | tf_op jit(solution)/shard_map/ppermute | solution.py:63
  270.5 7.0 %collective-permute-done.51.refs_1_ = bf16[208,768]{1,0:T(8,128)(2,1)S(1)} collective-permute-done((bf16[208,768]{1,0:T(8,128)(2,1)}, bf16[208,768]{1,0:T(8,128)(2,1)S(1)}, u32[]{:S(2)}, u32[]{:S(2)}) %collective-permute-start.51) | collective-permute-done | bytes 319520 | tf_op jit(solution)/shard_map/ppermute | solution.py:63
  278.3 2.6 fold_y.3
  287.5 18.3 %collective-permute-done.53 = bf16[64,1536]{1,0:T(8,128)(2,1)S(1)} collective-permute-done((bf16[64,1536]{1,0:T(8,128)(2,1)}, bf16[64,1536]{1,0:T(8,128)(2,1)S(1)}, u32[]{:S(2)}, u32[]{:S(2)}) %collective-permute-start.53) | collective-permute-done | bytes 196640 | tf_op jit(solution)/shard_map/ppermute | solution.py:63
  (265 shorter events, 77.2 us)
Async XLA Ops:
  4.8 11.3 %collective-permute-start.1 = (bf16[48,1152]{1,0:T(8,128)(2,1)S(1)}, bf16[48,1152]{1,0:T(8,128)(2,1)S(1)}, u32[]{:S(2)}, u32[]{:S(2)}) collective-permute-start(bf16[48,1152]{1,0:T(8,128)(2,1)S(1)} %bitcast.41), channel_id=1, source_target_pairs={{0,4},{2,6},{4,0},{6,2},{1,5},{3,7},{5,1},{7,3},{8,12},{10,14},{12... | collective-permute-start | bytes 331784 | tf_op jit(solution)/shard_map/ppermute | solution.py:63
  18.3 15.8 %collective-permute-start.3 = (bf16[48,3456]{1,0:T(8,128)(2,1)S(1)}, bf16[48,3456]{1,0:T(8,128)(2,1)S(1)}, u32[]{:S(2)}, u32[]{:S(2)}) collective-permute-start(bf16[48,3456]{1,0:T(8,128)(2,1)S(1)} %pad_maximum_fusion.1), channel_id=1, source_target_pairs={{0,2},{2,0},{4,6},{6,4},{1,3},{3,1},{5,7},{7,5},{8,10},{10,8},{12,... | collective-permute-start | bytes 995336 | tf_op jit(solution)/shard_map/ppermute | solution.py:63
  20.0 25.8 %collective-permute-start.4 = (bf16[48,3456]{1,0:T(8,128)(2,1)S(1)}, bf16[48,3456]{1,0:T(8,128)(2,1)S(1)}, u32[]{:S(2)}, u32[]{:S(2)}) collective-permute-start(bf16[48,3456]{1,0:T(8,128)(2,1)S(1)} %pad_maximum_fusion.1), channel_id=1, source_target_pairs={{0,4},{2,6},{4,0},{6,2},{1,5},{3,7},{5,1},{7,3},{8,12},{10,14},{12... | collective-permute-start | bytes 995336 | tf_op jit(solution)/shard_map/ppermute | solution.py:63
  22.1 23.7 %collective-permute-start.5 = (bf16[48,3456]{1,0:T(8,128)(2,1)S(1)}, bf16[48,3456]{1,0:T(8,128)(2,1)S(1)}, u32[]{:S(2)}, u32[]{:S(2)}) collective-permute-start(bf16[48,3456]{1,0:T(8,128)(2,1)S(1)} %pad_maximum_fusion.1), channel_id=1, source_target_pairs={{0,6},{2,4},{4,2},{6,0},{1,7},{3,5},{5,3},{7,1},{8,14},{10,12},{12... | collective-permute-start | bytes 995336 | tf_op jit(solution)/shard_map/ppermute | solution.py:63
  46.0 46.8 %collective-permute-start.18 = (bf16[192,3456]{1,0:T(8,128)(2,1)S(1)}, bf16[192,3456]{1,0:T(8,128)(2,1)S(1)}, u32[]{:S(2)}, u32[]{:S(2)}) collective-permute-start(bf16[192,3456]{1,0:T(8,128)(2,1)S(1)} %constant_dynamic-update-slice_fusion.refs_0_), channel_id=1, source_target_pairs={{0,16},{8,24},{16,0},{24,8},{1,17},{9,25},{17,1},{25,9},{2,18},{10... | collective-permute-start | bytes 3981320 | tf_op jit(solution)/shard_map/ppermute | solution.py:63
  47.6 13.6 %collective-permute-start.19 = (bf16[576,256]{1,0:T(8,128)(2,1)S(1)}, bf16[576,256]{1,0:T(8,128)(2,1)S(1)}, u32[]{:S(2)}, u32[]{:S(2)}) collective-permute-start(bf16[576,256]{1,0:T(8,128)(2,1)S(1)} %copy-done.41), channel_id=1, source_target_pairs={{0,2},{2,0},{4,6},{6,4},{1,3},{3,1},{5,7},{7,5},{8,10},{10,8},{12,... | collective-permute-start | bytes 884744 | tf_op jit(solution)/shard_map/ppermute | solution.py:63
  52.6 22.5 %collective-permute-start.20 = (bf16[576,256]{1,0:T(8,128)(2,1)S(1)}, bf16[576,256]{1,0:T(8,128)(2,1)S(1)}, u32[]{:S(2)}, u32[]{:S(2)}) collective-permute-start(bf16[576,256]{1,0:T(8,128)(2,1)S(1)} %copy-done.40), channel_id=1, source_target_pairs={{0,4},{2,6},{4,0},{6,2},{1,5},{3,7},{5,1},{7,3},{8,12},{10,14},{12... | collective-permute-start | bytes 884744 | tf_op jit(solution)/shard_map/ppermute | solution.py:63
  53.7 21.5 %collective-permute-start.21 = (bf16[576,256]{1,0:T(8,128)(2,1)S(1)}, bf16[576,256]{1,0:T(8,128)(2,1)S(1)}, u32[]{:S(2)}, u32[]{:S(2)}) collective-permute-start(bf16[576,256]{1,0:T(8,128)(2,1)S(1)} %copy-done.39), channel_id=1, source_target_pairs={{0,6},{2,4},{4,2},{6,0},{1,7},{3,5},{5,3},{7,1},{8,14},{10,12},{12... | collective-permute-start | bytes 884744 | tf_op jit(solution)/shard_map/ppermute | solution.py:63
  75.1 17.6 %collective-permute-start.28 = (bf16[48,1536]{1,0:T(8,128)(2,1)S(1)}, bf16[48,1536]{1,0:T(8,128)(2,1)S(1)}, u32[]{:S(2)}, u32[]{:S(2)}) collective-permute-start(bf16[48,1536]{1,0:T(8,128)(2,1)S(1)} %convert_bitcast_fusion), channel_id=1, source_target_pairs={{0,2},{2,0},{4,6},{6,4},{1,3},{3,1},{5,7},{7,5},{8,10},{10,8},{12,... | collective-permute-start | bytes 442376 | tf_op jit(solution)/shard_map/ppermute | solution.py:63
  79.0 13.8 %collective-permute-start.29 = (bf16[48,1536]{1,0:T(8,128)(2,1)S(1)}, bf16[48,1536]{1,0:T(8,128)(2,1)S(1)}, u32[]{:S(2)}, u32[]{:S(2)}) collective-permute-start(bf16[48,1536]{1,0:T(8,128)(2,1)S(1)} %convert_bitcast_fusion), channel_id=1, source_target_pairs={{0,4},{2,6},{4,0},{6,2},{1,5},{3,7},{5,1},{7,3},{8,12},{10,14},{12... | collective-permute-start | bytes 442376 | tf_op jit(solution)/shard_map/ppermute | solution.py:63
  79.8 12.9 %collective-permute-start.30 = (bf16[48,1536]{1,0:T(8,128)(2,1)S(1)}, bf16[48,1536]{1,0:T(8,128)(2,1)S(1)}, u32[]{:S(2)}, u32[]{:S(2)}) collective-permute-start(bf16[48,1536]{1,0:T(8,128)(2,1)S(1)} %convert_bitcast_fusion), channel_id=1, source_target_pairs={{0,6},{2,4},{4,2},{6,0},{1,7},{3,5},{5,3},{7,1},{8,14},{10,12},{12... | collective-permute-start | bytes 442376 | tf_op jit(solution)/shard_map/ppermute | solution.py:63
  93.5 16.8 %collective-permute-start.31 = (bf16[192,1536]{1,0:T(8,128)(2,1)S(1)}, bf16[192,1536]{1,0:T(8,128)(2,1)S(1)}, u32[]{:S(2)}, u32[]{:S(2)}) collective-permute-start(bf16[192,1536]{1,0:T(8,128)(2,1)S(1)} %constant_dynamic-update-slice_fusion.4.refs_0_), channel_id=1, source_target_pairs={{0,16},{8,24},{16,0},{24,8},{1,17},{9,25},{17,1},{25,9},{2,18},{10... | collective-permute-start | bytes 1769480 | tf_op jit(solution)/shard_map/ppermute | solution.py:63
  94.6 11.3 %collective-permute-start.24 = (bf16[192,256]{1,0:T(8,128)(2,1)}, bf16[192,256]{1,0:T(8,128)(2,1)S(1)}, u32[]{:S(2)}, u32[]{:S(2)}) collective-permute-start(bf16[192,256]{1,0:T(8,128)(2,1)} %get-tuple-element.121), channel_id=1, source_target_pairs={{0,2},{2,0},{4,6},{6,4},{1,3},{3,1},{5,7},{7,5},{8,10},{10,8},{12,... | collective-permute-start | bytes 294920 | tf_op jit(solution)/shard_map/ppermute | solution.py:63
  110.8 12.2 %collective-permute-start.27 = (bf16[256,768]{1,0:T(8,128)(2,1)}, bf16[256,768]{1,0:T(8,128)(2,1)S(1)}, u32[]{:S(2)}, u32[]{:S(2)}) collective-permute-start(bf16[256,768]{1,0:T(8,128)(2,1)} %get-tuple-element.124.own.refs_0_), channel_id=1, source_target_pairs={{0,1},{1,0},{2,3},{3,2},{4,5},{5,4},{6,7},{7,6},{8,9},{9,8},{10,11... | collective-permute-start | bytes 1179656 | tf_op jit(solution)/shard_map/ppermute | solution.py:63
  112.3 20.7 %collective-permute-start.35 = (bf16[256,768]{1,0:T(8,128)(2,1)}, bf16[256,768]{1,0:T(8,128)(2,1)S(1)}, u32[]{:S(2)}, u32[]{:S(2)}) collective-permute-start(bf16[256,768]{1,0:T(8,128)(2,1)} %get-tuple-element.137.own.refs_1_), channel_id=1, source_target_pairs={{0,1},{1,0},{2,3},{3,2},{4,5},{5,4},{6,7},{7,6},{8,9},{9,8},{10,11... | collective-permute-start | bytes 1179656 | tf_op jit(solution)/shard_map/ppermute | solution.py:63
  141.4 11.9 %collective-permute-start.36 = (bf16[256,768]{1,0:T(8,128)(2,1)}, bf16[256,768]{1,0:T(8,128)(2,1)S(1)}, u32[]{:S(2)}, u32[]{:S(2)}) collective-permute-start(bf16[256,768]{1,0:T(8,128)(2,1)} %get-tuple-element.139.own), channel_id=1, source_target_pairs={{0,1},{1,0},{2,3},{3,2},{4,5},{5,4},{6,7},{7,6},{8,9},{9,8},{10,11... | collective-permute-start | bytes 1179656 | tf_op jit(solution)/shard_map/ppermute | solution.py:63
  151.8 23.4 %collective-permute-start.37 = (bf16[256,768]{1,0:T(8,128)(2,1)}, bf16[256,768]{1,0:T(8,128)(2,1)S(1)}, u32[]{:S(2)}, u32[]{:S(2)}) collective-permute-start(bf16[256,768]{1,0:T(8,128)(2,1)} %get-tuple-element.146.refs_6_), channel_id=1, source_target_pairs={{0,1},{1,0},{2,3},{3,2},{4,5},{5,4},{6,7},{7,6},{8,9},{9,8},{10,11... | collective-permute-start | bytes 1179656 | tf_op jit(solution)/shard_map/ppermute | solution.py:63
  163.1 12.1 %collective-permute-start.38 = (bf16[256,768]{1,0:T(8,128)(2,1)}, bf16[256,768]{1,0:T(8,128)(2,1)S(1)}, u32[]{:S(2)}, u32[]{:S(2)}) collective-permute-start(bf16[256,768]{1,0:T(8,128)(2,1)} %get-tuple-element.147.refs_7_), channel_id=1, source_target_pairs={{0,1},{1,0},{2,3},{3,2},{4,5},{5,4},{6,7},{7,6},{8,9},{9,8},{10,11... | collective-permute-start | bytes 1179656 | tf_op jit(solution)/shard_map/ppermute | solution.py:63
  175.2 12.1 %collective-permute-start.42 = (bf16[384,4608]{1,0:T(8,128)(2,1)}, bf16[384,4608]{1,0:T(8,128)(2,1)S(1)}, u32[]{:S(2)}, u32[]{:S(2)}) collective-permute-start(bf16[384,4608]{1,0:T(8,128)(2,1)} %get-tuple-element.172), channel_id=1, source_target_pairs={{0,8},{8,0},{16,24},{24,16},{1,9},{9,1},{17,25},{25,17},{2,10},{10... | collective-permute-start | bytes 10616840 | tf_op jit(solution)/shard_map/ppermute | solution.py:63
  182.8 12.6 %collective-permute-start.39 = (bf16[192,256]{1,0:T(8,128)(2,1)}, bf16[192,256]{1,0:T(8,128)(2,1)S(1)}, u32[]{:S(2)}, u32[]{:S(2)}) collective-permute-start(bf16[192,256]{1,0:T(8,128)(2,1)} %get-tuple-element.168), channel_id=1, source_target_pairs={{0,2},{2,0},{4,6},{6,4},{1,3},{3,1},{5,7},{7,5},{8,10},{10,8},{12,... | collective-permute-start | bytes 294920 | tf_op jit(solution)/shard_map/ppermute | solution.py:63
  183.9 11.5 %collective-permute-start.40 = (bf16[192,256]{1,0:T(8,128)(2,1)}, bf16[192,256]{1,0:T(8,128)(2,1)S(1)}, u32[]{:S(2)}, u32[]{:S(2)}) collective-permute-start(bf16[192,256]{1,0:T(8,128)(2,1)} %get-tuple-element.169), channel_id=1, source_target_pairs={{0,4},{2,6},{4,0},{6,2},{1,5},{3,7},{5,1},{7,3},{8,12},{10,14},{12... | collective-permute-start | bytes 294920 | tf_op jit(solution)/shard_map/ppermute | solution.py:63
  195.5 39.7 %collective-permute-start.46 = (bf16[192,4608]{1,0:T(8,128)(2,1)}, bf16[192,4608]{1,0:T(8,128)(2,1)S(1)}, u32[]{:S(2)}, u32[]{:S(2)}) collective-permute-start(bf16[192,4608]{1,0:T(8,128)(2,1)} %get-tuple-element.186), channel_id=1, source_target_pairs={{0,16},{8,24},{16,0},{24,8},{1,17},{9,25},{17,1},{25,9},{2,18},{10... | collective-permute-start | bytes 5308424 | tf_op jit(solution)/shard_map/ppermute | solution.py:63
  211.5 29.6 %collective-permute-start.43 = (bf16[576,256]{1,0:T(8,128)(2,1)}, bf16[576,256]{1,0:T(8,128)(2,1)S(1)}, u32[]{:S(2)}, u32[]{:S(2)}) collective-permute-start(bf16[576,256]{1,0:T(8,128)(2,1)} %get-tuple-element.182), channel_id=1, source_target_pairs={{0,2},{2,0},{4,6},{6,4},{1,3},{3,1},{5,7},{7,5},{8,10},{10,8},{12,... | collective-permute-start | bytes 884744 | tf_op jit(solution)/shard_map/ppermute | solution.py:63
  212.2 28.9 %collective-permute-start.44 = (bf16[576,256]{1,0:T(8,128)(2,1)}, bf16[576,256]{1,0:T(8,128)(2,1)S(1)}, u32[]{:S(2)}, u32[]{:S(2)}) collective-permute-start(bf16[576,256]{1,0:T(8,128)(2,1)} %get-tuple-element.183), channel_id=1, source_target_pairs={{0,4},{2,6},{4,0},{6,2},{1,5},{3,7},{5,1},{7,3},{8,12},{10,14},{12... | collective-permute-start | bytes 884744 | tf_op jit(solution)/shard_map/ppermute | solution.py:63
  212.2 28.9 %collective-permute-start.45 = (bf16[576,256]{1,0:T(8,128)(2,1)}, bf16[576,256]{1,0:T(8,128)(2,1)S(1)}, u32[]{:S(2)}, u32[]{:S(2)}) collective-permute-start(bf16[576,256]{1,0:T(8,128)(2,1)} %get-tuple-element.184), channel_id=1, source_target_pairs={{0,6},{2,4},{4,2},{6,0},{1,7},{3,5},{5,3},{7,1},{8,14},{10,12},{12... | collective-permute-start | bytes 884744 | tf_op jit(solution)/shard_map/ppermute | solution.py:63
  248.1 20.2 %collective-permute-start.47 = (bf16[512,768]{1,0:T(8,128)(2,1)}, bf16[512,768]{1,0:T(8,128)(2,1)S(1)}, u32[]{:S(2)}, u32[]{:S(2)}) collective-permute-start(bf16[512,768]{1,0:T(8,128)(2,1)} %get-tuple-element.192), channel_id=1, source_target_pairs={{0,1},{1,0},{2,3},{3,2},{4,5},{5,4},{6,7},{7,6},{8,9},{9,8},{10,11... | collective-permute-start | bytes 2359304 | tf_op jit(solution)/shard_map/ppermute | solution.py:63
  249.6 20.9 %collective-permute-start.49 = (bf16[48,4608]{1,0:T(8,128)(2,1)S(1)}, bf16[48,4608]{1,0:T(8,128)(2,1)S(1)}, u32[]{:S(2)}, u32[]{:S(2)}) collective-permute-start(bf16[48,4608]{1,0:T(8,128)(2,1)S(1)} %copy-done.35), channel_id=1, source_target_pairs={{0,2},{2,0},{4,6},{6,4},{1,3},{3,1},{5,7},{7,5},{8,10},{10,8},{12,... | collective-permute-start | bytes 1327112 | tf_op jit(solution)/shard_map/ppermute | solution.py:63
  250.9 34.4 %collective-permute-start.55 = (bf16[48,4608]{1,0:T(8,128)(2,1)S(1)}, bf16[48,4608]{1,0:T(8,128)(2,1)S(1)}, u32[]{:S(2)}, u32[]{:S(2)}) collective-permute-start(bf16[48,4608]{1,0:T(8,128)(2,1)S(1)} %copy-done.34), channel_id=1, source_target_pairs={{0,4},{2,6},{4,0},{6,2},{1,5},{3,7},{5,1},{7,3},{8,12},{10,14},{12... | collective-permute-start | bytes 1327112 | tf_op jit(solution)/shard_map/ppermute | solution.py:63
  252.4 32.9 %collective-permute-start.56 = (bf16[48,4608]{1,0:T(8,128)(2,1)S(1)}, bf16[48,4608]{1,0:T(8,128)(2,1)S(1)}, u32[]{:S(2)}, u32[]{:S(2)}) collective-permute-start(bf16[48,4608]{1,0:T(8,128)(2,1)S(1)} %copy-done.33), channel_id=1, source_target_pairs={{0,6},{2,4},{4,2},{6,0},{1,7},{3,5},{5,3},{7,1},{8,14},{10,12},{12... | collective-permute-start | bytes 1327112 | tf_op jit(solution)/shard_map/ppermute | solution.py:63
  259.2 11.4 %collective-permute-start.50 = (bf16[208,768]{1,0:T(8,128)(2,1)}, bf16[208,768]{1,0:T(8,128)(2,1)S(1)}, u32[]{:S(2)}, u32[]{:S(2)}) collective-permute-start(bf16[208,768]{1,0:T(8,128)(2,1)} %get-tuple-element.197), channel_id=1, source_target_pairs={{0,16},{8,24},{16,0},{24,8},{1,17},{9,25},{17,1},{25,9},{2,18},{10... | collective-permute-start | bytes 958472 | tf_op jit(solution)/shard_map/ppermute | solution.py:63
  281.5 24.4 %collective-permute-start.53 = (bf16[64,1536]{1,0:T(8,128)(2,1)}, bf16[64,1536]{1,0:T(8,128)(2,1)S(1)}, u32[]{:S(2)}, u32[]{:S(2)}) collective-permute-start(bf16[64,1536]{1,0:T(8,128)(2,1)} %get-tuple-element.202), channel_id=1, source_target_pairs={{0,4},{2,6},{4,0},{6,2},{1,5},{3,7},{5,1},{7,3},{8,12},{10,14},{12... | collective-permute-start | bytes 589832 | tf_op jit(solution)/shard_map/ppermute | solution.py:63
  283.6 22.3 %collective-permute-start.54 = (bf16[64,1536]{1,0:T(8,128)(2,1)}, bf16[64,1536]{1,0:T(8,128)(2,1)S(1)}, u32[]{:S(2)}, u32[]{:S(2)}) collective-permute-start(bf16[64,1536]{1,0:T(8,128)(2,1)} %get-tuple-element.203), channel_id=1, source_target_pairs={{0,6},{2,4},{4,2},{6,0},{1,7},{3,5},{5,3},{7,1},{8,14},{10,12},{12... | collective-permute-start | bytes 589832 | tf_op jit(solution)/shard_map/ppermute | solution.py:63
  (88 other events, 616.0 us)

commit v6 on v5

--- a/solution.py
+++ b/solution.py
@@ -43,7 +43,7 @@
 
 def params(*semantics):
     return pltpu.CompilerParams(
-        dimension_semantics=semantics or None, vmem_limit_bytes=56 * 1024 * 1024
+        dimension_semantics=semantics or None, vmem_limit_bytes=20 * 1024 * 1024
     )
 
 

time: 311 us -> 295 us (0.949)
  Pallas kernels: 118 us -> 69.7 us
  waiting for transfers between devices: 94.1 us -> 127 us
  starting transfers between devices: 67.1 us -> 76 us
  local copies, waits for them, and re-layouts: 21.6 us -> 14.6 us
    ppermute x57, waiting for transfers between devices: 94.1 us -> 127 us  [swap(): return lax.ppermute(value, axis, xor_pairs(axis, distance))]
    ppermute x57, starting transfers between devices: 67.1 us -> 76 us  [swap(): return lax.ppermute(value, axis, xor_pairs(axis, distance))]
    pallas_call x2, Pallas kernels: 18 us -> 10.7 us  [unit_back(): pl.pallas_call(functools.partial(unit_back_kernel, n, s), grid=(steps,),...]
    pallas_call x2, Pallas kernels: 9.86 us -> 2.82 us  [assemble(): pl.pallas_call(functools.partial(assemble_kernel, n), grid=(3,), out_shap...]
    pallas_call x2, Pallas kernels: 15.3 us -> 8.43 us  [unit(): pl.pallas_call(unit_kernel, grid=(steps,), out_shape=[shape((tokens, mode...]
    pallas_call x2, Pallas kernels: 9.44 us -> 2.95 us  [fold_core(): pl.pallas_call(functools.partial(fold_core_kernel, extra), grid=(steps,),...]
    unnamed x133 -> x45, local copies, waits for them, and re-layouts: 14.1 us -> 8.79 us
    pallas_call x2, Pallas kernels: 7.22 us -> 2.65 us  [fold_y(): pl.pallas_call(functools.partial(fold_y_kernel, n, extra, parts), grid=(s...]
  transfers between devices with their start and end apart: 57 -> 57, of which waited for: 16 -> 26; matrix products, arithmetic and copies ran while one was open for 3% -> 2% of each run, Pallas kernels for 36% -> 22%
where the time goes in v6:
time: 295 us; the launch traced here: 294 us
  waiting for transfers between devices  127 us (43%)
  starting transfers between devices  76 us (26%)
  Pallas kernels  69.7 us (24%)
  local copies, waits for them, and re-layouts  14.6 us (5%)
  other arithmetic  5.89 us (2%)
    ppermute x57, waiting for transfers between devices, swap(): return lax.ppermute(value, axis, xor_pairs(axis, distance))  127 us
    ppermute x57, starting transfers between devices, swap(): return lax.ppermute(value, axis, xor_pairs(axis, distance))  76 us
    pallas_call x1, Pallas kernels, attend_back(): pl.pallas_call(functools.partial(attend_back_kernel, n, heads), grid=(per...  14.2 us
    pallas_call x2, Pallas kernels, unit_back(): pl.pallas_call(functools.partial(unit_back_kernel, n, s), grid=(steps,),...  10.7 us
    pallas_call x1, Pallas kernels, attend(): pl.pallas_call(functools.partial(attend_kernel, n, heads), grid=(per,), o...  9.94 us
    unnamed x45, local copies, waits for them, and re-layouts  8.79 us
    pallas_call x2, Pallas kernels, unit(): pl.pallas_call(unit_kernel, grid=(steps,), out_shape=[shape((tokens, mode...  8.43 us
    pallas_call x1, Pallas kernels, weight_grads(): pl.pallas_call(functools.partial(weight_kernel, steps, seqs), grid=(3 * s...  7.67 us
  transfers between devices with their start and end apart: 57, of which 26 were waited for; matrix products, arithmetic and copies ran while one was open for 2% of the time, Pallas kernels for 22%

profile of v6, /device:TPU:0, one launch (start us, length us, event | category | flops | bytes accessed | tf_op | source)
XLA Modules:
  0.0 294.0 jit_solution(16414349452246517789)
XLA Ops:
  1.6 3.1 %collective-permute-start = (bf16[48,1152]{1,0:T(8,128)(2,1)S(1)}, bf16[48,1152]{1,0:T(8,128)(2,1)S(1)}, u32[]{:S(2)}, u32[]{:S(2)}) collective-permute-start(bf16[48,1152]{1,0:T(8,128)(2,1)S(1)} %bitcast.35), channel_id=1, source_target_pairs={{0,2},{2,0},{4,6},{6,4},{1,3},{3,1},{5,7},{7,5},{8,10},{10,8},{12,... | collective-permute-start | bytes 331784 | tf_op jit(solution)/shard_map/ppermute | solution.py:63
  4.8 2.6 collective-permute-start.1
  11.7 4.4 %collective-permute-done.1.refs_2_ = bf16[48,1152]{1,0:T(8,128)(2,1)S(1)} collective-permute-done((bf16[48,1152]{1,0:T(8,128)(2,1)S(1)}, bf16[48,1152]{1,0:T(8,128)(2,1)S(1)}, u32[]{:S(2)}, u32[]{:S(2)}) %collective-permute-start.1) | collective-permute-done | bytes 110624 | tf_op jit(solution)/shard_map/ppermute | solution.py:63
  22.0 2.5 collective-permute-start.5
  33.9 12.0 %collective-permute-done.4 = bf16[48,3456]{1,0:T(8,128)(2,1)} collective-permute-done((bf16[48,3456]{1,0:T(8,128)(2,1)S(1)}, bf16[48,3456]{1,0:T(8,128)(2,1)}, u32[]{:S(2)}, u32[]{:S(2)}) %collective-permute-start.4) | collective-permute-done | bytes 331808 | tf_op jit(solution)/shard_map/ppermute | solution.py:63
  49.6 5.0 %collective-permute-start.19 = (bf16[576,256]{1,0:T(8,128)(2,1)S(1)}, bf16[576,256]{1,0:T(8,128)(2,1)S(1)}, u32[]{:S(2)}, u32[]{:S(2)}) collective-permute-start(bf16[576,256]{1,0:T(8,128)(2,1)S(1)} %get-tuple-element.115), channel_id=1, source_target_pairs={{0,2},{2,0},{4,6},{6,4},{1,3},{3,1},{5,7},{7,5},{8,10},{10,8},{12,... | collective-permute-start | bytes 884744 | tf_op jit(solution)/shard_map/ppermute | solution.py:63
  57.1 6.1 %collective-permute-done.19.refs_1_ = bf16[576,256]{1,0:T(8,128)(2,1)S(1)} collective-permute-done((bf16[576,256]{1,0:T(8,128)(2,1)S(1)}, bf16[576,256]{1,0:T(8,128)(2,1)S(1)}, u32[]{:S(2)}, u32[]{:S(2)}) %collective-permute-start.19) | collective-permute-done | bytes 294944 | tf_op jit(solution)/shard_map/ppermute | solution.py:63
  63.2 13.9 %collective-permute-done.20.refs_2_ = bf16[576,256]{1,0:T(8,128)(2,1)S(1)} collective-permute-done((bf16[576,256]{1,0:T(8,128)(2,1)S(1)}, bf16[576,256]{1,0:T(8,128)(2,1)S(1)}, u32[]{:S(2)}, u32[]{:S(2)}) %collective-permute-start.20) | collective-permute-done | bytes 294944 | tf_op jit(solution)/shard_map/ppermute | solution.py:63
  77.2 3.8 %collective-permute-start.28 = (bf16[48,1536]{1,0:T(8,128)(2,1)S(1)}, bf16[48,1536]{1,0:T(8,128)(2,1)S(1)}, u32[]{:S(2)}, u32[]{:S(2)}) collective-permute-start(bf16[48,1536]{1,0:T(8,128)(2,1)S(1)} %convert_bitcast_fusion), channel_id=1, source_target_pairs={{0,2},{2,0},{4,6},{6,4},{1,3},{3,1},{5,7},{7,5},{8,10},{10,8},{12,... | collective-permute-start | bytes 442376 | tf_op jit(solution)/shard_map/ppermute | solution.py:63
  83.4 9.9 %attend.1 = (bf16[192,256]{1,0:T(8,128)(2,1)S(1)}, bf16[192,256]{1,0:T(8,128)(2,1)S(1)}, bf16[192,256]{1,0:T(8,128)(2,1)S(1)}, bf16[192,256]{1,0:T(8,128)(2,1)S(...) custom-call(s32[4]{0:T(128)S(1)} %pad_add_fusion.ids, s32[2]{0:T(128)S(1)} %copy-done.9, f32[12]{0:T(128)S(1)} %copy-done.12, ...), custom_call_target="tpu_custom_call" | custom-call | flops 1610612736 | bytes 3000000 | tf_op jit(solution)/shard_map/attend/pallas_call | solution.py:226
  94.0 2.5 collective-permute-start.31
  102.6 5.2 %collective-permute-done.25.refs_2_ = bf16[192,256]{1,0:T(8,128)(2,1)S(1)} collective-permute-done((bf16[192,256]{1,0:T(8,128)(2,1)S(1)}, bf16[192,256]{1,0:T(8,128)(2,1)S(1)}, u32[]{:S(2)}, u32[]{:S(2)}) %collective-permute-start.25) | collective-permute-done | bytes 98336 | tf_op jit(solution)/shard_map/ppermute | solution.py:63
  114.0 8.6 %collective-permute-done.27.other.refs_2_ = bf16[256,768]{1,0:T(8,128)(2,1)S(1)} collective-permute-done((bf16[256,768]{1,0:T(8,128)(2,1)S(1)}, bf16[256,768]{1,0:T(8,128)(2,1)S(1)}, u32[]{:S(2)}, u32[]{:S(2)}) %collective-permute-start.27) | collective-permute-done | bytes 393248 | tf_op jit(solution)/shard_map/ppermute | solution.py:63
  122.5 4.2 %unit.2 = (f32[256,768]{1,0:T(8,128)S(1)}, bf16[256,768]{1,0:T(8,128)(2,1)S(1)}, bf16[256,1536]{1,0:T(8,128)(2,1)S(1)}, bf16[256,1536]{1,0:T(8,128)(2,1)S(1)}, b...) custom-call(bf16[512,768]{1,0:T(8,128)(2,1)S(1)} %bitcast.27, ...), custom_call_target="tpu_custom_call" | custom-call | flops 1811939328 | bytes 13000000 | tf_op jit(solution)/shard_map/unit/pallas_call | solution.py:411
  128.3 2.6 collective-permute-done.35.other.refs_3_
  131.0 4.2 %unit.3 = (f32[256,768]{1,0:T(8,128)S(1)}, bf16[256,768]{1,0:T(8,128)(2,1)S(1)}, bf16[256,1536]{1,0:T(8,128)(2,1)S(1)}, bf16[256,1536]{1,0:T(8,128)(2,1)S(1)}, b...) custom-call(bf16[512,768]{1,0:T(8,128)(2,1)S(1)} %bitcast.28, ...), custom_call_target="tpu_custom_call" | custom-call | flops 1811939328 | bytes 13000000 | tf_op jit(solution)/shard_map/unit/pallas_call | solution.py:411
  136.8 2.6 collective-permute-done.34.other
  139.4 5.4 %unit_back.2 = (bf16[256,768]{1,0:T(8,128)(2,1)S(1)}, f32[256,768]{1,0:T(8,128)S(1)}, bf16[256,768]{1,0:T(8,128)(2,1)S(1)}, bf16[256,1536]{1,0:T(8,128)(2,1)S(1)...) custom-call(s32[4]{0:T(128)S(1)} %pad_add_fusion.ids, s32[2]{0:T(128)S(1)} %copy-done.9, ...), custom_call_target="tpu_custom_call" | custom-call | flops 1811939328 | bytes 14000000 | tf_op jit(solution)/shard_map/unit_back/pallas_call | solution.py:477
  147.8 5.3 %unit_back.3 = (bf16[256,768]{1,0:T(8,128)(2,1)S(1)}, f32[256,768]{1,0:T(8,128)S(1)}, bf16[256,768]{1,0:T(8,128)(2,1)S(1)}, bf16[256,1536]{1,0:T(8,128)(2,1)S(1)...) custom-call(s32[4]{0:T(128)S(1)} %pad_add_fusion.ids, s32[2]{0:T(128)S(1)} %copy-done.9, ...), custom_call_target="tpu_custom_call" | custom-call | flops 1811939328 | bytes 14000000 | tf_op jit(solution)/shard_map/unit_back/pallas_call | solution.py:477
  154.7 7.7 %weight_grads.1 = (bf16[384,4608]{1,0:T(8,128)(2,1)S(1)}, bf16[384,4608]{1,0:T(8,128)(2,1)S(1)}) custom-call(s32[4]{0:T(128)S(1)} %pad_add_fusion.ids, bf16[256,768]{1,0:T(8,128)(2,1)S(1)} %get-tuple-element.148.refs_0_, bf16[256,768]{1,0:T(8,128)(2,1)S(1)} %get-tuple-element.149.refs_1_, bf16[256,768]{1,0:T(8,128)(2,1)S(1)} %get-tuple-element.150.refs_2_, ...), custom_call_target="tpu_custom_call" | custom-call | flops 3623878656 | bytes 14000000 | tf_op jit(solution)/shard_map/weight_grads/pallas_call | solution.py:557
  163.7 3.2 %mix_back.1 = (bf16[192,256]{1,0:T(8,128)(2,1)S(1)}, bf16[192,256]{1,0:T(8,128)(2,1)S(1)}, bf16[192,256]{1,0:T(8,128)(2,1)S(1)}, bf16[192,256]{1,0:T(8,128)(2,1)...) custom-call(s32[4]{0:T(128)S(1)} %pad_add_fusion.ids, ...), custom_call_target="tpu_custom_call" | custom-call | flops 603979776 | bytes 10000000 | tf_op jit(solution)/shard_map/mix_back/pallas_call | solution.py:621
  174.6 2.7 fold_core.2
  177.3 4.8 %collective-permute-done.40.refs_6_ = bf16[192,256]{1,0:T(8,128)(2,1)S(1)} collective-permute-done((bf16[192,256]{1,0:T(8,128)(2,1)S(1)}, bf16[192,256]{1,0:T(8,128)(2,1)S(1)}, u32[]{:S(2)}, u32[]{:S(2)}) %collective-permute-start.40) | collective-permute-done | bytes 98336 | tf_op jit(solution)/shard_map/ppermute | solution.py:63
  183.7 14.2 %attend_back.1 = (bf16[576,256]{1,0:T(8,128)(2,1)S(1)}, bf16[576,256]{1,0:T(8,128)(2,1)}, bf16[576,256]{1,0:T(8,128)(2,1)}, bf16[576,256]{1,0:T(8,128)(2,1)}) custom-call(s32[4]{0:T(128)S(1)} %pad_add_fusion.ids, s32[2]{0:T(128)S(1)} %copy-done.9, f32[12]{0:T(128)S(1)} %copy-done.12, bf16[576,256]{1,0:T(8,128)(2,1)S(1)} %get-tuple-element.114.refs_0_, ...), custom_call_target="tpu_custom_call" | custom-call | flops 4026531840 | bytes 5000000 | tf_op jit(solution)/shard_map/attend_back/pallas_call | solution.py:308
  203.2 18.4 %collective-permute-done.46.refs_0_ = bf16[192,4608]{1,0:T(8,128)(2,1)S(1)} collective-permute-done((bf16[192,4608]{1,0:T(8,128)(2,1)}, bf16[192,4608]{1,0:T(8,128)(2,1)S(1)}, u32[]{:S(2)}, u32[]{:S(2)}) %collective-permute-start.46) | collective-permute-done | bytes 1769504 | tf_op jit(solution)/shard_map/ppermute | solution.py:63
  225.9 4.0 %project_back.1 = (bf16[512,768]{1,0:T(8,128)(2,1)S(1)}, bf16[400,1536]{1,0:T(8,128)(2,1)S(1)}, bf16[400,1536]{1,0:T(8,128)(2,1)S(1)}) custom-call(s32[4]{0:T(128)S(1)} %pad_add_fusion.ids, bf16[512,768]{1,0:T(8,128)(2,1)S(1)} %bitcast.30, bf16[768,1152]{1,0:T(8,128)(2,1)S(1)} %copy-done.14, ...), custom_call_target="tpu_custom_call", output_to_operand_aliasing={{1}: (4, {}), {2}: (5, {})} | custom-call | flops 1811939328 | bytes 8000000 | tf_op jit(solution)/shard_map/project_back/pallas_call | solution.py:684
  231.6 4.7 %collective-permute-start.49 = (bf16[48,4608]{1,0:T(8,128)(2,1)S(1)}, bf16[48,4608]{1,0:T(8,128)(2,1)S(1)}, u32[]{:S(2)}, u32[]{:S(2)}) collective-permute-start(bf16[48,4608]{1,0:T(8,128)(2,1)S(1)} %get-tuple-element.196), channel_id=1, source_target_pairs={{0,2},{2,0},{4,6},{6,4},{1,3},{3,1},{5,7},{7,5},{8,10},{10,8},{12,... | collective-permute-start | bytes 1327112 | tf_op jit(solution)/shard_map/ppermute | solution.py:63
  240.1 9.8 %collective-permute-done.47 = bf16[512,768]{1,0:T(8,128)(2,1)S(1)} collective-permute-done((bf16[512,768]{1,0:T(8,128)(2,1)S(1)}, bf16[512,768]{1,0:T(8,128)(2,1)S(1)}, u32[]{:S(2)}, u32[]{:S(2)}) %collective-permute-start.47) | collective-permute-done | bytes 786464 | tf_op jit(solution)/shard_map/ppermute | solution.py:63
  254.0 4.9 %collective-permute-done.51.refs_1_ = bf16[208,768]{1,0:T(8,128)(2,1)S(1)} collective-permute-done((bf16[208,768]{1,0:T(8,128)(2,1)S(1)}, bf16[208,768]{1,0:T(8,128)(2,1)S(1)}, u32[]{:S(2)}, u32[]{:S(2)}) %collective-permute-start.51) | collective-permute-done | bytes 319520 | tf_op jit(solution)/shard_map/ppermute | solution.py:63
  259.7 4.1 %collective-permute-start.52 = (bf16[64,1536]{1,0:T(8,128)(2,1)S(1)}, bf16[64,1536]{1,0:T(8,128)(2,1)S(1)}, u32[]{:S(2)}, u32[]{:S(2)}) collective-permute-start(bf16[64,1536]{1,0:T(8,128)(2,1)S(1)} %get-tuple-element.201), channel_id=1, source_target_pairs={{0,2},{2,0},{4,6},{6,4},{1,3},{3,1},{5,7},{7,5},{8,10},{10,8},{12,... | collective-permute-start | bytes 589832 | tf_op jit(solution)/shard_map/ppermute | solution.py:63
  266.2 3.3 %collective-permute-done.55 = bf16[48,4608]{1,0:T(8,128)(2,1)S(1)} collective-permute-done((bf16[48,4608]{1,0:T(8,128)(2,1)S(1)}, bf16[48,4608]{1,0:T(8,128)(2,1)S(1)}, u32[]{:S(2)}, u32[]{:S(2)}) %collective-permute-start.55) | collective-permute-done | bytes 442400 | tf_op jit(solution)/shard_map/ppermute | solution.py:63
  272.0 19.4 %collective-permute-done.53 = bf16[64,1536]{1,0:T(8,128)(2,1)S(1)} collective-permute-done((bf16[64,1536]{1,0:T(8,128)(2,1)S(1)}, bf16[64,1536]{1,0:T(8,128)(2,1)S(1)}, u32[]{:S(2)}, u32[]{:S(2)}) %collective-permute-start.53) | collective-permute-done | bytes 196640 | tf_op jit(solution)/shard_map/ppermute | solution.py:63
  (177 shorter events, 87.6 us)
Async XLA Ops:
  4.8 11.3 %collective-permute-start.1 = (bf16[48,1152]{1,0:T(8,128)(2,1)S(1)}, bf16[48,1152]{1,0:T(8,128)(2,1)S(1)}, u32[]{:S(2)}, u32[]{:S(2)}) collective-permute-start(bf16[48,1152]{1,0:T(8,128)(2,1)S(1)} %bitcast.36), channel_id=1, source_target_pairs={{0,4},{2,6},{4,0},{6,2},{1,5},{3,7},{5,1},{7,3},{8,12},{10,14},{12... | collective-permute-start | bytes 331784 | tf_op jit(solution)/shard_map/ppermute | solution.py:63
  18.2 15.7 %collective-permute-start.3 = (bf16[48,3456]{1,0:T(8,128)(2,1)S(1)}, bf16[48,3456]{1,0:T(8,128)(2,1)S(1)}, u32[]{:S(2)}, u32[]{:S(2)}) collective-permute-start(bf16[48,3456]{1,0:T(8,128)(2,1)S(1)} %pad_maximum_fusion.1), channel_id=1, source_target_pairs={{0,2},{2,0},{4,6},{6,4},{1,3},{3,1},{5,7},{7,5},{8,10},{10,8},{12,... | collective-permute-start | bytes 995336 | tf_op jit(solution)/shard_map/ppermute | solution.py:63
  20.0 25.9 %collective-permute-start.4 = (bf16[48,3456]{1,0:T(8,128)(2,1)S(1)}, bf16[48,3456]{1,0:T(8,128)(2,1)}, u32[]{:S(2)}, u32[]{:S(2)}) collective-permute-start(bf16[48,3456]{1,0:T(8,128)(2,1)S(1)} %pad_maximum_fusion.1), channel_id=1, source_target_pairs={{0,4},{2,6},{4,0},{6,2},{1,5},{3,7},{5,1},{7,3},{8,12},{10,14},{12... | collective-permute-start | bytes 995336 | tf_op jit(solution)/shard_map/ppermute | solution.py:63
  22.0 23.8 %collective-permute-start.5 = (bf16[48,3456]{1,0:T(8,128)(2,1)S(1)}, bf16[48,3456]{1,0:T(8,128)(2,1)}, u32[]{:S(2)}, u32[]{:S(2)}) collective-permute-start(bf16[48,3456]{1,0:T(8,128)(2,1)S(1)} %pad_maximum_fusion.1), channel_id=1, source_target_pairs={{0,6},{2,4},{4,2},{6,0},{1,7},{3,5},{5,3},{7,1},{8,14},{10,12},{12... | collective-permute-start | bytes 995336 | tf_op jit(solution)/shard_map/ppermute | solution.py:63
  48.0 45.3 %collective-permute-start.18 = (bf16[192,3456]{1,0:T(8,128)(2,1)S(1)}, bf16[192,3456]{1,0:T(8,128)(2,1)S(1)}, u32[]{:S(2)}, u32[]{:S(2)}) collective-permute-start(bf16[192,3456]{1,0:T(8,128)(2,1)S(1)} %constant_dynamic-update-slice_fusion.refs_0_), channel_id=1, source_target_pairs={{0,16},{8,24},{16,0},{24,8},{1,17},{9,25},{17,1},{25,9},{2,18},{10... | collective-permute-start | bytes 3981320 | tf_op jit(solution)/shard_map/ppermute | solution.py:63
  49.6 13.6 %collective-permute-start.19 = (bf16[576,256]{1,0:T(8,128)(2,1)S(1)}, bf16[576,256]{1,0:T(8,128)(2,1)S(1)}, u32[]{:S(2)}, u32[]{:S(2)}) collective-permute-start(bf16[576,256]{1,0:T(8,128)(2,1)S(1)} %get-tuple-element.115), channel_id=1, source_target_pairs={{0,2},{2,0},{4,6},{6,4},{1,3},{3,1},{5,7},{7,5},{8,10},{10,8},{12,... | collective-permute-start | bytes 884744 | tf_op jit(solution)/shard_map/ppermute | solution.py:63
  54.7 22.5 %collective-permute-start.20 = (bf16[576,256]{1,0:T(8,128)(2,1)S(1)}, bf16[576,256]{1,0:T(8,128)(2,1)S(1)}, u32[]{:S(2)}, u32[]{:S(2)}) collective-permute-start(bf16[576,256]{1,0:T(8,128)(2,1)S(1)} %get-tuple-element.116), channel_id=1, source_target_pairs={{0,4},{2,6},{4,0},{6,2},{1,5},{3,7},{5,1},{7,3},{8,12},{10,14},{12... | collective-permute-start | bytes 884744 | tf_op jit(solution)/shard_map/ppermute | solution.py:63
  55.6 21.5 %collective-permute-start.21 = (bf16[576,256]{1,0:T(8,128)(2,1)S(1)}, bf16[576,256]{1,0:T(8,128)(2,1)S(1)}, u32[]{:S(2)}, u32[]{:S(2)}) collective-permute-start(bf16[576,256]{1,0:T(8,128)(2,1)S(1)} %get-tuple-element.117), channel_id=1, source_target_pairs={{0,6},{2,4},{4,2},{6,0},{1,7},{3,5},{5,3},{7,1},{8,14},{10,12},{12... | collective-permute-start | bytes 884744 | tf_op jit(solution)/shard_map/ppermute | solution.py:63
  77.2 16.1 %collective-permute-start.28 = (bf16[48,1536]{1,0:T(8,128)(2,1)S(1)}, bf16[48,1536]{1,0:T(8,128)(2,1)S(1)}, u32[]{:S(2)}, u32[]{:S(2)}) collective-permute-start(bf16[48,1536]{1,0:T(8,128)(2,1)S(1)} %convert_bitcast_fusion), channel_id=1, source_target_pairs={{0,2},{2,0},{4,6},{6,4},{1,3},{3,1},{5,7},{7,5},{8,10},{10,8},{12,... | collective-permute-start | bytes 442376 | tf_op jit(solution)/shard_map/ppermute | solution.py:63
  81.0 12.3 %collective-permute-start.29 = (bf16[48,1536]{1,0:T(8,128)(2,1)S(1)}, bf16[48,1536]{1,0:T(8,128)(2,1)S(1)}, u32[]{:S(2)}, u32[]{:S(2)}) collective-permute-start(bf16[48,1536]{1,0:T(8,128)(2,1)S(1)} %convert_bitcast_fusion), channel_id=1, source_target_pairs={{0,4},{2,6},{4,0},{6,2},{1,5},{3,7},{5,1},{7,3},{8,12},{10,14},{12... | collective-permute-start | bytes 442376 | tf_op jit(solution)/shard_map/ppermute | solution.py:63
  81.9 11.4 %collective-permute-start.30 = (bf16[48,1536]{1,0:T(8,128)(2,1)S(1)}, bf16[48,1536]{1,0:T(8,128)(2,1)S(1)}, u32[]{:S(2)}, u32[]{:S(2)}) collective-permute-start(bf16[48,1536]{1,0:T(8,128)(2,1)S(1)} %convert_bitcast_fusion), channel_id=1, source_target_pairs={{0,6},{2,4},{4,2},{6,0},{1,7},{3,5},{5,3},{7,1},{8,14},{10,12},{12... | collective-permute-start | bytes 442376 | tf_op jit(solution)/shard_map/ppermute | solution.py:63
  94.0 16.0 %collective-permute-start.31 = (bf16[192,1536]{1,0:T(8,128)(2,1)S(1)}, bf16[192,1536]{1,0:T(8,128)(2,1)S(1)}, u32[]{:S(2)}, u32[]{:S(2)}) collective-permute-start(bf16[192,1536]{1,0:T(8,128)(2,1)S(1)} %constant_dynamic-update-slice_fusion.4.refs_0_), channel_id=1, source_target_pairs={{0,16},{8,24},{16,0},{24,8},{1,17},{9,25},{17,1},{25,9},{2,18},{10... | collective-permute-start | bytes 1769480 | tf_op jit(solution)/shard_map/ppermute | solution.py:63
  110.5 12.0 %collective-permute-start.27 = (bf16[256,768]{1,0:T(8,128)(2,1)S(1)}, bf16[256,768]{1,0:T(8,128)(2,1)S(1)}, u32[]{:S(2)}, u32[]{:S(2)}) collective-permute-start(bf16[256,768]{1,0:T(8,128)(2,1)S(1)} %get-tuple-element.124.own.refs_0_), channel_id=1, source_target_pairs={{0,1},{1,0},{2,3},{3,2},{4,5},{5,4},{6,7},{7,6},{8,9},{9,8},{10,11... | collective-permute-start | bytes 1179656 | tf_op jit(solution)/shard_map/ppermute | solution.py:63
  112.1 18.9 %collective-permute-start.35 = (bf16[256,768]{1,0:T(8,128)(2,1)S(1)}, bf16[256,768]{1,0:T(8,128)(2,1)S(1)}, u32[]{:S(2)}, u32[]{:S(2)}) collective-permute-start(bf16[256,768]{1,0:T(8,128)(2,1)S(1)} %get-tuple-element.137.own.refs_1_), channel_id=1, source_target_pairs={{0,1},{1,0},{2,3},{3,2},{4,5},{5,4},{6,7},{7,6},{8,9},{9,8},{10,11... | collective-permute-start | bytes 1179656 | tf_op jit(solution)/shard_map/ppermute | solution.py:63
  126.8 12.6 %collective-permute-start.34 = (bf16[256,768]{1,0:T(8,128)(2,1)S(1)}, bf16[256,768]{1,0:T(8,128)(2,1)S(1)}, u32[]{:S(2)}, u32[]{:S(2)}) collective-permute-start(bf16[256,768]{1,0:T(8,128)(2,1)S(1)} %get-tuple-element.133.own), channel_id=1, source_target_pairs={{0,1},{1,0},{2,3},{3,2},{4,5},{5,4},{6,7},{7,6},{8,9},{9,8},{10,11... | collective-permute-start | bytes 1179656 | tf_op jit(solution)/shard_map/ppermute | solution.py:63
  135.2 12.6 %collective-permute-start.36 = (bf16[256,768]{1,0:T(8,128)(2,1)S(1)}, bf16[256,768]{1,0:T(8,128)(2,1)S(1)}, u32[]{:S(2)}, u32[]{:S(2)}) collective-permute-start(bf16[256,768]{1,0:T(8,128)(2,1)S(1)} %get-tuple-element.139.own), channel_id=1, source_target_pairs={{0,1},{1,0},{2,3},{3,2},{4,5},{5,4},{6,7},{7,6},{8,9},{9,8},{10,11... | collective-permute-start | bytes 1179656 | tf_op jit(solution)/shard_map/ppermute | solution.py:63
  144.7 17.7 %collective-permute-start.37 = (bf16[256,768]{1,0:T(8,128)(2,1)S(1)}, bf16[256,768]{1,0:T(8,128)(2,1)S(1)}, u32[]{:S(2)}, u32[]{:S(2)}) collective-permute-start(bf16[256,768]{1,0:T(8,128)(2,1)S(1)} %get-tuple-element.146.refs_6_), channel_id=1, source_target_pairs={{0,1},{1,0},{2,3},{3,2},{4,5},{5,4},{6,7},{7,6},{8,9},{9,8},{10,11... | collective-permute-start | bytes 1179656 | tf_op jit(solution)/shard_map/ppermute | solution.py:63
  153.2 10.5 %collective-permute-start.38 = (bf16[256,768]{1,0:T(8,128)(2,1)S(1)}, bf16[256,768]{1,0:T(8,128)(2,1)S(1)}, u32[]{:S(2)}, u32[]{:S(2)}) collective-permute-start(bf16[256,768]{1,0:T(8,128)(2,1)S(1)} %get-tuple-element.147.refs_7_), channel_id=1, source_target_pairs={{0,1},{1,0},{2,3},{3,2},{4,5},{5,4},{6,7},{7,6},{8,9},{9,8},{10,11... | collective-permute-start | bytes 1179656 | tf_op jit(solution)/shard_map/ppermute | solution.py:63
  163.7 10.9 %collective-permute-start.42 = (bf16[384,4608]{1,0:T(8,128)(2,1)S(1)}, bf16[384,4608]{1,0:T(8,128)(2,1)S(1)}, u32[]{:S(2)}, u32[]{:S(2)}) collective-permute-start(bf16[384,4608]{1,0:T(8,128)(2,1)S(1)} %get-tuple-element.172), channel_id=1, source_target_pairs={{0,8},{8,0},{16,24},{24,16},{1,9},{9,1},{17,25},{25,17},{2,10},{10... | collective-permute-start | bytes 10616840 | tf_op jit(solution)/shard_map/ppermute | solution.py:63
  171.3 10.8 %collective-permute-start.40 = (bf16[192,256]{1,0:T(8,128)(2,1)S(1)}, bf16[192,256]{1,0:T(8,128)(2,1)S(1)}, u32[]{:S(2)}, u32[]{:S(2)}) collective-permute-start(bf16[192,256]{1,0:T(8,128)(2,1)S(1)} %get-tuple-element.169), channel_id=1, source_target_pairs={{0,4},{2,6},{4,0},{6,2},{1,5},{3,7},{5,1},{7,3},{8,12},{10,14},{12... | collective-permute-start | bytes 294920 | tf_op jit(solution)/shard_map/ppermute | solution.py:63
  182.1 39.5 %collective-permute-start.46 = (bf16[192,4608]{1,0:T(8,128)(2,1)}, bf16[192,4608]{1,0:T(8,128)(2,1)S(1)}, u32[]{:S(2)}, u32[]{:S(2)}) collective-permute-start(bf16[192,4608]{1,0:T(8,128)(2,1)} %get-tuple-element.186), channel_id=1, source_target_pairs={{0,16},{8,24},{16,0},{24,8},{1,17},{9,25},{17,1},{25,9},{2,18},{10... | collective-permute-start | bytes 5308424 | tf_op jit(solution)/shard_map/ppermute | solution.py:63
  198.7 26.9 %collective-permute-start.43 = (bf16[576,256]{1,0:T(8,128)(2,1)}, bf16[576,256]{1,0:T(8,128)(2,1)}, u32[]{:S(2)}, u32[]{:S(2)}) collective-permute-start(bf16[576,256]{1,0:T(8,128)(2,1)} %get-tuple-element.182), channel_id=1, source_target_pairs={{0,2},{2,0},{4,6},{6,4},{1,3},{3,1},{5,7},{7,5},{8,10},{10,8},{12,... | collective-permute-start | bytes 884744 | tf_op jit(solution)/shard_map/ppermute | solution.py:63
  200.7 24.8 %collective-permute-start.44 = (bf16[576,256]{1,0:T(8,128)(2,1)}, bf16[576,256]{1,0:T(8,128)(2,1)}, u32[]{:S(2)}, u32[]{:S(2)}) collective-permute-start(bf16[576,256]{1,0:T(8,128)(2,1)} %get-tuple-element.183), channel_id=1, source_target_pairs={{0,4},{2,6},{4,0},{6,2},{1,5},{3,7},{5,1},{7,3},{8,12},{10,14},{12... | collective-permute-start | bytes 884744 | tf_op jit(solution)/shard_map/ppermute | solution.py:63
  200.7 24.8 %collective-permute-start.45 = (bf16[576,256]{1,0:T(8,128)(2,1)}, bf16[576,256]{1,0:T(8,128)(2,1)}, u32[]{:S(2)}, u32[]{:S(2)}) collective-permute-start(bf16[576,256]{1,0:T(8,128)(2,1)} %get-tuple-element.184), channel_id=1, source_target_pairs={{0,6},{2,4},{4,2},{6,0},{1,7},{3,5},{5,3},{7,1},{8,14},{10,12},{12... | collective-permute-start | bytes 884744 | tf_op jit(solution)/shard_map/ppermute | solution.py:63
  230.0 19.9 %collective-permute-start.47 = (bf16[512,768]{1,0:T(8,128)(2,1)S(1)}, bf16[512,768]{1,0:T(8,128)(2,1)S(1)}, u32[]{:S(2)}, u32[]{:S(2)}) collective-permute-start(bf16[512,768]{1,0:T(8,128)(2,1)S(1)} %get-tuple-element.192), channel_id=1, source_target_pairs={{0,1},{1,0},{2,3},{3,2},{4,5},{5,4},{6,7},{7,6},{8,9},{9,8},{10,11... | collective-permute-start | bytes 2359304 | tf_op jit(solution)/shard_map/ppermute | solution.py:63
  231.6 22.5 %collective-permute-start.49 = (bf16[48,4608]{1,0:T(8,128)(2,1)S(1)}, bf16[48,4608]{1,0:T(8,128)(2,1)S(1)}, u32[]{:S(2)}, u32[]{:S(2)}) collective-permute-start(bf16[48,4608]{1,0:T(8,128)(2,1)S(1)} %get-tuple-element.196), channel_id=1, source_target_pairs={{0,2},{2,0},{4,6},{6,4},{1,3},{3,1},{5,7},{7,5},{8,10},{10,8},{12,... | collective-permute-start | bytes 1327112 | tf_op jit(solution)/shard_map/ppermute | solution.py:63
  236.3 33.3 %collective-permute-start.55 = (bf16[48,4608]{1,0:T(8,128)(2,1)S(1)}, bf16[48,4608]{1,0:T(8,128)(2,1)S(1)}, u32[]{:S(2)}, u32[]{:S(2)}) collective-permute-start(bf16[48,4608]{1,0:T(8,128)(2,1)S(1)} %get-tuple-element.206), channel_id=1, source_target_pairs={{0,4},{2,6},{4,0},{6,2},{1,5},{3,7},{5,1},{7,3},{8,12},{10,14},{12... | collective-permute-start | bytes 1327112 | tf_op jit(solution)/shard_map/ppermute | solution.py:63
  236.3 33.3 %collective-permute-start.56 = (bf16[48,4608]{1,0:T(8,128)(2,1)S(1)}, bf16[48,4608]{1,0:T(8,128)(2,1)S(1)}, u32[]{:S(2)}, u32[]{:S(2)}) collective-permute-start(bf16[48,4608]{1,0:T(8,128)(2,1)S(1)} %get-tuple-element.207), channel_id=1, source_target_pairs={{0,6},{2,4},{4,2},{6,0},{1,7},{3,5},{5,3},{7,1},{8,14},{10,12},{12... | collective-permute-start | bytes 1327112 | tf_op jit(solution)/shard_map/ppermute | solution.py:63
  239.9 14.2 %collective-permute-start.50 = (bf16[208,768]{1,0:T(8,128)(2,1)S(1)}, bf16[208,768]{1,0:T(8,128)(2,1)S(1)}, u32[]{:S(2)}, u32[]{:S(2)}) collective-permute-start(bf16[208,768]{1,0:T(8,128)(2,1)S(1)} %get-tuple-element.197), channel_id=1, source_target_pairs={{0,16},{8,24},{16,0},{24,8},{1,17},{9,25},{17,1},{25,9},{2,18},{10... | collective-permute-start | bytes 958472 | tf_op jit(solution)/shard_map/ppermute | solution.py:63
  259.7 12.3 %collective-permute-start.52 = (bf16[64,1536]{1,0:T(8,128)(2,1)S(1)}, bf16[64,1536]{1,0:T(8,128)(2,1)S(1)}, u32[]{:S(2)}, u32[]{:S(2)}) collective-permute-start(bf16[64,1536]{1,0:T(8,128)(2,1)S(1)} %get-tuple-element.201), channel_id=1, source_target_pairs={{0,2},{2,0},{4,6},{6,4},{1,3},{3,1},{5,7},{7,5},{8,10},{10,8},{12,... | collective-permute-start | bytes 589832 | tf_op jit(solution)/shard_map/ppermute | solution.py:63
  263.8 27.6 %collective-permute-start.53 = (bf16[64,1536]{1,0:T(8,128)(2,1)S(1)}, bf16[64,1536]{1,0:T(8,128)(2,1)S(1)}, u32[]{:S(2)}, u32[]{:S(2)}) collective-permute-start(bf16[64,1536]{1,0:T(8,128)(2,1)S(1)} %get-tuple-element.202), channel_id=1, source_target_pairs={{0,4},{2,6},{4,0},{6,2},{1,5},{3,7},{5,1},{7,3},{8,12},{10,14},{12... | collective-permute-start | bytes 589832 | tf_op jit(solution)/shard_map/ppermute | solution.py:63
  263.8 27.6 %collective-permute-start.54 = (bf16[64,1536]{1,0:T(8,128)(2,1)S(1)}, bf16[64,1536]{1,0:T(8,128)(2,1)S(1)}, u32[]{:S(2)}, u32[]{:S(2)}) collective-permute-start(bf16[64,1536]{1,0:T(8,128)(2,1)S(1)} %get-tuple-element.203), channel_id=1, source_target_pairs={{0,6},{2,4},{4,2},{6,0},{1,7},{3,5},{5,3},{7,1},{8,14},{10,12},{12... | collective-permute-start | bytes 589832 | tf_op jit(solution)/shard_map/ppermute | solution.py:63
  (44 other events, 364.1 us)

commit v7 on v6

--- a/solution.py
+++ b/solution.py
@@ -617,18 +617,17 @@
     width = heads * HD
     size = seqs * heads // n * HD
     rows = model // 2 + EXTRA
-    last = pl.BlockSpec((rows, width), lambda i: (0, 3))
     return pl.pallas_call(
         functools.partial(mix_back_kernel, n, seqs, heads),
         grid=(1,),
         out_shape=[shape((size, slots), bf16)] * n
         + [shape((tokens, model), f32)]
-        + [shape((rows, 4 * width), bf16)] * 2
+        + [shape((rows, width), bf16)] * 2
         + [shape((8, model), f32)],
         in_specs=[SMEM, VMEM, VMEM]
         + [pl.BlockSpec((model, width), lambda i: (0, front.shape[1] // width - 1)), VMEM]
         + [VMEM] * (5 * seqs),
-        out_specs=[VMEM] * (n + 1) + [last, last, VMEM],
+        out_specs=[VMEM] * (n + 4),
         scratch_shapes=[
             pltpu.VMEM((size * n, slots), bf16),
             pltpu.VMEM((model, tokens), bf16),
@@ -672,9 +671,10 @@
     row = lax.broadcasted_iota(jnp.int32, (8, 1), 0)
     rows = jnp.where(row == 6, line, small[...])
     rows = jnp.concatenate([rows, jnp.zeros_like(rows)], axis=0).astype(bf16)
-    for ref in (send, keep):
-        ref[ref.shape[0] - EXTRA :, :] = jnp.zeros((EXTRA, ref.shape[1]), bf16)
+    for ref, before in ((send, far), (keep, near)):
         ref[ref.shape[0] - EXTRA :, : 2 * width] = rows
+        ref[ref.shape[0] - EXTRA :, 2 * width : 3 * width] = jnp.zeros((EXTRA, width), bf16)
+        ref[:, 3 * width :] = before[...]
 
 
 def project_back(ids, tok, whole, small, grads, blocks, n, seqs, heads):
@@ -683,18 +683,16 @@
     wide = whole.shape[1]
     return pl.pallas_call(
         functools.partial(project_back_kernel, n, seqs, heads),
-        grid=(1,),
-        out_shape=[shape((tokens, model), bf16)] + [shape(grads[0].shape, bf16)] * 2,
-        in_specs=[SMEM] + [VMEM] * 3 + [pl.BlockSpec(memory_space=pl.ANY)] * 2 + [VMEM] * n,
-        out_specs=[VMEM] + [pl.BlockSpec((grads[0].shape[0], wide), lambda i: (0, 0))] * 2,
-        input_output_aliases={4: 1, 5: 2},
+        out_shape=[shape((tokens, model), bf16)] + [shape((grads[0].shape[0], 4 * heads * HD), bf16)] * 2,
+        in_specs=[SMEM] + [VMEM] * (5 + n),
+        out_specs=[VMEM] * 3,
         scratch_shapes=[
             pltpu.VMEM((seqs * heads * 3 * HD, slots), bf16),
             pltpu.VMEM((tokens, wide), bf16),
             pltpu.VMEM((model, tokens), bf16),
             pltpu.VMEM((model, tokens), bf16),
         ],
-        compiler_params=params("arbitrary"),
+        compiler_params=params(),
         cost_estimate=cost(4 * tokens * model * wide, 8e6),
         name="project_back",
     )(ids, tok, whole, small, *grads, *blocks)

time: 295 us -> 293 us (level)
  starting transfers between devices: 76 us -> 68.3 us
  waiting for transfers between devices: 127 us -> 132 us
    ppermute x57, starting transfers between devices: 76 us -> 68.3 us  [swap(): return lax.ppermute(value, axis, xor_pairs(axis, distance))]
    ppermute x57, waiting for transfers between devices: 127 us -> 132 us  [swap(): return lax.ppermute(value, axis, xor_pairs(axis, distance))]
  transfers between devices with their start and end apart: 57 -> 57, of which waited for: 26 -> 26; matrix products, arithmetic and copies ran while one was open for 2% -> 2% of each run, Pallas kernels for 22% -> 23%
where the time goes in v7:
time: 293 us; the launch traced here: 290 us
  waiting for transfers between devices  132 us (45%)
  Pallas kernels  69.4 us (24%)
  starting transfers between devices  68.3 us (23%)
  local copies, waits for them, and re-layouts  13.5 us (5%)
  other arithmetic  5.86 us (2%)
    ppermute x57, waiting for transfers between devices, swap(): return lax.ppermute(value, axis, xor_pairs(axis, distance))  132 us
    ppermute x57, starting transfers between devices, swap(): return lax.ppermute(value, axis, xor_pairs(axis, distance))  68.3 us
    pallas_call x1, Pallas kernels, attend_back(): pl.pallas_call(functools.partial(attend_back_kernel, n, heads), grid=(per...  14.2 us
    pallas_call x2, Pallas kernels, unit_back(): pl.pallas_call(functools.partial(unit_back_kernel, n, s), grid=(steps,),...  10.7 us
    pallas_call x1, Pallas kernels, attend(): pl.pallas_call(functools.partial(attend_kernel, n, heads), grid=(per,), o...  9.95 us
    pallas_call x2, Pallas kernels, unit(): pl.pallas_call(unit_kernel, grid=(steps,), out_shape=[shape((tokens, mode...  8.4 us
    unnamed x45, local copies, waits for them, and re-layouts  7.76 us
    pallas_call x1, Pallas kernels, weight_grads(): pl.pallas_call(functools.partial(weight_kernel, steps, seqs), grid=(3 * s...  7.68 us
  transfers between devices with their start and end apart: 57, of which 26 were waited for; matrix products, arithmetic and copies ran while one was open for 2% of the time, Pallas kernels for 23%

profile of v7, /device:TPU:0, one launch (start us, length us, event | category | flops | bytes accessed | tf_op | source)
XLA Modules:
  0.0 289.8 jit_solution(6715925854710455499)
XLA Ops:
  1.6 3.1 %collective-permute-start = (bf16[48,1152]{1,0:T(8,128)(2,1)S(1)}, bf16[48,1152]{1,0:T(8,128)(2,1)S(1)}, u32[]{:S(2)}, u32[]{:S(2)}) collective-permute-start(bf16[48,1152]{1,0:T(8,128)(2,1)S(1)} %bitcast.35), channel_id=1, source_target_pairs={{0,2},{2,0},{4,6},{6,4},{1,3},{3,1},{5,7},{7,5},{8,10},{10,8},{12,... | collective-permute-start | bytes 331784 | tf_op jit(solution)/shard_map/ppermute | solution.py:63
  4.8 2.6 collective-permute-start.1
  11.7 4.4 %collective-permute-done.1.refs_2_ = bf16[48,1152]{1,0:T(8,128)(2,1)S(1)} collective-permute-done((bf16[48,1152]{1,0:T(8,128)(2,1)S(1)}, bf16[48,1152]{1,0:T(8,128)(2,1)S(1)}, u32[]{:S(2)}, u32[]{:S(2)}) %collective-permute-start.1) | collective-permute-done | bytes 110624 | tf_op jit(solution)/shard_map/ppermute | solution.py:63
  22.0 2.5 collective-permute-start.5
  33.9 12.0 %collective-permute-done.4 = bf16[48,3456]{1,0:T(8,128)(2,1)} collective-permute-done((bf16[48,3456]{1,0:T(8,128)(2,1)S(1)}, bf16[48,3456]{1,0:T(8,128)(2,1)}, u32[]{:S(2)}, u32[]{:S(2)}) %collective-permute-start.4) | collective-permute-done | bytes 331808 | tf_op jit(solution)/shard_map/ppermute | solution.py:63
  49.6 5.0 %collective-permute-start.19 = (bf16[576,256]{1,0:T(8,128)(2,1)S(1)}, bf16[576,256]{1,0:T(8,128)(2,1)S(1)}, u32[]{:S(2)}, u32[]{:S(2)}) collective-permute-start(bf16[576,256]{1,0:T(8,128)(2,1)S(1)} %get-tuple-element.115), channel_id=1, source_target_pairs={{0,2},{2,0},{4,6},{6,4},{1,3},{3,1},{5,7},{7,5},{8,10},{10,8},{12,... | collective-permute-start | bytes 884744 | tf_op jit(solution)/shard_map/ppermute | solution.py:63
  57.1 6.1 %collective-permute-done.19.refs_1_ = bf16[576,256]{1,0:T(8,128)(2,1)S(1)} collective-permute-done((bf16[576,256]{1,0:T(8,128)(2,1)S(1)}, bf16[576,256]{1,0:T(8,128)(2,1)S(1)}, u32[]{:S(2)}, u32[]{:S(2)}) %collective-permute-start.19) | collective-permute-done | bytes 294944 | tf_op jit(solution)/shard_map/ppermute | solution.py:63
  63.2 13.9 %collective-permute-done.20.refs_2_ = bf16[576,256]{1,0:T(8,128)(2,1)S(1)} collective-permute-done((bf16[576,256]{1,0:T(8,128)(2,1)S(1)}, bf16[576,256]{1,0:T(8,128)(2,1)S(1)}, u32[]{:S(2)}, u32[]{:S(2)}) %collective-permute-start.20) | collective-permute-done | bytes 294944 | tf_op jit(solution)/shard_map/ppermute | solution.py:63
  77.2 3.8 %collective-permute-start.28 = (bf16[48,1536]{1,0:T(8,128)(2,1)S(1)}, bf16[48,1536]{1,0:T(8,128)(2,1)S(1)}, u32[]{:S(2)}, u32[]{:S(2)}) collective-permute-start(bf16[48,1536]{1,0:T(8,128)(2,1)S(1)} %convert_bitcast_fusion), channel_id=1, source_target_pairs={{0,2},{2,0},{4,6},{6,4},{1,3},{3,1},{5,7},{7,5},{8,10},{10,8},{12,... | collective-permute-start | bytes 442376 | tf_op jit(solution)/shard_map/ppermute | solution.py:63
  83.4 9.9 %attend.1 = (bf16[192,256]{1,0:T(8,128)(2,1)S(1)}, bf16[192,256]{1,0:T(8,128)(2,1)S(1)}, bf16[192,256]{1,0:T(8,128)(2,1)S(1)}, bf16[192,256]{1,0:T(8,128)(2,1)S(...) custom-call(s32[4]{0:T(128)S(1)} %pad_add_fusion.ids, s32[2]{0:T(128)S(1)} %copy-done.7, f32[12]{0:T(128)S(1)} %copy-done.12, ...), custom_call_target="tpu_custom_call" | custom-call | flops 1610612736 | bytes 3000000 | tf_op jit(solution)/shard_map/attend/pallas_call | solution.py:226
  100.3 5.8 %collective-permute-done.25.refs_2_ = bf16[192,256]{1,0:T(8,128)(2,1)S(1)} collective-permute-done((bf16[192,256]{1,0:T(8,128)(2,1)S(1)}, bf16[192,256]{1,0:T(8,128)(2,1)S(1)}, u32[]{:S(2)}, u32[]{:S(2)}) %collective-permute-start.25) | collective-permute-done | bytes 98336 | tf_op jit(solution)/shard_map/ppermute | solution.py:63
  107.2 2.2 collective-permute-done.31.refs_2_
  113.3 8.6 %collective-permute-done.27.other.refs_2_ = bf16[256,768]{1,0:T(8,128)(2,1)S(1)} collective-permute-done((bf16[256,768]{1,0:T(8,128)(2,1)S(1)}, bf16[256,768]{1,0:T(8,128)(2,1)S(1)}, u32[]{:S(2)}, u32[]{:S(2)}) %collective-permute-start.27) | collective-permute-done | bytes 393248 | tf_op jit(solution)/shard_map/ppermute | solution.py:63
  121.9 4.2 %unit.2 = (f32[256,768]{1,0:T(8,128)S(1)}, bf16[256,768]{1,0:T(8,128)(2,1)S(1)}, bf16[256,1536]{1,0:T(8,128)(2,1)S(1)}, bf16[256,1536]{1,0:T(8,128)(2,1)S(1)}, b...) custom-call(bf16[512,768]{1,0:T(8,128)(2,1)S(1)} %bitcast.27, ...), custom_call_target="tpu_custom_call" | custom-call | flops 1811939328 | bytes 13000000 | tf_op jit(solution)/shard_map/unit/pallas_call | solution.py:411
  127.7 2.6 collective-permute-done.35.other.refs_3_
  130.3 4.2 %unit.3 = (f32[256,768]{1,0:T(8,128)S(1)}, bf16[256,768]{1,0:T(8,128)(2,1)S(1)}, bf16[256,1536]{1,0:T(8,128)(2,1)S(1)}, bf16[256,1536]{1,0:T(8,128)(2,1)S(1)}, b...) custom-call(bf16[512,768]{1,0:T(8,128)(2,1)S(1)} %bitcast.28, ...), custom_call_target="tpu_custom_call" | custom-call | flops 1811939328 | bytes 13000000 | tf_op jit(solution)/shard_map/unit/pallas_call | solution.py:411
  136.1 2.7 collective-permute-done.34.other
  138.7 5.3 %unit_back.2 = (bf16[256,768]{1,0:T(8,128)(2,1)S(1)}, f32[256,768]{1,0:T(8,128)S(1)}, bf16[256,768]{1,0:T(8,128)(2,1)S(1)}, bf16[256,1536]{1,0:T(8,128)(2,1)S(1)...) custom-call(s32[4]{0:T(128)S(1)} %pad_add_fusion.ids, s32[2]{0:T(128)S(1)} %copy-done.7, ...), custom_call_target="tpu_custom_call" | custom-call | flops 1811939328 | bytes 14000000 | tf_op jit(solution)/shard_map/unit_back/pallas_call | solution.py:477
  147.2 5.3 %unit_back.3 = (bf16[256,768]{1,0:T(8,128)(2,1)S(1)}, f32[256,768]{1,0:T(8,128)S(1)}, bf16[256,768]{1,0:T(8,128)(2,1)S(1)}, bf16[256,1536]{1,0:T(8,128)(2,1)S(1)...) custom-call(s32[4]{0:T(128)S(1)} %pad_add_fusion.ids, s32[2]{0:T(128)S(1)} %copy-done.7, ...), custom_call_target="tpu_custom_call" | custom-call | flops 1811939328 | bytes 14000000 | tf_op jit(solution)/shard_map/unit_back/pallas_call | solution.py:477
  154.1 7.7 %weight_grads.1 = (bf16[384,4608]{1,0:T(8,128)(2,1)S(1)}, bf16[384,4608]{1,0:T(8,128)(2,1)S(1)}) custom-call(s32[4]{0:T(128)S(1)} %pad_add_fusion.ids, bf16[256,768]{1,0:T(8,128)(2,1)S(1)} %get-tuple-element.148.refs_0_, bf16[256,768]{1,0:T(8,128)(2,1)S(1)} %get-tuple-element.149.refs_1_, bf16[256,768]{1,0:T(8,128)(2,1)S(1)} %get-tuple-element.150.refs_2_, ...), custom_call_target="tpu_custom_call" | custom-call | flops 3623878656 | bytes 14000000 | tf_op jit(solution)/shard_map/weight_grads/pallas_call | solution.py:557
  163.1 3.1 %mix_back.1 = (bf16[192,256]{1,0:T(8,128)(2,1)S(1)}, bf16[192,256]{1,0:T(8,128)(2,1)S(1)}, bf16[192,256]{1,0:T(8,128)(2,1)S(1)}, bf16[192,256]{1,0:T(8,128)(2,1)...) custom-call(s32[4]{0:T(128)S(1)} %pad_add_fusion.ids, ...), custom_call_target="tpu_custom_call" | custom-call | flops 603979776 | bytes 10000000 | tf_op jit(solution)/shard_map/mix_back/pallas_call | solution.py:620
  173.1 2.7 fold_core.2
  175.8 4.9 %collective-permute-done.40.refs_6_ = bf16[192,256]{1,0:T(8,128)(2,1)S(1)} collective-permute-done((bf16[192,256]{1,0:T(8,128)(2,1)S(1)}, bf16[192,256]{1,0:T(8,128)(2,1)S(1)}, u32[]{:S(2)}, u32[]{:S(2)}) %collective-permute-start.40) | collective-permute-done | bytes 98336 | tf_op jit(solution)/shard_map/ppermute | solution.py:63
  180.8 14.2 %attend_back.1 = (bf16[576,256]{1,0:T(8,128)(2,1)S(1)}, bf16[576,256]{1,0:T(8,128)(2,1)}, bf16[576,256]{1,0:T(8,128)(2,1)}, bf16[576,256]{1,0:T(8,128)(2,1)}) custom-call(s32[4]{0:T(128)S(1)} %pad_add_fusion.ids, s32[2]{0:T(128)S(1)} %copy-done.7, f32[12]{0:T(128)S(1)} %copy-done.12, bf16[576,256]{1,0:T(8,128)(2,1)S(1)} %get-tuple-element.114.refs_0_, ...), custom_call_target="tpu_custom_call" | custom-call | flops 4026531840 | bytes 5000000 | tf_op jit(solution)/shard_map/attend_back/pallas_call | solution.py:308
  197.9 2.4 collective-permute-start.45
  200.4 19.9 %collective-permute-done.46.refs_0_ = bf16[192,4608]{1,0:T(8,128)(2,1)S(1)} collective-permute-done((bf16[192,4608]{1,0:T(8,128)(2,1)}, bf16[192,4608]{1,0:T(8,128)(2,1)S(1)}, u32[]{:S(2)}, u32[]{:S(2)}) %collective-permute-start.46) | collective-permute-done | bytes 1769504 | tf_op jit(solution)/shard_map/ppermute | solution.py:63
  224.2 3.8 %project_back.1 = (bf16[512,768]{1,0:T(8,128)(2,1)S(1)}, bf16[400,1536]{1,0:T(8,128)(2,1)S(1)}, bf16[400,1536]{1,0:T(8,128)(2,1)S(1)}) custom-call(s32[4]{0:T(128)S(1)} %pad_add_fusion.ids, bf16[512,768]{1,0:T(8,128)(2,1)S(1)} %bitcast.30, bf16[768,1152]{1,0:T(8,128)(2,1)S(1)} %copy-done.14, f32[8,768]{1,0:T(8,128)S(1)} %concatenate.20.small, ...), custom_call_target="tpu_custom_call" | custom-call | flops 1811939328 | bytes 8000000 | tf_op jit(solution)/shard_map/project_back/pallas_call | solution.py:684
  229.6 2.5 collective-permute-start.49
  236.8 11.3 %collective-permute-done.47 = bf16[512,768]{1,0:T(8,128)(2,1)S(1)} collective-permute-done((bf16[512,768]{1,0:T(8,128)(2,1)S(1)}, bf16[512,768]{1,0:T(8,128)(2,1)S(1)}, u32[]{:S(2)}, u32[]{:S(2)}) %collective-permute-start.47) | collective-permute-done | bytes 786464 | tf_op jit(solution)/shard_map/ppermute | solution.py:63
  251.6 5.4 %collective-permute-done.51.refs_1_ = bf16[208,768]{1,0:T(8,128)(2,1)S(1)} collective-permute-done((bf16[208,768]{1,0:T(8,128)(2,1)S(1)}, bf16[208,768]{1,0:T(8,128)(2,1)S(1)}, u32[]{:S(2)}, u32[]{:S(2)}) %collective-permute-start.51) | collective-permute-done | bytes 319520 | tf_op jit(solution)/shard_map/ppermute | solution.py:63
  257.8 2.5 collective-permute-start.52
  268.8 18.4 %collective-permute-done.53 = bf16[64,1536]{1,0:T(8,128)(2,1)S(1)} collective-permute-done((bf16[64,1536]{1,0:T(8,128)(2,1)S(1)}, bf16[64,1536]{1,0:T(8,128)(2,1)S(1)}, u32[]{:S(2)}, u32[]{:S(2)}) %collective-permute-start.53) | collective-permute-done | bytes 196640 | tf_op jit(solution)/shard_map/ppermute | solution.py:63
  (177 shorter events, 85.7 us)
Async XLA Ops:
  4.8 11.3 %collective-permute-start.1 = (bf16[48,1152]{1,0:T(8,128)(2,1)S(1)}, bf16[48,1152]{1,0:T(8,128)(2,1)S(1)}, u32[]{:S(2)}, u32[]{:S(2)}) collective-permute-start(bf16[48,1152]{1,0:T(8,128)(2,1)S(1)} %bitcast.36), channel_id=1, source_target_pairs={{0,4},{2,6},{4,0},{6,2},{1,5},{3,7},{5,1},{7,3},{8,12},{10,14},{12... | collective-permute-start | bytes 331784 | tf_op jit(solution)/shard_map/ppermute | solution.py:63
  18.2 15.7 %collective-permute-start.3 = (bf16[48,3456]{1,0:T(8,128)(2,1)S(1)}, bf16[48,3456]{1,0:T(8,128)(2,1)S(1)}, u32[]{:S(2)}, u32[]{:S(2)}) collective-permute-start(bf16[48,3456]{1,0:T(8,128)(2,1)S(1)} %pad_maximum_fusion.1), channel_id=1, source_target_pairs={{0,2},{2,0},{4,6},{6,4},{1,3},{3,1},{5,7},{7,5},{8,10},{10,8},{12,... | collective-permute-start | bytes 995336 | tf_op jit(solution)/shard_map/ppermute | solution.py:63
  20.0 25.9 %collective-permute-start.4 = (bf16[48,3456]{1,0:T(8,128)(2,1)S(1)}, bf16[48,3456]{1,0:T(8,128)(2,1)}, u32[]{:S(2)}, u32[]{:S(2)}) collective-permute-start(bf16[48,3456]{1,0:T(8,128)(2,1)S(1)} %pad_maximum_fusion.1), channel_id=1, source_target_pairs={{0,4},{2,6},{4,0},{6,2},{1,5},{3,7},{5,1},{7,3},{8,12},{10,14},{12... | collective-permute-start | bytes 995336 | tf_op jit(solution)/shard_map/ppermute | solution.py:63
  22.0 23.8 %collective-permute-start.5 = (bf16[48,3456]{1,0:T(8,128)(2,1)S(1)}, bf16[48,3456]{1,0:T(8,128)(2,1)}, u32[]{:S(2)}, u32[]{:S(2)}) collective-permute-start(bf16[48,3456]{1,0:T(8,128)(2,1)S(1)} %pad_maximum_fusion.1), channel_id=1, source_target_pairs={{0,6},{2,4},{4,2},{6,0},{1,7},{3,5},{5,3},{7,1},{8,14},{10,12},{12... | collective-permute-start | bytes 995336 | tf_op jit(solution)/shard_map/ppermute | solution.py:63
  48.0 45.3 %collective-permute-start.18 = (bf16[192,3456]{1,0:T(8,128)(2,1)S(1)}, bf16[192,3456]{1,0:T(8,128)(2,1)S(1)}, u32[]{:S(2)}, u32[]{:S(2)}) collective-permute-start(bf16[192,3456]{1,0:T(8,128)(2,1)S(1)} %constant_dynamic-update-slice_fusion.refs_0_), channel_id=1, source_target_pairs={{0,16},{8,24},{16,0},{24,8},{1,17},{9,25},{17,1},{25,9},{2,18},{10... | collective-permute-start | bytes 3981320 | tf_op jit(solution)/shard_map/ppermute | solution.py:63
  49.6 13.6 %collective-permute-start.19 = (bf16[576,256]{1,0:T(8,128)(2,1)S(1)}, bf16[576,256]{1,0:T(8,128)(2,1)S(1)}, u32[]{:S(2)}, u32[]{:S(2)}) collective-permute-start(bf16[576,256]{1,0:T(8,128)(2,1)S(1)} %get-tuple-element.115), channel_id=1, source_target_pairs={{0,2},{2,0},{4,6},{6,4},{1,3},{3,1},{5,7},{7,5},{8,10},{10,8},{12,... | collective-permute-start | bytes 884744 | tf_op jit(solution)/shard_map/ppermute | solution.py:63
  54.7 22.5 %collective-permute-start.20 = (bf16[576,256]{1,0:T(8,128)(2,1)S(1)}, bf16[576,256]{1,0:T(8,128)(2,1)S(1)}, u32[]{:S(2)}, u32[]{:S(2)}) collective-permute-start(bf16[576,256]{1,0:T(8,128)(2,1)S(1)} %get-tuple-element.116), channel_id=1, source_target_pairs={{0,4},{2,6},{4,0},{6,2},{1,5},{3,7},{5,1},{7,3},{8,12},{10,14},{12... | collective-permute-start | bytes 884744 | tf_op jit(solution)/shard_map/ppermute | solution.py:63
  55.6 21.5 %collective-permute-start.21 = (bf16[576,256]{1,0:T(8,128)(2,1)S(1)}, bf16[576,256]{1,0:T(8,128)(2,1)S(1)}, u32[]{:S(2)}, u32[]{:S(2)}) collective-permute-start(bf16[576,256]{1,0:T(8,128)(2,1)S(1)} %get-tuple-element.117), channel_id=1, source_target_pairs={{0,6},{2,4},{4,2},{6,0},{1,7},{3,5},{5,3},{7,1},{8,14},{10,12},{12... | collective-permute-start | bytes 884744 | tf_op jit(solution)/shard_map/ppermute | solution.py:63
  77.2 16.1 %collective-permute-start.28 = (bf16[48,1536]{1,0:T(8,128)(2,1)S(1)}, bf16[48,1536]{1,0:T(8,128)(2,1)S(1)}, u32[]{:S(2)}, u32[]{:S(2)}) collective-permute-start(bf16[48,1536]{1,0:T(8,128)(2,1)S(1)} %convert_bitcast_fusion), channel_id=1, source_target_pairs={{0,2},{2,0},{4,6},{6,4},{1,3},{3,1},{5,7},{7,5},{8,10},{10,8},{12,... | collective-permute-start | bytes 442376 | tf_op jit(solution)/shard_map/ppermute | solution.py:63
  81.0 12.3 %collective-permute-start.29 = (bf16[48,1536]{1,0:T(8,128)(2,1)S(1)}, bf16[48,1536]{1,0:T(8,128)(2,1)S(1)}, u32[]{:S(2)}, u32[]{:S(2)}) collective-permute-start(bf16[48,1536]{1,0:T(8,128)(2,1)S(1)} %convert_bitcast_fusion), channel_id=1, source_target_pairs={{0,4},{2,6},{4,0},{6,2},{1,5},{3,7},{5,1},{7,3},{8,12},{10,14},{12... | collective-permute-start | bytes 442376 | tf_op jit(solution)/shard_map/ppermute | solution.py:63
  81.9 11.5 %collective-permute-start.30 = (bf16[48,1536]{1,0:T(8,128)(2,1)S(1)}, bf16[48,1536]{1,0:T(8,128)(2,1)S(1)}, u32[]{:S(2)}, u32[]{:S(2)}) collective-permute-start(bf16[48,1536]{1,0:T(8,128)(2,1)S(1)} %convert_bitcast_fusion), channel_id=1, source_target_pairs={{0,6},{2,4},{4,2},{6,0},{1,7},{3,5},{5,3},{7,1},{8,14},{10,12},{12... | collective-permute-start | bytes 442376 | tf_op jit(solution)/shard_map/ppermute | solution.py:63
  94.0 15.4 %collective-permute-start.31 = (bf16[192,1536]{1,0:T(8,128)(2,1)S(1)}, bf16[192,1536]{1,0:T(8,128)(2,1)S(1)}, u32[]{:S(2)}, u32[]{:S(2)}) collective-permute-start(bf16[192,1536]{1,0:T(8,128)(2,1)S(1)} %constant_dynamic-update-slice_fusion.4.refs_0_), channel_id=1, source_target_pairs={{0,16},{8,24},{16,0},{24,8},{1,17},{9,25},{17,1},{25,9},{2,18},{10... | collective-permute-start | bytes 1769480 | tf_op jit(solution)/shard_map/ppermute | solution.py:63
  95.6 10.5 %collective-permute-start.25 = (bf16[192,256]{1,0:T(8,128)(2,1)S(1)}, bf16[192,256]{1,0:T(8,128)(2,1)S(1)}, u32[]{:S(2)}, u32[]{:S(2)}) collective-permute-start(bf16[192,256]{1,0:T(8,128)(2,1)S(1)} %get-tuple-element.122), channel_id=1, source_target_pairs={{0,4},{2,6},{4,0},{6,2},{1,5},{3,7},{5,1},{7,3},{8,12},{10,14},{12... | collective-permute-start | bytes 294920 | tf_op jit(solution)/shard_map/ppermute | solution.py:63
  109.9 12.0 %collective-permute-start.27 = (bf16[256,768]{1,0:T(8,128)(2,1)S(1)}, bf16[256,768]{1,0:T(8,128)(2,1)S(1)}, u32[]{:S(2)}, u32[]{:S(2)}) collective-permute-start(bf16[256,768]{1,0:T(8,128)(2,1)S(1)} %get-tuple-element.124.own.refs_0_), channel_id=1, source_target_pairs={{0,1},{1,0},{2,3},{3,2},{4,5},{5,4},{6,7},{7,6},{8,9},{9,8},{10,11... | collective-permute-start | bytes 1179656 | tf_op jit(solution)/shard_map/ppermute | solution.py:63
  111.4 18.9 %collective-permute-start.35 = (bf16[256,768]{1,0:T(8,128)(2,1)S(1)}, bf16[256,768]{1,0:T(8,128)(2,1)S(1)}, u32[]{:S(2)}, u32[]{:S(2)}) collective-permute-start(bf16[256,768]{1,0:T(8,128)(2,1)S(1)} %get-tuple-element.137.own.refs_1_), channel_id=1, source_target_pairs={{0,1},{1,0},{2,3},{3,2},{4,5},{5,4},{6,7},{7,6},{8,9},{9,8},{10,11... | collective-permute-start | bytes 1179656 | tf_op jit(solution)/shard_map/ppermute | solution.py:63
  126.1 12.6 %collective-permute-start.34 = (bf16[256,768]{1,0:T(8,128)(2,1)S(1)}, bf16[256,768]{1,0:T(8,128)(2,1)S(1)}, u32[]{:S(2)}, u32[]{:S(2)}) collective-permute-start(bf16[256,768]{1,0:T(8,128)(2,1)S(1)} %get-tuple-element.133.own), channel_id=1, source_target_pairs={{0,1},{1,0},{2,3},{3,2},{4,5},{5,4},{6,7},{7,6},{8,9},{9,8},{10,11... | collective-permute-start | bytes 1179656 | tf_op jit(solution)/shard_map/ppermute | solution.py:63
  134.5 12.7 %collective-permute-start.36 = (bf16[256,768]{1,0:T(8,128)(2,1)S(1)}, bf16[256,768]{1,0:T(8,128)(2,1)S(1)}, u32[]{:S(2)}, u32[]{:S(2)}) collective-permute-start(bf16[256,768]{1,0:T(8,128)(2,1)S(1)} %get-tuple-element.139.own), channel_id=1, source_target_pairs={{0,1},{1,0},{2,3},{3,2},{4,5},{5,4},{6,7},{7,6},{8,9},{9,8},{10,11... | collective-permute-start | bytes 1179656 | tf_op jit(solution)/shard_map/ppermute | solution.py:63
  144.1 17.7 %collective-permute-start.37 = (bf16[256,768]{1,0:T(8,128)(2,1)S(1)}, bf16[256,768]{1,0:T(8,128)(2,1)S(1)}, u32[]{:S(2)}, u32[]{:S(2)}) collective-permute-start(bf16[256,768]{1,0:T(8,128)(2,1)S(1)} %get-tuple-element.146.refs_6_), channel_id=1, source_target_pairs={{0,1},{1,0},{2,3},{3,2},{4,5},{5,4},{6,7},{7,6},{8,9},{9,8},{10,11... | collective-permute-start | bytes 1179656 | tf_op jit(solution)/shard_map/ppermute | solution.py:63
  152.5 10.5 %collective-permute-start.38 = (bf16[256,768]{1,0:T(8,128)(2,1)S(1)}, bf16[256,768]{1,0:T(8,128)(2,1)S(1)}, u32[]{:S(2)}, u32[]{:S(2)}) collective-permute-start(bf16[256,768]{1,0:T(8,128)(2,1)S(1)} %get-tuple-element.147.refs_7_), channel_id=1, source_target_pairs={{0,1},{1,0},{2,3},{3,2},{4,5},{5,4},{6,7},{7,6},{8,9},{9,8},{10,11... | collective-permute-start | bytes 1179656 | tf_op jit(solution)/shard_map/ppermute | solution.py:63
  169.9 10.8 %collective-permute-start.40 = (bf16[192,256]{1,0:T(8,128)(2,1)S(1)}, bf16[192,256]{1,0:T(8,128)(2,1)S(1)}, u32[]{:S(2)}, u32[]{:S(2)}) collective-permute-start(bf16[192,256]{1,0:T(8,128)(2,1)S(1)} %get-tuple-element.169), channel_id=1, source_target_pairs={{0,4},{2,6},{4,0},{6,2},{1,5},{3,7},{5,1},{7,3},{8,12},{10,14},{12... | collective-permute-start | bytes 294920 | tf_op jit(solution)/shard_map/ppermute | solution.py:63
  180.7 39.6 %collective-permute-start.46 = (bf16[192,4608]{1,0:T(8,128)(2,1)}, bf16[192,4608]{1,0:T(8,128)(2,1)S(1)}, u32[]{:S(2)}, u32[]{:S(2)}) collective-permute-start(bf16[192,4608]{1,0:T(8,128)(2,1)} %get-tuple-element.186), channel_id=1, source_target_pairs={{0,16},{8,24},{16,0},{24,8},{1,17},{9,25},{17,1},{25,9},{2,18},{10... | collective-permute-start | bytes 5308424 | tf_op jit(solution)/shard_map/ppermute | solution.py:63
  195.8 28.4 %collective-permute-start.43 = (bf16[576,256]{1,0:T(8,128)(2,1)}, bf16[576,256]{1,0:T(8,128)(2,1)}, u32[]{:S(2)}, u32[]{:S(2)}) collective-permute-start(bf16[576,256]{1,0:T(8,128)(2,1)} %get-tuple-element.182), channel_id=1, source_target_pairs={{0,2},{2,0},{4,6},{6,4},{1,3},{3,1},{5,7},{7,5},{8,10},{10,8},{12,... | collective-permute-start | bytes 884744 | tf_op jit(solution)/shard_map/ppermute | solution.py:63
  197.9 26.3 %collective-permute-start.44 = (bf16[576,256]{1,0:T(8,128)(2,1)}, bf16[576,256]{1,0:T(8,128)(2,1)}, u32[]{:S(2)}, u32[]{:S(2)}) collective-permute-start(bf16[576,256]{1,0:T(8,128)(2,1)} %get-tuple-element.183), channel_id=1, source_target_pairs={{0,4},{2,6},{4,0},{6,2},{1,5},{3,7},{5,1},{7,3},{8,12},{10,14},{12... | collective-permute-start | bytes 884744 | tf_op jit(solution)/shard_map/ppermute | solution.py:63
  197.9 26.3 %collective-permute-start.45 = (bf16[576,256]{1,0:T(8,128)(2,1)}, bf16[576,256]{1,0:T(8,128)(2,1)}, u32[]{:S(2)}, u32[]{:S(2)}) collective-permute-start(bf16[576,256]{1,0:T(8,128)(2,1)} %get-tuple-element.184), channel_id=1, source_target_pairs={{0,6},{2,4},{4,2},{6,0},{1,7},{3,5},{5,3},{7,1},{8,14},{10,12},{12... | collective-permute-start | bytes 884744 | tf_op jit(solution)/shard_map/ppermute | solution.py:63
  228.1 19.9 %collective-permute-start.47 = (bf16[512,768]{1,0:T(8,128)(2,1)S(1)}, bf16[512,768]{1,0:T(8,128)(2,1)S(1)}, u32[]{:S(2)}, u32[]{:S(2)}) collective-permute-start(bf16[512,768]{1,0:T(8,128)(2,1)S(1)} %get-tuple-element.192), channel_id=1, source_target_pairs={{0,1},{1,0},{2,3},{3,2},{4,5},{5,4},{6,7},{7,6},{8,9},{9,8},{10,11... | collective-permute-start | bytes 2359304 | tf_op jit(solution)/shard_map/ppermute | solution.py:63
  229.6 22.0 %collective-permute-start.49 = (bf16[48,4608]{1,0:T(8,128)(2,1)S(1)}, bf16[48,4608]{1,0:T(8,128)(2,1)S(1)}, u32[]{:S(2)}, u32[]{:S(2)}) collective-permute-start(bf16[48,4608]{1,0:T(8,128)(2,1)S(1)} %get-tuple-element.196), channel_id=1, source_target_pairs={{0,2},{2,0},{4,6},{6,4},{1,3},{3,1},{5,7},{7,5},{8,10},{10,8},{12,... | collective-permute-start | bytes 1327112 | tf_op jit(solution)/shard_map/ppermute | solution.py:63
  232.1 32.9 %collective-permute-start.55 = (bf16[48,4608]{1,0:T(8,128)(2,1)S(1)}, bf16[48,4608]{1,0:T(8,128)(2,1)S(1)}, u32[]{:S(2)}, u32[]{:S(2)}) collective-permute-start(bf16[48,4608]{1,0:T(8,128)(2,1)S(1)} %get-tuple-element.206), channel_id=1, source_target_pairs={{0,4},{2,6},{4,0},{6,2},{1,5},{3,7},{5,1},{7,3},{8,12},{10,14},{12... | collective-permute-start | bytes 1327112 | tf_op jit(solution)/shard_map/ppermute | solution.py:63
  233.4 31.6 %collective-permute-start.56 = (bf16[48,4608]{1,0:T(8,128)(2,1)S(1)}, bf16[48,4608]{1,0:T(8,128)(2,1)S(1)}, u32[]{:S(2)}, u32[]{:S(2)}) collective-permute-start(bf16[48,4608]{1,0:T(8,128)(2,1)S(1)} %get-tuple-element.207), channel_id=1, source_target_pairs={{0,6},{2,4},{4,2},{6,0},{1,7},{3,5},{5,3},{7,1},{8,14},{10,12},{12... | collective-permute-start | bytes 1327112 | tf_op jit(solution)/shard_map/ppermute | solution.py:63
  236.1 15.5 %collective-permute-start.50 = (bf16[208,768]{1,0:T(8,128)(2,1)S(1)}, bf16[208,768]{1,0:T(8,128)(2,1)S(1)}, u32[]{:S(2)}, u32[]{:S(2)}) collective-permute-start(bf16[208,768]{1,0:T(8,128)(2,1)S(1)} %get-tuple-element.197), channel_id=1, source_target_pairs={{0,16},{8,24},{16,0},{24,8},{1,17},{9,25},{17,1},{25,9},{2,18},{10... | collective-permute-start | bytes 958472 | tf_op jit(solution)/shard_map/ppermute | solution.py:63
  257.8 11.0 %collective-permute-start.52 = (bf16[64,1536]{1,0:T(8,128)(2,1)S(1)}, bf16[64,1536]{1,0:T(8,128)(2,1)S(1)}, u32[]{:S(2)}, u32[]{:S(2)}) collective-permute-start(bf16[64,1536]{1,0:T(8,128)(2,1)S(1)} %get-tuple-element.201), channel_id=1, source_target_pairs={{0,2},{2,0},{4,6},{6,4},{1,3},{3,1},{5,7},{7,5},{8,10},{10,8},{12,... | collective-permute-start | bytes 589832 | tf_op jit(solution)/shard_map/ppermute | solution.py:63
  260.3 26.8 %collective-permute-start.53 = (bf16[64,1536]{1,0:T(8,128)(2,1)S(1)}, bf16[64,1536]{1,0:T(8,128)(2,1)S(1)}, u32[]{:S(2)}, u32[]{:S(2)}) collective-permute-start(bf16[64,1536]{1,0:T(8,128)(2,1)S(1)} %get-tuple-element.202), channel_id=1, source_target_pairs={{0,4},{2,6},{4,0},{6,2},{1,5},{3,7},{5,1},{7,3},{8,12},{10,14},{12... | collective-permute-start | bytes 589832 | tf_op jit(solution)/shard_map/ppermute | solution.py:63
  261.7 25.4 %collective-permute-start.54 = (bf16[64,1536]{1,0:T(8,128)(2,1)S(1)}, bf16[64,1536]{1,0:T(8,128)(2,1)S(1)}, u32[]{:S(2)}, u32[]{:S(2)}) collective-permute-start(bf16[64,1536]{1,0:T(8,128)(2,1)S(1)} %get-tuple-element.203), channel_id=1, source_target_pairs={{0,6},{2,4},{4,2},{6,0},{1,7},{3,5},{5,3},{7,1},{8,14},{10,12},{12... | collective-permute-start | bytes 589832 | tf_op jit(solution)/shard_map/ppermute | solution.py:63
  (44 other events, 355.7 us)

commit v8 on v7

--- a/solution.py
+++ b/solution.py
@@ -13,7 +13,7 @@
 HD = 64
 LOG2E = math.log2(math.e)
 FAR = 1e30
-TILE = 64
+TILE = 128
 BLOCK = 512
 WIDTH = 384
 EXTRA = 16

time: 293 us -> 291 us (level)
  Pallas kernels: 69.4 us -> 65.2 us
  transfers between devices with their start and end apart: 57 -> 57, of which waited for: 26 -> 27; matrix products, arithmetic and copies ran while one was open for 2% -> 2% of each run, Pallas kernels for 23% -> 21%
where the time goes in v8:
time: 291 us; the launch traced here: 290 us
  waiting for transfers between devices  134 us (46%)
  starting transfers between devices  70.2 us (24%)
  Pallas kernels  65.2 us (22%)
  local copies, waits for them, and re-layouts  13.5 us (5%)
  other arithmetic  5.86 us (2%)
    ppermute x57, waiting for transfers between devices, swap(): return lax.ppermute(value, axis, xor_pairs(axis, distance))  134 us
    ppermute x57, starting transfers between devices, swap(): return lax.ppermute(value, axis, xor_pairs(axis, distance))  70.2 us
    pallas_call x1, Pallas kernels, attend_back(): pl.pallas_call(functools.partial(attend_back_kernel, n, heads), grid=(per...  12.4 us
    pallas_call x2, Pallas kernels, unit_back(): pl.pallas_call(functools.partial(unit_back_kernel, n, s), grid=(steps,),...  10.7 us
    pallas_call x2, Pallas kernels, unit(): pl.pallas_call(unit_kernel, grid=(steps,), out_shape=[shape((tokens, mode...  8.4 us
    unnamed x45, local copies, waits for them, and re-layouts  7.76 us
    pallas_call x1, Pallas kernels, weight_grads(): pl.pallas_call(functools.partial(weight_kernel, steps, seqs), grid=(3 * s...  7.68 us
    pallas_call x1, Pallas kernels, attend(): pl.pallas_call(functools.partial(attend_kernel, n, heads), grid=(per,), o...  7.54 us
  transfers between devices with their start and end apart: 57, of which 27 were waited for; matrix products, arithmetic and copies ran while one was open for 2% of the time, Pallas kernels for 21%

profile of v8, /device:TPU:0, one launch (start us, length us, event | category | flops | bytes accessed | tf_op | source)
XLA Modules:
  0.0 289.8 jit_solution(8259073790406472842)
XLA Ops:
  1.6 3.1 %collective-permute-start = (bf16[48,1152]{1,0:T(8,128)(2,1)S(1)}, bf16[48,1152]{1,0:T(8,128)(2,1)S(1)}, u32[]{:S(2)}, u32[]{:S(2)}) collective-permute-start(bf16[48,1152]{1,0:T(8,128)(2,1)S(1)} %bitcast.35), channel_id=1, source_target_pairs={{0,2},{2,0},{4,6},{6,4},{1,3},{3,1},{5,7},{7,5},{8,10},{10,8},{12,... | collective-permute-start | bytes 331784 | tf_op jit(solution)/shard_map/ppermute | solution.py:63
  4.8 2.6 collective-permute-start.1
  11.7 4.4 %collective-permute-done.1.refs_2_ = bf16[48,1152]{1,0:T(8,128)(2,1)S(1)} collective-permute-done((bf16[48,1152]{1,0:T(8,128)(2,1)S(1)}, bf16[48,1152]{1,0:T(8,128)(2,1)S(1)}, u32[]{:S(2)}, u32[]{:S(2)}) %collective-permute-start.1) | collective-permute-done | bytes 110624 | tf_op jit(solution)/shard_map/ppermute | solution.py:63
  22.0 2.5 collective-permute-start.5
  33.9 12.0 %collective-permute-done.4 = bf16[48,3456]{1,0:T(8,128)(2,1)} collective-permute-done((bf16[48,3456]{1,0:T(8,128)(2,1)S(1)}, bf16[48,3456]{1,0:T(8,128)(2,1)}, u32[]{:S(2)}, u32[]{:S(2)}) %collective-permute-start.4) | collective-permute-done | bytes 331808 | tf_op jit(solution)/shard_map/ppermute | solution.py:63
  49.6 5.0 %collective-permute-start.19 = (bf16[576,256]{1,0:T(8,128)(2,1)S(1)}, bf16[576,256]{1,0:T(8,128)(2,1)S(1)}, u32[]{:S(2)}, u32[]{:S(2)}) collective-permute-start(bf16[576,256]{1,0:T(8,128)(2,1)S(1)} %get-tuple-element.115), channel_id=1, source_target_pairs={{0,2},{2,0},{4,6},{6,4},{1,3},{3,1},{5,7},{7,5},{8,10},{10,8},{12,... | collective-permute-start | bytes 884744 | tf_op jit(solution)/shard_map/ppermute | solution.py:63
  57.1 6.1 %collective-permute-done.19.refs_1_ = bf16[576,256]{1,0:T(8,128)(2,1)S(1)} collective-permute-done((bf16[576,256]{1,0:T(8,128)(2,1)S(1)}, bf16[576,256]{1,0:T(8,128)(2,1)S(1)}, u32[]{:S(2)}, u32[]{:S(2)}) %collective-permute-start.19) | collective-permute-done | bytes 294944 | tf_op jit(solution)/shard_map/ppermute | solution.py:63
  63.2 13.9 %collective-permute-done.20.refs_2_ = bf16[576,256]{1,0:T(8,128)(2,1)S(1)} collective-permute-done((bf16[576,256]{1,0:T(8,128)(2,1)S(1)}, bf16[576,256]{1,0:T(8,128)(2,1)S(1)}, u32[]{:S(2)}, u32[]{:S(2)}) %collective-permute-start.20) | collective-permute-done | bytes 294944 | tf_op jit(solution)/shard_map/ppermute | solution.py:63
  77.2 3.8 %collective-permute-start.28 = (bf16[48,1536]{1,0:T(8,128)(2,1)S(1)}, bf16[48,1536]{1,0:T(8,128)(2,1)S(1)}, u32[]{:S(2)}, u32[]{:S(2)}) collective-permute-start(bf16[48,1536]{1,0:T(8,128)(2,1)S(1)} %convert_bitcast_fusion), channel_id=1, source_target_pairs={{0,2},{2,0},{4,6},{6,4},{1,3},{3,1},{5,7},{7,5},{8,10},{10,8},{12,... | collective-permute-start | bytes 442376 | tf_op jit(solution)/shard_map/ppermute | solution.py:63
  83.4 7.5 %attend.1 = (bf16[192,256]{1,0:T(8,128)(2,1)S(1)}, bf16[192,256]{1,0:T(8,128)(2,1)S(1)}, bf16[192,256]{1,0:T(8,128)(2,1)S(1)}, bf16[192,256]{1,0:T(8,128)(2,1)S(...) custom-call(s32[4]{0:T(128)S(1)} %pad_add_fusion.ids, s32[2]{0:T(128)S(1)} %copy-done.7, f32[12]{0:T(128)S(1)} %copy-done.12, ...), custom_call_target="tpu_custom_call" | custom-call | flops 1610612736 | bytes 3000000 | tf_op jit(solution)/shard_map/attend/pallas_call | solution.py:226
  100.1 5.9 %collective-permute-done.25.refs_2_ = bf16[192,256]{1,0:T(8,128)(2,1)S(1)} collective-permute-done((bf16[192,256]{1,0:T(8,128)(2,1)S(1)}, bf16[192,256]{1,0:T(8,128)(2,1)S(1)}, u32[]{:S(2)}, u32[]{:S(2)}) %collective-permute-start.25) | collective-permute-done | bytes 98336 | tf_op jit(solution)/shard_map/ppermute | solution.py:63
  112.2 8.6 %collective-permute-done.27.other.refs_2_ = bf16[256,768]{1,0:T(8,128)(2,1)S(1)} collective-permute-done((bf16[256,768]{1,0:T(8,128)(2,1)S(1)}, bf16[256,768]{1,0:T(8,128)(2,1)S(1)}, u32[]{:S(2)}, u32[]{:S(2)}) %collective-permute-start.27) | collective-permute-done | bytes 393248 | tf_op jit(solution)/shard_map/ppermute | solution.py:63
  120.8 4.2 %unit.2 = (f32[256,768]{1,0:T(8,128)S(1)}, bf16[256,768]{1,0:T(8,128)(2,1)S(1)}, bf16[256,1536]{1,0:T(8,128)(2,1)S(1)}, bf16[256,1536]{1,0:T(8,128)(2,1)S(1)}, b...) custom-call(bf16[512,768]{1,0:T(8,128)(2,1)S(1)} %bitcast.27, ...), custom_call_target="tpu_custom_call" | custom-call | flops 1811939328 | bytes 13000000 | tf_op jit(solution)/shard_map/unit/pallas_call | solution.py:411
  126.6 2.6 collective-permute-done.35.other.refs_3_
  129.2 4.2 %unit.3 = (f32[256,768]{1,0:T(8,128)S(1)}, bf16[256,768]{1,0:T(8,128)(2,1)S(1)}, bf16[256,1536]{1,0:T(8,128)(2,1)S(1)}, bf16[256,1536]{1,0:T(8,128)(2,1)S(1)}, b...) custom-call(bf16[512,768]{1,0:T(8,128)(2,1)S(1)} %bitcast.28, ...), custom_call_target="tpu_custom_call" | custom-call | flops 1811939328 | bytes 13000000 | tf_op jit(solution)/shard_map/unit/pallas_call | solution.py:411
  134.9 2.7 collective-permute-done.34.other
  137.6 5.3 %unit_back.2 = (bf16[256,768]{1,0:T(8,128)(2,1)S(1)}, f32[256,768]{1,0:T(8,128)S(1)}, bf16[256,768]{1,0:T(8,128)(2,1)S(1)}, bf16[256,1536]{1,0:T(8,128)(2,1)S(1)...) custom-call(s32[4]{0:T(128)S(1)} %pad_add_fusion.ids, s32[2]{0:T(128)S(1)} %copy-done.7, ...), custom_call_target="tpu_custom_call" | custom-call | flops 1811939328 | bytes 14000000 | tf_op jit(solution)/shard_map/unit_back/pallas_call | solution.py:477
  146.0 5.3 %unit_back.3 = (bf16[256,768]{1,0:T(8,128)(2,1)S(1)}, f32[256,768]{1,0:T(8,128)S(1)}, bf16[256,768]{1,0:T(8,128)(2,1)S(1)}, bf16[256,1536]{1,0:T(8,128)(2,1)S(1)...) custom-call(s32[4]{0:T(128)S(1)} %pad_add_fusion.ids, s32[2]{0:T(128)S(1)} %copy-done.7, ...), custom_call_target="tpu_custom_call" | custom-call | flops 1811939328 | bytes 14000000 | tf_op jit(solution)/shard_map/unit_back/pallas_call | solution.py:477
  152.9 7.7 %weight_grads.1 = (bf16[384,4608]{1,0:T(8,128)(2,1)S(1)}, bf16[384,4608]{1,0:T(8,128)(2,1)S(1)}) custom-call(s32[4]{0:T(128)S(1)} %pad_add_fusion.ids, bf16[256,768]{1,0:T(8,128)(2,1)S(1)} %get-tuple-element.148.refs_0_, bf16[256,768]{1,0:T(8,128)(2,1)S(1)} %get-tuple-element.149.refs_1_, bf16[256,768]{1,0:T(8,128)(2,1)S(1)} %get-tuple-element.150.refs_2_, ...), custom_call_target="tpu_custom_call" | custom-call | flops 3623878656 | bytes 14000000 | tf_op jit(solution)/shard_map/weight_grads/pallas_call | solution.py:557
  161.9 3.1 %mix_back.1 = (bf16[192,256]{1,0:T(8,128)(2,1)S(1)}, bf16[192,256]{1,0:T(8,128)(2,1)S(1)}, bf16[192,256]{1,0:T(8,128)(2,1)S(1)}, bf16[192,256]{1,0:T(8,128)(2,1)...) custom-call(s32[4]{0:T(128)S(1)} %pad_add_fusion.ids, ...), custom_call_target="tpu_custom_call" | custom-call | flops 603979776 | bytes 10000000 | tf_op jit(solution)/shard_map/mix_back/pallas_call | solution.py:620
  172.5 2.7 fold_core.2
  175.1 5.1 %collective-permute-done.40.refs_6_ = bf16[192,256]{1,0:T(8,128)(2,1)S(1)} collective-permute-done((bf16[192,256]{1,0:T(8,128)(2,1)S(1)}, bf16[192,256]{1,0:T(8,128)(2,1)S(1)}, u32[]{:S(2)}, u32[]{:S(2)}) %collective-permute-start.40) | collective-permute-done | bytes 98336 | tf_op jit(solution)/shard_map/ppermute | solution.py:63
  180.7 12.4 %attend_back.1 = (bf16[576,256]{1,0:T(8,128)(2,1)S(1)}, bf16[576,256]{1,0:T(8,128)(2,1)}, bf16[576,256]{1,0:T(8,128)(2,1)}, bf16[576,256]{1,0:T(8,128)(2,1)}) custom-call(s32[4]{0:T(128)S(1)} %pad_add_fusion.ids, s32[2]{0:T(128)S(1)} %copy-done.7, f32[12]{0:T(128)S(1)} %copy-done.12, bf16[576,256]{1,0:T(8,128)(2,1)S(1)} %get-tuple-element.114.refs_0_, ...), custom_call_target="tpu_custom_call" | custom-call | flops 4026531840 | bytes 5000000 | tf_op jit(solution)/shard_map/attend_back/pallas_call | solution.py:308
  193.8 2.2 collective-permute-start.43
  196.0 2.4 collective-permute-start.45
  198.5 21.8 %collective-permute-done.46.refs_0_ = bf16[192,4608]{1,0:T(8,128)(2,1)S(1)} collective-permute-done((bf16[192,4608]{1,0:T(8,128)(2,1)}, bf16[192,4608]{1,0:T(8,128)(2,1)S(1)}, u32[]{:S(2)}, u32[]{:S(2)}) %collective-permute-start.46) | collective-permute-done | bytes 1769504 | tf_op jit(solution)/shard_map/ppermute | solution.py:63
  224.2 3.8 %project_back.1 = (bf16[512,768]{1,0:T(8,128)(2,1)S(1)}, bf16[400,1536]{1,0:T(8,128)(2,1)S(1)}, bf16[400,1536]{1,0:T(8,128)(2,1)S(1)}) custom-call(s32[4]{0:T(128)S(1)} %pad_add_fusion.ids, bf16[512,768]{1,0:T(8,128)(2,1)S(1)} %bitcast.30, bf16[768,1152]{1,0:T(8,128)(2,1)S(1)} %copy-done.14, f32[8,768]{1,0:T(8,128)S(1)} %concatenate.20.small, ...), custom_call_target="tpu_custom_call" | custom-call | flops 1811939328 | bytes 8000000 | tf_op jit(solution)/shard_map/project_back/pallas_call | solution.py:684
  229.6 2.5 collective-permute-start.49
  236.8 11.3 %collective-permute-done.47 = bf16[512,768]{1,0:T(8,128)(2,1)S(1)} collective-permute-done((bf16[512,768]{1,0:T(8,128)(2,1)S(1)}, bf16[512,768]{1,0:T(8,128)(2,1)S(1)}, u32[]{:S(2)}, u32[]{:S(2)}) %collective-permute-start.47) | collective-permute-done | bytes 786464 | tf_op jit(solution)/shard_map/ppermute | solution.py:63
  251.7 5.4 %collective-permute-done.51.refs_1_ = bf16[208,768]{1,0:T(8,128)(2,1)S(1)} collective-permute-done((bf16[208,768]{1,0:T(8,128)(2,1)S(1)}, bf16[208,768]{1,0:T(8,128)(2,1)S(1)}, u32[]{:S(2)}, u32[]{:S(2)}) %collective-permute-start.51) | collective-permute-done | bytes 319520 | tf_op jit(solution)/shard_map/ppermute | solution.py:63
  257.8 2.5 collective-permute-start.52
  268.8 18.3 %collective-permute-done.53 = bf16[64,1536]{1,0:T(8,128)(2,1)S(1)} collective-permute-done((bf16[64,1536]{1,0:T(8,128)(2,1)S(1)}, bf16[64,1536]{1,0:T(8,128)(2,1)S(1)}, u32[]{:S(2)}, u32[]{:S(2)}) %collective-permute-start.53) | collective-permute-done | bytes 196640 | tf_op jit(solution)/shard_map/ppermute | solution.py:63
  (177 shorter events, 87.8 us)
Async XLA Ops:
  4.8 11.3 %collective-permute-start.1 = (bf16[48,1152]{1,0:T(8,128)(2,1)S(1)}, bf16[48,1152]{1,0:T(8,128)(2,1)S(1)}, u32[]{:S(2)}, u32[]{:S(2)}) collective-permute-start(bf16[48,1152]{1,0:T(8,128)(2,1)S(1)} %bitcast.36), channel_id=1, source_target_pairs={{0,4},{2,6},{4,0},{6,2},{1,5},{3,7},{5,1},{7,3},{8,12},{10,14},{12... | collective-permute-start | bytes 331784 | tf_op jit(solution)/shard_map/ppermute | solution.py:63
  18.2 15.7 %collective-permute-start.3 = (bf16[48,3456]{1,0:T(8,128)(2,1)S(1)}, bf16[48,3456]{1,0:T(8,128)(2,1)S(1)}, u32[]{:S(2)}, u32[]{:S(2)}) collective-permute-start(bf16[48,3456]{1,0:T(8,128)(2,1)S(1)} %pad_maximum_fusion.1), channel_id=1, source_target_pairs={{0,2},{2,0},{4,6},{6,4},{1,3},{3,1},{5,7},{7,5},{8,10},{10,8},{12,... | collective-permute-start | bytes 995336 | tf_op jit(solution)/shard_map/ppermute | solution.py:63
  20.0 25.9 %collective-permute-start.4 = (bf16[48,3456]{1,0:T(8,128)(2,1)S(1)}, bf16[48,3456]{1,0:T(8,128)(2,1)}, u32[]{:S(2)}, u32[]{:S(2)}) collective-permute-start(bf16[48,3456]{1,0:T(8,128)(2,1)S(1)} %pad_maximum_fusion.1), channel_id=1, source_target_pairs={{0,4},{2,6},{4,0},{6,2},{1,5},{3,7},{5,1},{7,3},{8,12},{10,14},{12... | collective-permute-start | bytes 995336 | tf_op jit(solution)/shard_map/ppermute | solution.py:63
  22.0 23.8 %collective-permute-start.5 = (bf16[48,3456]{1,0:T(8,128)(2,1)S(1)}, bf16[48,3456]{1,0:T(8,128)(2,1)}, u32[]{:S(2)}, u32[]{:S(2)}) collective-permute-start(bf16[48,3456]{1,0:T(8,128)(2,1)S(1)} %pad_maximum_fusion.1), channel_id=1, source_target_pairs={{0,6},{2,4},{4,2},{6,0},{1,7},{3,5},{5,3},{7,1},{8,14},{10,12},{12... | collective-permute-start | bytes 995336 | tf_op jit(solution)/shard_map/ppermute | solution.py:63
  48.0 44.3 %collective-permute-start.18 = (bf16[192,3456]{1,0:T(8,128)(2,1)S(1)}, bf16[192,3456]{1,0:T(8,128)(2,1)S(1)}, u32[]{:S(2)}, u32[]{:S(2)}) collective-permute-start(bf16[192,3456]{1,0:T(8,128)(2,1)S(1)} %constant_dynamic-update-slice_fusion.refs_0_), channel_id=1, source_target_pairs={{0,16},{8,24},{16,0},{24,8},{1,17},{9,25},{17,1},{25,9},{2,18},{10... | collective-permute-start | bytes 3981320 | tf_op jit(solution)/shard_map/ppermute | solution.py:63
  49.6 13.6 %collective-permute-start.19 = (bf16[576,256]{1,0:T(8,128)(2,1)S(1)}, bf16[576,256]{1,0:T(8,128)(2,1)S(1)}, u32[]{:S(2)}, u32[]{:S(2)}) collective-permute-start(bf16[576,256]{1,0:T(8,128)(2,1)S(1)} %get-tuple-element.115), channel_id=1, source_target_pairs={{0,2},{2,0},{4,6},{6,4},{1,3},{3,1},{5,7},{7,5},{8,10},{10,8},{12,... | collective-permute-start | bytes 884744 | tf_op jit(solution)/shard_map/ppermute | solution.py:63
  54.7 22.5 %collective-permute-start.20 = (bf16[576,256]{1,0:T(8,128)(2,1)S(1)}, bf16[576,256]{1,0:T(8,128)(2,1)S(1)}, u32[]{:S(2)}, u32[]{:S(2)}) collective-permute-start(bf16[576,256]{1,0:T(8,128)(2,1)S(1)} %get-tuple-element.116), channel_id=1, source_target_pairs={{0,4},{2,6},{4,0},{6,2},{1,5},{3,7},{5,1},{7,3},{8,12},{10,14},{12... | collective-permute-start | bytes 884744 | tf_op jit(solution)/shard_map/ppermute | solution.py:63
  55.6 21.5 %collective-permute-start.21 = (bf16[576,256]{1,0:T(8,128)(2,1)S(1)}, bf16[576,256]{1,0:T(8,128)(2,1)S(1)}, u32[]{:S(2)}, u32[]{:S(2)}) collective-permute-start(bf16[576,256]{1,0:T(8,128)(2,1)S(1)} %get-tuple-element.117), channel_id=1, source_target_pairs={{0,6},{2,4},{4,2},{6,0},{1,7},{3,5},{5,3},{7,1},{8,14},{10,12},{12... | collective-permute-start | bytes 884744 | tf_op jit(solution)/shard_map/ppermute | solution.py:63
  77.2 13.7 %collective-permute-start.28 = (bf16[48,1536]{1,0:T(8,128)(2,1)S(1)}, bf16[48,1536]{1,0:T(8,128)(2,1)S(1)}, u32[]{:S(2)}, u32[]{:S(2)}) collective-permute-start(bf16[48,1536]{1,0:T(8,128)(2,1)S(1)} %convert_bitcast_fusion), channel_id=1, source_target_pairs={{0,2},{2,0},{4,6},{6,4},{1,3},{3,1},{5,7},{7,5},{8,10},{10,8},{12,... | collective-permute-start | bytes 442376 | tf_op jit(solution)/shard_map/ppermute | solution.py:63
  81.0 11.3 %collective-permute-start.29 = (bf16[48,1536]{1,0:T(8,128)(2,1)S(1)}, bf16[48,1536]{1,0:T(8,128)(2,1)S(1)}, u32[]{:S(2)}, u32[]{:S(2)}) collective-permute-start(bf16[48,1536]{1,0:T(8,128)(2,1)S(1)} %convert_bitcast_fusion), channel_id=1, source_target_pairs={{0,4},{2,6},{4,0},{6,2},{1,5},{3,7},{5,1},{7,3},{8,12},{10,14},{12... | collective-permute-start | bytes 442376 | tf_op jit(solution)/shard_map/ppermute | solution.py:63
  92.9 15.4 %collective-permute-start.31 = (bf16[192,1536]{1,0:T(8,128)(2,1)S(1)}, bf16[192,1536]{1,0:T(8,128)(2,1)S(1)}, u32[]{:S(2)}, u32[]{:S(2)}) collective-permute-start(bf16[192,1536]{1,0:T(8,128)(2,1)S(1)} %constant_dynamic-update-slice_fusion.4.refs_0_), channel_id=1, source_target_pairs={{0,16},{8,24},{16,0},{24,8},{1,17},{9,25},{17,1},{25,9},{2,18},{10... | collective-permute-start | bytes 1769480 | tf_op jit(solution)/shard_map/ppermute | solution.py:63
  95.6 10.5 %collective-permute-start.25 = (bf16[192,256]{1,0:T(8,128)(2,1)S(1)}, bf16[192,256]{1,0:T(8,128)(2,1)S(1)}, u32[]{:S(2)}, u32[]{:S(2)}) collective-permute-start(bf16[192,256]{1,0:T(8,128)(2,1)S(1)} %get-tuple-element.122), channel_id=1, source_target_pairs={{0,4},{2,6},{4,0},{6,2},{1,5},{3,7},{5,1},{7,3},{8,12},{10,14},{12... | collective-permute-start | bytes 294920 | tf_op jit(solution)/shard_map/ppermute | solution.py:63
  108.8 12.0 %collective-permute-start.27 = (bf16[256,768]{1,0:T(8,128)(2,1)S(1)}, bf16[256,768]{1,0:T(8,128)(2,1)S(1)}, u32[]{:S(2)}, u32[]{:S(2)}) collective-permute-start(bf16[256,768]{1,0:T(8,128)(2,1)S(1)} %get-tuple-element.124.own.refs_0_), channel_id=1, source_target_pairs={{0,1},{1,0},{2,3},{3,2},{4,5},{5,4},{6,7},{7,6},{8,9},{9,8},{10,11... | collective-permute-start | bytes 1179656 | tf_op jit(solution)/shard_map/ppermute | solution.py:63
  110.3 18.9 %collective-permute-start.35 = (bf16[256,768]{1,0:T(8,128)(2,1)S(1)}, bf16[256,768]{1,0:T(8,128)(2,1)S(1)}, u32[]{:S(2)}, u32[]{:S(2)}) collective-permute-start(bf16[256,768]{1,0:T(8,128)(2,1)S(1)} %get-tuple-element.137.own.refs_1_), channel_id=1, source_target_pairs={{0,1},{1,0},{2,3},{3,2},{4,5},{5,4},{6,7},{7,6},{8,9},{9,8},{10,11... | collective-permute-start | bytes 1179656 | tf_op jit(solution)/shard_map/ppermute | solution.py:63
  125.0 12.6 %collective-permute-start.34 = (bf16[256,768]{1,0:T(8,128)(2,1)S(1)}, bf16[256,768]{1,0:T(8,128)(2,1)S(1)}, u32[]{:S(2)}, u32[]{:S(2)}) collective-permute-start(bf16[256,768]{1,0:T(8,128)(2,1)S(1)} %get-tuple-element.133.own), channel_id=1, source_target_pairs={{0,1},{1,0},{2,3},{3,2},{4,5},{5,4},{6,7},{7,6},{8,9},{9,8},{10,11... | collective-permute-start | bytes 1179656 | tf_op jit(solution)/shard_map/ppermute | solution.py:63
  133.4 12.7 %collective-permute-start.36 = (bf16[256,768]{1,0:T(8,128)(2,1)S(1)}, bf16[256,768]{1,0:T(8,128)(2,1)S(1)}, u32[]{:S(2)}, u32[]{:S(2)}) collective-permute-start(bf16[256,768]{1,0:T(8,128)(2,1)S(1)} %get-tuple-element.139.own), channel_id=1, source_target_pairs={{0,1},{1,0},{2,3},{3,2},{4,5},{5,4},{6,7},{7,6},{8,9},{9,8},{10,11... | collective-permute-start | bytes 1179656 | tf_op jit(solution)/shard_map/ppermute | solution.py:63
  143.0 17.7 %collective-permute-start.37 = (bf16[256,768]{1,0:T(8,128)(2,1)S(1)}, bf16[256,768]{1,0:T(8,128)(2,1)S(1)}, u32[]{:S(2)}, u32[]{:S(2)}) collective-permute-start(bf16[256,768]{1,0:T(8,128)(2,1)S(1)} %get-tuple-element.146.refs_6_), channel_id=1, source_target_pairs={{0,1},{1,0},{2,3},{3,2},{4,5},{5,4},{6,7},{7,6},{8,9},{9,8},{10,11... | collective-permute-start | bytes 1179656 | tf_op jit(solution)/shard_map/ppermute | solution.py:63
  151.4 10.5 %collective-permute-start.38 = (bf16[256,768]{1,0:T(8,128)(2,1)S(1)}, bf16[256,768]{1,0:T(8,128)(2,1)S(1)}, u32[]{:S(2)}, u32[]{:S(2)}) collective-permute-start(bf16[256,768]{1,0:T(8,128)(2,1)S(1)} %get-tuple-element.147.refs_7_), channel_id=1, source_target_pairs={{0,1},{1,0},{2,3},{3,2},{4,5},{5,4},{6,7},{7,6},{8,9},{9,8},{10,11... | collective-permute-start | bytes 1179656 | tf_op jit(solution)/shard_map/ppermute | solution.py:63
  161.9 10.5 %collective-permute-start.42 = (bf16[384,4608]{1,0:T(8,128)(2,1)S(1)}, bf16[384,4608]{1,0:T(8,128)(2,1)S(1)}, u32[]{:S(2)}, u32[]{:S(2)}) collective-permute-start(bf16[384,4608]{1,0:T(8,128)(2,1)S(1)} %get-tuple-element.172), channel_id=1, source_target_pairs={{0,8},{8,0},{16,24},{24,16},{1,9},{9,1},{17,25},{25,17},{2,10},{10... | collective-permute-start | bytes 10616840 | tf_op jit(solution)/shard_map/ppermute | solution.py:63
  169.7 10.6 %collective-permute-start.40 = (bf16[192,256]{1,0:T(8,128)(2,1)S(1)}, bf16[192,256]{1,0:T(8,128)(2,1)S(1)}, u32[]{:S(2)}, u32[]{:S(2)}) collective-permute-start(bf16[192,256]{1,0:T(8,128)(2,1)S(1)} %get-tuple-element.169), channel_id=1, source_target_pairs={{0,4},{2,6},{4,0},{6,2},{1,5},{3,7},{5,1},{7,3},{8,12},{10,14},{12... | collective-permute-start | bytes 294920 | tf_op jit(solution)/shard_map/ppermute | solution.py:63
  180.3 40.0 %collective-permute-start.46 = (bf16[192,4608]{1,0:T(8,128)(2,1)}, bf16[192,4608]{1,0:T(8,128)(2,1)S(1)}, u32[]{:S(2)}, u32[]{:S(2)}) collective-permute-start(bf16[192,4608]{1,0:T(8,128)(2,1)} %get-tuple-element.186), channel_id=1, source_target_pairs={{0,16},{8,24},{16,0},{24,8},{1,17},{9,25},{17,1},{25,9},{2,18},{10... | collective-permute-start | bytes 5308424 | tf_op jit(solution)/shard_map/ppermute | solution.py:63
  193.8 30.3 %collective-permute-start.43 = (bf16[576,256]{1,0:T(8,128)(2,1)}, bf16[576,256]{1,0:T(8,128)(2,1)}, u32[]{:S(2)}, u32[]{:S(2)}) collective-permute-start(bf16[576,256]{1,0:T(8,128)(2,1)} %get-tuple-element.182), channel_id=1, source_target_pairs={{0,2},{2,0},{4,6},{6,4},{1,3},{3,1},{5,7},{7,5},{8,10},{10,8},{12,... | collective-permute-start | bytes 884744 | tf_op jit(solution)/shard_map/ppermute | solution.py:63
  196.0 28.2 %collective-permute-start.44 = (bf16[576,256]{1,0:T(8,128)(2,1)}, bf16[576,256]{1,0:T(8,128)(2,1)}, u32[]{:S(2)}, u32[]{:S(2)}) collective-permute-start(bf16[576,256]{1,0:T(8,128)(2,1)} %get-tuple-element.183), channel_id=1, source_target_pairs={{0,4},{2,6},{4,0},{6,2},{1,5},{3,7},{5,1},{7,3},{8,12},{10,14},{12... | collective-permute-start | bytes 884744 | tf_op jit(solution)/shard_map/ppermute | solution.py:63
  196.0 28.2 %collective-permute-start.45 = (bf16[576,256]{1,0:T(8,128)(2,1)}, bf16[576,256]{1,0:T(8,128)(2,1)}, u32[]{:S(2)}, u32[]{:S(2)}) collective-permute-start(bf16[576,256]{1,0:T(8,128)(2,1)} %get-tuple-element.184), channel_id=1, source_target_pairs={{0,6},{2,4},{4,2},{6,0},{1,7},{3,5},{5,3},{7,1},{8,14},{10,12},{12... | collective-permute-start | bytes 884744 | tf_op jit(solution)/shard_map/ppermute | solution.py:63
  228.1 19.9 %collective-permute-start.47 = (bf16[512,768]{1,0:T(8,128)(2,1)S(1)}, bf16[512,768]{1,0:T(8,128)(2,1)S(1)}, u32[]{:S(2)}, u32[]{:S(2)}) collective-permute-start(bf16[512,768]{1,0:T(8,128)(2,1)S(1)} %get-tuple-element.192), channel_id=1, source_target_pairs={{0,1},{1,0},{2,3},{3,2},{4,5},{5,4},{6,7},{7,6},{8,9},{9,8},{10,11... | collective-permute-start | bytes 2359304 | tf_op jit(solution)/shard_map/ppermute | solution.py:63
  229.6 22.0 %collective-permute-start.49 = (bf16[48,4608]{1,0:T(8,128)(2,1)S(1)}, bf16[48,4608]{1,0:T(8,128)(2,1)S(1)}, u32[]{:S(2)}, u32[]{:S(2)}) collective-permute-start(bf16[48,4608]{1,0:T(8,128)(2,1)S(1)} %get-tuple-element.196), channel_id=1, source_target_pairs={{0,2},{2,0},{4,6},{6,4},{1,3},{3,1},{5,7},{7,5},{8,10},{10,8},{12,... | collective-permute-start | bytes 1327112 | tf_op jit(solution)/shard_map/ppermute | solution.py:63
  232.1 32.9 %collective-permute-start.55 = (bf16[48,4608]{1,0:T(8,128)(2,1)S(1)}, bf16[48,4608]{1,0:T(8,128)(2,1)S(1)}, u32[]{:S(2)}, u32[]{:S(2)}) collective-permute-start(bf16[48,4608]{1,0:T(8,128)(2,1)S(1)} %get-tuple-element.206), channel_id=1, source_target_pairs={{0,4},{2,6},{4,0},{6,2},{1,5},{3,7},{5,1},{7,3},{8,12},{10,14},{12... | collective-permute-start | bytes 1327112 | tf_op jit(solution)/shard_map/ppermute | solution.py:63
  233.5 31.5 %collective-permute-start.56 = (bf16[48,4608]{1,0:T(8,128)(2,1)S(1)}, bf16[48,4608]{1,0:T(8,128)(2,1)S(1)}, u32[]{:S(2)}, u32[]{:S(2)}) collective-permute-start(bf16[48,4608]{1,0:T(8,128)(2,1)S(1)} %get-tuple-element.207), channel_id=1, source_target_pairs={{0,6},{2,4},{4,2},{6,0},{1,7},{3,5},{5,3},{7,1},{8,14},{10,12},{12... | collective-permute-start | bytes 1327112 | tf_op jit(solution)/shard_map/ppermute | solution.py:63
  236.2 15.5 %collective-permute-start.50 = (bf16[208,768]{1,0:T(8,128)(2,1)S(1)}, bf16[208,768]{1,0:T(8,128)(2,1)S(1)}, u32[]{:S(2)}, u32[]{:S(2)}) collective-permute-start(bf16[208,768]{1,0:T(8,128)(2,1)S(1)} %get-tuple-element.197), channel_id=1, source_target_pairs={{0,16},{8,24},{16,0},{24,8},{1,17},{9,25},{17,1},{25,9},{2,18},{10... | collective-permute-start | bytes 958472 | tf_op jit(solution)/shard_map/ppermute | solution.py:63
  257.8 11.0 %collective-permute-start.52 = (bf16[64,1536]{1,0:T(8,128)(2,1)S(1)}, bf16[64,1536]{1,0:T(8,128)(2,1)S(1)}, u32[]{:S(2)}, u32[]{:S(2)}) collective-permute-start(bf16[64,1536]{1,0:T(8,128)(2,1)S(1)} %get-tuple-element.201), channel_id=1, source_target_pairs={{0,2},{2,0},{4,6},{6,4},{1,3},{3,1},{5,7},{7,5},{8,10},{10,8},{12,... | collective-permute-start | bytes 589832 | tf_op jit(solution)/shard_map/ppermute | solution.py:63
  260.3 26.8 %collective-permute-start.53 = (bf16[64,1536]{1,0:T(8,128)(2,1)S(1)}, bf16[64,1536]{1,0:T(8,128)(2,1)S(1)}, u32[]{:S(2)}, u32[]{:S(2)}) collective-permute-start(bf16[64,1536]{1,0:T(8,128)(2,1)S(1)} %get-tuple-element.202), channel_id=1, source_target_pairs={{0,4},{2,6},{4,0},{6,2},{1,5},{3,7},{5,1},{7,3},{8,12},{10,14},{12... | collective-permute-start | bytes 589832 | tf_op jit(solution)/shard_map/ppermute | solution.py:63
  261.8 25.3 %collective-permute-start.54 = (bf16[64,1536]{1,0:T(8,128)(2,1)S(1)}, bf16[64,1536]{1,0:T(8,128)(2,1)S(1)}, u32[]{:S(2)}, u32[]{:S(2)}) collective-permute-start(bf16[64,1536]{1,0:T(8,128)(2,1)S(1)} %get-tuple-element.203), channel_id=1, source_target_pairs={{0,6},{2,4},{4,2},{6,0},{1,7},{3,5},{5,3},{7,1},{8,14},{10,12},{12... | collective-permute-start | bytes 589832 | tf_op jit(solution)/shard_map/ppermute | solution.py:63
  (44 other events, 357.3 us)

commit v9 on v8

--- a/solution.py
+++ b/solution.py
@@ -700,7 +700,8 @@
 
 def fold_core_kernel(extra, keep, recv, mine, *sends):
     half = (keep.shape[0] - extra) // 2
-    mine[0:half, :] = keep[0:half, :].astype(f32) + recv[0:half, :].astype(f32)
+    total = keep[0:half, :].astype(f32) + recv[0:half, :].astype(f32)
+    mine[0:half, :] = total.astype(mine.dtype)
     rest = (keep[half:, :].astype(f32) + recv[half:, :].astype(f32)).astype(bf16)
     size = sends[0].shape[1]
     for k, send in enumerate(sends):
@@ -718,7 +719,8 @@
     return pl.pallas_call(
         functools.partial(fold_core_kernel, extra),
         grid=(steps,),
-        out_shape=[shape((out, wide), f32)] + [shape((out, wide // parts), bf16)] * parts,
+        out_shape=[shape((out, wide), f32 if extra else bf16)]
+        + [shape((out, wide // parts), bf16)] * parts,
         in_specs=[column(rows)] * 2,
         out_specs=[column(out)]
         + [pl.BlockSpec((out, wide // steps // parts), lambda j: (0, j))] * parts,
@@ -734,7 +736,7 @@
     rows = mine.shape[0] - extra
     size = rows // n
     recv = jnp.concatenate([ref[...] for ref in recvs], axis=1)
-    stage[...] = mine[...] + recv.astype(f32)
+    stage[...] = mine[...].astype(f32) + recv.astype(f32)
     for d in range(n):
         block = stage[pl.ds(pl.multiple_of((z ^ d) * size, size), size), :]
         if d:

time: 291 us -> 289 us (level)
  local copies, waits for them, and re-layouts: 13.5 us -> 8.96 us
    unnamed x45 -> x41, local copies, waits for them, and re-layouts: 7.76 us -> 3.19 us
  transfers between devices with their start and end apart: 57 -> 57, of which waited for: 27 -> 27; matrix products, arithmetic and copies ran while one was open for 2% -> 2% of each run, Pallas kernels for 21% -> 22%
where the time goes in v9:
time: 289 us; the launch traced here: 287 us
  waiting for transfers between devices  132 us (46%)
  starting transfers between devices  71.9 us (25%)
  Pallas kernels  66.6 us (23%)
  local copies, waits for them, and re-layouts  8.96 us (3%)
  other arithmetic  5.86 us (2%)
    ppermute x57, waiting for transfers between devices, swap(): return lax.ppermute(value, axis, xor_pairs(axis, distance))  132 us
    ppermute x57, starting transfers between devices, swap(): return lax.ppermute(value, axis, xor_pairs(axis, distance))  71.9 us
    pallas_call x1, Pallas kernels, attend_back(): pl.pallas_call(functools.partial(attend_back_kernel, n, heads), grid=(per...  12.4 us
    pallas_call x2, Pallas kernels, unit_back(): pl.pallas_call(functools.partial(unit_back_kernel, n, s), grid=(steps,),...  10.7 us
    pallas_call x2, Pallas kernels, unit(): pl.pallas_call(unit_kernel, grid=(steps,), out_shape=[shape((tokens, mode...  8.44 us
    pallas_call x1, Pallas kernels, weight_grads(): pl.pallas_call(functools.partial(weight_kernel, steps, seqs), grid=(3 * s...  7.68 us
    pallas_call x1, Pallas kernels, attend(): pl.pallas_call(functools.partial(attend_kernel, n, heads), grid=(per,), o...  7.54 us
  transfers between devices with their start and end apart: 57, of which 27 were waited for; matrix products, arithmetic and copies ran while one was open for 2% of the time, Pallas kernels for 22%

profile of v9, /device:TPU:0, one launch (start us, length us, event | category | flops | bytes accessed | tf_op | source)
XLA Modules:
  0.0 286.8 jit_solution(15049505701224409970)
XLA Ops:
  1.6 3.1 %collective-permute-start = (bf16[48,1152]{1,0:T(8,128)(2,1)S(1)}, bf16[48,1152]{1,0:T(8,128)(2,1)S(1)}, u32[]{:S(2)}, u32[]{:S(2)}) collective-permute-start(bf16[48,1152]{1,0:T(8,128)(2,1)S(1)} %bitcast.35), channel_id=1, source_target_pairs={{0,2},{2,0},{4,6},{6,4},{1,3},{3,1},{5,7},{7,5},{8,10},{10,8},{12,... | collective-permute-start | bytes 331784 | tf_op jit(solution)/shard_map/ppermute | solution.py:63
  4.8 2.6 collective-permute-start.1
  11.7 4.4 %collective-permute-done.1.refs_2_ = bf16[48,1152]{1,0:T(8,128)(2,1)S(1)} collective-permute-done((bf16[48,1152]{1,0:T(8,128)(2,1)S(1)}, bf16[48,1152]{1,0:T(8,128)(2,1)S(1)}, u32[]{:S(2)}, u32[]{:S(2)}) %collective-permute-start.1) | collective-permute-done | bytes 110624 | tf_op jit(solution)/shard_map/ppermute | solution.py:63
  22.0 2.5 collective-permute-start.5
  33.9 12.0 %collective-permute-done.4 = bf16[48,3456]{1,0:T(8,128)(2,1)} collective-permute-done((bf16[48,3456]{1,0:T(8,128)(2,1)S(1)}, bf16[48,3456]{1,0:T(8,128)(2,1)}, u32[]{:S(2)}, u32[]{:S(2)}) %collective-permute-start.4) | collective-permute-done | bytes 331808 | tf_op jit(solution)/shard_map/ppermute | solution.py:63
  49.6 5.0 %collective-permute-start.19 = (bf16[576,256]{1,0:T(8,128)(2,1)S(1)}, bf16[576,256]{1,0:T(8,128)(2,1)S(1)}, u32[]{:S(2)}, u32[]{:S(2)}) collective-permute-start(bf16[576,256]{1,0:T(8,128)(2,1)S(1)} %get-tuple-element.115), channel_id=1, source_target_pairs={{0,2},{2,0},{4,6},{6,4},{1,3},{3,1},{5,7},{7,5},{8,10},{10,8},{12,... | collective-permute-start | bytes 884744 | tf_op jit(solution)/shard_map/ppermute | solution.py:63
  57.1 6.1 %collective-permute-done.19.refs_1_ = bf16[576,256]{1,0:T(8,128)(2,1)S(1)} collective-permute-done((bf16[576,256]{1,0:T(8,128)(2,1)S(1)}, bf16[576,256]{1,0:T(8,128)(2,1)S(1)}, u32[]{:S(2)}, u32[]{:S(2)}) %collective-permute-start.19) | collective-permute-done | bytes 294944 | tf_op jit(solution)/shard_map/ppermute | solution.py:63
  63.2 13.9 %collective-permute-done.20.refs_2_ = bf16[576,256]{1,0:T(8,128)(2,1)S(1)} collective-permute-done((bf16[576,256]{1,0:T(8,128)(2,1)S(1)}, bf16[576,256]{1,0:T(8,128)(2,1)S(1)}, u32[]{:S(2)}, u32[]{:S(2)}) %collective-permute-start.20) | collective-permute-done | bytes 294944 | tf_op jit(solution)/shard_map/ppermute | solution.py:63
  77.2 3.8 %collective-permute-start.28 = (bf16[48,1536]{1,0:T(8,128)(2,1)S(1)}, bf16[48,1536]{1,0:T(8,128)(2,1)S(1)}, u32[]{:S(2)}, u32[]{:S(2)}) collective-permute-start(bf16[48,1536]{1,0:T(8,128)(2,1)S(1)} %convert_bitcast_fusion), channel_id=1, source_target_pairs={{0,2},{2,0},{4,6},{6,4},{1,3},{3,1},{5,7},{7,5},{8,10},{10,8},{12,... | collective-permute-start | bytes 442376 | tf_op jit(solution)/shard_map/ppermute | solution.py:63
  83.4 7.5 %attend.1 = (bf16[192,256]{1,0:T(8,128)(2,1)S(1)}, bf16[192,256]{1,0:T(8,128)(2,1)S(1)}, bf16[192,256]{1,0:T(8,128)(2,1)S(1)}, bf16[192,256]{1,0:T(8,128)(2,1)S(...) custom-call(s32[4]{0:T(128)S(1)} %pad_add_fusion.ids, s32[2]{0:T(128)S(1)} %copy-done.5, f32[12]{0:T(128)S(1)} %copy-done.10, ...), custom_call_target="tpu_custom_call" | custom-call | flops 1610612736 | bytes 3000000 | tf_op jit(solution)/shard_map/attend/pallas_call | solution.py:226
  100.1 5.9 %collective-permute-done.25.refs_2_ = bf16[192,256]{1,0:T(8,128)(2,1)S(1)} collective-permute-done((bf16[192,256]{1,0:T(8,128)(2,1)S(1)}, bf16[192,256]{1,0:T(8,128)(2,1)S(1)}, u32[]{:S(2)}, u32[]{:S(2)}) %collective-permute-start.25) | collective-permute-done | bytes 98336 | tf_op jit(solution)/shard_map/ppermute | solution.py:63
  112.2 8.6 %collective-permute-done.27.other.refs_2_ = bf16[256,768]{1,0:T(8,128)(2,1)S(1)} collective-permute-done((bf16[256,768]{1,0:T(8,128)(2,1)S(1)}, bf16[256,768]{1,0:T(8,128)(2,1)S(1)}, u32[]{:S(2)}, u32[]{:S(2)}) %collective-permute-start.27) | collective-permute-done | bytes 393248 | tf_op jit(solution)/shard_map/ppermute | solution.py:63
  120.8 4.2 %unit.2 = (f32[256,768]{1,0:T(8,128)S(1)}, bf16[256,768]{1,0:T(8,128)(2,1)S(1)}, bf16[256,1536]{1,0:T(8,128)(2,1)S(1)}, bf16[256,1536]{1,0:T(8,128)(2,1)S(1)}, b...) custom-call(bf16[512,768]{1,0:T(8,128)(2,1)S(1)} %bitcast.27, ...), custom_call_target="tpu_custom_call" | custom-call | flops 1811939328 | bytes 13000000 | tf_op jit(solution)/shard_map/unit/pallas_call | solution.py:411
  126.6 2.6 collective-permute-done.35.other.refs_3_
  129.2 4.2 %unit.3 = (f32[256,768]{1,0:T(8,128)S(1)}, bf16[256,768]{1,0:T(8,128)(2,1)S(1)}, bf16[256,1536]{1,0:T(8,128)(2,1)S(1)}, bf16[256,1536]{1,0:T(8,128)(2,1)S(1)}, b...) custom-call(bf16[512,768]{1,0:T(8,128)(2,1)S(1)} %bitcast.28, ...), custom_call_target="tpu_custom_call" | custom-call | flops 1811939328 | bytes 13000000 | tf_op jit(solution)/shard_map/unit/pallas_call | solution.py:411
  135.0 2.6 collective-permute-done.34.other
  137.6 5.3 %unit_back.2 = (bf16[256,768]{1,0:T(8,128)(2,1)S(1)}, f32[256,768]{1,0:T(8,128)S(1)}, bf16[256,768]{1,0:T(8,128)(2,1)S(1)}, bf16[256,1536]{1,0:T(8,128)(2,1)S(1)...) custom-call(s32[4]{0:T(128)S(1)} %pad_add_fusion.ids, s32[2]{0:T(128)S(1)} %copy-done.5, ...), custom_call_target="tpu_custom_call" | custom-call | flops 1811939328 | bytes 14000000 | tf_op jit(solution)/shard_map/unit_back/pallas_call | solution.py:477
  146.0 5.3 %unit_back.3 = (bf16[256,768]{1,0:T(8,128)(2,1)S(1)}, f32[256,768]{1,0:T(8,128)S(1)}, bf16[256,768]{1,0:T(8,128)(2,1)S(1)}, bf16[256,1536]{1,0:T(8,128)(2,1)S(1)...) custom-call(s32[4]{0:T(128)S(1)} %pad_add_fusion.ids, s32[2]{0:T(128)S(1)} %copy-done.5, ...), custom_call_target="tpu_custom_call" | custom-call | flops 1811939328 | bytes 14000000 | tf_op jit(solution)/shard_map/unit_back/pallas_call | solution.py:477
  152.9 7.7 %weight_grads.1 = (bf16[384,4608]{1,0:T(8,128)(2,1)S(1)}, bf16[384,4608]{1,0:T(8,128)(2,1)S(1)}) custom-call(s32[4]{0:T(128)S(1)} %pad_add_fusion.ids, bf16[256,768]{1,0:T(8,128)(2,1)S(1)} %get-tuple-element.148.refs_0_, bf16[256,768]{1,0:T(8,128)(2,1)S(1)} %get-tuple-element.149.refs_1_, bf16[256,768]{1,0:T(8,128)(2,1)S(1)} %get-tuple-element.150.refs_2_, ...), custom_call_target="tpu_custom_call" | custom-call | flops 3623878656 | bytes 14000000 | tf_op jit(solution)/shard_map/weight_grads/pallas_call | solution.py:557
  161.9 3.1 %mix_back.1 = (bf16[192,256]{1,0:T(8,128)(2,1)S(1)}, bf16[192,256]{1,0:T(8,128)(2,1)S(1)}, bf16[192,256]{1,0:T(8,128)(2,1)S(1)}, bf16[192,256]{1,0:T(8,128)(2,1)...) custom-call(s32[4]{0:T(128)S(1)} %pad_add_fusion.ids, ...), custom_call_target="tpu_custom_call" | custom-call | flops 603979776 | bytes 10000000 | tf_op jit(solution)/shard_map/mix_back/pallas_call | solution.py:620
  170.0 2.7 fold_core.2
  172.7 5.1 %collective-permute-done.40.refs_6_ = bf16[192,256]{1,0:T(8,128)(2,1)S(1)} collective-permute-done((bf16[192,256]{1,0:T(8,128)(2,1)S(1)}, bf16[192,256]{1,0:T(8,128)(2,1)S(1)}, u32[]{:S(2)}, u32[]{:S(2)}) %collective-permute-start.40) | collective-permute-done | bytes 98336 | tf_op jit(solution)/shard_map/ppermute | solution.py:63
  178.2 12.4 %attend_back.1 = (bf16[576,256]{1,0:T(8,128)(2,1)S(1)}, bf16[576,256]{1,0:T(8,128)(2,1)}, bf16[576,256]{1,0:T(8,128)(2,1)}, bf16[576,256]{1,0:T(8,128)(2,1)}) custom-call(s32[4]{0:T(128)S(1)} %pad_add_fusion.ids, s32[2]{0:T(128)S(1)} %copy-done.5, f32[12]{0:T(128)S(1)} %copy-done.10, bf16[576,256]{1,0:T(8,128)(2,1)S(1)} %get-tuple-element.114.refs_0_, ...), custom_call_target="tpu_custom_call" | custom-call | flops 4026531840 | bytes 5000000 | tf_op jit(solution)/shard_map/attend_back/pallas_call | solution.py:308
  193.5 2.4 collective-permute-start.45
  196.0 21.9 %collective-permute-done.46.refs_0_ = bf16[192,4608]{1,0:T(8,128)(2,1)} collective-permute-done((bf16[192,4608]{1,0:T(8,128)(2,1)}, bf16[192,4608]{1,0:T(8,128)(2,1)}, u32[]{:S(2)}, u32[]{:S(2)}) %collective-permute-start.46) | collective-permute-done | bytes 1769504 | tf_op jit(solution)/shard_map/ppermute | solution.py:63
  217.9 3.3 %fold_y.2 = (f32[48,4608]{1,0:T(8,128)S(1)}, bf16[48,4608]{1,0:T(8,128)(2,1)S(1)}, bf16[48,4608]{1,0:T(8,128)(2,1)S(1)}, bf16[48,4608]{1,0:T(8,128)(2,1)S(1)}) custom-call(s32[4]{0:T(128)S(1)} %pad_add_fusion.ids, bf16[192,4608]{1,0:T(8,128)(2,1)S(1)} %get-tuple-element.185.mine, bf16[192,4608]{1,0:T(8,128)(2,1)} %collective-permute-done.46.refs_0_), custom_call_target="tpu_custom_call" | custom-call | flops 884736 | bytes 7962624 | tf_op jit(solution)/shard_map/fold_y/pallas_call | solution.py:758
  221.3 3.8 %project_back.1 = (bf16[512,768]{1,0:T(8,128)(2,1)S(1)}, bf16[400,1536]{1,0:T(8,128)(2,1)S(1)}, bf16[400,1536]{1,0:T(8,128)(2,1)S(1)}) custom-call(s32[4]{0:T(128)S(1)} %pad_add_fusion.ids, bf16[512,768]{1,0:T(8,128)(2,1)S(1)} %bitcast.30, bf16[768,1152]{1,0:T(8,128)(2,1)S(1)} %copy-done.12, f32[8,768]{1,0:T(8,128)S(1)} %concatenate.20.small, ...), custom_call_target="tpu_custom_call" | custom-call | flops 1811939328 | bytes 8000000 | tf_op jit(solution)/shard_map/project_back/pallas_call | solution.py:684
  226.7 2.5 collective-permute-start.49
  235.3 9.8 %collective-permute-done.47 = bf16[512,768]{1,0:T(8,128)(2,1)S(1)} collective-permute-done((bf16[512,768]{1,0:T(8,128)(2,1)S(1)}, bf16[512,768]{1,0:T(8,128)(2,1)S(1)}, u32[]{:S(2)}, u32[]{:S(2)}) %collective-permute-start.47) | collective-permute-done | bytes 786464 | tf_op jit(solution)/shard_map/ppermute | solution.py:63
  248.7 5.4 %collective-permute-done.51.refs_1_ = bf16[208,768]{1,0:T(8,128)(2,1)S(1)} collective-permute-done((bf16[208,768]{1,0:T(8,128)(2,1)S(1)}, bf16[208,768]{1,0:T(8,128)(2,1)S(1)}, u32[]{:S(2)}, u32[]{:S(2)}) %collective-permute-start.51) | collective-permute-done | bytes 319520 | tf_op jit(solution)/shard_map/ppermute | solution.py:63
  254.8 2.8 collective-permute-start.52
  265.9 18.3 %collective-permute-done.53 = bf16[64,1536]{1,0:T(8,128)(2,1)S(1)} collective-permute-done((bf16[64,1536]{1,0:T(8,128)(2,1)S(1)}, bf16[64,1536]{1,0:T(8,128)(2,1)S(1)}, u32[]{:S(2)}, u32[]{:S(2)}) %collective-permute-start.53) | collective-permute-done | bytes 196640 | tf_op jit(solution)/shard_map/ppermute | solution.py:63
  (173 shorter events, 84.8 us)
Async XLA Ops:
  4.8 11.3 %collective-permute-start.1 = (bf16[48,1152]{1,0:T(8,128)(2,1)S(1)}, bf16[48,1152]{1,0:T(8,128)(2,1)S(1)}, u32[]{:S(2)}, u32[]{:S(2)}) collective-permute-start(bf16[48,1152]{1,0:T(8,128)(2,1)S(1)} %bitcast.36), channel_id=1, source_target_pairs={{0,4},{2,6},{4,0},{6,2},{1,5},{3,7},{5,1},{7,3},{8,12},{10,14},{12... | collective-permute-start | bytes 331784 | tf_op jit(solution)/shard_map/ppermute | solution.py:63
  18.2 15.7 %collective-permute-start.3 = (bf16[48,3456]{1,0:T(8,128)(2,1)S(1)}, bf16[48,3456]{1,0:T(8,128)(2,1)S(1)}, u32[]{:S(2)}, u32[]{:S(2)}) collective-permute-start(bf16[48,3456]{1,0:T(8,128)(2,1)S(1)} %pad_maximum_fusion.1), channel_id=1, source_target_pairs={{0,2},{2,0},{4,6},{6,4},{1,3},{3,1},{5,7},{7,5},{8,10},{10,8},{12,... | collective-permute-start | bytes 995336 | tf_op jit(solution)/shard_map/ppermute | solution.py:63
  20.0 25.9 %collective-permute-start.4 = (bf16[48,3456]{1,0:T(8,128)(2,1)S(1)}, bf16[48,3456]{1,0:T(8,128)(2,1)}, u32[]{:S(2)}, u32[]{:S(2)}) collective-permute-start(bf16[48,3456]{1,0:T(8,128)(2,1)S(1)} %pad_maximum_fusion.1), channel_id=1, source_target_pairs={{0,4},{2,6},{4,0},{6,2},{1,5},{3,7},{5,1},{7,3},{8,12},{10,14},{12... | collective-permute-start | bytes 995336 | tf_op jit(solution)/shard_map/ppermute | solution.py:63
  22.0 23.8 %collective-permute-start.5 = (bf16[48,3456]{1,0:T(8,128)(2,1)S(1)}, bf16[48,3456]{1,0:T(8,128)(2,1)}, u32[]{:S(2)}, u32[]{:S(2)}) collective-permute-start(bf16[48,3456]{1,0:T(8,128)(2,1)S(1)} %pad_maximum_fusion.1), channel_id=1, source_target_pairs={{0,6},{2,4},{4,2},{6,0},{1,7},{3,5},{5,3},{7,1},{8,14},{10,12},{12... | collective-permute-start | bytes 995336 | tf_op jit(solution)/shard_map/ppermute | solution.py:63
  48.0 44.3 %collective-permute-start.18 = (bf16[192,3456]{1,0:T(8,128)(2,1)S(1)}, bf16[192,3456]{1,0:T(8,128)(2,1)S(1)}, u32[]{:S(2)}, u32[]{:S(2)}) collective-permute-start(bf16[192,3456]{1,0:T(8,128)(2,1)S(1)} %constant_dynamic-update-slice_fusion.refs_0_), channel_id=1, source_target_pairs={{0,16},{8,24},{16,0},{24,8},{1,17},{9,25},{17,1},{25,9},{2,18},{10... | collective-permute-start | bytes 3981320 | tf_op jit(solution)/shard_map/ppermute | solution.py:63
  49.6 13.6 %collective-permute-start.19 = (bf16[576,256]{1,0:T(8,128)(2,1)S(1)}, bf16[576,256]{1,0:T(8,128)(2,1)S(1)}, u32[]{:S(2)}, u32[]{:S(2)}) collective-permute-start(bf16[576,256]{1,0:T(8,128)(2,1)S(1)} %get-tuple-element.115), channel_id=1, source_target_pairs={{0,2},{2,0},{4,6},{6,4},{1,3},{3,1},{5,7},{7,5},{8,10},{10,8},{12,... | collective-permute-start | bytes 884744 | tf_op jit(solution)/shard_map/ppermute | solution.py:63
  54.7 22.5 %collective-permute-start.20 = (bf16[576,256]{1,0:T(8,128)(2,1)S(1)}, bf16[576,256]{1,0:T(8,128)(2,1)S(1)}, u32[]{:S(2)}, u32[]{:S(2)}) collective-permute-start(bf16[576,256]{1,0:T(8,128)(2,1)S(1)} %get-tuple-element.116), channel_id=1, source_target_pairs={{0,4},{2,6},{4,0},{6,2},{1,5},{3,7},{5,1},{7,3},{8,12},{10,14},{12... | collective-permute-start | bytes 884744 | tf_op jit(solution)/shard_map/ppermute | solution.py:63
  55.6 21.5 %collective-permute-start.21 = (bf16[576,256]{1,0:T(8,128)(2,1)S(1)}, bf16[576,256]{1,0:T(8,128)(2,1)S(1)}, u32[]{:S(2)}, u32[]{:S(2)}) collective-permute-start(bf16[576,256]{1,0:T(8,128)(2,1)S(1)} %get-tuple-element.117), channel_id=1, source_target_pairs={{0,6},{2,4},{4,2},{6,0},{1,7},{3,5},{5,3},{7,1},{8,14},{10,12},{12... | collective-permute-start | bytes 884744 | tf_op jit(solution)/shard_map/ppermute | solution.py:63
  77.2 13.7 %collective-permute-start.28 = (bf16[48,1536]{1,0:T(8,128)(2,1)S(1)}, bf16[48,1536]{1,0:T(8,128)(2,1)S(1)}, u32[]{:S(2)}, u32[]{:S(2)}) collective-permute-start(bf16[48,1536]{1,0:T(8,128)(2,1)S(1)} %convert_bitcast_fusion), channel_id=1, source_target_pairs={{0,2},{2,0},{4,6},{6,4},{1,3},{3,1},{5,7},{7,5},{8,10},{10,8},{12,... | collective-permute-start | bytes 442376 | tf_op jit(solution)/shard_map/ppermute | solution.py:63
  81.0 11.3 %collective-permute-start.29 = (bf16[48,1536]{1,0:T(8,128)(2,1)S(1)}, bf16[48,1536]{1,0:T(8,128)(2,1)S(1)}, u32[]{:S(2)}, u32[]{:S(2)}) collective-permute-start(bf16[48,1536]{1,0:T(8,128)(2,1)S(1)} %convert_bitcast_fusion), channel_id=1, source_target_pairs={{0,4},{2,6},{4,0},{6,2},{1,5},{3,7},{5,1},{7,3},{8,12},{10,14},{12... | collective-permute-start | bytes 442376 | tf_op jit(solution)/shard_map/ppermute | solution.py:63
  81.9 10.4 %collective-permute-start.30 = (bf16[48,1536]{1,0:T(8,128)(2,1)S(1)}, bf16[48,1536]{1,0:T(8,128)(2,1)S(1)}, u32[]{:S(2)}, u32[]{:S(2)}) collective-permute-start(bf16[48,1536]{1,0:T(8,128)(2,1)S(1)} %convert_bitcast_fusion), channel_id=1, source_target_pairs={{0,6},{2,4},{4,2},{6,0},{1,7},{3,5},{5,3},{7,1},{8,14},{10,12},{12... | collective-permute-start | bytes 442376 | tf_op jit(solution)/shard_map/ppermute | solution.py:63
  92.9 15.4 %collective-permute-start.31 = (bf16[192,1536]{1,0:T(8,128)(2,1)S(1)}, bf16[192,1536]{1,0:T(8,128)(2,1)S(1)}, u32[]{:S(2)}, u32[]{:S(2)}) collective-permute-start(bf16[192,1536]{1,0:T(8,128)(2,1)S(1)} %constant_dynamic-update-slice_fusion.4.refs_0_), channel_id=1, source_target_pairs={{0,16},{8,24},{16,0},{24,8},{1,17},{9,25},{17,1},{25,9},{2,18},{10... | collective-permute-start | bytes 1769480 | tf_op jit(solution)/shard_map/ppermute | solution.py:63
  95.6 10.5 %collective-permute-start.25 = (bf16[192,256]{1,0:T(8,128)(2,1)S(1)}, bf16[192,256]{1,0:T(8,128)(2,1)S(1)}, u32[]{:S(2)}, u32[]{:S(2)}) collective-permute-start(bf16[192,256]{1,0:T(8,128)(2,1)S(1)} %get-tuple-element.122), channel_id=1, source_target_pairs={{0,4},{2,6},{4,0},{6,2},{1,5},{3,7},{5,1},{7,3},{8,12},{10,14},{12... | collective-permute-start | bytes 294920 | tf_op jit(solution)/shard_map/ppermute | solution.py:63
  108.8 12.0 %collective-permute-start.27 = (bf16[256,768]{1,0:T(8,128)(2,1)S(1)}, bf16[256,768]{1,0:T(8,128)(2,1)S(1)}, u32[]{:S(2)}, u32[]{:S(2)}) collective-permute-start(bf16[256,768]{1,0:T(8,128)(2,1)S(1)} %get-tuple-element.124.own.refs_0_), channel_id=1, source_target_pairs={{0,1},{1,0},{2,3},{3,2},{4,5},{5,4},{6,7},{7,6},{8,9},{9,8},{10,11... | collective-permute-start | bytes 1179656 | tf_op jit(solution)/shard_map/ppermute | solution.py:63
  110.3 18.9 %collective-permute-start.35 = (bf16[256,768]{1,0:T(8,128)(2,1)S(1)}, bf16[256,768]{1,0:T(8,128)(2,1)S(1)}, u32[]{:S(2)}, u32[]{:S(2)}) collective-permute-start(bf16[256,768]{1,0:T(8,128)(2,1)S(1)} %get-tuple-element.137.own.refs_1_), channel_id=1, source_target_pairs={{0,1},{1,0},{2,3},{3,2},{4,5},{5,4},{6,7},{7,6},{8,9},{9,8},{10,11... | collective-permute-start | bytes 1179656 | tf_op jit(solution)/shard_map/ppermute | solution.py:63
  125.0 12.6 %collective-permute-start.34 = (bf16[256,768]{1,0:T(8,128)(2,1)S(1)}, bf16[256,768]{1,0:T(8,128)(2,1)S(1)}, u32[]{:S(2)}, u32[]{:S(2)}) collective-permute-start(bf16[256,768]{1,0:T(8,128)(2,1)S(1)} %get-tuple-element.133.own), channel_id=1, source_target_pairs={{0,1},{1,0},{2,3},{3,2},{4,5},{5,4},{6,7},{7,6},{8,9},{9,8},{10,11... | collective-permute-start | bytes 1179656 | tf_op jit(solution)/shard_map/ppermute | solution.py:63
  133.4 12.6 %collective-permute-start.36 = (bf16[256,768]{1,0:T(8,128)(2,1)S(1)}, bf16[256,768]{1,0:T(8,128)(2,1)S(1)}, u32[]{:S(2)}, u32[]{:S(2)}) collective-permute-start(bf16[256,768]{1,0:T(8,128)(2,1)S(1)} %get-tuple-element.139.own), channel_id=1, source_target_pairs={{0,1},{1,0},{2,3},{3,2},{4,5},{5,4},{6,7},{7,6},{8,9},{9,8},{10,11... | collective-permute-start | bytes 1179656 | tf_op jit(solution)/shard_map/ppermute | solution.py:63
  143.0 17.7 %collective-permute-start.37 = (bf16[256,768]{1,0:T(8,128)(2,1)S(1)}, bf16[256,768]{1,0:T(8,128)(2,1)S(1)}, u32[]{:S(2)}, u32[]{:S(2)}) collective-permute-start(bf16[256,768]{1,0:T(8,128)(2,1)S(1)} %get-tuple-element.146.refs_6_), channel_id=1, source_target_pairs={{0,1},{1,0},{2,3},{3,2},{4,5},{5,4},{6,7},{7,6},{8,9},{9,8},{10,11... | collective-permute-start | bytes 1179656 | tf_op jit(solution)/shard_map/ppermute | solution.py:63
  151.4 10.5 %collective-permute-start.38 = (bf16[256,768]{1,0:T(8,128)(2,1)S(1)}, bf16[256,768]{1,0:T(8,128)(2,1)S(1)}, u32[]{:S(2)}, u32[]{:S(2)}) collective-permute-start(bf16[256,768]{1,0:T(8,128)(2,1)S(1)} %get-tuple-element.147.refs_7_), channel_id=1, source_target_pairs={{0,1},{1,0},{2,3},{3,2},{4,5},{5,4},{6,7},{7,6},{8,9},{9,8},{10,11... | collective-permute-start | bytes 1179656 | tf_op jit(solution)/shard_map/ppermute | solution.py:63
  167.2 10.6 %collective-permute-start.40 = (bf16[192,256]{1,0:T(8,128)(2,1)S(1)}, bf16[192,256]{1,0:T(8,128)(2,1)S(1)}, u32[]{:S(2)}, u32[]{:S(2)}) collective-permute-start(bf16[192,256]{1,0:T(8,128)(2,1)S(1)} %get-tuple-element.169), channel_id=1, source_target_pairs={{0,4},{2,6},{4,0},{6,2},{1,5},{3,7},{5,1},{7,3},{8,12},{10,14},{12... | collective-permute-start | bytes 294920 | tf_op jit(solution)/shard_map/ppermute | solution.py:63
  177.8 40.1 %collective-permute-start.46 = (bf16[192,4608]{1,0:T(8,128)(2,1)}, bf16[192,4608]{1,0:T(8,128)(2,1)}, u32[]{:S(2)}, u32[]{:S(2)}) collective-permute-start(bf16[192,4608]{1,0:T(8,128)(2,1)} %get-tuple-element.186), channel_id=1, source_target_pairs={{0,16},{8,24},{16,0},{24,8},{1,17},{9,25},{17,1},{25,9},{2,18},{10... | collective-permute-start | bytes 5308424 | tf_op jit(solution)/shard_map/ppermute | solution.py:63
  191.4 29.8 %collective-permute-start.43 = (bf16[576,256]{1,0:T(8,128)(2,1)}, bf16[576,256]{1,0:T(8,128)(2,1)}, u32[]{:S(2)}, u32[]{:S(2)}) collective-permute-start(bf16[576,256]{1,0:T(8,128)(2,1)} %get-tuple-element.182), channel_id=1, source_target_pairs={{0,2},{2,0},{4,6},{6,4},{1,3},{3,1},{5,7},{7,5},{8,10},{10,8},{12,... | collective-permute-start | bytes 884744 | tf_op jit(solution)/shard_map/ppermute | solution.py:63
  193.5 27.7 %collective-permute-start.44 = (bf16[576,256]{1,0:T(8,128)(2,1)}, bf16[576,256]{1,0:T(8,128)(2,1)}, u32[]{:S(2)}, u32[]{:S(2)}) collective-permute-start(bf16[576,256]{1,0:T(8,128)(2,1)} %get-tuple-element.183), channel_id=1, source_target_pairs={{0,4},{2,6},{4,0},{6,2},{1,5},{3,7},{5,1},{7,3},{8,12},{10,14},{12... | collective-permute-start | bytes 884744 | tf_op jit(solution)/shard_map/ppermute | solution.py:63
  193.5 27.7 %collective-permute-start.45 = (bf16[576,256]{1,0:T(8,128)(2,1)}, bf16[576,256]{1,0:T(8,128)(2,1)}, u32[]{:S(2)}, u32[]{:S(2)}) collective-permute-start(bf16[576,256]{1,0:T(8,128)(2,1)} %get-tuple-element.184), channel_id=1, source_target_pairs={{0,6},{2,4},{4,2},{6,0},{1,7},{3,5},{5,3},{7,1},{8,14},{10,12},{12... | collective-permute-start | bytes 884744 | tf_op jit(solution)/shard_map/ppermute | solution.py:63
  225.1 19.9 %collective-permute-start.47 = (bf16[512,768]{1,0:T(8,128)(2,1)S(1)}, bf16[512,768]{1,0:T(8,128)(2,1)S(1)}, u32[]{:S(2)}, u32[]{:S(2)}) collective-permute-start(bf16[512,768]{1,0:T(8,128)(2,1)S(1)} %get-tuple-element.192), channel_id=1, source_target_pairs={{0,1},{1,0},{2,3},{3,2},{4,5},{5,4},{6,7},{7,6},{8,9},{9,8},{10,11... | collective-permute-start | bytes 2359304 | tf_op jit(solution)/shard_map/ppermute | solution.py:63
  226.7 22.0 %collective-permute-start.49 = (bf16[48,4608]{1,0:T(8,128)(2,1)S(1)}, bf16[48,4608]{1,0:T(8,128)(2,1)S(1)}, u32[]{:S(2)}, u32[]{:S(2)}) collective-permute-start(bf16[48,4608]{1,0:T(8,128)(2,1)S(1)} %get-tuple-element.196), channel_id=1, source_target_pairs={{0,2},{2,0},{4,6},{6,4},{1,3},{3,1},{5,7},{7,5},{8,10},{10,8},{12,... | collective-permute-start | bytes 1327112 | tf_op jit(solution)/shard_map/ppermute | solution.py:63
  229.1 32.9 %collective-permute-start.55 = (bf16[48,4608]{1,0:T(8,128)(2,1)S(1)}, bf16[48,4608]{1,0:T(8,128)(2,1)S(1)}, u32[]{:S(2)}, u32[]{:S(2)}) collective-permute-start(bf16[48,4608]{1,0:T(8,128)(2,1)S(1)} %get-tuple-element.206), channel_id=1, source_target_pairs={{0,4},{2,6},{4,0},{6,2},{1,5},{3,7},{5,1},{7,3},{8,12},{10,14},{12... | collective-permute-start | bytes 1327112 | tf_op jit(solution)/shard_map/ppermute | solution.py:63
  230.5 31.5 %collective-permute-start.56 = (bf16[48,4608]{1,0:T(8,128)(2,1)S(1)}, bf16[48,4608]{1,0:T(8,128)(2,1)S(1)}, u32[]{:S(2)}, u32[]{:S(2)}) collective-permute-start(bf16[48,4608]{1,0:T(8,128)(2,1)S(1)} %get-tuple-element.207), channel_id=1, source_target_pairs={{0,6},{2,4},{4,2},{6,0},{1,7},{3,5},{5,3},{7,1},{8,14},{10,12},{12... | collective-permute-start | bytes 1327112 | tf_op jit(solution)/shard_map/ppermute | solution.py:63
  233.2 15.5 %collective-permute-start.50 = (bf16[208,768]{1,0:T(8,128)(2,1)S(1)}, bf16[208,768]{1,0:T(8,128)(2,1)S(1)}, u32[]{:S(2)}, u32[]{:S(2)}) collective-permute-start(bf16[208,768]{1,0:T(8,128)(2,1)S(1)} %get-tuple-element.197), channel_id=1, source_target_pairs={{0,16},{8,24},{16,0},{24,8},{1,17},{9,25},{17,1},{25,9},{2,18},{10... | collective-permute-start | bytes 958472 | tf_op jit(solution)/shard_map/ppermute | solution.py:63
  254.8 11.0 %collective-permute-start.52 = (bf16[64,1536]{1,0:T(8,128)(2,1)S(1)}, bf16[64,1536]{1,0:T(8,128)(2,1)S(1)}, u32[]{:S(2)}, u32[]{:S(2)}) collective-permute-start(bf16[64,1536]{1,0:T(8,128)(2,1)S(1)} %get-tuple-element.201), channel_id=1, source_target_pairs={{0,2},{2,0},{4,6},{6,4},{1,3},{3,1},{5,7},{7,5},{8,10},{10,8},{12,... | collective-permute-start | bytes 589832 | tf_op jit(solution)/shard_map/ppermute | solution.py:63
  257.6 26.6 %collective-permute-start.53 = (bf16[64,1536]{1,0:T(8,128)(2,1)S(1)}, bf16[64,1536]{1,0:T(8,128)(2,1)S(1)}, u32[]{:S(2)}, u32[]{:S(2)}) collective-permute-start(bf16[64,1536]{1,0:T(8,128)(2,1)S(1)} %get-tuple-element.202), channel_id=1, source_target_pairs={{0,4},{2,6},{4,0},{6,2},{1,5},{3,7},{5,1},{7,3},{8,12},{10,14},{12... | collective-permute-start | bytes 589832 | tf_op jit(solution)/shard_map/ppermute | solution.py:63
  259.1 25.1 %collective-permute-start.54 = (bf16[64,1536]{1,0:T(8,128)(2,1)S(1)}, bf16[64,1536]{1,0:T(8,128)(2,1)S(1)}, u32[]{:S(2)}, u32[]{:S(2)}) collective-permute-start(bf16[64,1536]{1,0:T(8,128)(2,1)S(1)} %get-tuple-element.203), channel_id=1, source_target_pairs={{0,6},{2,4},{4,2},{6,0},{1,7},{3,5},{5,3},{7,1},{8,14},{10,12},{12... | collective-permute-start | bytes 589832 | tf_op jit(solution)/shard_map/ppermute | solution.py:63
  (42 other events, 360.8 us)
